TPU v7x, 128 devices: a whole 4x4x4 slice. The times are simulated.
128 devices in a mesh: row: 16 (over x, y), col: 8 (over z, core).
Axes of the slice: x: 4, y: 4, z: 4, core: 2. Of those that a mesh axis runs over, the one named last changes fastest.
Arguments:
- b_ingest: bfloat16 [131072, 1024], P(('row', 'col')), may hold values from -6 to 6
- source_point: int32 [131072], P(('row', 'col')), may hold values from 0 to 131071, as said below
- panels: bfloat16 [2, 8, 16, 1024, 1024], P(None, None, 'row', 'col'), may hold values from -0.1875 to 0.1875
- diag_inverse: bfloat16 [2, 1024, 1024], replicated, may hold values from -1 to 1.5, as said below
Outputs:
- updated: bfloat16 [8, 16, 1024, 1024], P(None, 'row', 'col')
Inputs may be any that keep to these rules, and one draw needn't show every extreme that they name: source_point is a permutation of 0 to 131071. Say point i lies in block b = i // 1024 at offset o = i mod 1024; it belongs to the device with row index b mod 16 and col index o // (1024 / 8). The shard of source_point on each device along row+col holds exactly 8 points of every device. diag_inverse[k] is lower triangular with diagonal entries between 0.5 and 1.5.
All inputs are finite; a program needn't handle non-finite values.
Results may differ from a plain program's by a relative error of at most 0.0056.
Values may be sent and summed in bfloat16 or wider, within the bound.
No kernel may reach another device: no remote copies, remote signals or barrier semaphores. Data moves between devices by JAX's collectives and lax.ppermute only.
A program may use at most 64 MiB of HBM per device.

v0:
```python
import functools

import jax
import jax.numpy as jnp
from jax import lax
from jax.experimental import pallas as pl
from jax.experimental.pallas import tpu as pltpu
from jax.sharding import PartitionSpec as P

AXES = ("row", "col")
BF16 = jnp.bfloat16
F32 = jnp.float32
VMEM = pl.BlockSpec(memory_space=pltpu.VMEM)


def device_id(x, y, z, k):
    return (x % 4 * 4 + y % 4) * 8 + z % 4 * 2 + k


def send(value, move, only=None):
    pairs = []
    for x in range(4):
        for y in range(4):
            for z in range(4):
                for k in range(2):
                    if only is None or only(x, y, z, k):
                        pairs.append((device_id(x, y, z, k), device_id(*move(x, y, z, k))))
    return lax.ppermute(value, AXES, pairs)


def swap(kind, at):
    return (at ^ 1, 3 - at, at ^ 2)[kind]


def along_first(kind):
    return lambda x, y, z, k: (swap(kind, x), y, z, k) if k == 0 else (x, swap(kind, y), z, k)


def along_second(kind):
    return lambda x, y, z, k: (x, swap(kind, y), z, k) if k == 0 else (swap(kind, x), y, z, k)


def along_z(kind):
    return lambda x, y, z, k: (x, y, swap(kind, z), k)


def other_core(x, y, z, k):
    return (x, y, z, 1 - k)


def iota(shape, axis):
    return lax.broadcasted_iota(jnp.int32, shape, axis)


def dot(a, b, contract):
    return lax.dot_general(a, b, ((contract[:1], contract[1:]), ((), ())), preferred_element_type=F32)


def order_kernel(points_ref, rows_hbm, out_hbm, rows_ref, out_ref, perm_ref, head_ref, in_sems, out_sems):
    count = rows_ref.shape[0]
    loads = []
    for q in range(4):
        cols = pl.ds(q * 256, 256)
        loads.append(pltpu.make_async_copy(rows_hbm.at[:, cols], rows_ref.at[:, cols], in_sems.at[q]))
        loads[q].start()
    points = points_ref[...]
    block = points >> 10
    offset = points & 1023
    target = (block & 15) * 8 + (offset >> 7)
    local = (block >> 4) * 128 + (offset & 127)
    wanted = (iota((128, count), 0) == target).astype(F32)
    earlier = (iota((count, count), 0) < iota((count, count), 1)).astype(F32).astype(BF16)
    seen = dot(wanted.astype(BF16), earlier, (1, 0))
    rank = jnp.sum(wanted * seen, axis=0, keepdims=True).astype(jnp.int32)
    slot = target * 8 + rank
    perm_ref[...] = (iota((count, count), 0) == slot).astype(F32).astype(BF16)
    part = iota((128, count), 0)
    digits = jnp.where(part < 10, jnp.where(part % 2 == 0, local >> 5, local & 31), 0).astype(F32).astype(BF16)
    ids = dot(perm_ref[...], digits, (1, 1))
    stores = []
    for q in range(4):
        loads[q].wait()
        part_rows = dot(perm_ref[...], rows_ref[:, q * 256 : q * 256 + 256], (1, 0))
        out_ref[:, 384 + q * 256 : 640 + q * 256] = part_rows.astype(BF16)
        head_ref[:, q * 256 : q * 256 + 256] = part_rows[0:128]
        cols = pl.ds(384 + q * 256, 256)
        stores.append(pltpu.make_async_copy(out_ref.at[:, cols], out_hbm.at[:, cols], out_sems.at[q]))
        stores[q].start()
    lane = iota((64, 128), 1)

    def both(value, first, odd):
        tiles = [value[first + 16 * z + 8 * odd : first + 16 * z + 8 * odd + 8] for z in range(4)]
        return jnp.concatenate([t for t in tiles for _ in range(2)], axis=0)

    shared = [both(ids, 64 * t, odd) for t in range(2) for odd in range(2)]
    heads = [[both(head_ref[:, 128 * i : 128 * i + 128], 64 * t, odd) for i in range(8)] for t in range(2) for odd in range(2)]
    for r in range(16):
        x, y = r // 4, r % 4
        rows = slice(r * 64, r * 64 + 64)
        mixed = ids[rows]
        for i in range(4):
            mixed = jnp.where(lane < 2 + 2 * i, mixed, shared[i])
        out_ref[rows, 256:384] = mixed.astype(BF16)
        for t in range(2):
            cut = None
            for p in range(4):
                tiles = heads[2 * t + p // 2]
                tile, at = (tiles[y], 32 * x) if p % 2 == 0 else (tiles[4 + x], 32 * y)
                moved = pltpu.roll(tile, (32 * p - at) % 128, 1) if (32 * p - at) % 128 else tile
                cut = moved if cut is None else jnp.where(lane < 32 * p, cut, moved)
            out_ref[rows, t * 128 : t * 128 + 128] = cut.astype(BF16)
    cols = pl.ds(0, 384)
    stores.append(pltpu.make_async_copy(out_ref.at[:, cols], out_hbm.at[:, cols], out_sems.at[4]))
    stores[4].start()
    for store in stores:
        store.wait()


def compact_kernel(early_ref, own_ref, lead_ref, next_ref):
    count = early_ref.shape[0]
    pick = iota((8, 128), 0)
    lane = iota((8, 128), 1)
    weight = jnp.where(lane == 2 * pick, 32.0, jnp.where(lane == 2 * pick + 1, 1.0, 0.0))
    weight = jnp.where(pick < 5, weight, 0.0).astype(BF16)
    locals_ = dot(weight, early_ref[:, 256:384], (1, 1)).astype(jnp.int32)
    own_ref[...] = locals_
    place = iota((128, count), 0)
    for t, ref in enumerate((lead_ref, next_ref)):
        data = early_ref[:, 128 * t : 128 * t + 128]
        for odd in range(2):
            i = 1 + 2 * t + odd
            hit = (place == locals_[i : i + 1]).astype(F32).astype(BF16)
            found = dot(data, hit, (0, 1))[64 * odd : 64 * odd + 64]
            ref[:, 128 * odd : 128 * odd + 128] = found.astype(BF16)


def gather_cols(refs, scratch):
    z = lax.axis_index("col") // 2
    for ref, at in zip(refs, (z, z ^ 1, 3 - z, z ^ 2)):
        scratch[at] = ref[...]
    return jnp.concatenate([scratch[i] for i in range(4)], axis=1)


def first_kernel(p0, p1, p2, p3, inverse_ref, next_ref, own_ref, other_ref, solved_ref, second_ref, scratch):
    lead = gather_cols((p0, p1, p2, p3), scratch)
    solved = dot(lead, inverse_ref[...], (1, 1)).astype(BF16)
    solved_ref[...] = solved
    own = dot(solved, own_ref[...], (1, 1))
    other = dot(solved, other_ref[...], (1, 1))
    even = lax.axis_index("col") % 2 == 0
    low = jnp.where(even, own, other)
    high = jnp.where(even, other, own)
    second_ref[:, 0:128] = (next_ref[:, 0:128].astype(F32) - low).astype(BF16)
    second_ref[:, 128:256] = (next_ref[:, 128:256].astype(F32) - high).astype(BF16)


def second_kernel(p0, p1, p2, p3, inverse_ref, solved_ref, both_ref, scratch):
    second = gather_cols((p0, p1, p2, p3), scratch)
    solved = dot(second, inverse_ref[...], (1, 1)).astype(BF16)
    even = lax.axis_index("col") % 2 == 0
    both_ref[:, 0:1024] = jnp.where(even, solved_ref[0:32], solved_ref[32:64])
    both_ref[:, 1024:2048] = jnp.where(even, solved[0:32], solved[32:64])


def scatter_kernel(own_ref, arrived_ref, out_ref, hit_ref, rows_ref, sem):
    count = arrived_ref.shape[0]
    copy = pltpu.make_async_copy(arrived_ref.at[:, 384:1408], rows_ref, sem)
    copy.start()
    hit_ref[...] = (iota((count, count), 0) == own_ref[0:1]).astype(F32).astype(BF16)
    copy.wait()
    for q in range(4):
        cols = slice(q * 256, q * 256 + 256)
        out_ref[:, cols] = dot(hit_ref[...], rows_ref[:, cols], (1, 0)).astype(BF16)


def place_of(kind):
    row = lax.axis_index("row")
    core = lax.axis_index("col") % 2
    x, y = row // 4, row % 4
    if kind:
        core = 1 - core
    return jnp.where(core == 0, x, y), jnp.where(core == 0, y, x), core


def load_kernel(source_hbm, first_ref, second_ref, sems):
    copies = [pltpu.make_async_copy(source_hbm.at[i], ref, sems.at[i]) for i, ref in enumerate((first_ref, second_ref))]
    for copy in copies:
        copy.start()
    for copy in copies:
        copy.wait()


def heads_of(panels_ref, head_ref):
    row = lax.axis_index("row")
    col = lax.axis_index("col")
    unit = (iota((128, 1024), 1) == iota((128, 1024), 0) + col * 128).astype(F32) * -1.0
    for p in range(2):
        kept = jnp.where(row < 2, 0.0, panels_ref[p, 0, 0].astype(F32))
        head_ref[p] = jnp.where(row == p, unit, kept).astype(BF16)


def product(panels_ref, head_ref, solved_t):
    s0 = solved_t[:, 0:1024]
    s1 = solved_t[:, 1024:2048]
    head = dot(head_ref[0], s0, (1, 1)) + dot(head_ref[1], s1, (1, 1))
    tail0 = panels_ref[0, 1:8, 0].reshape(896, 1024)
    tail1 = panels_ref[1, 1:8, 0].reshape(896, 1024)
    return head, dot(tail0, s0, (1, 1)) + dot(tail1, s1, (1, 1))


def update_kernel(lines, *refs):
    count = 2 * sum(parts for _, parts in lines)
    pieces = list(refs[:count])
    panels_ref, rows_hbm, out_hbm, solved_t, head_ref, in_ref, res_ref, sems = refs[count:]
    keep = jnp.where(lax.axis_index("row") < 2, 0.0, 1.0)
    draws = []
    for which, _ in lines:
        for kind in range(2):
            _, second, core = place_of(kind)
            at = second if which == 3 else swap(which, second)
            draws.append(pl.ds(pl.multiple_of(128 * (4 * core + at), 128), 128))
    loads = [pltpu.make_async_copy(rows_hbm.at[:, :, :, d], in_ref.at[i], sems.at[0, i]) for i, d in enumerate(draws)]
    for load in loads:
        load.start()
    heads_of(panels_ref, head_ref)
    stores = []
    for n, (_, parts) in enumerate(lines):
        for kind in range(2):
            first, _, _ = place_of(kind)
            places = (first, first ^ 1, 3 - first, first ^ 2)
            held = [pieces.pop(0) for _ in range(parts)]
            for j in range(4):
                at = pl.multiple_of(128 * kind + 32 * places[j], 32)
                ref, j = (held[0], j) if parts == 1 else (held[j // 2], j % 2)
                solved_t[n, pl.ds(at, 32), :] = ref[j * 32 : j * 32 + 32, :]
        head, tail = product(panels_ref, head_ref, solved_t.at[n])
        for kind in range(2):
            i = 2 * n + kind
            loads[i].wait()
            part = slice(128 * kind, 128 * kind + 128)
            res_ref[i, 0, 0] = (in_ref[i, 0, 0].astype(F32) * keep - head[:, part]).astype(BF16)
            rest = in_ref[i, 1:8, 0].reshape(896, 128).astype(F32) - tail[:, part]
            res_ref[i, 1:8, 0] = rest.astype(BF16).reshape(7, 128, 128)
            stores.append(pltpu.make_async_copy(res_ref.at[i], out_hbm.at[:, :, :, draws[i]], sems.at[1, i]))
            stores[i].start()
    for store in stores:
        store.wait()


HBM = pl.BlockSpec(memory_space=pltpu.HBM)
ANY = pl.BlockSpec(memory_space=pl.ANY)


def launch(kernel, args, outs, scratch=(), specs=None, out_specs=None, aliases=None, limit=16, flops=0, moved=0):
    return pl.pallas_call(
        kernel,
        out_shape=[jax.ShapeDtypeStruct(s, d) for s, d in outs],
        grid=(1,),
        in_specs=specs or [VMEM] * len(args),
        out_specs=out_specs or [VMEM] * len(outs),
        scratch_shapes=list(scratch),
        input_output_aliases=aliases or {},
        compiler_params=pltpu.CompilerParams(vmem_limit_bytes=limit << 20),
        cost_estimate=pl.CostEstimate(flops=flops, bytes_accessed=moved, transcendentals=0),
    )(*args)


def spread_along(value, first, source):
    def move(kind):
        return along_first(kind) if first else along_second(kind)

    return [send(value, move(kind), source) for kind in range(3)]


def spread_first(piece):
    return spread_along(piece, True, lambda x, y, z, k: x == 0 and y == 1)


def spread_second(piece):
    return spread_along(piece, False, lambda x, y, z, k: y == 1 if k == 0 else x == 0)


def around_cols(piece):
    return (piece, send(piece, along_z(0)), send(piece, along_z(1)), send(piece, along_z(2)))


def update(lines, pieces, panels, rows):
    count = 2 * len(lines)
    kernel = functools.partial(update_kernel, lines)
    return launch(
        kernel,
        (*pieces, panels, rows),
        [((8, 1, 128, 1024), BF16)],
        [
            pltpu.VMEM((len(lines), 256, 2048), BF16),
            pltpu.VMEM((2, 128, 1024), BF16),
            pltpu.VMEM((count, 8, 1, 128, 128), BF16),
            pltpu.VMEM((count, 8, 1, 128, 128), BF16),
            pltpu.SemaphoreType.DMA((2, count)),
        ],
        specs=[VMEM] * (len(pieces) + 1) + [HBM],
        out_specs=[HBM],
        aliases={len(pieces) + 1: 0},
        limit=22,
        flops=len(lines) << 30,
        moved=2 << 20,
    )[0]


def steps(b_ingest, source_point, panels, diag_inverse):
    row = lax.axis_index("row")
    piece = panels[0, 0, 0]
    line = spread_first(piece)
    (ordered,) = launch(
        order_kernel,
        (source_point.reshape(1, 1024), b_ingest),
        [((1024, 1408), BF16)],
        [
            pltpu.VMEM((1024, 1024), BF16),
            pltpu.VMEM((1024, 1408), BF16),
            pltpu.VMEM((1024, 1024), BF16),
            pltpu.VMEM((128, 1024), F32),
            pltpu.SemaphoreType.DMA((4,)),
            pltpu.SemaphoreType.DMA((5,)),
        ],
        specs=[VMEM, HBM],
        out_specs=[HBM],
        limit=63,
        flops=3 << 30,
        moved=5 << 20,
    )
    line = jnp.where(row == 1, piece, jnp.zeros_like(piece)) + line[0] + line[1] + line[2]
    line, ordered = lax.optimization_barrier((line, ordered))
    plane = spread_second(line)
    arrived = lax.all_to_all(ordered.reshape(128, 8, 1408), AXES, split_axis=0, concat_axis=0, tiled=True)
    inverses, _ = lax.optimization_barrier((diag_inverse, ordered))
    inverses = launch(
        load_kernel,
        (inverses,),
        [((1024, 1024), BF16)] * 2,
        [pltpu.SemaphoreType.DMA((2,))],
        specs=[HBM],
        limit=6,
        moved=8 << 20,
    )
    link = line + plane[0] + plane[1] + plane[2]
    link_other = send(link, other_core)
    arrived = arrived.reshape(1024, 1408)
    own, lead, follow = launch(
        compact_kernel,
        (arrived,),
        [((8, 1024), jnp.int32), ((64, 256), BF16), ((64, 256), BF16)],
        specs=[pl.BlockSpec((1024, 384), lambda i: (0, 0))],
        limit=12,
        flops=1 << 27,
        moved=1 << 20,
    )
    solved, second = launch(
        first_kernel,
        (*around_cols(lead), inverses[0], follow, link, link_other),
        [((64, 1024), BF16), ((64, 256), BF16)],
        [pltpu.VMEM((4, 64, 256), BF16)],
        limit=12,
        flops=1 << 28,
        moved=3 << 20,
    )
    (both,) = launch(
        second_kernel,
        (*around_cols(second), inverses[1], solved),
        [((32, 2048), BF16)],
        [pltpu.VMEM((4, 64, 256), BF16)],
        limit=12,
        flops=1 << 28,
        moved=3 << 20,
    )
    (rows,) = launch(
        scatter_kernel,
        (own, arrived),
        [((1024, 1024), BF16)],
        [pltpu.VMEM((1024, 1024), BF16), pltpu.VMEM((1024, 1024), BF16), pltpu.SemaphoreType.DMA],
        specs=[VMEM, ANY],
        limit=20,
        flops=1 << 31,
        moved=4 << 20,
    )
    rows = rows.reshape(8, 1, 128, 1024)
    line = [both] + [send(both, along_first(i)) for i in range(3)]
    line = jnp.concatenate(line, axis=0)
    side0, side1 = send(line, along_second(0)), send(line, along_second(1))
    far0, far1 = send(side1[0:64], along_second(0)), send(side0[64:128], along_second(1))
    rows = update(((3, 1),), (line, send(line, other_core)), panels, rows)
    pieces = (side0, send(side0, other_core), side1, send(side1, other_core))
    rows = update(((0, 1), (1, 1)), pieces, panels, rows)
    pieces = (far0, far1, send(far0, other_core), send(far1, other_core))
    return update(((2, 2),), pieces, panels, rows)


def solution(mesh):
    return jax.shard_map(
        steps,
        mesh=mesh,
        in_specs=(
            P(("row", "col"), None),
            P(("row", "col")),
            P(None, None, "row", "col", None),
            P(),
        ),
        out_specs=P(None, "row", "col", None),
        check_vma=False,
    )
```

profile of v0, /device:TPU:1, one launch (start us, length us, event | category | flops | bytes accessed | tf_op | source)
XLA Modules:
  0.0 125.6 jit_solution(3250388697442930592)
XLA Ops:
  0.0 1.0 slice_bitcast_fusion
  1.7 1.3 %collective-permute-start = (bf16[128,1024]{1,0:T(8,128)(2,1)S(1)}, bf16[128,1024]{1,0:T(8,128)(2,1)S(1)}, u32[]{:S(2)}, u32[]{:S(2)}) collective-permute-start(bf16[128,1024]{1,0:T(8,128)(2,1)S(1)} %slice_bitcast_fusion), channel_id=1, source_target_pairs={{8,40},{9,1},{10,42},{11,3},{12,44},{13,5},{14,46},{15,7}} | collective-permute-start | bytes 786440 | tf_op jit(solution)/shard_map/ppermute | solution.py:28
  3.0 1.4 %collective-permute-start.2 = (bf16[128,1024]{1,0:T(8,128)(2,1)S(1)}, bf16[128,1024]{1,0:T(8,128)(2,1)}, u32[]{:S(2)}, u32[]{:S(2)}) collective-permute-start(bf16[128,1024]{1,0:T(8,128)(2,1)S(1)} %slice_bitcast_fusion), channel_id=1, source_target_pairs={{8,72},{9,25},{10,74},{11,27},{12,76},{13,29},{14,78},{15,31}} | collective-permute-start | bytes 786440 | tf_op jit(solution)/shard_map/ppermute | solution.py:28
  4.3 8.0 %shard_map.46 = bf16[1024,1408]{1,0:T(8,128)(2,1)} custom-call(s32[1,1024]{1,0:T(1,128)} %bitcast.12, bf16[1024,1024]{1,0:T(8,128)(2,1)} %rows_hbm.1), custom_call_target="tpu_custom_call" | custom-call | flops 3221225472 | bytes 5242880 | tf_op jit(solution)/shard_map/pallas_call | solution.py:255
  12.4 1.1 add_add_fusion.1
  13.4 12.2 %all-to-all-start = ((bf16[128,8,1408]{2,1,0:T(8,128)(2,1)}), bf16[128,8,1408]{2,1,0:T(8,128)(2,1)S(1)}, u32[]{:S(2)}, u32[]{:S(2)}) async-start(bf16[128,8,1408]{2,1,0:T(8,128)(2,1)} %bitcast.11), calls=%async_computation | async-start | bytes 5767168 | tf_op jit(solution)/shard_map/all_to_all | solution.py:335
  25.7 4.8 %collective-permute-start.8 = (bf16[128,1024]{1,0:T(8,128)(2,1)S(1)}, bf16[128,1024]{1,0:T(8,128)(2,1)S(1)}, u32[]{:S(2)}, u32[]{:S(2)}) collective-permute-start(bf16[128,1024]{1,0:T(8,128)(2,1)S(1)} %add_add_fusion.1), channel_id=1, source_target_pairs={{1,65},{3,67},{5,69},{7,71},{8,24},{9,73},{10,26},{11,75},{12,28},... | collective-permute-start | bytes 786440 | tf_op jit(solution)/shard_map/ppermute | solution.py:28
  30.5 1.3 %collective-permute-start.7 = (bf16[128,1024]{1,0:T(8,128)(2,1)S(1)}, bf16[128,1024]{1,0:T(8,128)(2,1)S(1)}, u32[]{:S(2)}, u32[]{:S(2)}) collective-permute-start(bf16[128,1024]{1,0:T(8,128)(2,1)S(1)} %add_add_fusion.1), channel_id=1, source_target_pairs={{1,97},{3,99},{5,101},{7,103},{8,16},{9,105},{10,18},{11,107},{12,... | collective-permute-start | bytes 786440 | tf_op jit(solution)/shard_map/ppermute | solution.py:28
  31.8 1.3 %collective-permute-start.6 = (bf16[128,1024]{1,0:T(8,128)(2,1)S(1)}, bf16[128,1024]{1,0:T(8,128)(2,1)S(1)}, u32[]{:S(2)}, u32[]{:S(2)}) collective-permute-start(bf16[128,1024]{1,0:T(8,128)(2,1)S(1)} %add_add_fusion.1), channel_id=1, source_target_pairs={{1,33},{3,35},{5,37},{7,39},{8,0},{9,41},{10,2},{11,43},{12,4},{13... | collective-permute-start | bytes 786440 | tf_op jit(solution)/shard_map/ppermute | solution.py:28
  33.1 26.1 %collective-permute-done.8 = bf16[128,1024]{1,0:T(8,128)(2,1)S(1)} collective-permute-done((bf16[128,1024]{1,0:T(8,128)(2,1)S(1)}, bf16[128,1024]{1,0:T(8,128)(2,1)S(1)}, u32[]{:S(2)}, u32[]{:S(2)}) %collective-permute-start.8) | collective-permute-done | bytes 262176 | tf_op jit(solution)/shard_map/ppermute | solution.py:28
  59.2 2.8 %collective-permute-done.6 = bf16[128,1024]{1,0:T(8,128)(2,1)S(1)} collective-permute-done((bf16[128,1024]{1,0:T(8,128)(2,1)S(1)}, bf16[128,1024]{1,0:T(8,128)(2,1)S(1)}, u32[]{:S(2)}, u32[]{:S(2)}) %collective-permute-start.6) | collective-permute-done | bytes 262176 | tf_op jit(solution)/shard_map/ppermute | solution.py:28
  62.1 2.6 %collective-permute-start.9 = (bf16[128,1024]{1,0:T(8,128)(2,1)S(1)}, bf16[128,1024]{1,0:T(8,128)(2,1)S(1)}, u32[]{:S(2)}, u32[]{:S(2)}) collective-permute-start(bf16[128,1024]{1,0:T(8,128)(2,1)S(1)} %add_add_fusion.own_ref), channel_id=1, source_target_pairs={{0,1},{1,0},{2,3},{3,2},{4,5},{5,4},{6,7},{7,6},{8,9},{9,8},{10,11... | collective-permute-start | bytes 786440 | tf_op jit(solution)/shard_map/ppermute | solution.py:28
  65.3 3.5 %collective-permute-start.5 = (bf16[64,256]{1,0:T(8,128)(2,1)S(1)}, bf16[64,256]{1,0:T(8,128)(2,1)S(1)}, u32[]{:S(2)}, u32[]{:S(2)}) collective-permute-start(bf16[64,256]{1,0:T(8,128)(2,1)S(1)} %get-tuple-element.16.p0), channel_id=1, source_target_pairs={{0,4},{1,5},{2,6},{3,7},{4,0},{5,1},{6,2},{7,3},{8,12},{9,13},{10,... | collective-permute-start | bytes 98312 | tf_op jit(solution)/shard_map/ppermute | solution.py:28
  69.6 2.2 %copy-done.1 = bf16[2,1024,1024]{2,1,0:T(8,128)(2,1)S(1)} copy-done((bf16[2,1024,1024]{2,1,0:T(8,128)(2,1)S(1)}, bf16[2,1024,1024]{2,1,0:T(8,128)(2,1)}, u32[]{:S(2)}) %copy-start.1) | copy-done | bytes 4194328
  73.7 2.5 %collective-permute-start.12 = (bf16[64,256]{1,0:T(8,128)(2,1)S(1)}, bf16[64,256]{1,0:T(8,128)(2,1)S(1)}, u32[]{:S(2)}, u32[]{:S(2)}) collective-permute-start(bf16[64,256]{1,0:T(8,128)(2,1)S(1)} %get-tuple-element.21.p0), channel_id=1, source_target_pairs={{0,4},{1,5},{2,6},{3,7},{4,0},{5,1},{6,2},{7,3},{8,12},{9,13},{10,... | collective-permute-start | bytes 98312 | tf_op jit(solution)/shard_map/ppermute | solution.py:28
  76.6 1.5 %collective-permute-done.12.p3 = bf16[64,256]{1,0:T(8,128)(2,1)S(1)} collective-permute-done((bf16[64,256]{1,0:T(8,128)(2,1)S(1)}, bf16[64,256]{1,0:T(8,128)(2,1)S(1)}, u32[]{:S(2)}, u32[]{:S(2)}) %collective-permute-start.12) | collective-permute-done | bytes 32800 | tf_op jit(solution)/shard_map/ppermute | solution.py:28
  78.1 2.3 %collective-permute-done.11.p2 = bf16[64,256]{1,0:T(8,128)(2,1)S(1)} collective-permute-done((bf16[64,256]{1,0:T(8,128)(2,1)S(1)}, bf16[64,256]{1,0:T(8,128)(2,1)S(1)}, u32[]{:S(2)}, u32[]{:S(2)}) %collective-permute-start.11) | collective-permute-done | bytes 32800 | tf_op jit(solution)/shard_map/ppermute | solution.py:28
  81.5 1.3 %collective-permute-start.14 = (bf16[32,2048]{1,0:T(8,128)(2,1)S(1)}, bf16[32,2048]{1,0:T(8,128)(2,1)S(1)}, u32[]{:S(2)}, u32[]{:S(2)}) collective-permute-start(bf16[32,2048]{1,0:T(8,128)(2,1)S(1)} %shard_map.50), channel_id=1, source_target_pairs={{0,96},{1,25},{2,98},{3,27},{4,100},{5,29},{6,102},{7,31},{8,104},... | collective-permute-start | bytes 393224 | tf_op jit(solution)/shard_map/ppermute | solution.py:28
  82.8 1.0 collective-permute-start.13
  83.8 2.8 %collective-permute-done.15 = bf16[32,2048]{1,0:T(8,128)(2,1)S(1)} collective-permute-done((bf16[32,2048]{1,0:T(8,128)(2,1)S(1)}, bf16[32,2048]{1,0:T(8,128)(2,1)S(1)}, u32[]{:S(2)}, u32[]{:S(2)}) %collective-permute-start.15) | collective-permute-done | bytes 131104 | tf_op jit(solution)/shard_map/ppermute | solution.py:28
  86.6 1.6 %collective-permute-done.14 = bf16[32,2048]{1,0:T(8,128)(2,1)S(1)} collective-permute-done((bf16[32,2048]{1,0:T(8,128)(2,1)S(1)}, bf16[32,2048]{1,0:T(8,128)(2,1)S(1)}, u32[]{:S(2)}, u32[]{:S(2)}) %collective-permute-start.14) | collective-permute-done | bytes 131104 | tf_op jit(solution)/shard_map/ppermute | solution.py:28
  89.1 1.6 %collective-permute-start.16 = (bf16[128,2048]{1,0:T(8,128)(2,1)S(1)}, bf16[128,2048]{1,0:T(8,128)(2,1)S(1)}, u32[]{:S(2)}, u32[]{:S(2)}) collective-permute-start(bf16[128,2048]{1,0:T(8,128)(2,1)S(1)} %pad_maximum_fusion.refs_0_), channel_id=1, source_target_pairs={{0,24},{1,97},{2,26},{3,99},{4,28},{5,101},{6,30},{7,103},{8,16},{... | collective-permute-start | bytes 1572872 | tf_op jit(solution)/shard_map/ppermute | solution.py:28
  90.6 5.5 %collective-permute-start.24 = (bf16[128,2048]{1,0:T(8,128)(2,1)S(1)}, bf16[128,2048]{1,0:T(8,128)(2,1)S(1)}, u32[]{:S(2)}, u32[]{:S(2)}) collective-permute-start(bf16[128,2048]{1,0:T(8,128)(2,1)S(1)} %pad_maximum_fusion.refs_0_), channel_id=1, source_target_pairs={{0,1},{1,0},{2,3},{3,2},{4,5},{5,4},{6,7},{7,6},{8,9},{9,8},{10,11... | collective-permute-start | bytes 1572872 | tf_op jit(solution)/shard_map/ppermute | solution.py:28
  96.2 1.2 collective-permute-done.18.refs_0_
  97.4 4.8 %collective-permute-start.22 = (bf16[128,2048]{1,0:T(8,128)(2,1)S(1)}, bf16[128,2048]{1,0:T(8,128)(2,1)S(1)}, u32[]{:S(2)}, u32[]{:S(2)}) collective-permute-start(bf16[128,2048]{1,0:T(8,128)(2,1)S(1)} %collective-permute-done.18.refs_0_), channel_id=1, source_target_pairs={{0,1},{1,0},{2,3},{3,2},{4,5},{5,4},{6,7},{7,6},{8,9},{9,8},{10,11... | collective-permute-start | bytes 1572872 | tf_op jit(solution)/shard_map/ppermute | solution.py:28
  102.2 1.9 %collective-permute-start.23 = (bf16[128,2048]{1,0:T(8,128)(2,1)S(1)}, bf16[128,2048]{1,0:T(8,128)(2,1)S(1)}, u32[]{:S(2)}, u32[]{:S(2)}) collective-permute-start(bf16[128,2048]{1,0:T(8,128)(2,1)S(1)} %collective-permute-done.16.refs_2_), channel_id=1, source_target_pairs={{0,1},{1,0},{2,3},{3,2},{4,5},{5,4},{6,7},{7,6},{8,9},{9,8},{10,11... | collective-permute-start | bytes 1572872 | tf_op jit(solution)/shard_map/ppermute | solution.py:28
  104.1 1.6 %collective-permute-start.19 = (bf16[64,2048]{1,0:T(8,128)(2,1)S(1)}, bf16[64,2048]{1,0:T(8,128)(2,1)S(1)}, u32[]{:S(2)}, u32[]{:S(2)}) collective-permute-start(bf16[64,2048]{1,0:T(8,128)(2,1)S(1)} %slice.13), channel_id=1, source_target_pairs={{0,24},{1,97},{2,26},{3,99},{4,28},{5,101},{6,30},{7,103},{8,16},{... | collective-permute-start | bytes 786440 | tf_op jit(solution)/shard_map/ppermute | solution.py:28
  106.0 4.5 %shard_map.51 = bf16[1024,1024]{1,0:T(8,128)(2,1)} custom-call(s32[8,1024]{1,0:T(8,128)S(1)} %get-tuple-element.24.own_ref, bf16[1024,1408]{1,0:T(8,128)(2,1)S(1)} %bitcast.9), custom_call_target="tpu_custom_call" | custom-call | flops 2147483648 | bytes 4194304 | tf_op jit(solution)/shard_map/pallas_call | solution.py:255
  111.8 1.5 %collective-permute-start.20 = (bf16[64,2048]{1,0:T(8,128)(2,1)S(1)}, bf16[64,2048]{1,0:T(8,128)(2,1)S(1)}, u32[]{:S(2)}, u32[]{:S(2)}) collective-permute-start(bf16[64,2048]{1,0:T(8,128)(2,1)S(1)} %collective-permute-done.17.refs_0_), channel_id=1, source_target_pairs={{0,1},{1,0},{2,3},{3,2},{4,5},{5,4},{6,7},{7,6},{8,9},{9,8},{10,11... | collective-permute-start | bytes 786440 | tf_op jit(solution)/shard_map/ppermute | solution.py:28
  113.3 3.2 %shard_map.52.refs_5_ = bf16[8,1,128,1024]{3,2,1,0:T(8,128)(2,1)} custom-call(bf16[128,2048]{1,0:T(8,128)(2,1)S(1)} %pad_maximum_fusion.refs_0_, bf16[128,2048]{1,0:T(8,128)(2,1)S(1)} %collective-permute-done.24.refs_1_, bf16[2,8,1,128,1024]{4,3,2,1,0:T(8,128)(2,1)S(1)} %copy-done, bf16[8,1,128,1024]{3,2,1,0:T(8,128)(2,1)} %bitcast.10), custom_call_target="tpu_custom_call", output_to_operand_aliasing={{}: (3, {})} | custom-call | flops 1073741824 | bytes 2097152 | tf_op jit(solution)/shard_map/pallas_call | solution.py:255
  116.6 5.5 %shard_map.53.refs_5_ = bf16[8,1,128,1024]{3,2,1,0:T(8,128)(2,1)} custom-call(bf16[128,2048]{1,0:T(8,128)(2,1)S(1)} %collective-permute-done.18.refs_0_, bf16[128,2048]{1,0:T(8,128)(2,1)S(1)} %collective-permute-done.22.refs_1_, bf16[128,2048]{1,0:T(8,128)(2,1)S(1)} %collective-permute-done.16.refs_2_, ...), custom_call_target="tpu_custom_call", output_to_operand_aliasing={{}: (5, {})} | custom-call | flops 2147483648 | bytes 2097152 | tf_op jit(solution)/shard_map/pallas_call | solution.py:255
  122.2 3.2 %shard_map.54 = bf16[8,1,128,1024]{3,2,1,0:T(8,128)(2,1)} custom-call(bf16[64,2048]{1,0:T(8,128)(2,1)S(1)} %collective-permute-done.17.refs_0_, bf16[64,2048]{1,0:T(8,128)(2,1)S(1)} %collective-permute-done.19.refs_1_, bf16[64,2048]{1,0:T(8,128)(2,1)S(1)} %collective-permute-done.20.refs_2_, ...), custom_call_target="tpu_custom_call", output_to_operand_aliasing={{}: (5, {})} | custom-call | flops 1073741824 | bytes 2097152 | tf_op jit(solution)/shard_map/pallas_call | solution.py:255
  (39 shorter events, 8.2 us)
Async XLA Ops:
  1.0 11.4 %collective-permute-start.1 = (bf16[128,1024]{1,0:T(8,128)(2,1)S(1)}, bf16[128,1024]{1,0:T(8,128)(2,1)S(1)}, u32[]{:S(2)}, u32[]{:S(2)}) collective-permute-start(bf16[128,1024]{1,0:T(8,128)(2,1)S(1)} %slice_bitcast_fusion), channel_id=1, source_target_pairs={{8,104},{9,17},{10,106},{11,19},{12,108},{13,21},{14,110},{15,23}} | collective-permute-start | bytes 786440 | tf_op jit(solution)/shard_map/ppermute | solution.py:28
  1.7 10.7 %collective-permute-start = (bf16[128,1024]{1,0:T(8,128)(2,1)S(1)}, bf16[128,1024]{1,0:T(8,128)(2,1)S(1)}, u32[]{:S(2)}, u32[]{:S(2)}) collective-permute-start(bf16[128,1024]{1,0:T(8,128)(2,1)S(1)} %slice_bitcast_fusion), channel_id=1, source_target_pairs={{8,40},{9,1},{10,42},{11,3},{12,44},{13,5},{14,46},{15,7}} | collective-permute-start | bytes 786440 | tf_op jit(solution)/shard_map/ppermute | solution.py:28
  3.0 9.4 %collective-permute-start.2 = (bf16[128,1024]{1,0:T(8,128)(2,1)S(1)}, bf16[128,1024]{1,0:T(8,128)(2,1)}, u32[]{:S(2)}, u32[]{:S(2)}) collective-permute-start(bf16[128,1024]{1,0:T(8,128)(2,1)S(1)} %slice_bitcast_fusion), channel_id=1, source_target_pairs={{8,72},{9,25},{10,74},{11,27},{12,76},{13,29},{14,78},{15,31}} | collective-permute-start | bytes 786440 | tf_op jit(solution)/shard_map/ppermute | solution.py:28
  13.4 51.2 %all-to-all-start = ((bf16[128,8,1408]{2,1,0:T(8,128)(2,1)}), bf16[128,8,1408]{2,1,0:T(8,128)(2,1)S(1)}, u32[]{:S(2)}, u32[]{:S(2)}) async-start(bf16[128,8,1408]{2,1,0:T(8,128)(2,1)} %bitcast.11), calls=%async_computation | async-start | bytes 5767168 | tf_op jit(solution)/shard_map/all_to_all | solution.py:335
  25.7 33.6 %collective-permute-start.8 = (bf16[128,1024]{1,0:T(8,128)(2,1)S(1)}, bf16[128,1024]{1,0:T(8,128)(2,1)S(1)}, u32[]{:S(2)}, u32[]{:S(2)}) collective-permute-start(bf16[128,1024]{1,0:T(8,128)(2,1)S(1)} %add_add_fusion.1), channel_id=1, source_target_pairs={{1,65},{3,67},{5,69},{7,71},{8,24},{9,73},{10,26},{11,75},{12,28},... | collective-permute-start | bytes 786440 | tf_op jit(solution)/shard_map/ppermute | solution.py:28
  30.5 28.8 %collective-permute-start.7 = (bf16[128,1024]{1,0:T(8,128)(2,1)S(1)}, bf16[128,1024]{1,0:T(8,128)(2,1)S(1)}, u32[]{:S(2)}, u32[]{:S(2)}) collective-permute-start(bf16[128,1024]{1,0:T(8,128)(2,1)S(1)} %add_add_fusion.1), channel_id=1, source_target_pairs={{1,97},{3,99},{5,101},{7,103},{8,16},{9,105},{10,18},{11,107},{12,... | collective-permute-start | bytes 786440 | tf_op jit(solution)/shard_map/ppermute | solution.py:28
  31.8 30.3 %collective-permute-start.6 = (bf16[128,1024]{1,0:T(8,128)(2,1)S(1)}, bf16[128,1024]{1,0:T(8,128)(2,1)S(1)}, u32[]{:S(2)}, u32[]{:S(2)}) collective-permute-start(bf16[128,1024]{1,0:T(8,128)(2,1)S(1)} %add_add_fusion.1), channel_id=1, source_target_pairs={{1,33},{3,35},{5,37},{7,39},{8,0},{9,41},{10,2},{11,43},{12,4},{13... | collective-permute-start | bytes 786440 | tf_op jit(solution)/shard_map/ppermute | solution.py:28
  62.1 10.0 %collective-permute-start.9 = (bf16[128,1024]{1,0:T(8,128)(2,1)S(1)}, bf16[128,1024]{1,0:T(8,128)(2,1)S(1)}, u32[]{:S(2)}, u32[]{:S(2)}) collective-permute-start(bf16[128,1024]{1,0:T(8,128)(2,1)S(1)} %add_add_fusion.own_ref), channel_id=1, source_target_pairs={{0,1},{1,0},{2,3},{3,2},{4,5},{5,4},{6,7},{7,6},{8,9},{9,8},{10,11... | collective-permute-start | bytes 786440 | tf_op jit(solution)/shard_map/ppermute | solution.py:28
  65.3 6.8 %collective-permute-start.5 = (bf16[64,256]{1,0:T(8,128)(2,1)S(1)}, bf16[64,256]{1,0:T(8,128)(2,1)S(1)}, u32[]{:S(2)}, u32[]{:S(2)}) collective-permute-start(bf16[64,256]{1,0:T(8,128)(2,1)S(1)} %get-tuple-element.16.p0), channel_id=1, source_target_pairs={{0,4},{1,5},{2,6},{3,7},{4,0},{5,1},{6,2},{7,3},{8,12},{9,13},{10,... | collective-permute-start | bytes 98312 | tf_op jit(solution)/shard_map/ppermute | solution.py:28
  68.8 4.0 %collective-permute-start.4 = (bf16[64,256]{1,0:T(8,128)(2,1)S(1)}, bf16[64,256]{1,0:T(8,128)(2,1)S(1)}, u32[]{:S(2)}, u32[]{:S(2)}) collective-permute-start(bf16[64,256]{1,0:T(8,128)(2,1)S(1)} %get-tuple-element.16.p0), channel_id=1, source_target_pairs={{0,6},{1,7},{2,4},{3,5},{4,2},{5,3},{6,0},{7,1},{8,14},{9,15},{10,... | collective-permute-start | bytes 98312 | tf_op jit(solution)/shard_map/ppermute | solution.py:28
  69.2 3.6 %collective-permute-start.3 = (bf16[64,256]{1,0:T(8,128)(2,1)S(1)}, bf16[64,256]{1,0:T(8,128)(2,1)S(1)}, u32[]{:S(2)}, u32[]{:S(2)}) collective-permute-start(bf16[64,256]{1,0:T(8,128)(2,1)S(1)} %get-tuple-element.16.p0), channel_id=1, source_target_pairs={{0,2},{1,3},{2,0},{3,1},{4,6},{5,7},{6,4},{7,5},{8,10},{9,11},{10,... | collective-permute-start | bytes 98312 | tf_op jit(solution)/shard_map/ppermute | solution.py:28
  69.6 2.2 %copy-start.1 = (bf16[2,1024,1024]{2,1,0:T(8,128)(2,1)S(1)}, bf16[2,1024,1024]{2,1,0:T(8,128)(2,1)}, u32[]{:S(2)}) copy-start(bf16[2,1024,1024]{2,1,0:T(8,128)(2,1)} %source_hbm) | copy-start | bytes 12582916
  73.7 4.3 %collective-permute-start.12 = (bf16[64,256]{1,0:T(8,128)(2,1)S(1)}, bf16[64,256]{1,0:T(8,128)(2,1)S(1)}, u32[]{:S(2)}, u32[]{:S(2)}) collective-permute-start(bf16[64,256]{1,0:T(8,128)(2,1)S(1)} %get-tuple-element.21.p0), channel_id=1, source_target_pairs={{0,4},{1,5},{2,6},{3,7},{4,0},{5,1},{6,2},{7,3},{8,12},{9,13},{10,... | collective-permute-start | bytes 98312 | tf_op jit(solution)/shard_map/ppermute | solution.py:28
  76.2 4.1 %collective-permute-start.11 = (bf16[64,256]{1,0:T(8,128)(2,1)S(1)}, bf16[64,256]{1,0:T(8,128)(2,1)S(1)}, u32[]{:S(2)}, u32[]{:S(2)}) collective-permute-start(bf16[64,256]{1,0:T(8,128)(2,1)S(1)} %get-tuple-element.21.p0), channel_id=1, source_target_pairs={{0,6},{1,7},{2,4},{3,5},{4,2},{5,3},{6,0},{7,1},{8,14},{9,15},{10,... | collective-permute-start | bytes 98312 | tf_op jit(solution)/shard_map/ppermute | solution.py:28
  76.6 3.7 %collective-permute-start.10 = (bf16[64,256]{1,0:T(8,128)(2,1)S(1)}, bf16[64,256]{1,0:T(8,128)(2,1)S(1)}, u32[]{:S(2)}, u32[]{:S(2)}) collective-permute-start(bf16[64,256]{1,0:T(8,128)(2,1)S(1)} %get-tuple-element.21.p0), channel_id=1, source_target_pairs={{0,2},{1,3},{2,0},{3,1},{4,6},{5,7},{6,4},{7,5},{8,10},{9,11},{10,... | collective-permute-start | bytes 98312 | tf_op jit(solution)/shard_map/ppermute | solution.py:28
  81.1 5.5 %collective-permute-start.15 = (bf16[32,2048]{1,0:T(8,128)(2,1)S(1)}, bf16[32,2048]{1,0:T(8,128)(2,1)S(1)}, u32[]{:S(2)}, u32[]{:S(2)}) collective-permute-start(bf16[32,2048]{1,0:T(8,128)(2,1)S(1)} %shard_map.50), channel_id=1, source_target_pairs={{0,64},{1,17},{2,66},{3,19},{4,68},{5,21},{6,70},{7,23},{8,72},{9,... | collective-permute-start | bytes 393224 | tf_op jit(solution)/shard_map/ppermute | solution.py:28
  81.5 6.7 %collective-permute-start.14 = (bf16[32,2048]{1,0:T(8,128)(2,1)S(1)}, bf16[32,2048]{1,0:T(8,128)(2,1)S(1)}, u32[]{:S(2)}, u32[]{:S(2)}) collective-permute-start(bf16[32,2048]{1,0:T(8,128)(2,1)S(1)} %shard_map.50), channel_id=1, source_target_pairs={{0,96},{1,25},{2,98},{3,27},{4,100},{5,29},{6,102},{7,31},{8,104},... | collective-permute-start | bytes 393224 | tf_op jit(solution)/shard_map/ppermute | solution.py:28
  82.8 5.4 %collective-permute-start.13 = (bf16[32,2048]{1,0:T(8,128)(2,1)S(1)}, bf16[32,2048]{1,0:T(8,128)(2,1)S(1)}, u32[]{:S(2)}, u32[]{:S(2)}) collective-permute-start(bf16[32,2048]{1,0:T(8,128)(2,1)S(1)} %shard_map.50), channel_id=1, source_target_pairs={{0,32},{1,9},{2,34},{3,11},{4,36},{5,13},{6,38},{7,15},{8,40},{9,1... | collective-permute-start | bytes 393224 | tf_op jit(solution)/shard_map/ppermute | solution.py:28
  88.2 9.2 %collective-permute-start.18 = (bf16[128,2048]{1,0:T(8,128)(2,1)S(1)}, bf16[128,2048]{1,0:T(8,128)(2,1)S(1)}, u32[]{:S(2)}, u32[]{:S(2)}) collective-permute-start(bf16[128,2048]{1,0:T(8,128)(2,1)S(1)} %pad_maximum_fusion.refs_0_), channel_id=1, source_target_pairs={{0,8},{1,33},{2,10},{3,35},{4,12},{5,37},{6,14},{7,39},{8,0},{9,41... | collective-permute-start | bytes 1572872 | tf_op jit(solution)/shard_map/ppermute | solution.py:28
  89.1 13.1 %collective-permute-start.16 = (bf16[128,2048]{1,0:T(8,128)(2,1)S(1)}, bf16[128,2048]{1,0:T(8,128)(2,1)S(1)}, u32[]{:S(2)}, u32[]{:S(2)}) collective-permute-start(bf16[128,2048]{1,0:T(8,128)(2,1)S(1)} %pad_maximum_fusion.refs_0_), channel_id=1, source_target_pairs={{0,24},{1,97},{2,26},{3,99},{4,28},{5,101},{6,30},{7,103},{8,16},{... | collective-permute-start | bytes 1572872 | tf_op jit(solution)/shard_map/ppermute | solution.py:28
  90.6 22.7 %collective-permute-start.24 = (bf16[128,2048]{1,0:T(8,128)(2,1)S(1)}, bf16[128,2048]{1,0:T(8,128)(2,1)S(1)}, u32[]{:S(2)}, u32[]{:S(2)}) collective-permute-start(bf16[128,2048]{1,0:T(8,128)(2,1)S(1)} %pad_maximum_fusion.refs_0_), channel_id=1, source_target_pairs={{0,1},{1,0},{2,3},{3,2},{4,5},{5,4},{6,7},{7,6},{8,9},{9,8},{10,11... | collective-permute-start | bytes 1572872 | tf_op jit(solution)/shard_map/ppermute | solution.py:28
  97.4 19.2 %collective-permute-start.22 = (bf16[128,2048]{1,0:T(8,128)(2,1)S(1)}, bf16[128,2048]{1,0:T(8,128)(2,1)S(1)}, u32[]{:S(2)}, u32[]{:S(2)}) collective-permute-start(bf16[128,2048]{1,0:T(8,128)(2,1)S(1)} %collective-permute-done.18.refs_0_), channel_id=1, source_target_pairs={{0,1},{1,0},{2,3},{3,2},{4,5},{5,4},{6,7},{7,6},{8,9},{9,8},{10,11... | collective-permute-start | bytes 1572872 | tf_op jit(solution)/shard_map/ppermute | solution.py:28
  102.2 14.4 %collective-permute-start.23 = (bf16[128,2048]{1,0:T(8,128)(2,1)S(1)}, bf16[128,2048]{1,0:T(8,128)(2,1)S(1)}, u32[]{:S(2)}, u32[]{:S(2)}) collective-permute-start(bf16[128,2048]{1,0:T(8,128)(2,1)S(1)} %collective-permute-done.16.refs_2_), channel_id=1, source_target_pairs={{0,1},{1,0},{2,3},{3,2},{4,5},{5,4},{6,7},{7,6},{8,9},{9,8},{10,11... | collective-permute-start | bytes 1572872 | tf_op jit(solution)/shard_map/ppermute | solution.py:28
  104.1 6.8 %collective-permute-start.19 = (bf16[64,2048]{1,0:T(8,128)(2,1)S(1)}, bf16[64,2048]{1,0:T(8,128)(2,1)S(1)}, u32[]{:S(2)}, u32[]{:S(2)}) collective-permute-start(bf16[64,2048]{1,0:T(8,128)(2,1)S(1)} %slice.13), channel_id=1, source_target_pairs={{0,24},{1,97},{2,26},{3,99},{4,28},{5,101},{6,30},{7,103},{8,16},{... | collective-permute-start | bytes 786440 | tf_op jit(solution)/shard_map/ppermute | solution.py:28
  105.8 6.1 %collective-permute-start.17 = (bf16[64,2048]{1,0:T(8,128)(2,1)S(1)}, bf16[64,2048]{1,0:T(8,128)(2,1)S(1)}, u32[]{:S(2)}, u32[]{:S(2)}) collective-permute-start(bf16[64,2048]{1,0:T(8,128)(2,1)S(1)} %slice.12), channel_id=1, source_target_pairs={{0,8},{1,33},{2,10},{3,35},{4,12},{5,37},{6,14},{7,39},{8,0},{9,41... | collective-permute-start | bytes 786440 | tf_op jit(solution)/shard_map/ppermute | solution.py:28
  106.0 7.3 %copy-start = (bf16[2,8,1,128,1024]{4,3,2,1,0:T(8,128)(2,1)S(1)}, bf16[2,8,1,128,1024]{4,3,2,1,0:T(8,128)(2,1)}, u32[]{:S(2)}) copy-start(bf16[2,8,1,128,1024]{4,3,2,1,0:T(8,128)(2,1)} %refs_4_.3) | copy-start | bytes 12582916
  111.0 11.2 %collective-permute-start.21 = (bf16[64,2048]{1,0:T(8,128)(2,1)S(1)}, bf16[64,2048]{1,0:T(8,128)(2,1)S(1)}, u32[]{:S(2)}, u32[]{:S(2)}) collective-permute-start(bf16[64,2048]{1,0:T(8,128)(2,1)S(1)} %collective-permute-done.19.refs_1_), channel_id=1, source_target_pairs={{0,1},{1,0},{2,3},{3,2},{4,5},{5,4},{6,7},{7,6},{8,9},{9,8},{10,11... | collective-permute-start | bytes 786440 | tf_op jit(solution)/shard_map/ppermute | solution.py:28
  111.8 10.3 %collective-permute-start.20 = (bf16[64,2048]{1,0:T(8,128)(2,1)S(1)}, bf16[64,2048]{1,0:T(8,128)(2,1)S(1)}, u32[]{:S(2)}, u32[]{:S(2)}) collective-permute-start(bf16[64,2048]{1,0:T(8,128)(2,1)S(1)} %collective-permute-done.17.refs_0_), channel_id=1, source_target_pairs={{0,1},{1,0},{2,3},{3,2},{4,5},{5,4},{6,7},{7,6},{8,9},{9,8},{10,11... | collective-permute-start | bytes 786440 | tf_op jit(solution)/shard_map/ppermute | solution.py:28
where the time goes:
time: 126 us
  starting transfers between devices  54.3 us (43%)
  waiting for transfers between devices  39.4 us (31%)
  Pallas kernels  27.1 us (22%)
  local copies, waits for them, and re-layouts  3.2 us (3%)
    ppermute x25, starting transfers between devices, send(): return lax.ppermute(value, AXES, pairs)  42.1 us
    ppermute x25, waiting for transfers between devices, send(): return lax.ppermute(value, AXES, pairs)  39.4 us
    pallas_call x9, Pallas kernels, launch(): pl.pallas_call(kernel, out_shape=[jax.ShapeDtypeStruct(s, d) for s, d in...  27.1 us
    all_to_all x1, starting transfers between devices, steps(): lax.all_to_all(ordered.reshape(128, 8, 1408), AXES, split_axis=0, concat_...  12.2 us
  transfers between devices with their start and end apart: 26, of which 9 were waited for; matrix products, arithmetic and copies ran while one was open for 0% of the time, Pallas kernels for 18%

commit v1 on v0

--- a/solution.py
+++ b/solution.py
@@ -58,11 +58,8 @@
 
 def order_kernel(points_ref, rows_hbm, out_hbm, rows_ref, out_ref, perm_ref, head_ref, in_sems, out_sems):
     count = rows_ref.shape[0]
-    loads = []
-    for q in range(4):
-        cols = pl.ds(q * 256, 256)
-        loads.append(pltpu.make_async_copy(rows_hbm.at[:, cols], rows_ref.at[:, cols], in_sems.at[q]))
-        loads[q].start()
+    load = pltpu.make_async_copy(rows_hbm, rows_ref, in_sems.at[0])
+    load.start()
     points = points_ref[...]
     block = points >> 10
     offset = points & 1023
@@ -77,41 +74,39 @@
     part = iota((128, count), 0)
     digits = jnp.where(part < 10, jnp.where(part % 2 == 0, local >> 5, local & 31), 0).astype(F32).astype(BF16)
     ids = dot(perm_ref[...], digits, (1, 1))
-    stores = []
-    for q in range(4):
-        loads[q].wait()
-        part_rows = dot(perm_ref[...], rows_ref[:, q * 256 : q * 256 + 256], (1, 0))
-        out_ref[:, 384 + q * 256 : 640 + q * 256] = part_rows.astype(BF16)
-        head_ref[:, q * 256 : q * 256 + 256] = part_rows[0:128]
-        cols = pl.ds(384 + q * 256, 256)
-        stores.append(pltpu.make_async_copy(out_ref.at[:, cols], out_hbm.at[:, cols], out_sems.at[q]))
-        stores[q].start()
     lane = iota((64, 128), 1)
 
     def both(value, first, odd):
         tiles = [value[first + 16 * z + 8 * odd : first + 16 * z + 8 * odd + 8] for z in range(4)]
         return jnp.concatenate([t for t in tiles for _ in range(2)], axis=0)
 
-    shared = [both(ids, 64 * t, odd) for t in range(2) for odd in range(2)]
-    heads = [[both(head_ref[:, 128 * i : 128 * i + 128], 64 * t, odd) for i in range(8)] for t in range(2) for odd in range(2)]
-    for r in range(16):
-        x, y = r // 4, r % 4
-        rows = slice(r * 64, r * 64 + 64)
-        mixed = ids[rows]
-        for i in range(4):
-            mixed = jnp.where(lane < 2 + 2 * i, mixed, shared[i])
-        out_ref[rows, 256:384] = mixed.astype(BF16)
-        for t in range(2):
-            cut = None
-            for p in range(4):
-                tiles = heads[2 * t + p // 2]
-                tile, at = (tiles[y], 32 * x) if p % 2 == 0 else (tiles[4 + x], 32 * y)
-                moved = pltpu.roll(tile, (32 * p - at) % 128, 1) if (32 * p - at) % 128 else tile
-                cut = moved if cut is None else jnp.where(lane < 32 * p, cut, moved)
-            out_ref[rows, t * 128 : t * 128 + 128] = cut.astype(BF16)
-    cols = pl.ds(0, 384)
-    stores.append(pltpu.make_async_copy(out_ref.at[:, cols], out_hbm.at[:, cols], out_sems.at[4]))
-    stores[4].start()
+    kinds = [(64 * t, odd) for t in range(2) for odd in range(2)]
+    shared = [both(ids, *kind) for kind in kinds]
+    stores = []
+    load.wait()
+    for x in range(4):
+        chunk = slice(x * 256, x * 256 + 256)
+        part_rows = dot(perm_ref[chunk, :], rows_ref[...], (1, 0))
+        out_ref[chunk, 384:1408] = part_rows.astype(BF16)
+        if x == 0:
+            head_ref[...] = part_rows[0:128]
+        for y in range(4):
+            rows = slice(x * 256 + y * 64, x * 256 + y * 64 + 64)
+            mixed = ids[rows]
+            for i in range(4):
+                mixed = jnp.where(lane < 2 + 2 * i, mixed, shared[i])
+            out_ref[rows, 256:384] = mixed.astype(BF16)
+            for t in range(2):
+                cut = None
+                for p in range(4):
+                    tile, at = (y, 32 * x) if p % 2 == 0 else (4 + x, 32 * y)
+                    tile = both(head_ref[:, 128 * tile : 128 * tile + 128], *kinds[2 * t + p // 2])
+                    moved = pltpu.roll(tile, (32 * p - at) % 128, 1) if (32 * p - at) % 128 else tile
+                    cut = moved if cut is None else jnp.where(lane < 32 * p, cut, moved)
+                out_ref[rows, t * 128 : t * 128 + 128] = cut.astype(BF16)
+        span = pl.ds(x * 256, 256)
+        stores.append(pltpu.make_async_copy(out_ref.at[span], out_hbm.at[span], out_sems.at[x]))
+        stores[x].start()
     for store in stores:
         store.wait()
 
@@ -208,41 +203,36 @@
     return head, dot(tail0, s0, (1, 1)) + dot(tail1, s1, (1, 1))
 
 
-def update_kernel(lines, *refs):
-    count = 2 * sum(parts for _, parts in lines)
+def update_kernel(blocks, *refs):
+    count = sum(parts for _, _, parts in blocks)
     pieces = list(refs[:count])
     panels_ref, rows_hbm, out_hbm, solved_t, head_ref, in_ref, res_ref, sems = refs[count:]
     keep = jnp.where(lax.axis_index("row") < 2, 0.0, 1.0)
-    draws = []
-    for which, _ in lines:
-        for kind in range(2):
-            _, second, core = place_of(kind)
-            at = second if which == 3 else swap(which, second)
-            draws.append(pl.ds(pl.multiple_of(128 * (4 * core + at), 128), 128))
-    loads = [pltpu.make_async_copy(rows_hbm.at[:, :, :, d], in_ref.at[i], sems.at[0, i]) for i, d in enumerate(draws)]
-    for load in loads:
-        load.start()
+    draws, loads, stores = [], [], []
+    for i, (kind, which, _) in enumerate(blocks):
+        _, second, core = place_of(kind)
+        at = second if which == 3 else swap(which, second)
+        draws.append(pl.ds(pl.multiple_of(128 * (4 * core + at), 128), 128))
+        loads.append(pltpu.make_async_copy(rows_hbm.at[:, :, :, draws[i]], in_ref.at[i], sems.at[0, i]))
+        loads[i].start()
     heads_of(panels_ref, head_ref)
-    stores = []
-    for n, (_, parts) in enumerate(lines):
-        for kind in range(2):
-            first, _, _ = place_of(kind)
-            places = (first, first ^ 1, 3 - first, first ^ 2)
-            held = [pieces.pop(0) for _ in range(parts)]
-            for j in range(4):
-                at = pl.multiple_of(128 * kind + 32 * places[j], 32)
-                ref, j = (held[0], j) if parts == 1 else (held[j // 2], j % 2)
-                solved_t[n, pl.ds(at, 32), :] = ref[j * 32 : j * 32 + 32, :]
-        head, tail = product(panels_ref, head_ref, solved_t.at[n])
-        for kind in range(2):
-            i = 2 * n + kind
-            loads[i].wait()
-            part = slice(128 * kind, 128 * kind + 128)
-            res_ref[i, 0, 0] = (in_ref[i, 0, 0].astype(F32) * keep - head[:, part]).astype(BF16)
-            rest = in_ref[i, 1:8, 0].reshape(896, 128).astype(F32) - tail[:, part]
-            res_ref[i, 1:8, 0] = rest.astype(BF16).reshape(7, 128, 128)
-            stores.append(pltpu.make_async_copy(res_ref.at[i], out_hbm.at[:, :, :, draws[i]], sems.at[1, i]))
-            stores[i].start()
+    for i, (kind, _, parts) in enumerate(blocks):
+        first, _, _ = place_of(kind)
+        places = (first, first ^ 1, 3 - first, first ^ 2)
+        held = [pieces.pop(0) for _ in range(parts)]
+        for j in range(4):
+            at = pl.multiple_of(128 * i + 32 * places[j], 32)
+            ref, j = (held[0], j) if parts == 1 else (held[j // 2], j % 2)
+            solved_t[pl.ds(at, 32), :] = ref[j * 32 : j * 32 + 32, :]
+    head, tail = product(panels_ref, head_ref, solved_t)
+    for i in range(2):
+        loads[i].wait()
+        part = slice(128 * i, 128 * i + 128)
+        res_ref[i, 0, 0] = (in_ref[i, 0, 0].astype(F32) * keep - head[:, part]).astype(BF16)
+        rest = in_ref[i, 1:8, 0].reshape(896, 128).astype(F32) - tail[:, part]
+        res_ref[i, 1:8, 0] = rest.astype(BF16).reshape(7, 128, 128)
+        stores.append(pltpu.make_async_copy(res_ref.at[i], out_hbm.at[:, :, :, draws[i]], sems.at[1, i]))
+        stores[i].start()
     for store in stores:
         store.wait()
 
@@ -284,33 +274,29 @@
     return (piece, send(piece, along_z(0)), send(piece, along_z(1)), send(piece, along_z(2)))
 
 
-def update(lines, pieces, panels, rows):
-    count = 2 * len(lines)
-    kernel = functools.partial(update_kernel, lines)
+def update(blocks, pieces, panels, rows):
     return launch(
-        kernel,
+        functools.partial(update_kernel, blocks),
         (*pieces, panels, rows),
         [((8, 1, 128, 1024), BF16)],
         [
-            pltpu.VMEM((len(lines), 256, 2048), BF16),
+            pltpu.VMEM((256, 2048), BF16),
             pltpu.VMEM((2, 128, 1024), BF16),
-            pltpu.VMEM((count, 8, 1, 128, 128), BF16),
-            pltpu.VMEM((count, 8, 1, 128, 128), BF16),
-            pltpu.SemaphoreType.DMA((2, count)),
+            pltpu.VMEM((2, 8, 1, 128, 128), BF16),
+            pltpu.VMEM((2, 8, 1, 128, 128), BF16),
+            pltpu.SemaphoreType.DMA((2, 2)),
         ],
         specs=[VMEM] * (len(pieces) + 1) + [HBM],
         out_specs=[HBM],
         aliases={len(pieces) + 1: 0},
-        limit=22,
-        flops=len(lines) << 30,
+        limit=20,
+        flops=1 << 30,
         moved=2 << 20,
     )[0]
 
 
 def steps(b_ingest, source_point, panels, diag_inverse):
     row = lax.axis_index("row")
-    piece = panels[0, 0, 0]
-    line = spread_first(piece)
     (ordered,) = launch(
         order_kernel,
         (source_point.reshape(1, 1024), b_ingest),
@@ -320,8 +306,8 @@
             pltpu.VMEM((1024, 1408), BF16),
             pltpu.VMEM((1024, 1024), BF16),
             pltpu.VMEM((128, 1024), F32),
+            pltpu.SemaphoreType.DMA((1,)),
             pltpu.SemaphoreType.DMA((4,)),
-            pltpu.SemaphoreType.DMA((5,)),
         ],
         specs=[VMEM, HBM],
         out_specs=[HBM],
@@ -329,8 +315,9 @@
         flops=3 << 30,
         moved=5 << 20,
     )
+    piece = panels[0, 0, 0]
+    line = spread_first(piece)
     line = jnp.where(row == 1, piece, jnp.zeros_like(piece)) + line[0] + line[1] + line[2]
-    line, ordered = lax.optimization_barrier((line, ordered))
     plane = spread_second(line)
     arrived = lax.all_to_all(ordered.reshape(128, 8, 1408), AXES, split_axis=0, concat_axis=0, tiled=True)
     inverses, _ = lax.optimization_barrier((diag_inverse, ordered))
@@ -343,8 +330,6 @@
         limit=6,
         moved=8 << 20,
     )
-    link = line + plane[0] + plane[1] + plane[2]
-    link_other = send(link, other_core)
     arrived = arrived.reshape(1024, 1408)
     own, lead, follow = launch(
         compact_kernel,
@@ -355,6 +340,9 @@
         flops=1 << 27,
         moved=1 << 20,
     )
+    line, plane, _ = lax.optimization_barrier((line, plane, own))
+    link = line + plane[0] + plane[1] + plane[2]
+    link_other = send(link, other_core)
     solved, second = launch(
         first_kernel,
         (*around_cols(lead), inverses[0], follow, link, link_other),
@@ -388,11 +376,13 @@
     line = jnp.concatenate(line, axis=0)
     side0, side1 = send(line, along_second(0)), send(line, along_second(1))
     far0, far1 = send(side1[0:64], along_second(0)), send(side0[64:128], along_second(1))
-    rows = update(((3, 1),), (line, send(line, other_core)), panels, rows)
-    pieces = (side0, send(side0, other_core), side1, send(side1, other_core))
-    rows = update(((0, 1), (1, 1)), pieces, panels, rows)
-    pieces = (far0, far1, send(far0, other_core), send(far1, other_core))
-    return update(((2, 2),), pieces, panels, rows)
+    line_other = send(line, other_core)
+    side0_other, side1_other = send(side0, other_core), send(side1, other_core)
+    far_other = send(far0, other_core), send(far1, other_core)
+    rows = update(((0, 3, 1), (1, 3, 1)), (line, line_other), panels, rows)
+    rows = update(((0, 0, 1), (0, 1, 1)), (side0, side1), panels, rows)
+    rows = update(((1, 0, 1), (1, 1, 1)), (side0_other, side1_other), panels, rows)
+    return update(((0, 2, 2), (1, 2, 2)), (far0, far1, *far_other), panels, rows)
 
 
 def solution(mesh):

time: 126 us -> 129 us (1.024)
  waiting for transfers between devices: 39.4 us -> 43.8 us
  local copies, waits for them, and re-layouts: 3.2 us -> 1.02 us
    ppermute x25, waiting for transfers between devices: 39.4 us -> 43.8 us  [send(): return lax.ppermute(value, AXES, pairs)]
    unnamed x4, local copies, waits for them, and re-layouts: 2.19 us -> 0.01 us
    ppermute x25, starting transfers between devices: 42.1 us -> 43.4 us  [send(): return lax.ppermute(value, AXES, pairs)]
    pallas_call x9 -> x10, Pallas kernels: 27.1 us -> 26.4 us  [launch(): pl.pallas_call(kernel, out_shape=[jax.ShapeDtypeStruct(s, d) for s, d in...]
  transfers between devices with their start and end apart: 26 -> 26, of which waited for: 9 -> 9; matrix products, arithmetic and copies ran while one was open for 0% -> 2% of each run, Pallas kernels for 18% -> 12%
where the time goes in v1:
time: 129 us
  starting transfers between devices  54.9 us (43%)
  waiting for transfers between devices  43.8 us (34%)
  Pallas kernels  26.4 us (20%)
  other arithmetic  2.28 us (2%)
    ppermute x25, waiting for transfers between devices, send(): return lax.ppermute(value, AXES, pairs)  43.8 us
    ppermute x25, starting transfers between devices, send(): return lax.ppermute(value, AXES, pairs)  43.4 us
    pallas_call x10, Pallas kernels, launch(): pl.pallas_call(kernel, out_shape=[jax.ShapeDtypeStruct(s, d) for s, d in...  26.4 us
    all_to_all x1, starting transfers between devices, steps(): lax.all_to_all(ordered.reshape(128, 8, 1408), AXES, split_axis=0, concat_...  11.5 us
  transfers between devices with their start and end apart: 26, of which 9 were waited for; matrix products, arithmetic and copies ran while one was open for 2% of the time, Pallas kernels for 12%

profile of v1, /device:TPU:1, one launch (start us, length us, event | category | flops | bytes accessed | tf_op | source)
XLA Modules:
  0.0 128.7 jit_solution(8728023761699034896)
XLA Ops:
  0.0 6.4 %shard_map.46 = bf16[1024,1408]{1,0:T(8,128)(2,1)} custom-call(s32[1,1024]{1,0:T(1,128)} %bitcast.12, bf16[1024,1024]{1,0:T(8,128)(2,1)} %rows_hbm.1), custom_call_target="tpu_custom_call" | custom-call | flops 3221225472 | bytes 5242880 | tf_op jit(solution)/shard_map/pallas_call | solution.py:245
  6.4 11.5 %all-to-all-start = ((bf16[128,8,1408]{2,1,0:T(8,128)(2,1)}), bf16[128,8,1408]{2,1,0:T(8,128)(2,1)S(1)}, u32[]{:S(2)}, u32[]{:S(2)}) async-start(bf16[128,8,1408]{2,1,0:T(8,128)(2,1)} %bitcast.11), calls=%async_computation | async-start | bytes 5767168 | tf_op jit(solution)/shard_map/all_to_all | solution.py:322
  19.5 1.3 %collective-permute-start.3 = (bf16[128,1024]{1,0:T(8,128)(2,1)S(1)}, bf16[128,1024]{1,0:T(8,128)(2,1)}, u32[]{:S(2)}, u32[]{:S(2)}) collective-permute-start(bf16[128,1024]{1,0:T(8,128)(2,1)S(1)} %slice_bitcast_fusion), channel_id=1, source_target_pairs={{8,40},{9,1},{10,42},{11,3},{12,44},{13,5},{14,46},{15,7}} | collective-permute-start | bytes 786440 | tf_op jit(solution)/shard_map/ppermute | solution.py:28
  20.8 1.4 %collective-permute-start.5 = (bf16[128,1024]{1,0:T(8,128)(2,1)S(1)}, bf16[128,1024]{1,0:T(8,128)(2,1)}, u32[]{:S(2)}, u32[]{:S(2)}) collective-permute-start(bf16[128,1024]{1,0:T(8,128)(2,1)S(1)} %slice_bitcast_fusion), channel_id=1, source_target_pairs={{8,72},{9,25},{10,74},{11,27},{12,76},{13,29},{14,78},{15,31}} | collective-permute-start | bytes 786440 | tf_op jit(solution)/shard_map/ppermute | solution.py:28
  22.2 31.3 %collective-permute-done.3 = bf16[128,1024]{1,0:T(8,128)(2,1)} collective-permute-done((bf16[128,1024]{1,0:T(8,128)(2,1)S(1)}, bf16[128,1024]{1,0:T(8,128)(2,1)}, u32[]{:S(2)}, u32[]{:S(2)}) %collective-permute-start.3) | collective-permute-done | bytes 262176 | tf_op jit(solution)/shard_map/ppermute | solution.py:28
  53.5 1.2 add_add_fusion.1
  54.7 1.3 %collective-permute-start.8 = (bf16[128,1024]{1,0:T(8,128)(2,1)S(1)}, bf16[128,1024]{1,0:T(8,128)(2,1)S(1)}, u32[]{:S(2)}, u32[]{:S(2)}) collective-permute-start(bf16[128,1024]{1,0:T(8,128)(2,1)S(1)} %add_add_fusion.1), channel_id=1, source_target_pairs={{1,65},{3,67},{5,69},{7,71},{8,24},{9,73},{10,26},{11,75},{12,28},... | collective-permute-start | bytes 786440 | tf_op jit(solution)/shard_map/ppermute | solution.py:28
  56.0 2.0 %collective-permute-start.7 = (bf16[128,1024]{1,0:T(8,128)(2,1)S(1)}, bf16[128,1024]{1,0:T(8,128)(2,1)}, u32[]{:S(2)}, u32[]{:S(2)}) collective-permute-start(bf16[128,1024]{1,0:T(8,128)(2,1)S(1)} %add_add_fusion.1), channel_id=1, source_target_pairs={{1,97},{3,99},{5,101},{7,103},{8,16},{9,105},{10,18},{11,107},{12,... | collective-permute-start | bytes 786440 | tf_op jit(solution)/shard_map/ppermute | solution.py:28
  58.0 2.0 %collective-permute-start.6 = (bf16[128,1024]{1,0:T(8,128)(2,1)S(1)}, bf16[128,1024]{1,0:T(8,128)(2,1)}, u32[]{:S(2)}, u32[]{:S(2)}) collective-permute-start(bf16[128,1024]{1,0:T(8,128)(2,1)S(1)} %add_add_fusion.1), channel_id=1, source_target_pairs={{1,33},{3,35},{5,37},{7,39},{8,0},{9,41},{10,2},{11,43},{12,4},{13... | collective-permute-start | bytes 786440 | tf_op jit(solution)/shard_map/ppermute | solution.py:28
  60.7 1.9 %collective-permute-done.6 = bf16[128,1024]{1,0:T(8,128)(2,1)} collective-permute-done((bf16[128,1024]{1,0:T(8,128)(2,1)S(1)}, bf16[128,1024]{1,0:T(8,128)(2,1)}, u32[]{:S(2)}, u32[]{:S(2)}) %collective-permute-start.6) | collective-permute-done | bytes 262176 | tf_op jit(solution)/shard_map/ppermute | solution.py:28
  62.6 1.1 add_add_fusion.own_ref
  63.7 4.0 %collective-permute-start.9 = (bf16[128,1024]{1,0:T(8,128)(2,1)S(1)}, bf16[128,1024]{1,0:T(8,128)(2,1)S(1)}, u32[]{:S(2)}, u32[]{:S(2)}) collective-permute-start(bf16[128,1024]{1,0:T(8,128)(2,1)S(1)} %add_add_fusion.own_ref), channel_id=1, source_target_pairs={{0,1},{1,0},{2,3},{3,2},{4,5},{5,4},{6,7},{7,6},{8,9},{9,8},{10,11... | collective-permute-start | bytes 786440 | tf_op jit(solution)/shard_map/ppermute | solution.py:28
  67.6 3.2 %collective-permute-start.2 = (bf16[64,256]{1,0:T(8,128)(2,1)S(1)}, bf16[64,256]{1,0:T(8,128)(2,1)S(1)}, u32[]{:S(2)}, u32[]{:S(2)}) collective-permute-start(bf16[64,256]{1,0:T(8,128)(2,1)S(1)} %get-tuple-element.17.p0), channel_id=1, source_target_pairs={{0,4},{1,5},{2,6},{3,7},{4,0},{5,1},{6,2},{7,3},{8,12},{9,13},{10,... | collective-permute-start | bytes 98312 | tf_op jit(solution)/shard_map/ppermute | solution.py:28
  72.1 2.7 %collective-permute-done.1.p2 = bf16[64,256]{1,0:T(8,128)(2,1)S(1)} collective-permute-done((bf16[64,256]{1,0:T(8,128)(2,1)S(1)}, bf16[64,256]{1,0:T(8,128)(2,1)S(1)}, u32[]{:S(2)}, u32[]{:S(2)}) %collective-permute-start.1) | collective-permute-done | bytes 32800 | tf_op jit(solution)/shard_map/ppermute | solution.py:28
  75.7 1.5 %collective-permute-start.12 = (bf16[64,256]{1,0:T(8,128)(2,1)S(1)}, bf16[64,256]{1,0:T(8,128)(2,1)S(1)}, u32[]{:S(2)}, u32[]{:S(2)}) collective-permute-start(bf16[64,256]{1,0:T(8,128)(2,1)S(1)} %get-tuple-element.26.p0), channel_id=1, source_target_pairs={{0,4},{1,5},{2,6},{3,7},{4,0},{5,1},{6,2},{7,3},{8,12},{9,13},{10,... | collective-permute-start | bytes 98312 | tf_op jit(solution)/shard_map/ppermute | solution.py:28
  78.4 1.6 %collective-permute-done.12.p3 = bf16[64,256]{1,0:T(8,128)(2,1)S(1)} collective-permute-done((bf16[64,256]{1,0:T(8,128)(2,1)S(1)}, bf16[64,256]{1,0:T(8,128)(2,1)S(1)}, u32[]{:S(2)}, u32[]{:S(2)}) %collective-permute-start.12) | collective-permute-done | bytes 32800 | tf_op jit(solution)/shard_map/ppermute | solution.py:28
  80.1 1.1 collective-permute-done.11.p2
  82.0 1.6 %collective-permute-start.14 = (bf16[32,2048]{1,0:T(8,128)(2,1)S(1)}, bf16[32,2048]{1,0:T(8,128)(2,1)S(1)}, u32[]{:S(2)}, u32[]{:S(2)}) collective-permute-start(bf16[32,2048]{1,0:T(8,128)(2,1)S(1)} %shard_map.50), channel_id=1, source_target_pairs={{0,96},{1,25},{2,98},{3,27},{4,100},{5,29},{6,102},{7,31},{8,104},... | collective-permute-start | bytes 393224 | tf_op jit(solution)/shard_map/ppermute | solution.py:28
  83.6 1.0 collective-permute-start.13
  84.7 2.8 %collective-permute-done.15 = bf16[32,2048]{1,0:T(8,128)(2,1)S(1)} collective-permute-done((bf16[32,2048]{1,0:T(8,128)(2,1)S(1)}, bf16[32,2048]{1,0:T(8,128)(2,1)S(1)}, u32[]{:S(2)}, u32[]{:S(2)}) %collective-permute-start.15) | collective-permute-done | bytes 131104 | tf_op jit(solution)/shard_map/ppermute | solution.py:28
  87.4 1.1 collective-permute-done.14
  88.6 1.8 %collective-permute-start.18 = (bf16[128,2048]{1,0:T(8,128)(2,1)S(1)}, bf16[128,2048]{1,0:T(8,128)(2,1)S(1)}, u32[]{:S(2)}, u32[]{:S(2)}) collective-permute-start(bf16[128,2048]{1,0:T(8,128)(2,1)S(1)} %pad_maximum_fusion.refs_0_), channel_id=1, source_target_pairs={{0,8},{1,33},{2,10},{3,35},{4,12},{5,37},{6,14},{7,39},{8,0},{9,41... | collective-permute-start | bytes 1572872 | tf_op jit(solution)/shard_map/ppermute | solution.py:28
  90.4 2.4 %collective-permute-start.16 = (bf16[128,2048]{1,0:T(8,128)(2,1)S(1)}, bf16[128,2048]{1,0:T(8,128)(2,1)S(1)}, u32[]{:S(2)}, u32[]{:S(2)}) collective-permute-start(bf16[128,2048]{1,0:T(8,128)(2,1)S(1)} %pad_maximum_fusion.refs_0_), channel_id=1, source_target_pairs={{0,24},{1,97},{2,26},{3,99},{4,28},{5,101},{6,30},{7,103},{8,16},{... | collective-permute-start | bytes 1572872 | tf_op jit(solution)/shard_map/ppermute | solution.py:28
  92.8 5.6 %collective-permute-start.24 = (bf16[128,2048]{1,0:T(8,128)(2,1)S(1)}, bf16[128,2048]{1,0:T(8,128)(2,1)S(1)}, u32[]{:S(2)}, u32[]{:S(2)}) collective-permute-start(bf16[128,2048]{1,0:T(8,128)(2,1)S(1)} %pad_maximum_fusion.refs_0_), channel_id=1, source_target_pairs={{0,1},{1,0},{2,3},{3,2},{4,5},{5,4},{6,7},{7,6},{8,9},{9,8},{10,11... | collective-permute-start | bytes 1572872 | tf_op jit(solution)/shard_map/ppermute | solution.py:28
  98.4 6.7 %collective-permute-start.22 = (bf16[128,2048]{1,0:T(8,128)(2,1)S(1)}, bf16[128,2048]{1,0:T(8,128)(2,1)S(1)}, u32[]{:S(2)}, u32[]{:S(2)}) collective-permute-start(bf16[128,2048]{1,0:T(8,128)(2,1)S(1)} %collective-permute-done.18.refs_0_), channel_id=1, source_target_pairs={{0,1},{1,0},{2,3},{3,2},{4,5},{5,4},{6,7},{7,6},{8,9},{9,8},{10,11... | collective-permute-start | bytes 1572872 | tf_op jit(solution)/shard_map/ppermute | solution.py:28
  105.1 1.3 %collective-permute-start.23 = (bf16[128,2048]{1,0:T(8,128)(2,1)S(1)}, bf16[128,2048]{1,0:T(8,128)(2,1)S(1)}, u32[]{:S(2)}, u32[]{:S(2)}) collective-permute-start(bf16[128,2048]{1,0:T(8,128)(2,1)S(1)} %collective-permute-done.16.refs_1_), channel_id=1, source_target_pairs={{0,1},{1,0},{2,3},{3,2},{4,5},{5,4},{6,7},{7,6},{8,9},{9,8},{10,11... | collective-permute-start | bytes 1572872 | tf_op jit(solution)/shard_map/ppermute | solution.py:28
  106.4 2.7 %collective-permute-start.19 = (bf16[64,2048]{1,0:T(8,128)(2,1)S(1)}, bf16[64,2048]{1,0:T(8,128)(2,1)S(1)}, u32[]{:S(2)}, u32[]{:S(2)}) collective-permute-start(bf16[64,2048]{1,0:T(8,128)(2,1)S(1)} %slice.13), channel_id=1, source_target_pairs={{0,24},{1,97},{2,26},{3,99},{4,28},{5,101},{6,30},{7,103},{8,16},{... | collective-permute-start | bytes 786440 | tf_op jit(solution)/shard_map/ppermute | solution.py:28
  109.4 4.5 %shard_map.51 = bf16[1024,1024]{1,0:T(8,128)(2,1)} custom-call(s32[8,1024]{1,0:T(8,128)S(1)} %get-tuple-element.21.own_ref, bf16[1024,1408]{1,0:T(8,128)(2,1)S(1)} %bitcast.9), custom_call_target="tpu_custom_call" | custom-call | flops 2147483648 | bytes 4194304 | tf_op jit(solution)/shard_map/pallas_call | solution.py:245
  115.5 3.2 %shard_map.52.refs_3_ = bf16[8,1,128,1024]{3,2,1,0:T(8,128)(2,1)} custom-call(bf16[128,2048]{1,0:T(8,128)(2,1)S(1)} %pad_maximum_fusion.refs_0_, bf16[128,2048]{1,0:T(8,128)(2,1)S(1)} %collective-permute-done.24.refs_1_, bf16[2,8,1,128,1024]{4,3,2,1,0:T(8,128)(2,1)S(1)} %copy-done, bf16[8,1,128,1024]{3,2,1,0:T(8,128)(2,1)} %bitcast.10), custom_call_target="tpu_custom_call", output_to_operand_aliasing={{}: (3, {})} | custom-call | flops 1073741824 | bytes 2097152 | tf_op jit(solution)/shard_map/pallas_call | solution.py:245
  118.8 3.2 %shard_map.53.refs_3_ = bf16[8,1,128,1024]{3,2,1,0:T(8,128)(2,1)} custom-call(bf16[128,2048]{1,0:T(8,128)(2,1)S(1)} %collective-permute-done.18.refs_0_, bf16[128,2048]{1,0:T(8,128)(2,1)S(1)} %collective-permute-done.16.refs_1_, bf16[2,8,1,128,1024]{4,3,2,1,0:T(8,128)(2,1)S(1)} %copy-done, ...), custom_call_target="tpu_custom_call", output_to_operand_aliasing={{}: (3, {})} | custom-call | flops 1073741824 | bytes 2097152 | tf_op jit(solution)/shard_map/pallas_call | solution.py:245
  122.1 3.2 %shard_map.54.refs_5_ = bf16[8,1,128,1024]{3,2,1,0:T(8,128)(2,1)} custom-call(bf16[128,2048]{1,0:T(8,128)(2,1)S(1)} %collective-permute-done.22.refs_0_, bf16[128,2048]{1,0:T(8,128)(2,1)S(1)} %collective-permute-done.23.refs_1_, bf16[2,8,1,128,1024]{4,3,2,1,0:T(8,128)(2,1)S(1)} %copy-done, ...), custom_call_target="tpu_custom_call", output_to_operand_aliasing={{}: (3, {})} | custom-call | flops 1073741824 | bytes 2097152 | tf_op jit(solution)/shard_map/pallas_call | solution.py:245
  125.3 3.2 %shard_map.55 = bf16[8,1,128,1024]{3,2,1,0:T(8,128)(2,1)} custom-call(bf16[64,2048]{1,0:T(8,128)(2,1)S(1)} %collective-permute-done.17.refs_0_, bf16[64,2048]{1,0:T(8,128)(2,1)S(1)} %collective-permute-done.19.refs_1_, bf16[64,2048]{1,0:T(8,128)(2,1)S(1)} %collective-permute-done.20.refs_2_, ...), custom_call_target="tpu_custom_call", output_to_operand_aliasing={{}: (5, {})} | custom-call | flops 1073741824 | bytes 2097152 | tf_op jit(solution)/shard_map/pallas_call | solution.py:245
  (40 shorter events, 8.6 us)
Async XLA Ops:
  6.4 53.6 %all-to-all-start = ((bf16[128,8,1408]{2,1,0:T(8,128)(2,1)}), bf16[128,8,1408]{2,1,0:T(8,128)(2,1)S(1)}, u32[]{:S(2)}, u32[]{:S(2)}) async-start(bf16[128,8,1408]{2,1,0:T(8,128)(2,1)} %bitcast.11), calls=%async_computation | async-start | bytes 5767168 | tf_op jit(solution)/shard_map/all_to_all | solution.py:322
  18.9 3.4 %collective-permute-start.4 = (bf16[128,1024]{1,0:T(8,128)(2,1)S(1)}, bf16[128,1024]{1,0:T(8,128)(2,1)S(1)}, u32[]{:S(2)}, u32[]{:S(2)}) collective-permute-start(bf16[128,1024]{1,0:T(8,128)(2,1)S(1)} %slice_bitcast_fusion), channel_id=1, source_target_pairs={{8,104},{9,17},{10,106},{11,19},{12,108},{13,21},{14,110},{15,23}} | collective-permute-start | bytes 786440 | tf_op jit(solution)/shard_map/ppermute | solution.py:28
  19.5 34.0 %collective-permute-start.3 = (bf16[128,1024]{1,0:T(8,128)(2,1)S(1)}, bf16[128,1024]{1,0:T(8,128)(2,1)}, u32[]{:S(2)}, u32[]{:S(2)}) collective-permute-start(bf16[128,1024]{1,0:T(8,128)(2,1)S(1)} %slice_bitcast_fusion), channel_id=1, source_target_pairs={{8,40},{9,1},{10,42},{11,3},{12,44},{13,5},{14,46},{15,7}} | collective-permute-start | bytes 786440 | tf_op jit(solution)/shard_map/ppermute | solution.py:28
  20.8 32.7 %collective-permute-start.5 = (bf16[128,1024]{1,0:T(8,128)(2,1)S(1)}, bf16[128,1024]{1,0:T(8,128)(2,1)}, u32[]{:S(2)}, u32[]{:S(2)}) collective-permute-start(bf16[128,1024]{1,0:T(8,128)(2,1)S(1)} %slice_bitcast_fusion), channel_id=1, source_target_pairs={{8,72},{9,25},{10,74},{11,27},{12,76},{13,29},{14,78},{15,31}} | collective-permute-start | bytes 786440 | tf_op jit(solution)/shard_map/ppermute | solution.py:28
  54.7 6.0 %collective-permute-start.8 = (bf16[128,1024]{1,0:T(8,128)(2,1)S(1)}, bf16[128,1024]{1,0:T(8,128)(2,1)S(1)}, u32[]{:S(2)}, u32[]{:S(2)}) collective-permute-start(bf16[128,1024]{1,0:T(8,128)(2,1)S(1)} %add_add_fusion.1), channel_id=1, source_target_pairs={{1,65},{3,67},{5,69},{7,71},{8,24},{9,73},{10,26},{11,75},{12,28},... | collective-permute-start | bytes 786440 | tf_op jit(solution)/shard_map/ppermute | solution.py:28
  56.0 4.6 %collective-permute-start.7 = (bf16[128,1024]{1,0:T(8,128)(2,1)S(1)}, bf16[128,1024]{1,0:T(8,128)(2,1)}, u32[]{:S(2)}, u32[]{:S(2)}) collective-permute-start(bf16[128,1024]{1,0:T(8,128)(2,1)S(1)} %add_add_fusion.1), channel_id=1, source_target_pairs={{1,97},{3,99},{5,101},{7,103},{8,16},{9,105},{10,18},{11,107},{12,... | collective-permute-start | bytes 786440 | tf_op jit(solution)/shard_map/ppermute | solution.py:28
  58.0 4.6 %collective-permute-start.6 = (bf16[128,1024]{1,0:T(8,128)(2,1)S(1)}, bf16[128,1024]{1,0:T(8,128)(2,1)}, u32[]{:S(2)}, u32[]{:S(2)}) collective-permute-start(bf16[128,1024]{1,0:T(8,128)(2,1)S(1)} %add_add_fusion.1), channel_id=1, source_target_pairs={{1,33},{3,35},{5,37},{7,39},{8,0},{9,41},{10,2},{11,43},{12,4},{13... | collective-permute-start | bytes 786440 | tf_op jit(solution)/shard_map/ppermute | solution.py:28
  60.0 11.4 %copy-start.1 = (bf16[2,1024,1024]{2,1,0:T(8,128)(2,1)S(1)}, bf16[2,1024,1024]{2,1,0:T(8,128)(2,1)}, u32[]{:S(2)}) copy-start(bf16[2,1024,1024]{2,1,0:T(8,128)(2,1)} %source_hbm) | copy-start | bytes 12582916
  63.7 11.1 %collective-permute-start.9 = (bf16[128,1024]{1,0:T(8,128)(2,1)S(1)}, bf16[128,1024]{1,0:T(8,128)(2,1)S(1)}, u32[]{:S(2)}, u32[]{:S(2)}) collective-permute-start(bf16[128,1024]{1,0:T(8,128)(2,1)S(1)} %add_add_fusion.own_ref), channel_id=1, source_target_pairs={{0,1},{1,0},{2,3},{3,2},{4,5},{5,4},{6,7},{7,6},{8,9},{9,8},{10,11... | collective-permute-start | bytes 786440 | tf_op jit(solution)/shard_map/ppermute | solution.py:28
  67.6 4.5 %collective-permute-start.2 = (bf16[64,256]{1,0:T(8,128)(2,1)S(1)}, bf16[64,256]{1,0:T(8,128)(2,1)S(1)}, u32[]{:S(2)}, u32[]{:S(2)}) collective-permute-start(bf16[64,256]{1,0:T(8,128)(2,1)S(1)} %get-tuple-element.17.p0), channel_id=1, source_target_pairs={{0,4},{1,5},{2,6},{3,7},{4,0},{5,1},{6,2},{7,3},{8,12},{9,13},{10,... | collective-permute-start | bytes 98312 | tf_op jit(solution)/shard_map/ppermute | solution.py:28
  70.8 4.0 %collective-permute-start.1 = (bf16[64,256]{1,0:T(8,128)(2,1)S(1)}, bf16[64,256]{1,0:T(8,128)(2,1)S(1)}, u32[]{:S(2)}, u32[]{:S(2)}) collective-permute-start(bf16[64,256]{1,0:T(8,128)(2,1)S(1)} %get-tuple-element.17.p0), channel_id=1, source_target_pairs={{0,6},{1,7},{2,4},{3,5},{4,2},{5,3},{6,0},{7,1},{8,14},{9,15},{10,... | collective-permute-start | bytes 98312 | tf_op jit(solution)/shard_map/ppermute | solution.py:28
  71.4 3.4 %collective-permute-start = (bf16[64,256]{1,0:T(8,128)(2,1)S(1)}, bf16[64,256]{1,0:T(8,128)(2,1)S(1)}, u32[]{:S(2)}, u32[]{:S(2)}) collective-permute-start(bf16[64,256]{1,0:T(8,128)(2,1)S(1)} %get-tuple-element.17.p0), channel_id=1, source_target_pairs={{0,2},{1,3},{2,0},{3,1},{4,6},{5,7},{6,4},{7,5},{8,10},{9,11},{10,... | collective-permute-start | bytes 98312 | tf_op jit(solution)/shard_map/ppermute | solution.py:28
  75.7 4.3 %collective-permute-start.12 = (bf16[64,256]{1,0:T(8,128)(2,1)S(1)}, bf16[64,256]{1,0:T(8,128)(2,1)S(1)}, u32[]{:S(2)}, u32[]{:S(2)}) collective-permute-start(bf16[64,256]{1,0:T(8,128)(2,1)S(1)} %get-tuple-element.26.p0), channel_id=1, source_target_pairs={{0,4},{1,5},{2,6},{3,7},{4,0},{5,1},{6,2},{7,3},{8,12},{9,13},{10,... | collective-permute-start | bytes 98312 | tf_op jit(solution)/shard_map/ppermute | solution.py:28
  77.2 4.0 %collective-permute-start.11 = (bf16[64,256]{1,0:T(8,128)(2,1)S(1)}, bf16[64,256]{1,0:T(8,128)(2,1)S(1)}, u32[]{:S(2)}, u32[]{:S(2)}) collective-permute-start(bf16[64,256]{1,0:T(8,128)(2,1)S(1)} %get-tuple-element.26.p0), channel_id=1, source_target_pairs={{0,6},{1,7},{2,4},{3,5},{4,2},{5,3},{6,0},{7,1},{8,14},{9,15},{10,... | collective-permute-start | bytes 98312 | tf_op jit(solution)/shard_map/ppermute | solution.py:28
  77.9 3.3 %collective-permute-start.10 = (bf16[64,256]{1,0:T(8,128)(2,1)S(1)}, bf16[64,256]{1,0:T(8,128)(2,1)S(1)}, u32[]{:S(2)}, u32[]{:S(2)}) collective-permute-start(bf16[64,256]{1,0:T(8,128)(2,1)S(1)} %get-tuple-element.26.p0), channel_id=1, source_target_pairs={{0,2},{1,3},{2,0},{3,1},{4,6},{5,7},{6,4},{7,5},{8,10},{9,11},{10,... | collective-permute-start | bytes 98312 | tf_op jit(solution)/shard_map/ppermute | solution.py:28
  81.9 5.5 %collective-permute-start.15 = (bf16[32,2048]{1,0:T(8,128)(2,1)S(1)}, bf16[32,2048]{1,0:T(8,128)(2,1)S(1)}, u32[]{:S(2)}, u32[]{:S(2)}) collective-permute-start(bf16[32,2048]{1,0:T(8,128)(2,1)S(1)} %shard_map.50), channel_id=1, source_target_pairs={{0,64},{1,17},{2,66},{3,19},{4,68},{5,21},{6,70},{7,23},{8,72},{9,... | collective-permute-start | bytes 393224 | tf_op jit(solution)/shard_map/ppermute | solution.py:28
  82.0 6.5 %collective-permute-start.14 = (bf16[32,2048]{1,0:T(8,128)(2,1)S(1)}, bf16[32,2048]{1,0:T(8,128)(2,1)S(1)}, u32[]{:S(2)}, u32[]{:S(2)}) collective-permute-start(bf16[32,2048]{1,0:T(8,128)(2,1)S(1)} %shard_map.50), channel_id=1, source_target_pairs={{0,96},{1,25},{2,98},{3,27},{4,100},{5,29},{6,102},{7,31},{8,104},... | collective-permute-start | bytes 393224 | tf_op jit(solution)/shard_map/ppermute | solution.py:28
  83.6 4.9 %collective-permute-start.13 = (bf16[32,2048]{1,0:T(8,128)(2,1)S(1)}, bf16[32,2048]{1,0:T(8,128)(2,1)S(1)}, u32[]{:S(2)}, u32[]{:S(2)}) collective-permute-start(bf16[32,2048]{1,0:T(8,128)(2,1)S(1)} %shard_map.50), channel_id=1, source_target_pairs={{0,32},{1,9},{2,34},{3,11},{4,36},{5,13},{6,38},{7,15},{8,40},{9,1... | collective-permute-start | bytes 393224 | tf_op jit(solution)/shard_map/ppermute | solution.py:28
  88.6 9.8 %collective-permute-start.18 = (bf16[128,2048]{1,0:T(8,128)(2,1)S(1)}, bf16[128,2048]{1,0:T(8,128)(2,1)S(1)}, u32[]{:S(2)}, u32[]{:S(2)}) collective-permute-start(bf16[128,2048]{1,0:T(8,128)(2,1)S(1)} %pad_maximum_fusion.refs_0_), channel_id=1, source_target_pairs={{0,8},{1,33},{2,10},{3,35},{4,12},{5,37},{6,14},{7,39},{8,0},{9,41... | collective-permute-start | bytes 1572872 | tf_op jit(solution)/shard_map/ppermute | solution.py:28
  90.4 14.7 %collective-permute-start.16 = (bf16[128,2048]{1,0:T(8,128)(2,1)S(1)}, bf16[128,2048]{1,0:T(8,128)(2,1)S(1)}, u32[]{:S(2)}, u32[]{:S(2)}) collective-permute-start(bf16[128,2048]{1,0:T(8,128)(2,1)S(1)} %pad_maximum_fusion.refs_0_), channel_id=1, source_target_pairs={{0,24},{1,97},{2,26},{3,99},{4,28},{5,101},{6,30},{7,103},{8,16},{... | collective-permute-start | bytes 1572872 | tf_op jit(solution)/shard_map/ppermute | solution.py:28
  92.8 22.8 %collective-permute-start.24 = (bf16[128,2048]{1,0:T(8,128)(2,1)S(1)}, bf16[128,2048]{1,0:T(8,128)(2,1)S(1)}, u32[]{:S(2)}, u32[]{:S(2)}) collective-permute-start(bf16[128,2048]{1,0:T(8,128)(2,1)S(1)} %pad_maximum_fusion.refs_0_), channel_id=1, source_target_pairs={{0,1},{1,0},{2,3},{3,2},{4,5},{5,4},{6,7},{7,6},{8,9},{9,8},{10,11... | collective-permute-start | bytes 1572872 | tf_op jit(solution)/shard_map/ppermute | solution.py:28
  98.4 23.7 %collective-permute-start.22 = (bf16[128,2048]{1,0:T(8,128)(2,1)S(1)}, bf16[128,2048]{1,0:T(8,128)(2,1)S(1)}, u32[]{:S(2)}, u32[]{:S(2)}) collective-permute-start(bf16[128,2048]{1,0:T(8,128)(2,1)S(1)} %collective-permute-done.18.refs_0_), channel_id=1, source_target_pairs={{0,1},{1,0},{2,3},{3,2},{4,5},{5,4},{6,7},{7,6},{8,9},{9,8},{10,11... | collective-permute-start | bytes 1572872 | tf_op jit(solution)/shard_map/ppermute | solution.py:28
  105.1 17.0 %collective-permute-start.23 = (bf16[128,2048]{1,0:T(8,128)(2,1)S(1)}, bf16[128,2048]{1,0:T(8,128)(2,1)S(1)}, u32[]{:S(2)}, u32[]{:S(2)}) collective-permute-start(bf16[128,2048]{1,0:T(8,128)(2,1)S(1)} %collective-permute-done.16.refs_1_), channel_id=1, source_target_pairs={{0,1},{1,0},{2,3},{3,2},{4,5},{5,4},{6,7},{7,6},{8,9},{9,8},{10,11... | collective-permute-start | bytes 1572872 | tf_op jit(solution)/shard_map/ppermute | solution.py:28
  106.4 7.5 %collective-permute-start.19 = (bf16[64,2048]{1,0:T(8,128)(2,1)S(1)}, bf16[64,2048]{1,0:T(8,128)(2,1)S(1)}, u32[]{:S(2)}, u32[]{:S(2)}) collective-permute-start(bf16[64,2048]{1,0:T(8,128)(2,1)S(1)} %slice.13), channel_id=1, source_target_pairs={{0,24},{1,97},{2,26},{3,99},{4,28},{5,101},{6,30},{7,103},{8,16},{... | collective-permute-start | bytes 786440 | tf_op jit(solution)/shard_map/ppermute | solution.py:28
  109.1 6.4 %copy-start = (bf16[2,8,1,128,1024]{4,3,2,1,0:T(8,128)(2,1)S(1)}, bf16[2,8,1,128,1024]{4,3,2,1,0:T(8,128)(2,1)}, u32[]{:S(2)}) copy-start(bf16[2,8,1,128,1024]{4,3,2,1,0:T(8,128)(2,1)} %refs_4_.1) | copy-start | bytes 12582916
  109.1 5.8 %collective-permute-start.17 = (bf16[64,2048]{1,0:T(8,128)(2,1)S(1)}, bf16[64,2048]{1,0:T(8,128)(2,1)S(1)}, u32[]{:S(2)}, u32[]{:S(2)}) collective-permute-start(bf16[64,2048]{1,0:T(8,128)(2,1)S(1)} %slice.12), channel_id=1, source_target_pairs={{0,8},{1,33},{2,10},{3,35},{4,12},{5,37},{6,14},{7,39},{8,0},{9,41... | collective-permute-start | bytes 786440 | tf_op jit(solution)/shard_map/ppermute | solution.py:28
  113.9 11.4 %collective-permute-start.21 = (bf16[64,2048]{1,0:T(8,128)(2,1)S(1)}, bf16[64,2048]{1,0:T(8,128)(2,1)S(1)}, u32[]{:S(2)}, u32[]{:S(2)}) collective-permute-start(bf16[64,2048]{1,0:T(8,128)(2,1)S(1)} %collective-permute-done.19.refs_1_), channel_id=1, source_target_pairs={{0,1},{1,0},{2,3},{3,2},{4,5},{5,4},{6,7},{7,6},{8,9},{9,8},{10,11... | collective-permute-start | bytes 786440 | tf_op jit(solution)/shard_map/ppermute | solution.py:28
  114.9 10.4 %collective-permute-start.20 = (bf16[64,2048]{1,0:T(8,128)(2,1)S(1)}, bf16[64,2048]{1,0:T(8,128)(2,1)S(1)}, u32[]{:S(2)}, u32[]{:S(2)}) collective-permute-start(bf16[64,2048]{1,0:T(8,128)(2,1)S(1)} %collective-permute-done.17.refs_0_), channel_id=1, source_target_pairs={{0,1},{1,0},{2,3},{3,2},{4,5},{5,4},{6,7},{7,6},{8,9},{9,8},{10,11... | collective-permute-start | bytes 786440 | tf_op jit(solution)/shard_map/ppermute | solution.py:28

commit v2 on v1

--- a/solution.py
+++ b/solution.py
@@ -56,10 +56,12 @@
     return lax.dot_general(a, b, ((contract[:1], contract[1:]), ((), ())), preferred_element_type=F32)
 
 
-def order_kernel(points_ref, rows_hbm, out_hbm, rows_ref, out_ref, perm_ref, head_ref, in_sems, out_sems):
+def order_kernel(points_ref, rows_hbm, panels_hbm, out_hbm, piece_ref, rows_ref, out_ref, perm_ref, head_ref, in_sems, out_sems):
     count = rows_ref.shape[0]
     load = pltpu.make_async_copy(rows_hbm, rows_ref, in_sems.at[0])
     load.start()
+    piece = pltpu.make_async_copy(panels_hbm.at[0, 0, 0], piece_ref, in_sems.at[1])
+    piece.start()
     points = points_ref[...]
     block = points >> 10
     offset = points & 1023
@@ -107,6 +109,7 @@
         span = pl.ds(x * 256, 256)
         stores.append(pltpu.make_async_copy(out_ref.at[span], out_hbm.at[span], out_sems.at[x]))
         stores[x].start()
+    piece.wait()
     for store in stores:
         store.wait()
 
@@ -157,15 +160,22 @@
     both_ref[:, 1024:2048] = jnp.where(even, solved[0:32], solved[32:64])
 
 
-def scatter_kernel(own_ref, arrived_ref, out_ref, hit_ref, rows_ref, sem):
-    count = arrived_ref.shape[0]
-    copy = pltpu.make_async_copy(arrived_ref.at[:, 384:1408], rows_ref, sem)
-    copy.start()
+def scatter_kernel(own_ref, arrived_hbm, out_hbm, hit_ref, rows_ref, out_ref, sems):
+    count = hit_ref.shape[0]
+    loads, stores = [], []
+    for q in range(4):
+        cols = pl.ds(q * 256, 256)
+        loads.append(pltpu.make_async_copy(arrived_hbm.at[:, pl.ds(384 + q * 256, 256)], rows_ref.at[:, cols], sems.at[0, q]))
+        loads[q].start()
     hit_ref[...] = (iota((count, count), 0) == own_ref[0:1]).astype(F32).astype(BF16)
-    copy.wait()
     for q in range(4):
-        cols = slice(q * 256, q * 256 + 256)
+        cols = pl.ds(q * 256, 256)
+        loads[q].wait()
         out_ref[:, cols] = dot(hit_ref[...], rows_ref[:, cols], (1, 0)).astype(BF16)
+        stores.append(pltpu.make_async_copy(out_ref.at[:, cols], out_hbm.at[:, cols], sems.at[1, q]))
+        stores[q].start()
+    for store in stores:
+        store.wait()
 
 
 def place_of(kind):
@@ -224,15 +234,17 @@
             at = pl.multiple_of(128 * i + 32 * places[j], 32)
             ref, j = (held[0], j) if parts == 1 else (held[j // 2], j % 2)
             solved_t[pl.ds(at, 32), :] = ref[j * 32 : j * 32 + 32, :]
-    head, tail = product(panels_ref, head_ref, solved_t)
-    for i in range(2):
-        loads[i].wait()
-        part = slice(128 * i, 128 * i + 128)
-        res_ref[i, 0, 0] = (in_ref[i, 0, 0].astype(F32) * keep - head[:, part]).astype(BF16)
-        rest = in_ref[i, 1:8, 0].reshape(896, 128).astype(F32) - tail[:, part]
-        res_ref[i, 1:8, 0] = rest.astype(BF16).reshape(7, 128, 128)
-        stores.append(pltpu.make_async_copy(res_ref.at[i], out_hbm.at[:, :, :, draws[i]], sems.at[1, i]))
-        stores[i].start()
+        if i % 2 == 0:
+            continue
+        head, tail = product(panels_ref, head_ref, solved_t.at[128 * i - 128 : 128 * i + 128])
+        for n in (i - 1, i):
+            loads[n].wait()
+            part = slice(128 * (n % 2), 128 * (n % 2) + 128)
+            res_ref[n, 0, 0] = (in_ref[n, 0, 0].astype(F32) * keep - head[:, part]).astype(BF16)
+            rest = in_ref[n, 1:8, 0].reshape(896, 128).astype(F32) - tail[:, part]
+            res_ref[n, 1:8, 0] = rest.astype(BF16).reshape(7, 128, 128)
+            stores.append(pltpu.make_async_copy(res_ref.at[n], out_hbm.at[:, :, :, draws[n]], sems.at[1, n]))
+            stores[n].start()
     for store in stores:
         store.wait()
 
@@ -280,11 +292,11 @@
         (*pieces, panels, rows),
         [((8, 1, 128, 1024), BF16)],
         [
-            pltpu.VMEM((256, 2048), BF16),
+            pltpu.VMEM((128 * len(blocks), 2048), BF16),
             pltpu.VMEM((2, 128, 1024), BF16),
-            pltpu.VMEM((2, 8, 1, 128, 128), BF16),
-            pltpu.VMEM((2, 8, 1, 128, 128), BF16),
-            pltpu.SemaphoreType.DMA((2, 2)),
+            pltpu.VMEM((len(blocks), 8, 1, 128, 128), BF16),
+            pltpu.VMEM((len(blocks), 8, 1, 128, 128), BF16),
+            pltpu.SemaphoreType.DMA((2, len(blocks))),
         ],
         specs=[VMEM] * (len(pieces) + 1) + [HBM],
         out_specs=[HBM],
@@ -297,25 +309,24 @@
 
 def steps(b_ingest, source_point, panels, diag_inverse):
     row = lax.axis_index("row")
-    (ordered,) = launch(
+    ordered, piece = launch(
         order_kernel,
-        (source_point.reshape(1, 1024), b_ingest),
-        [((1024, 1408), BF16)],
+        (source_point.reshape(1, 1024), b_ingest, panels),
+        [((1024, 1408), BF16), ((128, 1024), BF16)],
         [
             pltpu.VMEM((1024, 1024), BF16),
             pltpu.VMEM((1024, 1408), BF16),
             pltpu.VMEM((1024, 1024), BF16),
             pltpu.VMEM((128, 1024), F32),
-            pltpu.SemaphoreType.DMA((1,)),
+            pltpu.SemaphoreType.DMA((2,)),
             pltpu.SemaphoreType.DMA((4,)),
         ],
-        specs=[VMEM, HBM],
-        out_specs=[HBM],
+        specs=[VMEM, HBM, HBM],
+        out_specs=[HBM, VMEM],
         limit=63,
         flops=3 << 30,
         moved=5 << 20,
     )
-    piece = panels[0, 0, 0]
     line = spread_first(piece)
     line = jnp.where(row == 1, piece, jnp.zeros_like(piece)) + line[0] + line[1] + line[2]
     plane = spread_second(line)
@@ -340,7 +351,7 @@
         flops=1 << 27,
         moved=1 << 20,
     )
-    line, plane, _ = lax.optimization_barrier((line, plane, own))
+    plane, inverses = lax.optimization_barrier((plane, inverses))
     link = line + plane[0] + plane[1] + plane[2]
     link_other = send(link, other_core)
     solved, second = launch(
@@ -365,8 +376,9 @@
         scatter_kernel,
         (own, arrived),
         [((1024, 1024), BF16)],
-        [pltpu.VMEM((1024, 1024), BF16), pltpu.VMEM((1024, 1024), BF16), pltpu.SemaphoreType.DMA],
-        specs=[VMEM, ANY],
+        [pltpu.VMEM((1024, 1024), BF16)] * 3 + [pltpu.SemaphoreType.DMA((2, 4))],
+        specs=[VMEM, HBM],
+        out_specs=[HBM],
         limit=20,
         flops=1 << 31,
         moved=4 << 20,
@@ -381,8 +393,8 @@
     far_other = send(far0, other_core), send(far1, other_core)
     rows = update(((0, 3, 1), (1, 3, 1)), (line, line_other), panels, rows)
     rows = update(((0, 0, 1), (0, 1, 1)), (side0, side1), panels, rows)
-    rows = update(((1, 0, 1), (1, 1, 1)), (side0_other, side1_other), panels, rows)
-    return update(((0, 2, 2), (1, 2, 2)), (far0, far1, *far_other), panels, rows)
+    blocks = ((1, 0, 1), (1, 1, 1), (0, 2, 2), (1, 2, 2))
+    return update(blocks, (side0_other, side1_other, far0, far1, *far_other), panels, rows)
 
 
 def solution(mesh):

time: 129 us -> 134 us (1.039)
  local copies, waits for them, and re-layouts: 1.02 us -> 4.91 us
  starting transfers between devices: 54.9 us -> 51.8 us
  waiting for transfers between devices: 43.8 us -> 46.8 us
  Pallas kernels: 26.4 us -> 28.3 us
    unnamed x4 -> x14, local copies, waits for them, and re-layouts: 0.01 us -> 4.87 us
    ppermute x25, starting transfers between devices: 43.4 us -> 40.3 us  [send(): return lax.ppermute(value, AXES, pairs)]
    ppermute x25, waiting for transfers between devices: 43.8 us -> 46.8 us  [send(): return lax.ppermute(value, AXES, pairs)]
    pallas_call x10 -> x9, Pallas kernels: 26.4 us -> 28.3 us  [launch(): pl.pallas_call(kernel, out_shape=[jax.ShapeDtypeStruct(s, d) for s, d in...]
  transfers between devices with their start and end apart: 26 -> 26, of which waited for: 9 -> 8; matrix products, arithmetic and copies ran while one was open for 2% -> 1% of each run, Pallas kernels for 12% -> 11%
where the time goes in v2:
time: 134 us; the launch traced here: 133 us
  starting transfers between devices  51.8 us (39%)
  waiting for transfers between devices  46.8 us (35%)
  Pallas kernels  28.3 us (21%)
  local copies, waits for them, and re-layouts  4.91 us (4%)
    ppermute x25, waiting for transfers between devices, send(): return lax.ppermute(value, AXES, pairs)  46.8 us
    ppermute x25, starting transfers between devices, send(): return lax.ppermute(value, AXES, pairs)  40.3 us
    pallas_call x9, Pallas kernels, launch(): pl.pallas_call(kernel, out_shape=[jax.ShapeDtypeStruct(s, d) for s, d in...  28.3 us
    all_to_all x1, starting transfers between devices, steps(): lax.all_to_all(ordered.reshape(128, 8, 1408), AXES, split_axis=0, concat_...  11.5 us
    unnamed x14, local copies, waits for them, and re-layouts  4.87 us
  transfers between devices with their start and end apart: 26, of which 8 were waited for; matrix products, arithmetic and copies ran while one was open for 1% of the time, Pallas kernels for 11%

profile of v2, /device:TPU:1, one launch (start us, length us, event | category | flops | bytes accessed | tf_op | source)
XLA Modules:
  0.0 133.5 jit_solution(11668581196488985000)
XLA Ops:
  0.0 7.1 %shard_map.46 = (bf16[1024,1408]{1,0:T(8,128)(2,1)}, bf16[128,1024]{1,0:T(8,128)(2,1)}) custom-call(s32[1,1024]{1,0:T(1,128)} %bitcast.8, bf16[1024,1024]{1,0:T(8,128)(2,1)} %rows_hbm.1, bf16[2,8,1,128,1024]{4,3,2,1,0:T(8,128)(2,1)} %refs_6_.1), custom_call_target="tpu_custom_call" | custom-call | flops 3221225472 | bytes 5242880 | tf_op jit(solution)/shard_map/pallas_call | solution.py:257
  7.1 11.5 %all-to-all-start = ((bf16[128,8,1408]{2,1,0:T(8,128)(2,1)}), bf16[128,8,1408]{2,1,0:T(8,128)(2,1)S(1)}, u32[]{:S(2)}, u32[]{:S(2)}) async-start(bf16[128,8,1408]{2,1,0:T(8,128)(2,1)} %bitcast.7), calls=%async_computation | async-start | bytes 5767168 | tf_op jit(solution)/shard_map/all_to_all | solution.py:333
  19.3 1.4 %collective-permute-start.4 = (bf16[128,1024]{1,0:T(8,128)(2,1)S(1)}, bf16[128,1024]{1,0:T(8,128)(2,1)}, u32[]{:S(2)}, u32[]{:S(2)}) collective-permute-start(bf16[128,1024]{1,0:T(8,128)(2,1)S(1)} %copy-done.6), channel_id=1, source_target_pairs={{8,104},{9,17},{10,106},{11,19},{12,108},{13,21},{14,110},{15,23}} | collective-permute-start | bytes 786440 | tf_op jit(solution)/shard_map/ppermute | solution.py:28
  20.6 1.3 collective-permute-start.3
  22.0 35.1 %collective-permute-done.3 = bf16[128,1024]{1,0:T(8,128)(2,1)} collective-permute-done((bf16[128,1024]{1,0:T(8,128)(2,1)S(1)}, bf16[128,1024]{1,0:T(8,128)(2,1)}, u32[]{:S(2)}, u32[]{:S(2)}) %collective-permute-start.3) | collective-permute-done | bytes 262176 | tf_op jit(solution)/shard_map/ppermute | solution.py:28
  57.0 1.1 add_add_fusion.1
  58.1 1.3 collective-permute-start.8
  59.4 1.3 collective-permute-start.7
  60.7 1.3 collective-permute-start.6
  62.1 2.2 %copy-done.1 = bf16[2,1024,1024]{2,1,0:T(8,128)(2,1)S(1)} copy-done((bf16[2,1024,1024]{2,1,0:T(8,128)(2,1)S(1)}, bf16[2,1024,1024]{2,1,0:T(8,128)(2,1)}, u32[]{:S(2)}) %copy-start.1) | copy-done | bytes 4194328
  64.6 1.3 %copy-done.2 = bf16[1024,1024]{1,0:T(8,128)(2,1)} copy-done((bf16[1024,1024]{1,0:T(8,128)(2,1)}, bf16[1024,1024]{1,0:T(8,128)(2,1)S(1)}, u32[]{:S(2)}) %copy-start.2) | copy-done | bytes 2097176
  65.9 1.3 copy-done.4
  68.1 3.3 %collective-permute-start.2 = (bf16[64,256]{1,0:T(8,128)(2,1)S(1)}, bf16[64,256]{1,0:T(8,128)(2,1)S(1)}, u32[]{:S(2)}, u32[]{:S(2)}) collective-permute-start(bf16[64,256]{1,0:T(8,128)(2,1)S(1)} %get-tuple-element.21.p0), channel_id=1, source_target_pairs={{0,4},{1,5},{2,6},{3,7},{4,0},{5,1},{6,2},{7,3},{8,12},{9,13},{10,... | collective-permute-start | bytes 98312 | tf_op jit(solution)/shard_map/ppermute | solution.py:28
  72.7 2.7 %collective-permute-done.1.p2 = bf16[64,256]{1,0:T(8,128)(2,1)S(1)} collective-permute-done((bf16[64,256]{1,0:T(8,128)(2,1)S(1)}, bf16[64,256]{1,0:T(8,128)(2,1)S(1)}, u32[]{:S(2)}, u32[]{:S(2)}) %collective-permute-start.1) | collective-permute-done | bytes 32800 | tf_op jit(solution)/shard_map/ppermute | solution.py:28
  75.4 0.9 shard_map.49
  76.3 1.6 %collective-permute-start.12 = (bf16[64,256]{1,0:T(8,128)(2,1)S(1)}, bf16[64,256]{1,0:T(8,128)(2,1)S(1)}, u32[]{:S(2)}, u32[]{:S(2)}) collective-permute-start(bf16[64,256]{1,0:T(8,128)(2,1)S(1)} %get-tuple-element.31.p0), channel_id=1, source_target_pairs={{0,4},{1,5},{2,6},{3,7},{4,0},{5,1},{6,2},{7,3},{8,12},{9,13},{10,... | collective-permute-start | bytes 98312 | tf_op jit(solution)/shard_map/ppermute | solution.py:28
  79.0 1.6 %collective-permute-done.12.p3 = bf16[64,256]{1,0:T(8,128)(2,1)S(1)} collective-permute-done((bf16[64,256]{1,0:T(8,128)(2,1)S(1)}, bf16[64,256]{1,0:T(8,128)(2,1)S(1)}, u32[]{:S(2)}, u32[]{:S(2)}) %collective-permute-start.12) | collective-permute-done | bytes 32800 | tf_op jit(solution)/shard_map/ppermute | solution.py:28
  80.6 1.2 collective-permute-done.11.p2
  82.7 1.9 %collective-permute-start.14 = (bf16[32,2048]{1,0:T(8,128)(2,1)S(1)}, bf16[32,2048]{1,0:T(8,128)(2,1)S(1)}, u32[]{:S(2)}, u32[]{:S(2)}) collective-permute-start(bf16[32,2048]{1,0:T(8,128)(2,1)S(1)} %shard_map.50), channel_id=1, source_target_pairs={{0,96},{1,25},{2,98},{3,27},{4,100},{5,29},{6,102},{7,31},{8,104},... | collective-permute-start | bytes 393224 | tf_op jit(solution)/shard_map/ppermute | solution.py:28
  85.3 2.8 %collective-permute-done.15 = bf16[32,2048]{1,0:T(8,128)(2,1)S(1)} collective-permute-done((bf16[32,2048]{1,0:T(8,128)(2,1)S(1)}, bf16[32,2048]{1,0:T(8,128)(2,1)S(1)}, u32[]{:S(2)}, u32[]{:S(2)}) %collective-permute-start.15) | collective-permute-done | bytes 131104 | tf_op jit(solution)/shard_map/ppermute | solution.py:28
  88.1 1.1 collective-permute-done.14
  89.3 1.7 %collective-permute-start.16 = (bf16[128,2048]{1,0:T(8,128)(2,1)S(1)}, bf16[128,2048]{1,0:T(8,128)(2,1)S(1)}, u32[]{:S(2)}, u32[]{:S(2)}) collective-permute-start(bf16[128,2048]{1,0:T(8,128)(2,1)S(1)} %pad_maximum_fusion.refs_0_), channel_id=1, source_target_pairs={{0,8},{1,33},{2,10},{3,35},{4,12},{5,37},{6,14},{7,39},{8,0},{9,41... | collective-permute-start | bytes 1572872 | tf_op jit(solution)/shard_map/ppermute | solution.py:28
  91.1 6.1 %collective-permute-start.24 = (bf16[128,2048]{1,0:T(8,128)(2,1)S(1)}, bf16[128,2048]{1,0:T(8,128)(2,1)S(1)}, u32[]{:S(2)}, u32[]{:S(2)}) collective-permute-start(bf16[128,2048]{1,0:T(8,128)(2,1)S(1)} %pad_maximum_fusion.refs_0_), channel_id=1, source_target_pairs={{0,1},{1,0},{2,3},{3,2},{4,5},{5,4},{6,7},{7,6},{8,9},{9,8},{10,11... | collective-permute-start | bytes 1572872 | tf_op jit(solution)/shard_map/ppermute | solution.py:28
  97.2 1.6 %collective-permute-done.18.refs_1_ = bf16[128,2048]{1,0:T(8,128)(2,1)S(1)} collective-permute-done((bf16[128,2048]{1,0:T(8,128)(2,1)S(1)}, bf16[128,2048]{1,0:T(8,128)(2,1)S(1)}, u32[]{:S(2)}, u32[]{:S(2)}) %collective-permute-start.18) | collective-permute-done | bytes 524320 | tf_op jit(solution)/shard_map/ppermute | solution.py:28
  99.5 0.8 collective-permute-start.21
  100.2 8.7 %collective-permute-start.19 = (bf16[128,2048]{1,0:T(8,128)(2,1)S(1)}, bf16[128,2048]{1,0:T(8,128)(2,1)S(1)}, u32[]{:S(2)}, u32[]{:S(2)}) collective-permute-start(bf16[128,2048]{1,0:T(8,128)(2,1)S(1)} %collective-permute-done.18.refs_1_), channel_id=1, source_target_pairs={{0,1},{1,0},{2,3},{3,2},{4,5},{5,4},{6,7},{7,6},{8,9},{9,8},{10,11... | collective-permute-start | bytes 1572872 | tf_op jit(solution)/shard_map/ppermute | solution.py:28
  108.9 4.3 %collective-permute-start.22 = (bf16[64,2048]{1,0:T(8,128)(2,1)S(1)}, bf16[64,2048]{1,0:T(8,128)(2,1)S(1)}, u32[]{:S(2)}, u32[]{:S(2)}) collective-permute-start(bf16[64,2048]{1,0:T(8,128)(2,1)S(1)} %collective-permute-done.20.refs_2_), channel_id=1, source_target_pairs={{0,1},{1,0},{2,3},{3,2},{4,5},{5,4},{6,7},{7,6},{8,9},{9,8},{10,11... | collective-permute-start | bytes 786440 | tf_op jit(solution)/shard_map/ppermute | solution.py:28
  113.2 1.3 %collective-permute-start.23 = (bf16[64,2048]{1,0:T(8,128)(2,1)S(1)}, bf16[64,2048]{1,0:T(8,128)(2,1)S(1)}, u32[]{:S(2)}, u32[]{:S(2)}) collective-permute-start(bf16[64,2048]{1,0:T(8,128)(2,1)S(1)} %collective-permute-done.21.refs_3_), channel_id=1, source_target_pairs={{0,1},{1,0},{2,3},{3,2},{4,5},{5,4},{6,7},{7,6},{8,9},{9,8},{10,11... | collective-permute-start | bytes 786440 | tf_op jit(solution)/shard_map/ppermute | solution.py:28
  114.6 6.6 %shard_map.51 = bf16[1024,1024]{1,0:T(8,128)(2,1)} custom-call(s32[8,1024]{1,0:T(8,128)S(1)} %get-tuple-element.34.own_ref, bf16[1024,1408]{1,0:T(8,128)(2,1)S(1)} %bitcast.5), custom_call_target="tpu_custom_call" | custom-call | flops 2147483648 | bytes 4194304 | tf_op jit(solution)/shard_map/pallas_call | solution.py:257
  121.2 3.2 %shard_map.52.refs_3_ = bf16[8,1,128,1024]{3,2,1,0:T(8,128)(2,1)} custom-call(bf16[128,2048]{1,0:T(8,128)(2,1)S(1)} %pad_maximum_fusion.refs_0_, bf16[128,2048]{1,0:T(8,128)(2,1)S(1)} %collective-permute-done.24.refs_1_, bf16[2,8,1,128,1024]{4,3,2,1,0:T(8,128)(2,1)S(1)} %copy-done, bf16[8,1,128,1024]{3,2,1,0:T(8,128)(2,1)} %bitcast.6), custom_call_target="tpu_custom_call", output_to_operand_aliasing={{}: (3, {})} | custom-call | flops 1073741824 | bytes 2097152 | tf_op jit(solution)/shard_map/pallas_call | solution.py:257
  124.5 3.2 %shard_map.53.refs_7_ = bf16[8,1,128,1024]{3,2,1,0:T(8,128)(2,1)} custom-call(bf16[128,2048]{1,0:T(8,128)(2,1)S(1)} %collective-permute-done.16.refs_0_, bf16[128,2048]{1,0:T(8,128)(2,1)S(1)} %collective-permute-done.18.refs_1_, bf16[2,8,1,128,1024]{4,3,2,1,0:T(8,128)(2,1)S(1)} %copy-done, ...), custom_call_target="tpu_custom_call", output_to_operand_aliasing={{}: (3, {})} | custom-call | flops 1073741824 | bytes 2097152 | tf_op jit(solution)/shard_map/pallas_call | solution.py:257
  127.8 5.5 %shard_map.54 = bf16[8,1,128,1024]{3,2,1,0:T(8,128)(2,1)} custom-call(bf16[128,2048]{1,0:T(8,128)(2,1)S(1)} %collective-permute-done.17.refs_0_, bf16[128,2048]{1,0:T(8,128)(2,1)S(1)} %collective-permute-done.19.refs_1_, bf16[64,2048]{1,0:T(8,128)(2,1)S(1)} %collective-permute-done.20.refs_2_, ...), custom_call_target="tpu_custom_call", output_to_operand_aliasing={{}: (7, {})} | custom-call | flops 1073741824 | bytes 2097152 | tf_op jit(solution)/shard_map/pallas_call | solution.py:257
  (48 shorter events, 6.6 us)
Async XLA Ops:
  7.1 11.5 %copy-start.6 = (bf16[128,1024]{1,0:T(8,128)(2,1)S(1)}, bf16[128,1024]{1,0:T(8,128)(2,1)}, u32[]{:S(2)}) copy-start(bf16[128,1024]{1,0:T(8,128)(2,1)} %get-tuple-element.22) | copy-start | bytes 786436
  7.1 60.3 %all-to-all-start = ((bf16[128,8,1408]{2,1,0:T(8,128)(2,1)}), bf16[128,8,1408]{2,1,0:T(8,128)(2,1)S(1)}, u32[]{:S(2)}, u32[]{:S(2)}) async-start(bf16[128,8,1408]{2,1,0:T(8,128)(2,1)} %bitcast.7), calls=%async_computation | async-start | bytes 5767168 | tf_op jit(solution)/shard_map/all_to_all | solution.py:333
  18.6 3.3 %collective-permute-start.5 = (bf16[128,1024]{1,0:T(8,128)(2,1)S(1)}, bf16[128,1024]{1,0:T(8,128)(2,1)S(1)}, u32[]{:S(2)}, u32[]{:S(2)}) collective-permute-start(bf16[128,1024]{1,0:T(8,128)(2,1)S(1)} %copy-done.6), channel_id=1, source_target_pairs={{8,72},{9,25},{10,74},{11,27},{12,76},{13,29},{14,78},{15,31}} | collective-permute-start | bytes 786440 | tf_op jit(solution)/shard_map/ppermute | solution.py:28
  19.3 2.7 %collective-permute-start.4 = (bf16[128,1024]{1,0:T(8,128)(2,1)S(1)}, bf16[128,1024]{1,0:T(8,128)(2,1)}, u32[]{:S(2)}, u32[]{:S(2)}) collective-permute-start(bf16[128,1024]{1,0:T(8,128)(2,1)S(1)} %copy-done.6), channel_id=1, source_target_pairs={{8,104},{9,17},{10,106},{11,19},{12,108},{13,21},{14,110},{15,23}} | collective-permute-start | bytes 786440 | tf_op jit(solution)/shard_map/ppermute | solution.py:28
  20.6 36.4 %collective-permute-start.3 = (bf16[128,1024]{1,0:T(8,128)(2,1)S(1)}, bf16[128,1024]{1,0:T(8,128)(2,1)}, u32[]{:S(2)}, u32[]{:S(2)}) collective-permute-start(bf16[128,1024]{1,0:T(8,128)(2,1)S(1)} %copy-done.6), channel_id=1, source_target_pairs={{8,40},{9,1},{10,42},{11,3},{12,44},{13,5},{14,46},{15,7}} | collective-permute-start | bytes 786440 | tf_op jit(solution)/shard_map/ppermute | solution.py:28
  58.1 9.1 %collective-permute-start.8 = (bf16[128,1024]{1,0:T(8,128)(2,1)S(1)}, bf16[128,1024]{1,0:T(8,128)(2,1)S(1)}, u32[]{:S(2)}, u32[]{:S(2)}) collective-permute-start(bf16[128,1024]{1,0:T(8,128)(2,1)S(1)} %add_add_fusion.1), channel_id=1, source_target_pairs={{1,65},{3,67},{5,69},{7,71},{8,24},{9,73},{10,26},{11,75},{12,28},... | collective-permute-start | bytes 786440 | tf_op jit(solution)/shard_map/ppermute | solution.py:28
  59.4 7.8 %collective-permute-start.7 = (bf16[128,1024]{1,0:T(8,128)(2,1)S(1)}, bf16[128,1024]{1,0:T(8,128)(2,1)S(1)}, u32[]{:S(2)}, u32[]{:S(2)}) collective-permute-start(bf16[128,1024]{1,0:T(8,128)(2,1)S(1)} %add_add_fusion.1), channel_id=1, source_target_pairs={{1,97},{3,99},{5,101},{7,103},{8,16},{9,105},{10,18},{11,107},{12,... | collective-permute-start | bytes 786440 | tf_op jit(solution)/shard_map/ppermute | solution.py:28
  60.7 6.5 %collective-permute-start.6 = (bf16[128,1024]{1,0:T(8,128)(2,1)S(1)}, bf16[128,1024]{1,0:T(8,128)(2,1)S(1)}, u32[]{:S(2)}, u32[]{:S(2)}) collective-permute-start(bf16[128,1024]{1,0:T(8,128)(2,1)S(1)} %add_add_fusion.1), channel_id=1, source_target_pairs={{1,33},{3,35},{5,37},{7,39},{8,0},{9,41},{10,2},{11,43},{12,4},{13... | collective-permute-start | bytes 786440 | tf_op jit(solution)/shard_map/ppermute | solution.py:28
  62.1 2.2 %copy-start.1 = (bf16[2,1024,1024]{2,1,0:T(8,128)(2,1)S(1)}, bf16[2,1024,1024]{2,1,0:T(8,128)(2,1)}, u32[]{:S(2)}) copy-start(bf16[2,1024,1024]{2,1,0:T(8,128)(2,1)} %source_hbm) | copy-start | bytes 12582916
  64.6 1.4 %copy-start.2 = (bf16[1024,1024]{1,0:T(8,128)(2,1)}, bf16[1024,1024]{1,0:T(8,128)(2,1)S(1)}, u32[]{:S(2)}) copy-start(bf16[1024,1024]{1,0:T(8,128)(2,1)S(1)} %get-tuple-element.32.inverse_ref) | copy-start | bytes 6291460
  67.3 4.7 %collective-permute-start.9 = (bf16[128,1024]{1,0:T(8,128)(2,1)S(1)}, bf16[128,1024]{1,0:T(8,128)(2,1)S(1)}, u32[]{:S(2)}, u32[]{:S(2)}) collective-permute-start(bf16[128,1024]{1,0:T(8,128)(2,1)S(1)} %add_add_fusion.own_ref), channel_id=1, source_target_pairs={{0,1},{1,0},{2,3},{3,2},{4,5},{5,4},{6,7},{7,6},{8,9},{9,8},{10,11... | collective-permute-start | bytes 786440 | tf_op jit(solution)/shard_map/ppermute | solution.py:28
  67.4 7.9 %copy-start.5 = (bf16[1024,1024]{1,0:T(8,128)(2,1)S(1)}, bf16[1024,1024]{1,0:T(8,128)(2,1)}, u32[]{:S(2)}) copy-start(bf16[1024,1024]{1,0:T(8,128)(2,1)} %copy-done.4) | copy-start | bytes 6291460
  68.1 13.8 %copy-start.3 = (bf16[1024,1024]{1,0:T(8,128)(2,1)S(1)}, bf16[1024,1024]{1,0:T(8,128)(2,1)}, u32[]{:S(2)}) copy-start(bf16[1024,1024]{1,0:T(8,128)(2,1)} %copy-done.2) | copy-start | bytes 6291460
  68.1 4.6 %collective-permute-start.2 = (bf16[64,256]{1,0:T(8,128)(2,1)S(1)}, bf16[64,256]{1,0:T(8,128)(2,1)S(1)}, u32[]{:S(2)}, u32[]{:S(2)}) collective-permute-start(bf16[64,256]{1,0:T(8,128)(2,1)S(1)} %get-tuple-element.21.p0), channel_id=1, source_target_pairs={{0,4},{1,5},{2,6},{3,7},{4,0},{5,1},{6,2},{7,3},{8,12},{9,13},{10,... | collective-permute-start | bytes 98312 | tf_op jit(solution)/shard_map/ppermute | solution.py:28
  71.4 4.0 %collective-permute-start.1 = (bf16[64,256]{1,0:T(8,128)(2,1)S(1)}, bf16[64,256]{1,0:T(8,128)(2,1)S(1)}, u32[]{:S(2)}, u32[]{:S(2)}) collective-permute-start(bf16[64,256]{1,0:T(8,128)(2,1)S(1)} %get-tuple-element.21.p0), channel_id=1, source_target_pairs={{0,6},{1,7},{2,4},{3,5},{4,2},{5,3},{6,0},{7,1},{8,14},{9,15},{10,... | collective-permute-start | bytes 98312 | tf_op jit(solution)/shard_map/ppermute | solution.py:28
  71.7 3.6 %collective-permute-start = (bf16[64,256]{1,0:T(8,128)(2,1)S(1)}, bf16[64,256]{1,0:T(8,128)(2,1)S(1)}, u32[]{:S(2)}, u32[]{:S(2)}) collective-permute-start(bf16[64,256]{1,0:T(8,128)(2,1)S(1)} %get-tuple-element.21.p0), channel_id=1, source_target_pairs={{0,2},{1,3},{2,0},{3,1},{4,6},{5,7},{6,4},{7,5},{8,10},{9,11},{10,... | collective-permute-start | bytes 98312 | tf_op jit(solution)/shard_map/ppermute | solution.py:28
  76.3 4.3 %collective-permute-start.12 = (bf16[64,256]{1,0:T(8,128)(2,1)S(1)}, bf16[64,256]{1,0:T(8,128)(2,1)S(1)}, u32[]{:S(2)}, u32[]{:S(2)}) collective-permute-start(bf16[64,256]{1,0:T(8,128)(2,1)S(1)} %get-tuple-element.31.p0), channel_id=1, source_target_pairs={{0,4},{1,5},{2,6},{3,7},{4,0},{5,1},{6,2},{7,3},{8,12},{9,13},{10,... | collective-permute-start | bytes 98312 | tf_op jit(solution)/shard_map/ppermute | solution.py:28
  77.9 4.0 %collective-permute-start.11 = (bf16[64,256]{1,0:T(8,128)(2,1)S(1)}, bf16[64,256]{1,0:T(8,128)(2,1)S(1)}, u32[]{:S(2)}, u32[]{:S(2)}) collective-permute-start(bf16[64,256]{1,0:T(8,128)(2,1)S(1)} %get-tuple-element.31.p0), channel_id=1, source_target_pairs={{0,6},{1,7},{2,4},{3,5},{4,2},{5,3},{6,0},{7,1},{8,14},{9,15},{10,... | collective-permute-start | bytes 98312 | tf_op jit(solution)/shard_map/ppermute | solution.py:28
  78.3 3.5 %collective-permute-start.10 = (bf16[64,256]{1,0:T(8,128)(2,1)S(1)}, bf16[64,256]{1,0:T(8,128)(2,1)S(1)}, u32[]{:S(2)}, u32[]{:S(2)}) collective-permute-start(bf16[64,256]{1,0:T(8,128)(2,1)S(1)} %get-tuple-element.31.p0), channel_id=1, source_target_pairs={{0,2},{1,3},{2,0},{3,1},{4,6},{5,7},{6,4},{7,5},{8,10},{9,11},{10,... | collective-permute-start | bytes 98312 | tf_op jit(solution)/shard_map/ppermute | solution.py:28
  82.6 5.5 %collective-permute-start.15 = (bf16[32,2048]{1,0:T(8,128)(2,1)S(1)}, bf16[32,2048]{1,0:T(8,128)(2,1)S(1)}, u32[]{:S(2)}, u32[]{:S(2)}) collective-permute-start(bf16[32,2048]{1,0:T(8,128)(2,1)S(1)} %shard_map.50), channel_id=1, source_target_pairs={{0,64},{1,17},{2,66},{3,19},{4,68},{5,21},{6,70},{7,23},{8,72},{9,... | collective-permute-start | bytes 393224 | tf_op jit(solution)/shard_map/ppermute | solution.py:28
  82.7 6.5 %collective-permute-start.14 = (bf16[32,2048]{1,0:T(8,128)(2,1)S(1)}, bf16[32,2048]{1,0:T(8,128)(2,1)S(1)}, u32[]{:S(2)}, u32[]{:S(2)}) collective-permute-start(bf16[32,2048]{1,0:T(8,128)(2,1)S(1)} %shard_map.50), channel_id=1, source_target_pairs={{0,96},{1,25},{2,98},{3,27},{4,100},{5,29},{6,102},{7,31},{8,104},... | collective-permute-start | bytes 393224 | tf_op jit(solution)/shard_map/ppermute | solution.py:28
  84.6 4.6 %collective-permute-start.13 = (bf16[32,2048]{1,0:T(8,128)(2,1)S(1)}, bf16[32,2048]{1,0:T(8,128)(2,1)S(1)}, u32[]{:S(2)}, u32[]{:S(2)}) collective-permute-start(bf16[32,2048]{1,0:T(8,128)(2,1)S(1)} %shard_map.50), channel_id=1, source_target_pairs={{0,32},{1,9},{2,34},{3,11},{4,36},{5,13},{6,38},{7,15},{8,40},{9,1... | collective-permute-start | bytes 393224 | tf_op jit(solution)/shard_map/ppermute | solution.py:28
  89.3 9.5 %collective-permute-start.18 = (bf16[128,2048]{1,0:T(8,128)(2,1)S(1)}, bf16[128,2048]{1,0:T(8,128)(2,1)S(1)}, u32[]{:S(2)}, u32[]{:S(2)}) collective-permute-start(bf16[128,2048]{1,0:T(8,128)(2,1)S(1)} %pad_maximum_fusion.refs_0_), channel_id=1, source_target_pairs={{0,24},{1,97},{2,26},{3,99},{4,28},{5,101},{6,30},{7,103},{8,16},{... | collective-permute-start | bytes 1572872 | tf_op jit(solution)/shard_map/ppermute | solution.py:28
  89.3 10.1 %collective-permute-start.16 = (bf16[128,2048]{1,0:T(8,128)(2,1)S(1)}, bf16[128,2048]{1,0:T(8,128)(2,1)S(1)}, u32[]{:S(2)}, u32[]{:S(2)}) collective-permute-start(bf16[128,2048]{1,0:T(8,128)(2,1)S(1)} %pad_maximum_fusion.refs_0_), channel_id=1, source_target_pairs={{0,8},{1,33},{2,10},{3,35},{4,12},{5,37},{6,14},{7,39},{8,0},{9,41... | collective-permute-start | bytes 1572872 | tf_op jit(solution)/shard_map/ppermute | solution.py:28
  91.1 30.1 %collective-permute-start.24 = (bf16[128,2048]{1,0:T(8,128)(2,1)S(1)}, bf16[128,2048]{1,0:T(8,128)(2,1)S(1)}, u32[]{:S(2)}, u32[]{:S(2)}) collective-permute-start(bf16[128,2048]{1,0:T(8,128)(2,1)S(1)} %pad_maximum_fusion.refs_0_), channel_id=1, source_target_pairs={{0,1},{1,0},{2,3},{3,2},{4,5},{5,4},{6,7},{7,6},{8,9},{9,8},{10,11... | collective-permute-start | bytes 1572872 | tf_op jit(solution)/shard_map/ppermute | solution.py:28
  98.8 10.1 %collective-permute-start.20 = (bf16[64,2048]{1,0:T(8,128)(2,1)S(1)}, bf16[64,2048]{1,0:T(8,128)(2,1)S(1)}, u32[]{:S(2)}, u32[]{:S(2)}) collective-permute-start(bf16[64,2048]{1,0:T(8,128)(2,1)S(1)} %slice.8), channel_id=1, source_target_pairs={{0,8},{1,33},{2,10},{3,35},{4,12},{5,37},{6,14},{7,39},{8,0},{9,41... | collective-permute-start | bytes 786440 | tf_op jit(solution)/shard_map/ppermute | solution.py:28
  99.5 13.8 %collective-permute-start.21 = (bf16[64,2048]{1,0:T(8,128)(2,1)S(1)}, bf16[64,2048]{1,0:T(8,128)(2,1)S(1)}, u32[]{:S(2)}, u32[]{:S(2)}) collective-permute-start(bf16[64,2048]{1,0:T(8,128)(2,1)S(1)} %slice.9), channel_id=1, source_target_pairs={{0,24},{1,97},{2,26},{3,99},{4,28},{5,101},{6,30},{7,103},{8,16},{... | collective-permute-start | bytes 786440 | tf_op jit(solution)/shard_map/ppermute | solution.py:28
  100.2 27.5 %collective-permute-start.19 = (bf16[128,2048]{1,0:T(8,128)(2,1)S(1)}, bf16[128,2048]{1,0:T(8,128)(2,1)S(1)}, u32[]{:S(2)}, u32[]{:S(2)}) collective-permute-start(bf16[128,2048]{1,0:T(8,128)(2,1)S(1)} %collective-permute-done.18.refs_1_), channel_id=1, source_target_pairs={{0,1},{1,0},{2,3},{3,2},{4,5},{5,4},{6,7},{7,6},{8,9},{9,8},{10,11... | collective-permute-start | bytes 1572872 | tf_op jit(solution)/shard_map/ppermute | solution.py:28
  108.9 18.9 %collective-permute-start.17 = (bf16[128,2048]{1,0:T(8,128)(2,1)S(1)}, bf16[128,2048]{1,0:T(8,128)(2,1)S(1)}, u32[]{:S(2)}, u32[]{:S(2)}) collective-permute-start(bf16[128,2048]{1,0:T(8,128)(2,1)S(1)} %collective-permute-done.16.refs_0_), channel_id=1, source_target_pairs={{0,1},{1,0},{2,3},{3,2},{4,5},{5,4},{6,7},{7,6},{8,9},{9,8},{10,11... | collective-permute-start | bytes 1572872 | tf_op jit(solution)/shard_map/ppermute | solution.py:28
  108.9 18.9 %collective-permute-start.22 = (bf16[64,2048]{1,0:T(8,128)(2,1)S(1)}, bf16[64,2048]{1,0:T(8,128)(2,1)S(1)}, u32[]{:S(2)}, u32[]{:S(2)}) collective-permute-start(bf16[64,2048]{1,0:T(8,128)(2,1)S(1)} %collective-permute-done.20.refs_2_), channel_id=1, source_target_pairs={{0,1},{1,0},{2,3},{3,2},{4,5},{5,4},{6,7},{7,6},{8,9},{9,8},{10,11... | collective-permute-start | bytes 786440 | tf_op jit(solution)/shard_map/ppermute | solution.py:28
  113.2 14.5 %collective-permute-start.23 = (bf16[64,2048]{1,0:T(8,128)(2,1)S(1)}, bf16[64,2048]{1,0:T(8,128)(2,1)S(1)}, u32[]{:S(2)}, u32[]{:S(2)}) collective-permute-start(bf16[64,2048]{1,0:T(8,128)(2,1)S(1)} %collective-permute-done.21.refs_3_), channel_id=1, source_target_pairs={{0,1},{1,0},{2,3},{3,2},{4,5},{5,4},{6,7},{7,6},{8,9},{9,8},{10,11... | collective-permute-start | bytes 786440 | tf_op jit(solution)/shard_map/ppermute | solution.py:28
  114.6 6.6 %copy-start = (bf16[2,8,1,128,1024]{4,3,2,1,0:T(8,128)(2,1)S(1)}, bf16[2,8,1,128,1024]{4,3,2,1,0:T(8,128)(2,1)}, u32[]{:S(2)}) copy-start(bf16[2,8,1,128,1024]{4,3,2,1,0:T(8,128)(2,1)} %refs_6_.1) | copy-start | bytes 12582916
  (1 other events, 1.3 us)

commit v3 on v1

--- a/solution.py
+++ b/solution.py
@@ -136,12 +136,14 @@
     return jnp.concatenate([scratch[i] for i in range(4)], axis=1)
 
 
-def first_kernel(p0, p1, p2, p3, inverse_ref, next_ref, own_ref, other_ref, solved_ref, second_ref, scratch):
+def first_kernel(p0, p1, p2, p3, inverse_ref, next_ref, *refs):
+    own_ref, other_ref = refs[0:4], refs[4:8]
+    solved_ref, second_ref, scratch = refs[8:]
     lead = gather_cols((p0, p1, p2, p3), scratch)
     solved = dot(lead, inverse_ref[...], (1, 1)).astype(BF16)
     solved_ref[...] = solved
-    own = dot(solved, own_ref[...], (1, 1))
-    other = dot(solved, other_ref[...], (1, 1))
+    own = dot(solved, sum(ref[...] for ref in own_ref), (1, 1))
+    other = dot(solved, sum(ref[...] for ref in other_ref), (1, 1))
     even = lax.axis_index("col") % 2 == 0
     low = jnp.where(even, own, other)
     high = jnp.where(even, other, own)
@@ -203,19 +205,10 @@
     return head, dot(tail0, s0, (1, 1)) + dot(tail1, s1, (1, 1))
 
 
-def update_kernel(blocks, *refs):
-    count = sum(parts for _, _, parts in blocks)
-    pieces = list(refs[:count])
-    panels_ref, rows_hbm, out_hbm, solved_t, head_ref, in_ref, res_ref, sems = refs[count:]
+def updated_blocks(blocks, pieces, panels_ref, rows_ref, solved_t, head_ref, write):
     keep = jnp.where(lax.axis_index("row") < 2, 0.0, 1.0)
-    draws, loads, stores = [], [], []
-    for i, (kind, which, _) in enumerate(blocks):
-        _, second, core = place_of(kind)
-        at = second if which == 3 else swap(which, second)
-        draws.append(pl.ds(pl.multiple_of(128 * (4 * core + at), 128), 128))
-        loads.append(pltpu.make_async_copy(rows_hbm.at[:, :, :, draws[i]], in_ref.at[i], sems.at[0, i]))
-        loads[i].start()
     heads_of(panels_ref, head_ref)
+    pieces = list(pieces)
     for i, (kind, _, parts) in enumerate(blocks):
         first, _, _ = place_of(kind)
         places = (first, first ^ 1, 3 - first, first ^ 2)
@@ -224,17 +217,45 @@
             at = pl.multiple_of(128 * i + 32 * places[j], 32)
             ref, j = (held[0], j) if parts == 1 else (held[j // 2], j % 2)
             solved_t[pl.ds(at, 32), :] = ref[j * 32 : j * 32 + 32, :]
-    head, tail = product(panels_ref, head_ref, solved_t)
-    for i in range(2):
-        loads[i].wait()
-        part = slice(128 * i, 128 * i + 128)
-        res_ref[i, 0, 0] = (in_ref[i, 0, 0].astype(F32) * keep - head[:, part]).astype(BF16)
-        rest = in_ref[i, 1:8, 0].reshape(896, 128).astype(F32) - tail[:, part]
-        res_ref[i, 1:8, 0] = rest.astype(BF16).reshape(7, 128, 128)
-        stores.append(pltpu.make_async_copy(res_ref.at[i], out_hbm.at[:, :, :, draws[i]], sems.at[1, i]))
-        stores[i].start()
-    for store in stores:
-        store.wait()
+        if i % 2 == 0:
+            continue
+        head, tail = product(panels_ref, head_ref, solved_t.at[128 * i - 128 : 128 * i + 128])
+        for n in (i - 1, i):
+            draws = draws_of(blocks[n])
+            part = slice(128 * (n % 2), 128 * (n % 2) + 128)
+            write(n, slice(0, 128), rows_ref[0:128, draws].astype(F32) * keep - head[:, part])
+            write(n, slice(128, 1024), rows_ref[128:1024, draws].astype(F32) - tail[:, part])
+
+
+def draws_of(block):
+    kind, which, _ = block
+    _, second, core = place_of(kind)
+    at = second if which == 3 else swap(which, second)
+    return pl.ds(pl.multiple_of(128 * (4 * core + at), 128), 128)
+
+
+def update_kernel(blocks, *refs):
+    count = sum(parts for _, _, parts in blocks)
+    panels_ref, rows_ref, out_ref, solved_t, head_ref = refs[count:]
+
+    def write(n, rows, value):
+        out_ref[rows, 128 * n : 128 * n + 128] = value.astype(BF16)
+
+    updated_blocks(blocks, refs[:count], panels_ref, rows_ref, solved_t, head_ref, write)
+
+
+def last_kernel(before, blocks, *refs):
+    count = sum(parts for _, _, parts in blocks)
+    pieces, refs = refs[:count], refs[count:]
+    done, (panels_ref, rows_ref, out_ref, solved_t, head_ref) = refs[: len(before)], refs[len(before) :]
+    for held, ref in zip(before, done):
+        for n, block in enumerate(held):
+            out_ref[:, draws_of(block)] = ref[:, 128 * n : 128 * n + 128]
+
+    def write(n, rows, value):
+        out_ref[rows, draws_of(blocks[n])] = value.astype(BF16)
+
+    updated_blocks(blocks, pieces, panels_ref, rows_ref, solved_t, head_ref, write)
 
 
 HBM = pl.BlockSpec(memory_space=pltpu.HBM)
@@ -250,7 +271,7 @@
         out_specs=out_specs or [VMEM] * len(outs),
         scratch_shapes=list(scratch),
         input_output_aliases=aliases or {},
-        compiler_params=pltpu.CompilerParams(vmem_limit_bytes=limit << 20),
+        compiler_params=pltpu.CompilerParams(vmem_limit_bytes=int(limit * (1 << 20))),
         cost_estimate=pl.CostEstimate(flops=flops, bytes_accessed=moved, transcendentals=0),
     )(*args)
 
@@ -270,27 +291,22 @@
     return spread_along(piece, False, lambda x, y, z, k: y == 1 if k == 0 else x == 0)
 
 
+def spread_third(line):
+    return spread_along(line, True, lambda x, y, z, k: x == 0 if k == 0 else y == 1)
+
+
 def around_cols(piece):
     return (piece, send(piece, along_z(0)), send(piece, along_z(1)), send(piece, along_z(2)))
 
 
-def update(blocks, pieces, panels, rows):
+def update(kernel, blocks, pieces, panels, rows, width):
     return launch(
-        functools.partial(update_kernel, blocks),
+        kernel,
         (*pieces, panels, rows),
-        [((8, 1, 128, 1024), BF16)],
-        [
-            pltpu.VMEM((256, 2048), BF16),
-            pltpu.VMEM((2, 128, 1024), BF16),
-            pltpu.VMEM((2, 8, 1, 128, 128), BF16),
-            pltpu.VMEM((2, 8, 1, 128, 128), BF16),
-            pltpu.SemaphoreType.DMA((2, 2)),
-        ],
-        specs=[VMEM] * (len(pieces) + 1) + [HBM],
-        out_specs=[HBM],
-        aliases={len(pieces) + 1: 0},
-        limit=20,
-        flops=1 << 30,
+        [((1024, width), BF16)],
+        [pltpu.VMEM((128 * len(blocks), 2048), BF16), pltpu.VMEM((2, 128, 1024), BF16)],
+        limit=16,
+        flops=len(blocks) << 29,
         moved=2 << 20,
     )[0]
 
@@ -311,14 +327,16 @@
         ],
         specs=[VMEM, HBM],
         out_specs=[HBM],
-        limit=63,
+        limit=61.4,
         flops=3 << 30,
         moved=5 << 20,
     )
     piece = panels[0, 0, 0]
     line = spread_first(piece)
     line = jnp.where(row == 1, piece, jnp.zeros_like(piece)) + line[0] + line[1] + line[2]
-    plane = spread_second(line)
+    plane = [line] + spread_second(line)
+    other = send(line, other_core)
+    other = [other] + spread_third(other)
     arrived = lax.all_to_all(ordered.reshape(128, 8, 1408), AXES, split_axis=0, concat_axis=0, tiled=True)
     inverses, _ = lax.optimization_barrier((diag_inverse, ordered))
     inverses = launch(
@@ -340,12 +358,9 @@
         flops=1 << 27,
         moved=1 << 20,
     )
-    line, plane, _ = lax.optimization_barrier((line, plane, own))
-    link = line + plane[0] + plane[1] + plane[2]
-    link_other = send(link, other_core)
     solved, second = launch(
         first_kernel,
-        (*around_cols(lead), inverses[0], follow, link, link_other),
+        (*around_cols(lead), inverses[0], follow, *plane, *other),
         [((64, 1024), BF16), ((64, 256), BF16)],
         [pltpu.VMEM((4, 64, 256), BF16)],
         limit=12,
@@ -371,7 +386,6 @@
         flops=1 << 31,
         moved=4 << 20,
     )
-    rows = rows.reshape(8, 1, 128, 1024)
     line = [both] + [send(both, along_first(i)) for i in range(3)]
     line = jnp.concatenate(line, axis=0)
     side0, side1 = send(line, along_second(0)), send(line, along_second(1))
@@ -379,10 +393,14 @@
     line_other = send(line, other_core)
     side0_other, side1_other = send(side0, other_core), send(side1, other_core)
     far_other = send(far0, other_core), send(far1, other_core)
-    rows = update(((0, 3, 1), (1, 3, 1)), (line, line_other), panels, rows)
-    rows = update(((0, 0, 1), (0, 1, 1)), (side0, side1), panels, rows)
-    rows = update(((1, 0, 1), (1, 1, 1)), (side0_other, side1_other), panels, rows)
-    return update(((0, 2, 2), (1, 2, 2)), (far0, far1, *far_other), panels, rows)
+    lines = ((0, 3, 1), (1, 3, 1))
+    sides = ((0, 0, 1), (0, 1, 1))
+    rest = ((1, 0, 1), (1, 1, 1), (0, 2, 2), (1, 2, 2))
+    part0 = update(functools.partial(update_kernel, lines), lines, (line, line_other), panels, rows, 256)
+    part1 = update(functools.partial(update_kernel, sides), sides, (side0, side1), panels, rows, 256)
+    pieces = (side0_other, side1_other, far0, far1, *far_other, part0, part1)
+    kernel = functools.partial(last_kernel, (lines, sides), rest)
+    return update(kernel, rest, pieces, panels, rows, 1024).reshape(8, 1, 128, 1024)
 
 
 def solution(mesh):

time: 129 us -> 130 us (level)
  waiting for transfers between devices: 43.8 us -> 54 us
  starting transfers between devices: 54.9 us -> 49.2 us
  Pallas kernels: 26.4 us -> 21.1 us
  local copies, waits for them, and re-layouts: 1.02 us -> 3.91 us
    ppermute x25 -> x28, waiting for transfers between devices: 43.8 us -> 54 us  [send(): return lax.ppermute(value, AXES, pairs)]
    ppermute x25 -> x28, starting transfers between devices: 43.4 us -> 37.7 us  [send(): return lax.ppermute(value, AXES, pairs)]
    pallas_call x10 -> x9, Pallas kernels: 26.4 us -> 21.1 us  [launch(): pl.pallas_call(kernel, out_shape=[jax.ShapeDtypeStruct(s, d) for s, d in...]
    unnamed x4 -> x8, local copies, waits for them, and re-layouts: 0.01 us -> 2.9 us
  transfers between devices with their start and end apart: 26 -> 29, of which waited for: 9 -> 8; matrix products, arithmetic and copies ran while one was open for 2% -> 2% of each run, Pallas kernels for 12% -> 6%
where the time goes in v3:
time: 130 us
  waiting for transfers between devices  54 us (42%)
  starting transfers between devices  49.2 us (38%)
  Pallas kernels  21.1 us (16%)
  local copies, waits for them, and re-layouts  3.91 us (3%)
    ppermute x28, waiting for transfers between devices, send(): return lax.ppermute(value, AXES, pairs)  54 us
    ppermute x28, starting transfers between devices, send(): return lax.ppermute(value, AXES, pairs)  37.7 us
    pallas_call x9, Pallas kernels, launch(): pl.pallas_call(kernel, out_shape=[jax.ShapeDtypeStruct(s, d) for s, d in...  21.1 us
    all_to_all x1, starting transfers between devices, steps(): lax.all_to_all(ordered.reshape(128, 8, 1408), AXES, split_axis=0, concat_...  11.5 us
    unnamed x8, local copies, waits for them, and re-layouts  2.9 us
  transfers between devices with their start and end apart: 29, of which 8 were waited for; matrix products, arithmetic and copies ran while one was open for 2% of the time, Pallas kernels for 6%

profile of v3, /device:TPU:1, one launch (start us, length us, event | category | flops | bytes accessed | tf_op | source)
XLA Modules:
  0.0 129.7 jit_solution(16866981178178496270)
XLA Ops:
  0.0 6.4 %shard_map.46 = bf16[1024,1408]{1,0:T(8,128)(2,1)} custom-call(s32[1,1024]{1,0:T(1,128)} %bitcast.13, bf16[1024,1024]{1,0:T(8,128)(2,1)} %rows_hbm.1), custom_call_target="tpu_custom_call" | custom-call | flops 3221225472 | bytes 5242880 | tf_op jit(solution)/shard_map/pallas_call | solution.py:266
  6.4 11.5 %all-to-all-start = ((bf16[128,8,1408]{2,1,0:T(8,128)(2,1)}), bf16[128,8,1408]{2,1,0:T(8,128)(2,1)S(1)}, u32[]{:S(2)}, u32[]{:S(2)}) async-start(bf16[128,8,1408]{2,1,0:T(8,128)(2,1)} %bitcast.12), calls=%async_computation | async-start | bytes 5767168 | tf_op jit(solution)/shard_map/all_to_all | solution.py:340
  17.9 1.0 slice_bitcast_fusion
  19.5 1.3 collective-permute-start.3
  20.8 1.4 %collective-permute-start.5 = (bf16[128,1024]{1,0:T(8,128)(2,1)S(1)}, bf16[128,1024]{1,0:T(8,128)(2,1)}, u32[]{:S(2)}, u32[]{:S(2)}) collective-permute-start(bf16[128,1024]{1,0:T(8,128)(2,1)S(1)} %slice_bitcast_fusion), channel_id=1, source_target_pairs={{8,72},{9,25},{10,74},{11,27},{12,76},{13,29},{14,78},{15,31}} | collective-permute-start | bytes 786440 | tf_op jit(solution)/shard_map/ppermute | solution.py:28
  22.2 31.3 %collective-permute-done.3 = bf16[128,1024]{1,0:T(8,128)(2,1)} collective-permute-done((bf16[128,1024]{1,0:T(8,128)(2,1)S(1)}, bf16[128,1024]{1,0:T(8,128)(2,1)}, u32[]{:S(2)}, u32[]{:S(2)}) %collective-permute-start.3) | collective-permute-done | bytes 262176 | tf_op jit(solution)/shard_map/ppermute | solution.py:28
  53.5 1.2 add_add_fusion.refs_0_
  54.8 1.3 %collective-permute-start.8 = (bf16[128,1024]{1,0:T(8,128)(2,1)S(1)}, bf16[128,1024]{1,0:T(8,128)(2,1)S(1)}, u32[]{:S(2)}, u32[]{:S(2)}) collective-permute-start(bf16[128,1024]{1,0:T(8,128)(2,1)S(1)} %add_add_fusion.refs_0_), channel_id=1, source_target_pairs={{1,65},{3,67},{5,69},{7,71},{8,24},{9,73},{10,26},{11,75},{12,28},... | collective-permute-start | bytes 786440 | tf_op jit(solution)/shard_map/ppermute | solution.py:28
  56.1 2.0 %collective-permute-start.7 = (bf16[128,1024]{1,0:T(8,128)(2,1)S(1)}, bf16[128,1024]{1,0:T(8,128)(2,1)}, u32[]{:S(2)}, u32[]{:S(2)}) collective-permute-start(bf16[128,1024]{1,0:T(8,128)(2,1)S(1)} %add_add_fusion.refs_0_), channel_id=1, source_target_pairs={{1,97},{3,99},{5,101},{7,103},{8,16},{9,105},{10,18},{11,107},{12,... | collective-permute-start | bytes 786440 | tf_op jit(solution)/shard_map/ppermute | solution.py:28
  58.1 2.0 %collective-permute-start.6 = (bf16[128,1024]{1,0:T(8,128)(2,1)S(1)}, bf16[128,1024]{1,0:T(8,128)(2,1)}, u32[]{:S(2)}, u32[]{:S(2)}) collective-permute-start(bf16[128,1024]{1,0:T(8,128)(2,1)S(1)} %add_add_fusion.refs_0_), channel_id=1, source_target_pairs={{1,33},{3,35},{5,37},{7,39},{8,0},{9,41},{10,2},{11,43},{12,4},{13... | collective-permute-start | bytes 786440 | tf_op jit(solution)/shard_map/ppermute | solution.py:28
  60.1 1.4 %collective-permute-start.12 = (bf16[128,1024]{1,0:T(8,128)(2,1)S(1)}, bf16[128,1024]{1,0:T(8,128)(2,1)}, u32[]{:S(2)}, u32[]{:S(2)}) collective-permute-start(bf16[128,1024]{1,0:T(8,128)(2,1)S(1)} %collective-permute-done.9.refs_4_), channel_id=1, source_target_pairs={{0,64},{2,66},{4,68},{6,70},{8,72},{9,25},{10,74},{11,27},{12,76},... | collective-permute-start | bytes 786440 | tf_op jit(solution)/shard_map/ppermute | solution.py:28
  61.5 1.4 %collective-permute-start.11 = (bf16[128,1024]{1,0:T(8,128)(2,1)S(1)}, bf16[128,1024]{1,0:T(8,128)(2,1)}, u32[]{:S(2)}, u32[]{:S(2)}) collective-permute-start(bf16[128,1024]{1,0:T(8,128)(2,1)S(1)} %collective-permute-done.9.refs_4_), channel_id=1, source_target_pairs={{0,96},{2,98},{4,100},{6,102},{8,104},{9,17},{10,106},{11,19},{12,... | collective-permute-start | bytes 786440 | tf_op jit(solution)/shard_map/ppermute | solution.py:28
  63.5 1.3 collective-permute-start.10
  65.5 3.5 %collective-permute-start.2 = (bf16[64,256]{1,0:T(8,128)(2,1)S(1)}, bf16[64,256]{1,0:T(8,128)(2,1)S(1)}, u32[]{:S(2)}, u32[]{:S(2)}) collective-permute-start(bf16[64,256]{1,0:T(8,128)(2,1)S(1)} %get-tuple-element.13.p0), channel_id=1, source_target_pairs={{0,4},{1,5},{2,6},{3,7},{4,0},{5,1},{6,2},{7,3},{8,12},{9,13},{10,... | collective-permute-start | bytes 98312 | tf_op jit(solution)/shard_map/ppermute | solution.py:28
  69.3 2.2 %copy-done.1 = bf16[2,1024,1024]{2,1,0:T(8,128)(2,1)S(1)} copy-done((bf16[2,1024,1024]{2,1,0:T(8,128)(2,1)S(1)}, bf16[2,1024,1024]{2,1,0:T(8,128)(2,1)}, u32[]{:S(2)}) %copy-start.1) | copy-done | bytes 4194328
  71.9 5.1 %collective-permute-done.10.refs_5_ = bf16[128,1024]{1,0:T(8,128)(2,1)} collective-permute-done((bf16[128,1024]{1,0:T(8,128)(2,1)S(1)}, bf16[128,1024]{1,0:T(8,128)(2,1)}, u32[]{:S(2)}, u32[]{:S(2)}) %collective-permute-start.10) | collective-permute-done | bytes 262176 | tf_op jit(solution)/shard_map/ppermute | solution.py:28
  77.0 2.3 %shard_map.49 = (bf16[64,1024]{1,0:T(8,128)(2,1)S(1)}, bf16[64,256]{1,0:T(8,128)(2,1)S(1)}) custom-call(bf16[64,256]{1,0:T(8,128)(2,1)S(1)} %get-tuple-element.13.p0, bf16[64,256]{1,0:T(8,128)(2,1)S(1)} %collective-permute-done.p1, bf16[64,256]{1,0:T(8,128)(2,1)S(1)} %collective-permute-done.1.p2, bf16[64,256]{1,0:T(8,128)(2,1)S(1)} %collective-permute-done.2.p3, ...), custom_call_target="tpu_custom_call" | custom-call | flops 268435456 | bytes 3145728 | tf_op jit(solution)/shard_map/pallas_call | solution.py:266
  79.3 3.0 %collective-permute-start.15 = (bf16[64,256]{1,0:T(8,128)(2,1)S(1)}, bf16[64,256]{1,0:T(8,128)(2,1)S(1)}, u32[]{:S(2)}, u32[]{:S(2)}) collective-permute-start(bf16[64,256]{1,0:T(8,128)(2,1)S(1)} %get-tuple-element.17.p0), channel_id=1, source_target_pairs={{0,4},{1,5},{2,6},{3,7},{4,0},{5,1},{6,2},{7,3},{8,12},{9,13},{10,... | collective-permute-start | bytes 98312 | tf_op jit(solution)/shard_map/ppermute | solution.py:28
  83.6 3.0 %collective-permute-done.14.p2 = bf16[64,256]{1,0:T(8,128)(2,1)S(1)} collective-permute-done((bf16[64,256]{1,0:T(8,128)(2,1)S(1)}, bf16[64,256]{1,0:T(8,128)(2,1)S(1)}, u32[]{:S(2)}, u32[]{:S(2)}) %collective-permute-start.14) | collective-permute-done | bytes 32800 | tf_op jit(solution)/shard_map/ppermute | solution.py:28
  86.6 0.8 shard_map.50
  87.4 6.5 %collective-permute-start.17 = (bf16[32,2048]{1,0:T(8,128)(2,1)S(1)}, bf16[32,2048]{1,0:T(8,128)(2,1)S(1)}, u32[]{:S(2)}, u32[]{:S(2)}) collective-permute-start(bf16[32,2048]{1,0:T(8,128)(2,1)S(1)} %shard_map.50), channel_id=1, source_target_pairs={{0,96},{1,25},{2,98},{3,27},{4,100},{5,29},{6,102},{7,31},{8,104},... | collective-permute-start | bytes 393224 | tf_op jit(solution)/shard_map/ppermute | solution.py:28
  93.9 2.6 %collective-permute-done.17 = bf16[32,2048]{1,0:T(8,128)(2,1)S(1)} collective-permute-done((bf16[32,2048]{1,0:T(8,128)(2,1)S(1)}, bf16[32,2048]{1,0:T(8,128)(2,1)S(1)}, u32[]{:S(2)}, u32[]{:S(2)}) %collective-permute-start.17) | collective-permute-done | bytes 131104 | tf_op jit(solution)/shard_map/ppermute | solution.py:28
  96.5 1.2 collective-permute-done.16
  97.9 9.4 %collective-permute-done.21.refs_1_ = bf16[128,2048]{1,0:T(8,128)(2,1)S(1)} collective-permute-done((bf16[128,2048]{1,0:T(8,128)(2,1)S(1)}, bf16[128,2048]{1,0:T(8,128)(2,1)S(1)}, u32[]{:S(2)}, u32[]{:S(2)}) %collective-permute-start.21) | collective-permute-done | bytes 524320 | tf_op jit(solution)/shard_map/ppermute | solution.py:28
  107.5 1.4 %collective-permute-start.24 = (bf16[64,2048]{1,0:T(8,128)(2,1)S(1)}, bf16[64,2048]{1,0:T(8,128)(2,1)S(1)}, u32[]{:S(2)}, u32[]{:S(2)}) collective-permute-start(bf16[64,2048]{1,0:T(8,128)(2,1)S(1)} %slice.13), channel_id=1, source_target_pairs={{0,24},{1,97},{2,26},{3,99},{4,28},{5,101},{6,30},{7,103},{8,16},{... | collective-permute-start | bytes 786440 | tf_op jit(solution)/shard_map/ppermute | solution.py:28
  108.9 2.9 %collective-permute-start.27 = (bf16[128,2048]{1,0:T(8,128)(2,1)S(1)}, bf16[128,2048]{1,0:T(8,128)(2,1)S(1)}, u32[]{:S(2)}, u32[]{:S(2)}) collective-permute-start(bf16[128,2048]{1,0:T(8,128)(2,1)S(1)} %pad_maximum_fusion.refs_0_), channel_id=1, source_target_pairs={{0,1},{1,0},{2,3},{3,2},{4,5},{5,4},{6,7},{7,6},{8,9},{9,8},{10,11... | collective-permute-start | bytes 1572872 | tf_op jit(solution)/shard_map/ppermute | solution.py:28
  113.0 2.5 %collective-permute-start.25 = (bf16[64,2048]{1,0:T(8,128)(2,1)S(1)}, bf16[64,2048]{1,0:T(8,128)(2,1)S(1)}, u32[]{:S(2)}, u32[]{:S(2)}) collective-permute-start(bf16[64,2048]{1,0:T(8,128)(2,1)S(1)} %collective-permute-done.23.refs_2_), channel_id=1, source_target_pairs={{0,1},{1,0},{2,3},{3,2},{4,5},{5,4},{6,7},{7,6},{8,9},{9,8},{10,11... | collective-permute-start | bytes 786440 | tf_op jit(solution)/shard_map/ppermute | solution.py:28
  115.5 3.3 %collective-permute-start.26 = (bf16[64,2048]{1,0:T(8,128)(2,1)S(1)}, bf16[64,2048]{1,0:T(8,128)(2,1)S(1)}, u32[]{:S(2)}, u32[]{:S(2)}) collective-permute-start(bf16[64,2048]{1,0:T(8,128)(2,1)S(1)} %collective-permute-done.24.refs_3_), channel_id=1, source_target_pairs={{0,1},{1,0},{2,3},{3,2},{4,5},{5,4},{6,7},{7,6},{8,9},{9,8},{10,11... | collective-permute-start | bytes 786440 | tf_op jit(solution)/shard_map/ppermute | solution.py:28
  118.8 3.2 %shard_map.51.refs_3_.refs_9_ = bf16[1024,1024]{1,0:T(8,128)(2,1)S(1)} custom-call(s32[8,1024]{1,0:T(8,128)S(1)} %get-tuple-element.20.own_ref, bf16[1024,1408]{1,0:T(8,128)(2,1)S(1)} %bitcast.11), custom_call_target="tpu_custom_call" | custom-call | flops 2147483648 | bytes 4194304 | tf_op jit(solution)/shard_map/pallas_call | solution.py:266
  122.0 1.6 %shard_map.53.refs_7_ = bf16[1024,256]{1,0:T(8,128)(2,1)S(1)} custom-call(bf16[128,2048]{1,0:T(8,128)(2,1)S(1)} %collective-permute-done.19.refs_0_, bf16[128,2048]{1,0:T(8,128)(2,1)S(1)} %collective-permute-done.21.refs_1_, bf16[2,8,1,128,1024]{4,3,2,1,0:T(8,128)(2,1)S(1)} %copy-done, bf16[1024,1024]{1,0:T(8,128)(2,1)S(1)} %shard_map.51.refs_3_.refs_9_), custom_call_target="tpu_custom_call" | custom-call | flops 1073741824 | bytes 2097152 | tf_op jit(solution)/shard_map/pallas_call | solution.py:266
  123.6 1.6 %shard_map.52.refs_6_ = bf16[1024,256]{1,0:T(8,128)(2,1)S(1)} custom-call(bf16[128,2048]{1,0:T(8,128)(2,1)S(1)} %pad_maximum_fusion.refs_0_, bf16[128,2048]{1,0:T(8,128)(2,1)S(1)} %collective-permute-done.27.refs_1_, bf16[2,8,1,128,1024]{4,3,2,1,0:T(8,128)(2,1)S(1)} %copy-done, bf16[1024,1024]{1,0:T(8,128)(2,1)S(1)} %shard_map.51.refs_3_.refs_9_), custom_call_target="tpu_custom_call" | custom-call | flops 1073741824 | bytes 2097152 | tf_op jit(solution)/shard_map/pallas_call | solution.py:266
  125.2 4.5 %shard_map.54 = bf16[1024,1024]{1,0:T(8,128)(2,1)} custom-call(bf16[128,2048]{1,0:T(8,128)(2,1)S(1)} %collective-permute-done.20.refs_0_, bf16[128,2048]{1,0:T(8,128)(2,1)S(1)} %collective-permute-done.22.refs_1_, bf16[64,2048]{1,0:T(8,128)(2,1)S(1)} %collective-permute-done.23.refs_2_, bf16[64,2048]{1,0:T(8,128)(2,1)S(1)} %collective-permute-done.24.refs_3_, ...), custom_call_target="tpu_custom_call" | custom-call | flops 2147483648 | bytes 2097152 | tf_op jit(solution)/shard_map/pallas_call | solution.py:266
  (48 shorter events, 5.7 us)
Async XLA Ops:
  6.4 58.4 %all-to-all-start = ((bf16[128,8,1408]{2,1,0:T(8,128)(2,1)}), bf16[128,8,1408]{2,1,0:T(8,128)(2,1)S(1)}, u32[]{:S(2)}, u32[]{:S(2)}) async-start(bf16[128,8,1408]{2,1,0:T(8,128)(2,1)} %bitcast.12), calls=%async_computation | async-start | bytes 5767168 | tf_op jit(solution)/shard_map/all_to_all | solution.py:340
  18.8 3.4 %collective-permute-start.4 = (bf16[128,1024]{1,0:T(8,128)(2,1)S(1)}, bf16[128,1024]{1,0:T(8,128)(2,1)S(1)}, u32[]{:S(2)}, u32[]{:S(2)}) collective-permute-start(bf16[128,1024]{1,0:T(8,128)(2,1)S(1)} %slice_bitcast_fusion), channel_id=1, source_target_pairs={{8,104},{9,17},{10,106},{11,19},{12,108},{13,21},{14,110},{15,23}} | collective-permute-start | bytes 786440 | tf_op jit(solution)/shard_map/ppermute | solution.py:28
  19.5 34.0 %collective-permute-start.3 = (bf16[128,1024]{1,0:T(8,128)(2,1)S(1)}, bf16[128,1024]{1,0:T(8,128)(2,1)}, u32[]{:S(2)}, u32[]{:S(2)}) collective-permute-start(bf16[128,1024]{1,0:T(8,128)(2,1)S(1)} %slice_bitcast_fusion), channel_id=1, source_target_pairs={{8,40},{9,1},{10,42},{11,3},{12,44},{13,5},{14,46},{15,7}} | collective-permute-start | bytes 786440 | tf_op jit(solution)/shard_map/ppermute | solution.py:28
  20.8 32.7 %collective-permute-start.5 = (bf16[128,1024]{1,0:T(8,128)(2,1)S(1)}, bf16[128,1024]{1,0:T(8,128)(2,1)}, u32[]{:S(2)}, u32[]{:S(2)}) collective-permute-start(bf16[128,1024]{1,0:T(8,128)(2,1)S(1)} %slice_bitcast_fusion), channel_id=1, source_target_pairs={{8,72},{9,25},{10,74},{11,27},{12,76},{13,29},{14,78},{15,31}} | collective-permute-start | bytes 786440 | tf_op jit(solution)/shard_map/ppermute | solution.py:28
  54.7 5.4 %collective-permute-start.9 = (bf16[128,1024]{1,0:T(8,128)(2,1)S(1)}, bf16[128,1024]{1,0:T(8,128)(2,1)S(1)}, u32[]{:S(2)}, u32[]{:S(2)}) collective-permute-start(bf16[128,1024]{1,0:T(8,128)(2,1)S(1)} %add_add_fusion.refs_0_), channel_id=1, source_target_pairs={{0,1},{1,0},{2,3},{3,2},{4,5},{5,4},{6,7},{7,6},{8,9},{9,8},{10,11... | collective-permute-start | bytes 786440 | tf_op jit(solution)/shard_map/ppermute | solution.py:28
  54.8 8.1 %collective-permute-start.8 = (bf16[128,1024]{1,0:T(8,128)(2,1)S(1)}, bf16[128,1024]{1,0:T(8,128)(2,1)S(1)}, u32[]{:S(2)}, u32[]{:S(2)}) collective-permute-start(bf16[128,1024]{1,0:T(8,128)(2,1)S(1)} %add_add_fusion.refs_0_), channel_id=1, source_target_pairs={{1,65},{3,67},{5,69},{7,71},{8,24},{9,73},{10,26},{11,75},{12,28},... | collective-permute-start | bytes 786440 | tf_op jit(solution)/shard_map/ppermute | solution.py:28
  56.1 9.4 %collective-permute-start.7 = (bf16[128,1024]{1,0:T(8,128)(2,1)S(1)}, bf16[128,1024]{1,0:T(8,128)(2,1)}, u32[]{:S(2)}, u32[]{:S(2)}) collective-permute-start(bf16[128,1024]{1,0:T(8,128)(2,1)S(1)} %add_add_fusion.refs_0_), channel_id=1, source_target_pairs={{1,97},{3,99},{5,101},{7,103},{8,16},{9,105},{10,18},{11,107},{12,... | collective-permute-start | bytes 786440 | tf_op jit(solution)/shard_map/ppermute | solution.py:28
  58.1 10.9 %collective-permute-start.6 = (bf16[128,1024]{1,0:T(8,128)(2,1)S(1)}, bf16[128,1024]{1,0:T(8,128)(2,1)}, u32[]{:S(2)}, u32[]{:S(2)}) collective-permute-start(bf16[128,1024]{1,0:T(8,128)(2,1)S(1)} %add_add_fusion.refs_0_), channel_id=1, source_target_pairs={{1,33},{3,35},{5,37},{7,39},{8,0},{9,41},{10,2},{11,43},{12,4},{13... | collective-permute-start | bytes 786440 | tf_op jit(solution)/shard_map/ppermute | solution.py:28
  60.1 9.3 %collective-permute-start.12 = (bf16[128,1024]{1,0:T(8,128)(2,1)S(1)}, bf16[128,1024]{1,0:T(8,128)(2,1)}, u32[]{:S(2)}, u32[]{:S(2)}) collective-permute-start(bf16[128,1024]{1,0:T(8,128)(2,1)S(1)} %collective-permute-done.9.refs_4_), channel_id=1, source_target_pairs={{0,64},{2,66},{4,68},{6,70},{8,72},{9,25},{10,74},{11,27},{12,76},... | collective-permute-start | bytes 786440 | tf_op jit(solution)/shard_map/ppermute | solution.py:28
  61.5 10.4 %collective-permute-start.11 = (bf16[128,1024]{1,0:T(8,128)(2,1)S(1)}, bf16[128,1024]{1,0:T(8,128)(2,1)}, u32[]{:S(2)}, u32[]{:S(2)}) collective-permute-start(bf16[128,1024]{1,0:T(8,128)(2,1)S(1)} %collective-permute-done.9.refs_4_), channel_id=1, source_target_pairs={{0,96},{2,98},{4,100},{6,102},{8,104},{9,17},{10,106},{11,19},{12,... | collective-permute-start | bytes 786440 | tf_op jit(solution)/shard_map/ppermute | solution.py:28
  63.5 13.4 %collective-permute-start.10 = (bf16[128,1024]{1,0:T(8,128)(2,1)S(1)}, bf16[128,1024]{1,0:T(8,128)(2,1)}, u32[]{:S(2)}, u32[]{:S(2)}) collective-permute-start(bf16[128,1024]{1,0:T(8,128)(2,1)S(1)} %collective-permute-done.9.refs_4_), channel_id=1, source_target_pairs={{0,32},{2,34},{4,36},{6,38},{8,40},{9,1},{10,42},{11,3},{12,44},{1... | collective-permute-start | bytes 786440 | tf_op jit(solution)/shard_map/ppermute | solution.py:28
  64.8 12.2 %copy-start.3 = (bf16[128,1024]{1,0:T(8,128)(2,1)S(1)}, bf16[128,1024]{1,0:T(8,128)(2,1)}, u32[]{:S(2)}) copy-start(bf16[128,1024]{1,0:T(8,128)(2,1)} %copy-done.2) | copy-start | bytes 786436
  65.5 11.5 %collective-permute-start.2 = (bf16[64,256]{1,0:T(8,128)(2,1)S(1)}, bf16[64,256]{1,0:T(8,128)(2,1)S(1)}, u32[]{:S(2)}, u32[]{:S(2)}) collective-permute-start(bf16[64,256]{1,0:T(8,128)(2,1)S(1)} %get-tuple-element.13.p0), channel_id=1, source_target_pairs={{0,4},{1,5},{2,6},{3,7},{4,0},{5,1},{6,2},{7,3},{8,12},{9,13},{10,... | collective-permute-start | bytes 98312 | tf_op jit(solution)/shard_map/ppermute | solution.py:28
  69.0 8.0 %collective-permute-start.1 = (bf16[64,256]{1,0:T(8,128)(2,1)S(1)}, bf16[64,256]{1,0:T(8,128)(2,1)S(1)}, u32[]{:S(2)}, u32[]{:S(2)}) collective-permute-start(bf16[64,256]{1,0:T(8,128)(2,1)S(1)} %get-tuple-element.13.p0), channel_id=1, source_target_pairs={{0,6},{1,7},{2,4},{3,5},{4,2},{5,3},{6,0},{7,1},{8,14},{9,15},{10,... | collective-permute-start | bytes 98312 | tf_op jit(solution)/shard_map/ppermute | solution.py:28
  69.3 7.6 %collective-permute-start = (bf16[64,256]{1,0:T(8,128)(2,1)S(1)}, bf16[64,256]{1,0:T(8,128)(2,1)S(1)}, u32[]{:S(2)}, u32[]{:S(2)}) collective-permute-start(bf16[64,256]{1,0:T(8,128)(2,1)S(1)} %get-tuple-element.13.p0), channel_id=1, source_target_pairs={{0,2},{1,3},{2,0},{3,1},{4,6},{5,7},{6,4},{7,5},{8,10},{9,11},{10,... | collective-permute-start | bytes 98312 | tf_op jit(solution)/shard_map/ppermute | solution.py:28
  69.3 2.2 %copy-start.1 = (bf16[2,1024,1024]{2,1,0:T(8,128)(2,1)S(1)}, bf16[2,1024,1024]{2,1,0:T(8,128)(2,1)}, u32[]{:S(2)}) copy-start(bf16[2,1024,1024]{2,1,0:T(8,128)(2,1)} %source_hbm) | copy-start | bytes 12582916
  79.3 4.3 %collective-permute-start.15 = (bf16[64,256]{1,0:T(8,128)(2,1)S(1)}, bf16[64,256]{1,0:T(8,128)(2,1)S(1)}, u32[]{:S(2)}, u32[]{:S(2)}) collective-permute-start(bf16[64,256]{1,0:T(8,128)(2,1)S(1)} %get-tuple-element.17.p0), channel_id=1, source_target_pairs={{0,4},{1,5},{2,6},{3,7},{4,0},{5,1},{6,2},{7,3},{8,12},{9,13},{10,... | collective-permute-start | bytes 98312 | tf_op jit(solution)/shard_map/ppermute | solution.py:28
  82.3 4.3 %collective-permute-start.14 = (bf16[64,256]{1,0:T(8,128)(2,1)S(1)}, bf16[64,256]{1,0:T(8,128)(2,1)S(1)}, u32[]{:S(2)}, u32[]{:S(2)}) collective-permute-start(bf16[64,256]{1,0:T(8,128)(2,1)S(1)} %get-tuple-element.17.p0), channel_id=1, source_target_pairs={{0,6},{1,7},{2,4},{3,5},{4,2},{5,3},{6,0},{7,1},{8,14},{9,15},{10,... | collective-permute-start | bytes 98312 | tf_op jit(solution)/shard_map/ppermute | solution.py:28
  82.9 3.7 %collective-permute-start.13 = (bf16[64,256]{1,0:T(8,128)(2,1)S(1)}, bf16[64,256]{1,0:T(8,128)(2,1)S(1)}, u32[]{:S(2)}, u32[]{:S(2)}) collective-permute-start(bf16[64,256]{1,0:T(8,128)(2,1)S(1)} %get-tuple-element.17.p0), channel_id=1, source_target_pairs={{0,2},{1,3},{2,0},{3,1},{4,6},{5,7},{6,4},{7,5},{8,10},{9,11},{10,... | collective-permute-start | bytes 98312 | tf_op jit(solution)/shard_map/ppermute | solution.py:28
  87.3 6.6 %collective-permute-start.18 = (bf16[32,2048]{1,0:T(8,128)(2,1)S(1)}, bf16[32,2048]{1,0:T(8,128)(2,1)S(1)}, u32[]{:S(2)}, u32[]{:S(2)}) collective-permute-start(bf16[32,2048]{1,0:T(8,128)(2,1)S(1)} %shard_map.50), channel_id=1, source_target_pairs={{0,64},{1,17},{2,66},{3,19},{4,68},{5,21},{6,70},{7,23},{8,72},{9,... | collective-permute-start | bytes 393224 | tf_op jit(solution)/shard_map/ppermute | solution.py:28
  87.4 9.1 %collective-permute-start.17 = (bf16[32,2048]{1,0:T(8,128)(2,1)S(1)}, bf16[32,2048]{1,0:T(8,128)(2,1)S(1)}, u32[]{:S(2)}, u32[]{:S(2)}) collective-permute-start(bf16[32,2048]{1,0:T(8,128)(2,1)S(1)} %shard_map.50), channel_id=1, source_target_pairs={{0,96},{1,25},{2,98},{3,27},{4,100},{5,29},{6,102},{7,31},{8,104},... | collective-permute-start | bytes 393224 | tf_op jit(solution)/shard_map/ppermute | solution.py:28
  93.9 3.8 %collective-permute-start.16 = (bf16[32,2048]{1,0:T(8,128)(2,1)S(1)}, bf16[32,2048]{1,0:T(8,128)(2,1)S(1)}, u32[]{:S(2)}, u32[]{:S(2)}) collective-permute-start(bf16[32,2048]{1,0:T(8,128)(2,1)S(1)} %shard_map.50), channel_id=1, source_target_pairs={{0,32},{1,9},{2,34},{3,11},{4,36},{5,13},{6,38},{7,15},{8,40},{9,1... | collective-permute-start | bytes 393224 | tf_op jit(solution)/shard_map/ppermute | solution.py:28
  97.8 9.6 %collective-permute-start.21 = (bf16[128,2048]{1,0:T(8,128)(2,1)S(1)}, bf16[128,2048]{1,0:T(8,128)(2,1)S(1)}, u32[]{:S(2)}, u32[]{:S(2)}) collective-permute-start(bf16[128,2048]{1,0:T(8,128)(2,1)S(1)} %pad_maximum_fusion.refs_0_), channel_id=1, source_target_pairs={{0,24},{1,97},{2,26},{3,99},{4,28},{5,101},{6,30},{7,103},{8,16},{... | collective-permute-start | bytes 1572872 | tf_op jit(solution)/shard_map/ppermute | solution.py:28
  97.8 9.6 %collective-permute-start.19 = (bf16[128,2048]{1,0:T(8,128)(2,1)S(1)}, bf16[128,2048]{1,0:T(8,128)(2,1)S(1)}, u32[]{:S(2)}, u32[]{:S(2)}) collective-permute-start(bf16[128,2048]{1,0:T(8,128)(2,1)S(1)} %pad_maximum_fusion.refs_0_), channel_id=1, source_target_pairs={{0,8},{1,33},{2,10},{3,35},{4,12},{5,37},{6,14},{7,39},{8,0},{9,41... | collective-permute-start | bytes 1572872 | tf_op jit(solution)/shard_map/ppermute | solution.py:28
  107.4 5.6 %collective-permute-start.23 = (bf16[64,2048]{1,0:T(8,128)(2,1)S(1)}, bf16[64,2048]{1,0:T(8,128)(2,1)S(1)}, u32[]{:S(2)}, u32[]{:S(2)}) collective-permute-start(bf16[64,2048]{1,0:T(8,128)(2,1)S(1)} %slice.12), channel_id=1, source_target_pairs={{0,8},{1,33},{2,10},{3,35},{4,12},{5,37},{6,14},{7,39},{8,0},{9,41... | collective-permute-start | bytes 786440 | tf_op jit(solution)/shard_map/ppermute | solution.py:28
  107.5 7.9 %collective-permute-start.24 = (bf16[64,2048]{1,0:T(8,128)(2,1)S(1)}, bf16[64,2048]{1,0:T(8,128)(2,1)S(1)}, u32[]{:S(2)}, u32[]{:S(2)}) collective-permute-start(bf16[64,2048]{1,0:T(8,128)(2,1)S(1)} %slice.13), channel_id=1, source_target_pairs={{0,24},{1,97},{2,26},{3,99},{4,28},{5,101},{6,30},{7,103},{8,16},{... | collective-permute-start | bytes 786440 | tf_op jit(solution)/shard_map/ppermute | solution.py:28
  108.9 14.6 %collective-permute-start.27 = (bf16[128,2048]{1,0:T(8,128)(2,1)S(1)}, bf16[128,2048]{1,0:T(8,128)(2,1)S(1)}, u32[]{:S(2)}, u32[]{:S(2)}) collective-permute-start(bf16[128,2048]{1,0:T(8,128)(2,1)S(1)} %pad_maximum_fusion.refs_0_), channel_id=1, source_target_pairs={{0,1},{1,0},{2,3},{3,2},{4,5},{5,4},{6,7},{7,6},{8,9},{9,8},{10,11... | collective-permute-start | bytes 1572872 | tf_op jit(solution)/shard_map/ppermute | solution.py:28
  111.8 13.3 %collective-permute-start.22 = (bf16[128,2048]{1,0:T(8,128)(2,1)S(1)}, bf16[128,2048]{1,0:T(8,128)(2,1)S(1)}, u32[]{:S(2)}, u32[]{:S(2)}) collective-permute-start(bf16[128,2048]{1,0:T(8,128)(2,1)S(1)} %collective-permute-done.21.refs_1_), channel_id=1, source_target_pairs={{0,1},{1,0},{2,3},{3,2},{4,5},{5,4},{6,7},{7,6},{8,9},{9,8},{10,11... | collective-permute-start | bytes 1572872 | tf_op jit(solution)/shard_map/ppermute | solution.py:28
  111.8 13.3 %collective-permute-start.20 = (bf16[128,2048]{1,0:T(8,128)(2,1)S(1)}, bf16[128,2048]{1,0:T(8,128)(2,1)S(1)}, u32[]{:S(2)}, u32[]{:S(2)}) collective-permute-start(bf16[128,2048]{1,0:T(8,128)(2,1)S(1)} %collective-permute-done.19.refs_0_), channel_id=1, source_target_pairs={{0,1},{1,0},{2,3},{3,2},{4,5},{5,4},{6,7},{7,6},{8,9},{9,8},{10,11... | collective-permute-start | bytes 1572872 | tf_op jit(solution)/shard_map/ppermute | solution.py:28
  113.0 12.2 %collective-permute-start.25 = (bf16[64,2048]{1,0:T(8,128)(2,1)S(1)}, bf16[64,2048]{1,0:T(8,128)(2,1)S(1)}, u32[]{:S(2)}, u32[]{:S(2)}) collective-permute-start(bf16[64,2048]{1,0:T(8,128)(2,1)S(1)} %collective-permute-done.23.refs_2_), channel_id=1, source_target_pairs={{0,1},{1,0},{2,3},{3,2},{4,5},{5,4},{6,7},{7,6},{8,9},{9,8},{10,11... | collective-permute-start | bytes 786440 | tf_op jit(solution)/shard_map/ppermute | solution.py:28
  115.5 9.7 %collective-permute-start.26 = (bf16[64,2048]{1,0:T(8,128)(2,1)S(1)}, bf16[64,2048]{1,0:T(8,128)(2,1)S(1)}, u32[]{:S(2)}, u32[]{:S(2)}) collective-permute-start(bf16[64,2048]{1,0:T(8,128)(2,1)S(1)} %collective-permute-done.24.refs_3_), channel_id=1, source_target_pairs={{0,1},{1,0},{2,3},{3,2},{4,5},{5,4},{6,7},{7,6},{8,9},{9,8},{10,11... | collective-permute-start | bytes 786440 | tf_op jit(solution)/shard_map/ppermute | solution.py:28
  118.8 3.2 %copy-start = (bf16[2,8,1,128,1024]{4,3,2,1,0:T(8,128)(2,1)S(1)}, bf16[2,8,1,128,1024]{4,3,2,1,0:T(8,128)(2,1)}, u32[]{:S(2)}) copy-start(bf16[2,8,1,128,1024]{4,3,2,1,0:T(8,128)(2,1)} %refs_8_.1) | copy-start | bytes 12582916
  (1 other events, 0.7 us)

commit v4 on v3

--- a/solution.py
+++ b/solution.py
@@ -136,14 +136,12 @@
     return jnp.concatenate([scratch[i] for i in range(4)], axis=1)
 
 
-def first_kernel(p0, p1, p2, p3, inverse_ref, next_ref, *refs):
-    own_ref, other_ref = refs[0:4], refs[4:8]
-    solved_ref, second_ref, scratch = refs[8:]
+def first_kernel(p0, p1, p2, p3, inverse_ref, next_ref, own_ref, other_ref, solved_ref, second_ref, scratch):
     lead = gather_cols((p0, p1, p2, p3), scratch)
     solved = dot(lead, inverse_ref[...], (1, 1)).astype(BF16)
     solved_ref[...] = solved
-    own = dot(solved, sum(ref[...] for ref in own_ref), (1, 1))
-    other = dot(solved, sum(ref[...] for ref in other_ref), (1, 1))
+    own = dot(solved, own_ref[...], (1, 1))
+    other = dot(solved, other_ref[...], (1, 1))
     even = lax.axis_index("col") % 2 == 0
     low = jnp.where(even, own, other)
     high = jnp.where(even, other, own)
@@ -208,45 +206,34 @@
 def updated_blocks(blocks, pieces, panels_ref, rows_ref, solved_t, head_ref, write):
     keep = jnp.where(lax.axis_index("row") < 2, 0.0, 1.0)
     heads_of(panels_ref, head_ref)
-    pieces = list(pieces)
-    for i, (kind, _, parts) in enumerate(blocks):
+    for i, (kind, _) in enumerate(blocks):
         first, _, _ = place_of(kind)
-        places = (first, first ^ 1, 3 - first, first ^ 2)
-        held = [pieces.pop(0) for _ in range(parts)]
-        for j in range(4):
-            at = pl.multiple_of(128 * i + 32 * places[j], 32)
-            ref, j = (held[0], j) if parts == 1 else (held[j // 2], j % 2)
-            solved_t[pl.ds(at, 32), :] = ref[j * 32 : j * 32 + 32, :]
-        if i % 2 == 0:
-            continue
-        head, tail = product(panels_ref, head_ref, solved_t.at[128 * i - 128 : 128 * i + 128])
-        for n in (i - 1, i):
-            draws = draws_of(blocks[n])
-            part = slice(128 * (n % 2), 128 * (n % 2) + 128)
-            write(n, slice(0, 128), rows_ref[0:128, draws].astype(F32) * keep - head[:, part])
-            write(n, slice(128, 1024), rows_ref[128:1024, draws].astype(F32) - tail[:, part])
+        for j, place in enumerate((first, first ^ 1, 3 - first, first ^ 2)):
+            at = pl.multiple_of(128 * i + 32 * place, 32)
+            solved_t[pl.ds(at, 32), :] = pieces[i][j * 32 : j * 32 + 32, :]
+    head, tail = product(panels_ref, head_ref, solved_t)
+    for n in range(2):
+        draws = draws_of(blocks[n])
+        part = slice(128 * n, 128 * n + 128)
+        write(n, slice(0, 128), rows_ref[0:128, draws].astype(F32) * keep - head[:, part])
+        write(n, slice(128, 1024), rows_ref[128:1024, draws].astype(F32) - tail[:, part])
 
 
 def draws_of(block):
-    kind, which, _ = block
+    kind, which = block
     _, second, core = place_of(kind)
     at = second if which == 3 else swap(which, second)
     return pl.ds(pl.multiple_of(128 * (4 * core + at), 128), 128)
 
 
-def update_kernel(blocks, *refs):
-    count = sum(parts for _, _, parts in blocks)
-    panels_ref, rows_ref, out_ref, solved_t, head_ref = refs[count:]
-
+def update_kernel(blocks, a_ref, b_ref, panels_ref, rows_ref, out_ref, solved_t, head_ref):
     def write(n, rows, value):
         out_ref[rows, 128 * n : 128 * n + 128] = value.astype(BF16)
 
-    updated_blocks(blocks, refs[:count], panels_ref, rows_ref, solved_t, head_ref, write)
-
-
-def last_kernel(before, blocks, *refs):
-    count = sum(parts for _, _, parts in blocks)
-    pieces, refs = refs[:count], refs[count:]
+    updated_blocks(blocks, (a_ref, b_ref), panels_ref, rows_ref, solved_t, head_ref, write)
+
+
+def last_kernel(before, blocks, a_ref, b_ref, *refs):
     done, (panels_ref, rows_ref, out_ref, solved_t, head_ref) = refs[: len(before)], refs[len(before) :]
     for held, ref in zip(before, done):
         for n, block in enumerate(held):
@@ -255,7 +242,7 @@
     def write(n, rows, value):
         out_ref[rows, draws_of(blocks[n])] = value.astype(BF16)
 
-    updated_blocks(blocks, pieces, panels_ref, rows_ref, solved_t, head_ref, write)
+    updated_blocks(blocks, (a_ref, b_ref), panels_ref, rows_ref, solved_t, head_ref, write)
 
 
 HBM = pl.BlockSpec(memory_space=pltpu.HBM)
@@ -291,22 +278,18 @@
     return spread_along(piece, False, lambda x, y, z, k: y == 1 if k == 0 else x == 0)
 
 
-def spread_third(line):
-    return spread_along(line, True, lambda x, y, z, k: x == 0 if k == 0 else y == 1)
-
-
 def around_cols(piece):
     return (piece, send(piece, along_z(0)), send(piece, along_z(1)), send(piece, along_z(2)))
 
 
-def update(kernel, blocks, pieces, panels, rows, width):
+def update(kernel, blocks, pieces, panels, rows, width=256):
     return launch(
-        kernel,
+        functools.partial(kernel, blocks),
         (*pieces, panels, rows),
         [((1024, width), BF16)],
-        [pltpu.VMEM((128 * len(blocks), 2048), BF16), pltpu.VMEM((2, 128, 1024), BF16)],
+        [pltpu.VMEM((256, 2048), BF16), pltpu.VMEM((2, 128, 1024), BF16)],
         limit=16,
-        flops=len(blocks) << 29,
+        flops=1 << 30,
         moved=2 << 20,
     )[0]
 
@@ -334,9 +317,7 @@
     piece = panels[0, 0, 0]
     line = spread_first(piece)
     line = jnp.where(row == 1, piece, jnp.zeros_like(piece)) + line[0] + line[1] + line[2]
-    plane = [line] + spread_second(line)
-    other = send(line, other_core)
-    other = [other] + spread_third(other)
+    plane = spread_second(line)
     arrived = lax.all_to_all(ordered.reshape(128, 8, 1408), AXES, split_axis=0, concat_axis=0, tiled=True)
     inverses, _ = lax.optimization_barrier((diag_inverse, ordered))
     inverses = launch(
@@ -358,9 +339,12 @@
         flops=1 << 27,
         moved=1 << 20,
     )
+    line, plane, _ = lax.optimization_barrier((line, plane, own))
+    link = line + plane[0] + plane[1] + plane[2]
+    link_other = send(link, other_core)
     solved, second = launch(
         first_kernel,
-        (*around_cols(lead), inverses[0], follow, *plane, *other),
+        (*around_cols(lead), inverses[0], follow, link, link_other),
         [((64, 1024), BF16), ((64, 256), BF16)],
         [pltpu.VMEM((4, 64, 256), BF16)],
         limit=12,
@@ -388,19 +372,21 @@
     )
     line = [both] + [send(both, along_first(i)) for i in range(3)]
     line = jnp.concatenate(line, axis=0)
-    side0, side1 = send(line, along_second(0)), send(line, along_second(1))
-    far0, far1 = send(side1[0:64], along_second(0)), send(side0[64:128], along_second(1))
+    side2, side0 = send(line, along_second(2)), send(line, along_second(0))
+    side1 = send(line, along_second(1))
     line_other = send(line, other_core)
-    side0_other, side1_other = send(side0, other_core), send(side1, other_core)
-    far_other = send(far0, other_core), send(far1, other_core)
-    lines = ((0, 3, 1), (1, 3, 1))
-    sides = ((0, 0, 1), (0, 1, 1))
-    rest = ((1, 0, 1), (1, 1, 1), (0, 2, 2), (1, 2, 2))
-    part0 = update(functools.partial(update_kernel, lines), lines, (line, line_other), panels, rows, 256)
-    part1 = update(functools.partial(update_kernel, sides), sides, (side0, side1), panels, rows, 256)
-    pieces = (side0_other, side1_other, far0, far1, *far_other, part0, part1)
-    kernel = functools.partial(last_kernel, (lines, sides), rest)
-    return update(kernel, rest, pieces, panels, rows, 1024).reshape(8, 1, 128, 1024)
+    side2_other, side0_other = send(side2, other_core), send(side0, other_core)
+    side1_other = send(side1, other_core)
+    lines = ((0, 3), (1, 3))
+    owns = ((0, 2), (0, 0))
+    others = ((1, 2), (1, 0))
+    last = ((0, 1), (1, 1))
+    part0 = update(update_kernel, lines, (line, line_other), panels, rows)
+    part1 = update(update_kernel, owns, (side2, side0), panels, rows)
+    part2 = update(update_kernel, others, (side2_other, side0_other), panels, rows)
+    kernel = functools.partial(last_kernel, (lines, owns, others))
+    pieces = (side1, side1_other, part0, part1, part2)
+    return update(kernel, last, pieces, panels, rows, 1024).reshape(8, 1, 128, 1024)
 
 
 def solution(mesh):

time: 130 us -> 127 us (0.977)
  starting transfers between devices: 49.2 us -> 59 us
  waiting for transfers between devices: 54 us -> 44.4 us
  local copies, waits for them, and re-layouts: 3.91 us -> 0.98 us
    ppermute x28 -> x23, starting transfers between devices: 37.7 us -> 47.5 us  [send(): return lax.ppermute(value, AXES, pairs)]
    ppermute x28 -> x23, waiting for transfers between devices: 54 us -> 44.4 us  [send(): return lax.ppermute(value, AXES, pairs)]
    unnamed x8 -> x4, local copies, waits for them, and re-layouts: 2.9 us -> 0.01 us
    pallas_call x9 -> x10, Pallas kernels: 21.1 us -> 20.1 us  [launch(): pl.pallas_call(kernel, out_shape=[jax.ShapeDtypeStruct(s, d) for s, d in...]
  transfers between devices with their start and end apart: 29 -> 24, of which waited for: 8 -> 9; matrix products, arithmetic and copies ran while one was open for 2% -> 2% of each run, Pallas kernels for 6% -> 7%
where the time goes in v4:
time: 127 us
  starting transfers between devices  59 us (46%)
  waiting for transfers between devices  44.4 us (35%)
  Pallas kernels  20.1 us (16%)
  other arithmetic  2.28 us (2%)
    ppermute x23, starting transfers between devices, send(): return lax.ppermute(value, AXES, pairs)  47.5 us
    ppermute x23, waiting for transfers between devices, send(): return lax.ppermute(value, AXES, pairs)  44.4 us
    pallas_call x10, Pallas kernels, launch(): pl.pallas_call(kernel, out_shape=[jax.ShapeDtypeStruct(s, d) for s, d in...  20.1 us
    all_to_all x1, starting transfers between devices, steps(): lax.all_to_all(ordered.reshape(128, 8, 1408), AXES, split_axis=0, concat_...  11.5 us
  transfers between devices with their start and end apart: 24, of which 9 were waited for; matrix products, arithmetic and copies ran while one was open for 2% of the time, Pallas kernels for 7%

profile of v4, /device:TPU:1, one launch (start us, length us, event | category | flops | bytes accessed | tf_op | source)
XLA Modules:
  0.0 126.9 jit_solution(8252787685934584390)
XLA Ops:
  0.0 6.4 %shard_map.46 = bf16[1024,1408]{1,0:T(8,128)(2,1)} custom-call(s32[1,1024]{1,0:T(1,128)} %bitcast.13, bf16[1024,1024]{1,0:T(8,128)(2,1)} %rows_hbm.1), custom_call_target="tpu_custom_call" | custom-call | flops 3221225472 | bytes 5242880 | tf_op jit(solution)/shard_map/pallas_call | solution.py:253
  6.4 11.5 %all-to-all-start = ((bf16[128,8,1408]{2,1,0:T(8,128)(2,1)}), bf16[128,8,1408]{2,1,0:T(8,128)(2,1)S(1)}, u32[]{:S(2)}, u32[]{:S(2)}) async-start(bf16[128,8,1408]{2,1,0:T(8,128)(2,1)} %bitcast.12), calls=%async_computation | async-start | bytes 5767168 | tf_op jit(solution)/shard_map/all_to_all | solution.py:321
  19.5 1.3 %collective-permute-start.3 = (bf16[128,1024]{1,0:T(8,128)(2,1)S(1)}, bf16[128,1024]{1,0:T(8,128)(2,1)}, u32[]{:S(2)}, u32[]{:S(2)}) collective-permute-start(bf16[128,1024]{1,0:T(8,128)(2,1)S(1)} %slice_bitcast_fusion), channel_id=1, source_target_pairs={{8,40},{9,1},{10,42},{11,3},{12,44},{13,5},{14,46},{15,7}} | collective-permute-start | bytes 786440 | tf_op jit(solution)/shard_map/ppermute | solution.py:28
  20.8 1.4 %collective-permute-start.5 = (bf16[128,1024]{1,0:T(8,128)(2,1)S(1)}, bf16[128,1024]{1,0:T(8,128)(2,1)}, u32[]{:S(2)}, u32[]{:S(2)}) collective-permute-start(bf16[128,1024]{1,0:T(8,128)(2,1)S(1)} %slice_bitcast_fusion), channel_id=1, source_target_pairs={{8,72},{9,25},{10,74},{11,27},{12,76},{13,29},{14,78},{15,31}} | collective-permute-start | bytes 786440 | tf_op jit(solution)/shard_map/ppermute | solution.py:28
  22.2 31.3 %collective-permute-done.3 = bf16[128,1024]{1,0:T(8,128)(2,1)} collective-permute-done((bf16[128,1024]{1,0:T(8,128)(2,1)S(1)}, bf16[128,1024]{1,0:T(8,128)(2,1)}, u32[]{:S(2)}, u32[]{:S(2)}) %collective-permute-start.3) | collective-permute-done | bytes 262176 | tf_op jit(solution)/shard_map/ppermute | solution.py:28
  53.5 1.2 add_add_fusion.1
  54.7 1.3 %collective-permute-start.8 = (bf16[128,1024]{1,0:T(8,128)(2,1)S(1)}, bf16[128,1024]{1,0:T(8,128)(2,1)S(1)}, u32[]{:S(2)}, u32[]{:S(2)}) collective-permute-start(bf16[128,1024]{1,0:T(8,128)(2,1)S(1)} %add_add_fusion.1), channel_id=1, source_target_pairs={{1,65},{3,67},{5,69},{7,71},{8,24},{9,73},{10,26},{11,75},{12,28},... | collective-permute-start | bytes 786440 | tf_op jit(solution)/shard_map/ppermute | solution.py:28
  56.0 2.0 %collective-permute-start.7 = (bf16[128,1024]{1,0:T(8,128)(2,1)S(1)}, bf16[128,1024]{1,0:T(8,128)(2,1)}, u32[]{:S(2)}, u32[]{:S(2)}) collective-permute-start(bf16[128,1024]{1,0:T(8,128)(2,1)S(1)} %add_add_fusion.1), channel_id=1, source_target_pairs={{1,97},{3,99},{5,101},{7,103},{8,16},{9,105},{10,18},{11,107},{12,... | collective-permute-start | bytes 786440 | tf_op jit(solution)/shard_map/ppermute | solution.py:28
  58.0 2.0 %collective-permute-start.6 = (bf16[128,1024]{1,0:T(8,128)(2,1)S(1)}, bf16[128,1024]{1,0:T(8,128)(2,1)}, u32[]{:S(2)}, u32[]{:S(2)}) collective-permute-start(bf16[128,1024]{1,0:T(8,128)(2,1)S(1)} %add_add_fusion.1), channel_id=1, source_target_pairs={{1,33},{3,35},{5,37},{7,39},{8,0},{9,41},{10,2},{11,43},{12,4},{13... | collective-permute-start | bytes 786440 | tf_op jit(solution)/shard_map/ppermute | solution.py:28
  60.6 1.9 %collective-permute-done.6 = bf16[128,1024]{1,0:T(8,128)(2,1)} collective-permute-done((bf16[128,1024]{1,0:T(8,128)(2,1)S(1)}, bf16[128,1024]{1,0:T(8,128)(2,1)}, u32[]{:S(2)}, u32[]{:S(2)}) %collective-permute-start.6) | collective-permute-done | bytes 262176 | tf_op jit(solution)/shard_map/ppermute | solution.py:28
  62.6 1.1 add_add_fusion.own_ref
  63.7 4.0 %collective-permute-start.9 = (bf16[128,1024]{1,0:T(8,128)(2,1)S(1)}, bf16[128,1024]{1,0:T(8,128)(2,1)S(1)}, u32[]{:S(2)}, u32[]{:S(2)}) collective-permute-start(bf16[128,1024]{1,0:T(8,128)(2,1)S(1)} %add_add_fusion.own_ref), channel_id=1, source_target_pairs={{0,1},{1,0},{2,3},{3,2},{4,5},{5,4},{6,7},{7,6},{8,9},{9,8},{10,11... | collective-permute-start | bytes 786440 | tf_op jit(solution)/shard_map/ppermute | solution.py:28
  67.6 3.2 %collective-permute-start.2 = (bf16[64,256]{1,0:T(8,128)(2,1)S(1)}, bf16[64,256]{1,0:T(8,128)(2,1)S(1)}, u32[]{:S(2)}, u32[]{:S(2)}) collective-permute-start(bf16[64,256]{1,0:T(8,128)(2,1)S(1)} %get-tuple-element.17.p0), channel_id=1, source_target_pairs={{0,4},{1,5},{2,6},{3,7},{4,0},{5,1},{6,2},{7,3},{8,12},{9,13},{10,... | collective-permute-start | bytes 98312 | tf_op jit(solution)/shard_map/ppermute | solution.py:28
  72.1 2.7 %collective-permute-done.1.p2 = bf16[64,256]{1,0:T(8,128)(2,1)S(1)} collective-permute-done((bf16[64,256]{1,0:T(8,128)(2,1)S(1)}, bf16[64,256]{1,0:T(8,128)(2,1)S(1)}, u32[]{:S(2)}, u32[]{:S(2)}) %collective-permute-start.1) | collective-permute-done | bytes 32800 | tf_op jit(solution)/shard_map/ppermute | solution.py:28
  75.7 1.5 %collective-permute-start.12 = (bf16[64,256]{1,0:T(8,128)(2,1)S(1)}, bf16[64,256]{1,0:T(8,128)(2,1)S(1)}, u32[]{:S(2)}, u32[]{:S(2)}) collective-permute-start(bf16[64,256]{1,0:T(8,128)(2,1)S(1)} %get-tuple-element.26.p0), channel_id=1, source_target_pairs={{0,4},{1,5},{2,6},{3,7},{4,0},{5,1},{6,2},{7,3},{8,12},{9,13},{10,... | collective-permute-start | bytes 98312 | tf_op jit(solution)/shard_map/ppermute | solution.py:28
  78.4 1.6 %collective-permute-done.12.p3 = bf16[64,256]{1,0:T(8,128)(2,1)S(1)} collective-permute-done((bf16[64,256]{1,0:T(8,128)(2,1)S(1)}, bf16[64,256]{1,0:T(8,128)(2,1)S(1)}, u32[]{:S(2)}, u32[]{:S(2)}) %collective-permute-start.12) | collective-permute-done | bytes 32800 | tf_op jit(solution)/shard_map/ppermute | solution.py:28
  80.0 1.1 collective-permute-done.11.p2
  82.0 1.6 %collective-permute-start.14 = (bf16[32,2048]{1,0:T(8,128)(2,1)S(1)}, bf16[32,2048]{1,0:T(8,128)(2,1)S(1)}, u32[]{:S(2)}, u32[]{:S(2)}) collective-permute-start(bf16[32,2048]{1,0:T(8,128)(2,1)S(1)} %shard_map.50), channel_id=1, source_target_pairs={{0,96},{1,25},{2,98},{3,27},{4,100},{5,29},{6,102},{7,31},{8,104},... | collective-permute-start | bytes 393224 | tf_op jit(solution)/shard_map/ppermute | solution.py:28
  84.6 2.8 %collective-permute-done.15 = bf16[32,2048]{1,0:T(8,128)(2,1)S(1)} collective-permute-done((bf16[32,2048]{1,0:T(8,128)(2,1)S(1)}, bf16[32,2048]{1,0:T(8,128)(2,1)S(1)}, u32[]{:S(2)}, u32[]{:S(2)}) %collective-permute-start.15) | collective-permute-done | bytes 131104 | tf_op jit(solution)/shard_map/ppermute | solution.py:28
  87.4 1.1 collective-permute-done.14
  88.6 1.8 %collective-permute-start.20 = (bf16[128,2048]{1,0:T(8,128)(2,1)S(1)}, bf16[128,2048]{1,0:T(8,128)(2,1)S(1)}, u32[]{:S(2)}, u32[]{:S(2)}) collective-permute-start(bf16[128,2048]{1,0:T(8,128)(2,1)S(1)} %pad_maximum_fusion.a_ref), channel_id=1, source_target_pairs={{0,8},{1,33},{2,10},{3,35},{4,12},{5,37},{6,14},{7,39},{8,0},{9,41... | collective-permute-start | bytes 1572872 | tf_op jit(solution)/shard_map/ppermute | solution.py:28
  90.4 2.2 %collective-permute-start.19 = (bf16[128,2048]{1,0:T(8,128)(2,1)S(1)}, bf16[128,2048]{1,0:T(8,128)(2,1)S(1)}, u32[]{:S(2)}, u32[]{:S(2)}) collective-permute-start(bf16[128,2048]{1,0:T(8,128)(2,1)S(1)} %pad_maximum_fusion.a_ref), channel_id=1, source_target_pairs={{0,16},{1,65},{2,18},{3,67},{4,20},{5,69},{6,22},{7,71},{8,24},{9,... | collective-permute-start | bytes 1572872 | tf_op jit(solution)/shard_map/ppermute | solution.py:28
  92.8 7.4 %collective-permute-start.18 = (bf16[128,2048]{1,0:T(8,128)(2,1)S(1)}, bf16[128,2048]{1,0:T(8,128)(2,1)S(1)}, u32[]{:S(2)}, u32[]{:S(2)}) collective-permute-start(bf16[128,2048]{1,0:T(8,128)(2,1)S(1)} %pad_maximum_fusion.a_ref), channel_id=1, source_target_pairs={{0,1},{1,0},{2,3},{3,2},{4,5},{5,4},{6,7},{7,6},{8,9},{9,8},{10,11... | collective-permute-start | bytes 1572872 | tf_op jit(solution)/shard_map/ppermute | solution.py:28
  100.2 4.5 %collective-permute-start.22 = (bf16[128,2048]{1,0:T(8,128)(2,1)S(1)}, bf16[128,2048]{1,0:T(8,128)(2,1)S(1)}, u32[]{:S(2)}, u32[]{:S(2)}) collective-permute-start(bf16[128,2048]{1,0:T(8,128)(2,1)S(1)} %collective-permute-done.20.b_ref), channel_id=1, source_target_pairs={{0,1},{1,0},{2,3},{3,2},{4,5},{5,4},{6,7},{7,6},{8,9},{9,8},{10,11... | collective-permute-start | bytes 1572872 | tf_op jit(solution)/shard_map/ppermute | solution.py:28
  104.7 1.5 %collective-permute-done.19.a_ref = bf16[128,2048]{1,0:T(8,128)(2,1)S(1)} collective-permute-done((bf16[128,2048]{1,0:T(8,128)(2,1)S(1)}, bf16[128,2048]{1,0:T(8,128)(2,1)S(1)}, u32[]{:S(2)}, u32[]{:S(2)}) %collective-permute-start.19) | collective-permute-done | bytes 524320 | tf_op jit(solution)/shard_map/ppermute | solution.py:28
  106.2 6.4 %collective-permute-start.21 = (bf16[128,2048]{1,0:T(8,128)(2,1)S(1)}, bf16[128,2048]{1,0:T(8,128)(2,1)S(1)}, u32[]{:S(2)}, u32[]{:S(2)}) collective-permute-start(bf16[128,2048]{1,0:T(8,128)(2,1)S(1)} %collective-permute-done.19.a_ref), channel_id=1, source_target_pairs={{0,1},{1,0},{2,3},{3,2},{4,5},{5,4},{6,7},{7,6},{8,9},{9,8},{10,11... | collective-permute-start | bytes 1572872 | tf_op jit(solution)/shard_map/ppermute | solution.py:28
  112.6 3.1 %collective-permute-start.17 = (bf16[128,2048]{1,0:T(8,128)(2,1)S(1)}, bf16[128,2048]{1,0:T(8,128)(2,1)S(1)}, u32[]{:S(2)}, u32[]{:S(2)}) collective-permute-start(bf16[128,2048]{1,0:T(8,128)(2,1)S(1)} %collective-permute-done.16.a_ref), channel_id=1, source_target_pairs={{0,1},{1,0},{2,3},{3,2},{4,5},{5,4},{6,7},{7,6},{8,9},{9,8},{10,11... | collective-permute-start | bytes 1572872 | tf_op jit(solution)/shard_map/ppermute | solution.py:28
  115.8 3.2 %shard_map.51.rows_ref.refs_4_ = bf16[1024,1024]{1,0:T(8,128)(2,1)S(1)} custom-call(s32[8,1024]{1,0:T(8,128)S(1)} %get-tuple-element.21.own_ref, bf16[1024,1408]{1,0:T(8,128)(2,1)S(1)} %bitcast.11), custom_call_target="tpu_custom_call" | custom-call | flops 2147483648 | bytes 4194304 | tf_op jit(solution)/shard_map/pallas_call | solution.py:253
  118.9 1.6 %shard_map.53.refs_1_ = bf16[1024,256]{1,0:T(8,128)(2,1)S(1)} custom-call(bf16[128,2048]{1,0:T(8,128)(2,1)S(1)} %collective-permute-done.19.a_ref, bf16[128,2048]{1,0:T(8,128)(2,1)S(1)} %collective-permute-done.20.b_ref, bf16[2,8,1,128,1024]{4,3,2,1,0:T(8,128)(2,1)S(1)} %copy-done, bf16[1024,1024]{1,0:T(8,128)(2,1)S(1)} %shard_map.51.rows_ref.refs_4_), custom_call_target="tpu_custom_call" | custom-call | flops 1073741824 | bytes 2097152 | tf_op jit(solution)/shard_map/pallas_call | solution.py:253
  120.5 1.6 %shard_map.52.refs_0_ = bf16[1024,256]{1,0:T(8,128)(2,1)S(1)} custom-call(bf16[128,2048]{1,0:T(8,128)(2,1)S(1)} %pad_maximum_fusion.a_ref, bf16[128,2048]{1,0:T(8,128)(2,1)S(1)} %collective-permute-done.18.b_ref, bf16[2,8,1,128,1024]{4,3,2,1,0:T(8,128)(2,1)S(1)} %copy-done, bf16[1024,1024]{1,0:T(8,128)(2,1)S(1)} %shard_map.51.rows_ref.refs_4_), custom_call_target="tpu_custom_call" | custom-call | flops 1073741824 | bytes 2097152 | tf_op jit(solution)/shard_map/pallas_call | solution.py:253
  122.1 1.6 %shard_map.54.refs_2_ = bf16[1024,256]{1,0:T(8,128)(2,1)S(1)} custom-call(bf16[128,2048]{1,0:T(8,128)(2,1)S(1)} %collective-permute-done.21.a_ref, bf16[128,2048]{1,0:T(8,128)(2,1)S(1)} %collective-permute-done.22.b_ref, bf16[2,8,1,128,1024]{4,3,2,1,0:T(8,128)(2,1)S(1)} %copy-done, bf16[1024,1024]{1,0:T(8,128)(2,1)S(1)} %shard_map.51.rows_ref.refs_4_), custom_call_target="tpu_custom_call" | custom-call | flops 1073741824 | bytes 2097152 | tf_op jit(solution)/shard_map/pallas_call | solution.py:253
  123.7 3.3 %shard_map.55 = bf16[1024,1024]{1,0:T(8,128)(2,1)} custom-call(bf16[128,2048]{1,0:T(8,128)(2,1)S(1)} %collective-permute-done.16.a_ref, bf16[128,2048]{1,0:T(8,128)(2,1)S(1)} %collective-permute-done.17.b_ref, bf16[1024,256]{1,0:T(8,128)(2,1)S(1)} %shard_map.52.refs_0_, bf16[1024,256]{1,0:T(8,128)(2,1)S(1)} %shard_map.53.refs_1_, ...), custom_call_target="tpu_custom_call" | custom-call | flops 1073741824 | bytes 2097152 | tf_op jit(solution)/shard_map/pallas_call | solution.py:253
  (34 shorter events, 7.9 us)
Async XLA Ops:
  6.4 53.6 %all-to-all-start = ((bf16[128,8,1408]{2,1,0:T(8,128)(2,1)}), bf16[128,8,1408]{2,1,0:T(8,128)(2,1)S(1)}, u32[]{:S(2)}, u32[]{:S(2)}) async-start(bf16[128,8,1408]{2,1,0:T(8,128)(2,1)} %bitcast.12), calls=%async_computation | async-start | bytes 5767168 | tf_op jit(solution)/shard_map/all_to_all | solution.py:321
  18.8 3.4 %collective-permute-start.4 = (bf16[128,1024]{1,0:T(8,128)(2,1)S(1)}, bf16[128,1024]{1,0:T(8,128)(2,1)S(1)}, u32[]{:S(2)}, u32[]{:S(2)}) collective-permute-start(bf16[128,1024]{1,0:T(8,128)(2,1)S(1)} %slice_bitcast_fusion), channel_id=1, source_target_pairs={{8,104},{9,17},{10,106},{11,19},{12,108},{13,21},{14,110},{15,23}} | collective-permute-start | bytes 786440 | tf_op jit(solution)/shard_map/ppermute | solution.py:28
  19.5 34.0 %collective-permute-start.3 = (bf16[128,1024]{1,0:T(8,128)(2,1)S(1)}, bf16[128,1024]{1,0:T(8,128)(2,1)}, u32[]{:S(2)}, u32[]{:S(2)}) collective-permute-start(bf16[128,1024]{1,0:T(8,128)(2,1)S(1)} %slice_bitcast_fusion), channel_id=1, source_target_pairs={{8,40},{9,1},{10,42},{11,3},{12,44},{13,5},{14,46},{15,7}} | collective-permute-start | bytes 786440 | tf_op jit(solution)/shard_map/ppermute | solution.py:28
  20.8 32.7 %collective-permute-start.5 = (bf16[128,1024]{1,0:T(8,128)(2,1)S(1)}, bf16[128,1024]{1,0:T(8,128)(2,1)}, u32[]{:S(2)}, u32[]{:S(2)}) collective-permute-start(bf16[128,1024]{1,0:T(8,128)(2,1)S(1)} %slice_bitcast_fusion), channel_id=1, source_target_pairs={{8,72},{9,25},{10,74},{11,27},{12,76},{13,29},{14,78},{15,31}} | collective-permute-start | bytes 786440 | tf_op jit(solution)/shard_map/ppermute | solution.py:28
  54.7 5.9 %collective-permute-start.8 = (bf16[128,1024]{1,0:T(8,128)(2,1)S(1)}, bf16[128,1024]{1,0:T(8,128)(2,1)S(1)}, u32[]{:S(2)}, u32[]{:S(2)}) collective-permute-start(bf16[128,1024]{1,0:T(8,128)(2,1)S(1)} %add_add_fusion.1), channel_id=1, source_target_pairs={{1,65},{3,67},{5,69},{7,71},{8,24},{9,73},{10,26},{11,75},{12,28},... | collective-permute-start | bytes 786440 | tf_op jit(solution)/shard_map/ppermute | solution.py:28
  56.0 4.6 %collective-permute-start.7 = (bf16[128,1024]{1,0:T(8,128)(2,1)S(1)}, bf16[128,1024]{1,0:T(8,128)(2,1)}, u32[]{:S(2)}, u32[]{:S(2)}) collective-permute-start(bf16[128,1024]{1,0:T(8,128)(2,1)S(1)} %add_add_fusion.1), channel_id=1, source_target_pairs={{1,97},{3,99},{5,101},{7,103},{8,16},{9,105},{10,18},{11,107},{12,... | collective-permute-start | bytes 786440 | tf_op jit(solution)/shard_map/ppermute | solution.py:28
  58.0 4.6 %collective-permute-start.6 = (bf16[128,1024]{1,0:T(8,128)(2,1)S(1)}, bf16[128,1024]{1,0:T(8,128)(2,1)}, u32[]{:S(2)}, u32[]{:S(2)}) collective-permute-start(bf16[128,1024]{1,0:T(8,128)(2,1)S(1)} %add_add_fusion.1), channel_id=1, source_target_pairs={{1,33},{3,35},{5,37},{7,39},{8,0},{9,41},{10,2},{11,43},{12,4},{13... | collective-permute-start | bytes 786440 | tf_op jit(solution)/shard_map/ppermute | solution.py:28
  60.0 11.4 %copy-start.1 = (bf16[2,1024,1024]{2,1,0:T(8,128)(2,1)S(1)}, bf16[2,1024,1024]{2,1,0:T(8,128)(2,1)}, u32[]{:S(2)}) copy-start(bf16[2,1024,1024]{2,1,0:T(8,128)(2,1)} %source_hbm) | copy-start | bytes 12582916
  63.7 11.1 %collective-permute-start.9 = (bf16[128,1024]{1,0:T(8,128)(2,1)S(1)}, bf16[128,1024]{1,0:T(8,128)(2,1)S(1)}, u32[]{:S(2)}, u32[]{:S(2)}) collective-permute-start(bf16[128,1024]{1,0:T(8,128)(2,1)S(1)} %add_add_fusion.own_ref), channel_id=1, source_target_pairs={{0,1},{1,0},{2,3},{3,2},{4,5},{5,4},{6,7},{7,6},{8,9},{9,8},{10,11... | collective-permute-start | bytes 786440 | tf_op jit(solution)/shard_map/ppermute | solution.py:28
  67.6 4.5 %collective-permute-start.2 = (bf16[64,256]{1,0:T(8,128)(2,1)S(1)}, bf16[64,256]{1,0:T(8,128)(2,1)S(1)}, u32[]{:S(2)}, u32[]{:S(2)}) collective-permute-start(bf16[64,256]{1,0:T(8,128)(2,1)S(1)} %get-tuple-element.17.p0), channel_id=1, source_target_pairs={{0,4},{1,5},{2,6},{3,7},{4,0},{5,1},{6,2},{7,3},{8,12},{9,13},{10,... | collective-permute-start | bytes 98312 | tf_op jit(solution)/shard_map/ppermute | solution.py:28
  70.8 4.0 %collective-permute-start.1 = (bf16[64,256]{1,0:T(8,128)(2,1)S(1)}, bf16[64,256]{1,0:T(8,128)(2,1)S(1)}, u32[]{:S(2)}, u32[]{:S(2)}) collective-permute-start(bf16[64,256]{1,0:T(8,128)(2,1)S(1)} %get-tuple-element.17.p0), channel_id=1, source_target_pairs={{0,6},{1,7},{2,4},{3,5},{4,2},{5,3},{6,0},{7,1},{8,14},{9,15},{10,... | collective-permute-start | bytes 98312 | tf_op jit(solution)/shard_map/ppermute | solution.py:28
  71.4 3.4 %collective-permute-start = (bf16[64,256]{1,0:T(8,128)(2,1)S(1)}, bf16[64,256]{1,0:T(8,128)(2,1)S(1)}, u32[]{:S(2)}, u32[]{:S(2)}) collective-permute-start(bf16[64,256]{1,0:T(8,128)(2,1)S(1)} %get-tuple-element.17.p0), channel_id=1, source_target_pairs={{0,2},{1,3},{2,0},{3,1},{4,6},{5,7},{6,4},{7,5},{8,10},{9,11},{10,... | collective-permute-start | bytes 98312 | tf_op jit(solution)/shard_map/ppermute | solution.py:28
  75.7 4.3 %collective-permute-start.12 = (bf16[64,256]{1,0:T(8,128)(2,1)S(1)}, bf16[64,256]{1,0:T(8,128)(2,1)S(1)}, u32[]{:S(2)}, u32[]{:S(2)}) collective-permute-start(bf16[64,256]{1,0:T(8,128)(2,1)S(1)} %get-tuple-element.26.p0), channel_id=1, source_target_pairs={{0,4},{1,5},{2,6},{3,7},{4,0},{5,1},{6,2},{7,3},{8,12},{9,13},{10,... | collective-permute-start | bytes 98312 | tf_op jit(solution)/shard_map/ppermute | solution.py:28
  77.2 4.0 %collective-permute-start.11 = (bf16[64,256]{1,0:T(8,128)(2,1)S(1)}, bf16[64,256]{1,0:T(8,128)(2,1)S(1)}, u32[]{:S(2)}, u32[]{:S(2)}) collective-permute-start(bf16[64,256]{1,0:T(8,128)(2,1)S(1)} %get-tuple-element.26.p0), channel_id=1, source_target_pairs={{0,6},{1,7},{2,4},{3,5},{4,2},{5,3},{6,0},{7,1},{8,14},{9,15},{10,... | collective-permute-start | bytes 98312 | tf_op jit(solution)/shard_map/ppermute | solution.py:28
  77.8 3.3 %collective-permute-start.10 = (bf16[64,256]{1,0:T(8,128)(2,1)S(1)}, bf16[64,256]{1,0:T(8,128)(2,1)S(1)}, u32[]{:S(2)}, u32[]{:S(2)}) collective-permute-start(bf16[64,256]{1,0:T(8,128)(2,1)S(1)} %get-tuple-element.26.p0), channel_id=1, source_target_pairs={{0,2},{1,3},{2,0},{3,1},{4,6},{5,7},{6,4},{7,5},{8,10},{9,11},{10,... | collective-permute-start | bytes 98312 | tf_op jit(solution)/shard_map/ppermute | solution.py:28
  81.9 5.5 %collective-permute-start.15 = (bf16[32,2048]{1,0:T(8,128)(2,1)S(1)}, bf16[32,2048]{1,0:T(8,128)(2,1)S(1)}, u32[]{:S(2)}, u32[]{:S(2)}) collective-permute-start(bf16[32,2048]{1,0:T(8,128)(2,1)S(1)} %shard_map.50), channel_id=1, source_target_pairs={{0,64},{1,17},{2,66},{3,19},{4,68},{5,21},{6,70},{7,23},{8,72},{9,... | collective-permute-start | bytes 393224 | tf_op jit(solution)/shard_map/ppermute | solution.py:28
  82.0 6.5 %collective-permute-start.14 = (bf16[32,2048]{1,0:T(8,128)(2,1)S(1)}, bf16[32,2048]{1,0:T(8,128)(2,1)S(1)}, u32[]{:S(2)}, u32[]{:S(2)}) collective-permute-start(bf16[32,2048]{1,0:T(8,128)(2,1)S(1)} %shard_map.50), channel_id=1, source_target_pairs={{0,96},{1,25},{2,98},{3,27},{4,100},{5,29},{6,102},{7,31},{8,104},... | collective-permute-start | bytes 393224 | tf_op jit(solution)/shard_map/ppermute | solution.py:28
  83.6 4.9 %collective-permute-start.13 = (bf16[32,2048]{1,0:T(8,128)(2,1)S(1)}, bf16[32,2048]{1,0:T(8,128)(2,1)S(1)}, u32[]{:S(2)}, u32[]{:S(2)}) collective-permute-start(bf16[32,2048]{1,0:T(8,128)(2,1)S(1)} %shard_map.50), channel_id=1, source_target_pairs={{0,32},{1,9},{2,34},{3,11},{4,36},{5,13},{6,38},{7,15},{8,40},{9,1... | collective-permute-start | bytes 393224 | tf_op jit(solution)/shard_map/ppermute | solution.py:28
  88.6 30.4 %copy-start = (bf16[2,8,1,128,1024]{4,3,2,1,0:T(8,128)(2,1)S(1)}, bf16[2,8,1,128,1024]{4,3,2,1,0:T(8,128)(2,1)}, u32[]{:S(2)}) copy-start(bf16[2,8,1,128,1024]{4,3,2,1,0:T(8,128)(2,1)} %refs_3_.1) | copy-start | bytes 12582916
  88.6 11.7 %collective-permute-start.20 = (bf16[128,2048]{1,0:T(8,128)(2,1)S(1)}, bf16[128,2048]{1,0:T(8,128)(2,1)S(1)}, u32[]{:S(2)}, u32[]{:S(2)}) collective-permute-start(bf16[128,2048]{1,0:T(8,128)(2,1)S(1)} %pad_maximum_fusion.a_ref), channel_id=1, source_target_pairs={{0,8},{1,33},{2,10},{3,35},{4,12},{5,37},{6,14},{7,39},{8,0},{9,41... | collective-permute-start | bytes 1572872 | tf_op jit(solution)/shard_map/ppermute | solution.py:28
  90.4 15.8 %collective-permute-start.19 = (bf16[128,2048]{1,0:T(8,128)(2,1)S(1)}, bf16[128,2048]{1,0:T(8,128)(2,1)S(1)}, u32[]{:S(2)}, u32[]{:S(2)}) collective-permute-start(bf16[128,2048]{1,0:T(8,128)(2,1)S(1)} %pad_maximum_fusion.a_ref), channel_id=1, source_target_pairs={{0,16},{1,65},{2,18},{3,67},{4,20},{5,69},{6,22},{7,71},{8,24},{9,... | collective-permute-start | bytes 1572872 | tf_op jit(solution)/shard_map/ppermute | solution.py:28
  92.6 20.0 %collective-permute-start.16 = (bf16[128,2048]{1,0:T(8,128)(2,1)S(1)}, bf16[128,2048]{1,0:T(8,128)(2,1)S(1)}, u32[]{:S(2)}, u32[]{:S(2)}) collective-permute-start(bf16[128,2048]{1,0:T(8,128)(2,1)S(1)} %pad_maximum_fusion.a_ref), channel_id=1, source_target_pairs={{0,24},{1,97},{2,26},{3,99},{4,28},{5,101},{6,30},{7,103},{8,16},{... | collective-permute-start | bytes 1572872 | tf_op jit(solution)/shard_map/ppermute | solution.py:28
  92.8 27.7 %collective-permute-start.18 = (bf16[128,2048]{1,0:T(8,128)(2,1)S(1)}, bf16[128,2048]{1,0:T(8,128)(2,1)S(1)}, u32[]{:S(2)}, u32[]{:S(2)}) collective-permute-start(bf16[128,2048]{1,0:T(8,128)(2,1)S(1)} %pad_maximum_fusion.a_ref), channel_id=1, source_target_pairs={{0,1},{1,0},{2,3},{3,2},{4,5},{5,4},{6,7},{7,6},{8,9},{9,8},{10,11... | collective-permute-start | bytes 1572872 | tf_op jit(solution)/shard_map/ppermute | solution.py:28
  100.2 21.8 %collective-permute-start.22 = (bf16[128,2048]{1,0:T(8,128)(2,1)S(1)}, bf16[128,2048]{1,0:T(8,128)(2,1)S(1)}, u32[]{:S(2)}, u32[]{:S(2)}) collective-permute-start(bf16[128,2048]{1,0:T(8,128)(2,1)S(1)} %collective-permute-done.20.b_ref), channel_id=1, source_target_pairs={{0,1},{1,0},{2,3},{3,2},{4,5},{5,4},{6,7},{7,6},{8,9},{9,8},{10,11... | collective-permute-start | bytes 1572872 | tf_op jit(solution)/shard_map/ppermute | solution.py:28
  106.2 15.9 %collective-permute-start.21 = (bf16[128,2048]{1,0:T(8,128)(2,1)S(1)}, bf16[128,2048]{1,0:T(8,128)(2,1)S(1)}, u32[]{:S(2)}, u32[]{:S(2)}) collective-permute-start(bf16[128,2048]{1,0:T(8,128)(2,1)S(1)} %collective-permute-done.19.a_ref), channel_id=1, source_target_pairs={{0,1},{1,0},{2,3},{3,2},{4,5},{5,4},{6,7},{7,6},{8,9},{9,8},{10,11... | collective-permute-start | bytes 1572872 | tf_op jit(solution)/shard_map/ppermute | solution.py:28
  112.6 11.1 %collective-permute-start.17 = (bf16[128,2048]{1,0:T(8,128)(2,1)S(1)}, bf16[128,2048]{1,0:T(8,128)(2,1)S(1)}, u32[]{:S(2)}, u32[]{:S(2)}) collective-permute-start(bf16[128,2048]{1,0:T(8,128)(2,1)S(1)} %collective-permute-done.16.a_ref), channel_id=1, source_target_pairs={{0,1},{1,0},{2,3},{3,2},{4,5},{5,4},{6,7},{7,6},{8,9},{9,8},{10,11... | collective-permute-start | bytes 1572872 | tf_op jit(solution)/shard_map/ppermute | solution.py:28

commit v5 on v4

--- a/solution.py
+++ b/solution.py
@@ -206,11 +206,7 @@
 def updated_blocks(blocks, pieces, panels_ref, rows_ref, solved_t, head_ref, write):
     keep = jnp.where(lax.axis_index("row") < 2, 0.0, 1.0)
     heads_of(panels_ref, head_ref)
-    for i, (kind, _) in enumerate(blocks):
-        first, _, _ = place_of(kind)
-        for j, place in enumerate((first, first ^ 1, 3 - first, first ^ 2)):
-            at = pl.multiple_of(128 * i + 32 * place, 32)
-            solved_t[pl.ds(at, 32), :] = pieces[i][j * 32 : j * 32 + 32, :]
+    place_blocks(blocks, pieces, solved_t)
     head, tail = product(panels_ref, head_ref, solved_t)
     for n in range(2):
         draws = draws_of(blocks[n])
@@ -219,6 +215,14 @@
         write(n, slice(128, 1024), rows_ref[128:1024, draws].astype(F32) - tail[:, part])
 
 
+def place_blocks(blocks, pieces, solved_t):
+    for i, (kind, _) in enumerate(blocks):
+        first, _, _ = place_of(kind)
+        for j, place in enumerate((first, first ^ 1, 3 - first, first ^ 2)):
+            at = pl.multiple_of(128 * i + 32 * place, 32)
+            solved_t[pl.ds(at, 32), :] = pieces[i][j * 32 : j * 32 + 32, :]
+
+
 def draws_of(block):
     kind, which = block
     _, second, core = place_of(kind)
@@ -234,15 +238,34 @@
 
 
 def last_kernel(before, blocks, a_ref, b_ref, *refs):
-    done, (panels_ref, rows_ref, out_ref, solved_t, head_ref) = refs[: len(before)], refs[len(before) :]
-    for held, ref in zip(before, done):
-        for n, block in enumerate(held):
-            out_ref[:, draws_of(block)] = ref[:, 128 * n : 128 * n + 128]
-
-    def write(n, rows, value):
-        out_ref[rows, draws_of(blocks[n])] = value.astype(BF16)
-
-    updated_blocks(blocks, (a_ref, b_ref), panels_ref, rows_ref, solved_t, head_ref, write)
+    done, (panels_ref, rows_ref, out_hbm, solved_t, head_ref, out_ref, sems) = refs[: len(before)], refs[len(before) :]
+    keep = jnp.where(lax.axis_index("row") < 2, 0.0, 1.0)
+    heads_of(panels_ref, head_ref)
+    place_blocks(blocks, (a_ref, b_ref), solved_t)
+    stores = []
+    for q in range(4):
+        value = 0.0
+        for p in range(2):
+            solved = solved_t[:, p * 1024 : p * 1024 + 1024]
+            if q == 0:
+                factor = jnp.concatenate([head_ref[p], panels_ref[p, 1, 0]], axis=0)
+            else:
+                factor = panels_ref[p, 2 * q : 2 * q + 2, 0].reshape(256, 1024)
+            value = value + dot(factor, solved, (1, 1))
+        span = slice(q * 256, q * 256 + 256)
+        for held, ref in zip(before, done):
+            for n, block in enumerate(held):
+                out_ref[span, draws_of(block)] = ref[span, 128 * n : 128 * n + 128]
+        for n in range(2):
+            draws = draws_of(blocks[n])
+            rest = rows_ref[span, draws].astype(F32)
+            if q == 0:
+                rest = rest * jnp.where(iota((256, 128), 0) < 128, keep, 1.0)
+            out_ref[span, draws] = (rest - value[:, 128 * n : 128 * n + 128]).astype(BF16)
+        stores.append(pltpu.make_async_copy(out_ref.at[pl.ds(q * 256, 256)], out_hbm.at[pl.ds(q * 256, 256)], sems.at[q]))
+        stores[q].start()
+    for store in stores:
+        store.wait()
 
 
 HBM = pl.BlockSpec(memory_space=pltpu.HBM)
@@ -271,7 +294,12 @@
 
 
 def spread_first(piece):
-    return spread_along(piece, True, lambda x, y, z, k: x == 0 and y == 1)
+    moved = [send(piece, along_first(kind)) for kind in range(3)]
+    first, second, core = place_of(0)
+    source = jnp.where(core == 0, 0, 1)
+    line = jnp.where(first ^ 1 == source, moved[0], jnp.where(3 - first == source, moved[1], moved[2]))
+    line = jnp.where(first == source, piece, line)
+    return jnp.where(second == 1 - source, line, jnp.zeros_like(line))
 
 
 def spread_second(piece):
@@ -282,12 +310,13 @@
     return (piece, send(piece, along_z(0)), send(piece, along_z(1)), send(piece, along_z(2)))
 
 
-def update(kernel, blocks, pieces, panels, rows, width=256):
+def update(kernel, blocks, pieces, panels, rows, width=256, extra=(), out=VMEM):
     return launch(
         functools.partial(kernel, blocks),
         (*pieces, panels, rows),
         [((1024, width), BF16)],
-        [pltpu.VMEM((256, 2048), BF16), pltpu.VMEM((2, 128, 1024), BF16)],
+        [pltpu.VMEM((256, 2048), BF16), pltpu.VMEM((2, 128, 1024), BF16), *extra],
+        out_specs=[out],
         limit=16,
         flops=1 << 30,
         moved=2 << 20,
@@ -295,7 +324,6 @@
 
 
 def steps(b_ingest, source_point, panels, diag_inverse):
-    row = lax.axis_index("row")
     (ordered,) = launch(
         order_kernel,
         (source_point.reshape(1, 1024), b_ingest),
@@ -316,7 +344,6 @@
     )
     piece = panels[0, 0, 0]
     line = spread_first(piece)
-    line = jnp.where(row == 1, piece, jnp.zeros_like(piece)) + line[0] + line[1] + line[2]
     plane = spread_second(line)
     arrived = lax.all_to_all(ordered.reshape(128, 8, 1408), AXES, split_axis=0, concat_axis=0, tiled=True)
     inverses, _ = lax.optimization_barrier((diag_inverse, ordered))
@@ -386,7 +413,9 @@
     part2 = update(update_kernel, others, (side2_other, side0_other), panels, rows)
     kernel = functools.partial(last_kernel, (lines, owns, others))
     pieces = (side1, side1_other, part0, part1, part2)
-    return update(kernel, last, pieces, panels, rows, 1024).reshape(8, 1, 128, 1024)
+    extra = (pltpu.VMEM((1024, 1024), BF16), pltpu.SemaphoreType.DMA((4,)))
+    updated = update(kernel, last, pieces, panels, rows, 1024, extra, HBM)
+    return updated.reshape(8, 1, 128, 1024)
 
 
 def solution(mesh):

time: 127 us -> 130 us (1.024)
  waiting for transfers between devices: 44.4 us -> 47.6 us
    ppermute x23, waiting for transfers between devices: 44.4 us -> 47.6 us  [send(): return lax.ppermute(value, AXES, pairs)]
  transfers between devices with their start and end apart: 24 -> 24, of which waited for: 9 -> 10; matrix products, arithmetic and copies ran while one was open for 2% -> 2% of each run, Pallas kernels for 7% -> 7%
where the time goes in v5:
time: 130 us; the launch traced here: 129 us
  starting transfers between devices  58.5 us (45%)
  waiting for transfers between devices  47.6 us (37%)
  Pallas kernels  19.6 us (15%)
  other arithmetic  2.21 us (2%)
    ppermute x23, waiting for transfers between devices, send(): return lax.ppermute(value, AXES, pairs)  47.6 us
    ppermute x23, starting transfers between devices, send(): return lax.ppermute(value, AXES, pairs)  47 us
    pallas_call x10, Pallas kernels, launch(): pl.pallas_call(kernel, out_shape=[jax.ShapeDtypeStruct(s, d) for s, d in...  19.6 us
    all_to_all x1, starting transfers between devices, steps(): lax.all_to_all(ordered.reshape(128, 8, 1408), AXES, split_axis=0, concat_...  11.5 us
  transfers between devices with their start and end apart: 24, of which 10 were waited for; matrix products, arithmetic and copies ran while one was open for 2% of the time, Pallas kernels for 7%

profile of v5, /device:TPU:1, one launch (start us, length us, event | category | flops | bytes accessed | tf_op | source)
XLA Modules:
  0.0 129.3 jit_solution(1466204010925513957)
XLA Ops:
  0.0 6.4 %shard_map.46 = bf16[1024,1408]{1,0:T(8,128)(2,1)} custom-call(s32[1,1024]{1,0:T(1,128)} %bitcast.13, bf16[1024,1024]{1,0:T(8,128)(2,1)} %rows_hbm.1), custom_call_target="tpu_custom_call" | custom-call | flops 3221225472 | bytes 5242880 | tf_op jit(solution)/shard_map/pallas_call | solution.py:276
  6.4 11.5 %all-to-all-start = ((bf16[128,8,1408]{2,1,0:T(8,128)(2,1)}), bf16[128,8,1408]{2,1,0:T(8,128)(2,1)S(1)}, u32[]{:S(2)}, u32[]{:S(2)}) async-start(bf16[128,8,1408]{2,1,0:T(8,128)(2,1)} %bitcast.12), calls=%async_computation | async-start | bytes 5767168 | tf_op jit(solution)/shard_map/all_to_all | solution.py:348
  18.8 2.9 %collective-permute-start.5 = (bf16[128,1024]{1,0:T(8,128)(2,1)S(1)}, bf16[128,1024]{1,0:T(8,128)(2,1)S(1)}, u32[]{:S(2)}, u32[]{:S(2)}) collective-permute-start(bf16[128,1024]{1,0:T(8,128)(2,1)S(1)} %slice_bitcast_fusion), channel_id=1, source_target_pairs={{0,64},{1,17},{2,66},{3,19},{4,68},{5,21},{6,70},{7,23},{8,72},{9,... | collective-permute-start | bytes 786440 | tf_op jit(solution)/shard_map/ppermute | solution.py:28
  22.7 32.6 %collective-permute-done.5 = bf16[128,1024]{1,0:T(8,128)(2,1)S(1)} collective-permute-done((bf16[128,1024]{1,0:T(8,128)(2,1)S(1)}, bf16[128,1024]{1,0:T(8,128)(2,1)S(1)}, u32[]{:S(2)}, u32[]{:S(2)}) %collective-permute-start.5) | collective-permute-done | bytes 262176 | tf_op jit(solution)/shard_map/ppermute | solution.py:28
  55.3 2.4 %collective-permute-done.4 = bf16[128,1024]{1,0:T(8,128)(2,1)} collective-permute-done((bf16[128,1024]{1,0:T(8,128)(2,1)S(1)}, bf16[128,1024]{1,0:T(8,128)(2,1)}, u32[]{:S(2)}, u32[]{:S(2)}) %collective-permute-start.4) | collective-permute-done | bytes 262176 | tf_op jit(solution)/shard_map/ppermute | solution.py:28
  57.6 1.1 select_select_fusion
  58.7 4.4 %collective-permute-start.8 = (bf16[128,1024]{1,0:T(8,128)(2,1)S(1)}, bf16[128,1024]{1,0:T(8,128)(2,1)S(1)}, u32[]{:S(2)}, u32[]{:S(2)}) collective-permute-start(bf16[128,1024]{1,0:T(8,128)(2,1)S(1)} %select_select_fusion), channel_id=1, source_target_pairs={{1,65},{3,67},{5,69},{7,71},{8,24},{9,73},{10,26},{11,75},{12,28},... | collective-permute-start | bytes 786440 | tf_op jit(solution)/shard_map/ppermute | solution.py:28
  63.1 2.0 %collective-permute-start.7 = (bf16[128,1024]{1,0:T(8,128)(2,1)S(1)}, bf16[128,1024]{1,0:T(8,128)(2,1)}, u32[]{:S(2)}, u32[]{:S(2)}) collective-permute-start(bf16[128,1024]{1,0:T(8,128)(2,1)S(1)} %select_select_fusion), channel_id=1, source_target_pairs={{1,97},{3,99},{5,101},{7,103},{8,16},{9,105},{10,18},{11,107},{12,... | collective-permute-start | bytes 786440 | tf_op jit(solution)/shard_map/ppermute | solution.py:28
  65.1 2.0 %collective-permute-start.6 = (bf16[128,1024]{1,0:T(8,128)(2,1)S(1)}, bf16[128,1024]{1,0:T(8,128)(2,1)}, u32[]{:S(2)}, u32[]{:S(2)}) collective-permute-start(bf16[128,1024]{1,0:T(8,128)(2,1)S(1)} %select_select_fusion), channel_id=1, source_target_pairs={{1,33},{3,35},{5,37},{7,39},{8,0},{9,41},{10,2},{11,43},{12,4},{13... | collective-permute-start | bytes 786440 | tf_op jit(solution)/shard_map/ppermute | solution.py:28
  67.8 1.9 %collective-permute-done.6 = bf16[128,1024]{1,0:T(8,128)(2,1)} collective-permute-done((bf16[128,1024]{1,0:T(8,128)(2,1)S(1)}, bf16[128,1024]{1,0:T(8,128)(2,1)}, u32[]{:S(2)}, u32[]{:S(2)}) %collective-permute-start.6) | collective-permute-done | bytes 262176 | tf_op jit(solution)/shard_map/ppermute | solution.py:28
  69.7 1.1 add_add_fusion.own_ref
  70.8 2.7 %collective-permute-start.9 = (bf16[128,1024]{1,0:T(8,128)(2,1)S(1)}, bf16[128,1024]{1,0:T(8,128)(2,1)S(1)}, u32[]{:S(2)}, u32[]{:S(2)}) collective-permute-start(bf16[128,1024]{1,0:T(8,128)(2,1)S(1)} %add_add_fusion.own_ref), channel_id=1, source_target_pairs={{0,1},{1,0},{2,3},{3,2},{4,5},{5,4},{6,7},{7,6},{8,9},{9,8},{10,11... | collective-permute-start | bytes 786440 | tf_op jit(solution)/shard_map/ppermute | solution.py:28
  73.5 3.2 %collective-permute-start.2 = (bf16[64,256]{1,0:T(8,128)(2,1)S(1)}, bf16[64,256]{1,0:T(8,128)(2,1)S(1)}, u32[]{:S(2)}, u32[]{:S(2)}) collective-permute-start(bf16[64,256]{1,0:T(8,128)(2,1)S(1)} %get-tuple-element.17.p0), channel_id=1, source_target_pairs={{0,4},{1,5},{2,6},{3,7},{4,0},{5,1},{6,2},{7,3},{8,12},{9,13},{10,... | collective-permute-start | bytes 98312 | tf_op jit(solution)/shard_map/ppermute | solution.py:28
  78.4 2.3 %collective-permute-done.1.p2 = bf16[64,256]{1,0:T(8,128)(2,1)S(1)} collective-permute-done((bf16[64,256]{1,0:T(8,128)(2,1)S(1)}, bf16[64,256]{1,0:T(8,128)(2,1)S(1)}, u32[]{:S(2)}, u32[]{:S(2)}) %collective-permute-start.1) | collective-permute-done | bytes 32800 | tf_op jit(solution)/shard_map/ppermute | solution.py:28
  81.6 1.5 %collective-permute-start.12 = (bf16[64,256]{1,0:T(8,128)(2,1)S(1)}, bf16[64,256]{1,0:T(8,128)(2,1)S(1)}, u32[]{:S(2)}, u32[]{:S(2)}) collective-permute-start(bf16[64,256]{1,0:T(8,128)(2,1)S(1)} %get-tuple-element.26.p0), channel_id=1, source_target_pairs={{0,4},{1,5},{2,6},{3,7},{4,0},{5,1},{6,2},{7,3},{8,12},{9,13},{10,... | collective-permute-start | bytes 98312 | tf_op jit(solution)/shard_map/ppermute | solution.py:28
  84.4 1.6 %collective-permute-done.12.p3 = bf16[64,256]{1,0:T(8,128)(2,1)S(1)} collective-permute-done((bf16[64,256]{1,0:T(8,128)(2,1)S(1)}, bf16[64,256]{1,0:T(8,128)(2,1)S(1)}, u32[]{:S(2)}, u32[]{:S(2)}) %collective-permute-start.12) | collective-permute-done | bytes 32800 | tf_op jit(solution)/shard_map/ppermute | solution.py:28
  86.0 1.1 collective-permute-done.11.p2
  88.0 1.5 %collective-permute-start.14 = (bf16[32,2048]{1,0:T(8,128)(2,1)S(1)}, bf16[32,2048]{1,0:T(8,128)(2,1)S(1)}, u32[]{:S(2)}, u32[]{:S(2)}) collective-permute-start(bf16[32,2048]{1,0:T(8,128)(2,1)S(1)} %shard_map.50), channel_id=1, source_target_pairs={{0,96},{1,25},{2,98},{3,27},{4,100},{5,29},{6,102},{7,31},{8,104},... | collective-permute-start | bytes 393224 | tf_op jit(solution)/shard_map/ppermute | solution.py:28
  89.5 1.1 collective-permute-start.13
  90.6 2.8 %collective-permute-done.15 = bf16[32,2048]{1,0:T(8,128)(2,1)S(1)} collective-permute-done((bf16[32,2048]{1,0:T(8,128)(2,1)S(1)}, bf16[32,2048]{1,0:T(8,128)(2,1)S(1)}, u32[]{:S(2)}, u32[]{:S(2)}) %collective-permute-start.15) | collective-permute-done | bytes 131104 | tf_op jit(solution)/shard_map/ppermute | solution.py:28
  93.4 1.1 collective-permute-done.14
  94.9 1.5 %collective-permute-start.19 = (bf16[128,2048]{1,0:T(8,128)(2,1)S(1)}, bf16[128,2048]{1,0:T(8,128)(2,1)S(1)}, u32[]{:S(2)}, u32[]{:S(2)}) collective-permute-start(bf16[128,2048]{1,0:T(8,128)(2,1)S(1)} %pad_maximum_fusion.a_ref), channel_id=1, source_target_pairs={{0,16},{1,65},{2,18},{3,67},{4,20},{5,69},{6,22},{7,71},{8,24},{9,... | collective-permute-start | bytes 1572872 | tf_op jit(solution)/shard_map/ppermute | solution.py:28
  96.4 2.0 %collective-permute-start.16 = (bf16[128,2048]{1,0:T(8,128)(2,1)S(1)}, bf16[128,2048]{1,0:T(8,128)(2,1)S(1)}, u32[]{:S(2)}, u32[]{:S(2)}) collective-permute-start(bf16[128,2048]{1,0:T(8,128)(2,1)S(1)} %pad_maximum_fusion.a_ref), channel_id=1, source_target_pairs={{0,24},{1,97},{2,26},{3,99},{4,28},{5,101},{6,30},{7,103},{8,16},{... | collective-permute-start | bytes 1572872 | tf_op jit(solution)/shard_map/ppermute | solution.py:28
  98.5 6.4 %collective-permute-start.18 = (bf16[128,2048]{1,0:T(8,128)(2,1)S(1)}, bf16[128,2048]{1,0:T(8,128)(2,1)S(1)}, u32[]{:S(2)}, u32[]{:S(2)}) collective-permute-start(bf16[128,2048]{1,0:T(8,128)(2,1)S(1)} %pad_maximum_fusion.a_ref), channel_id=1, source_target_pairs={{0,1},{1,0},{2,3},{3,2},{4,5},{5,4},{6,7},{7,6},{8,9},{9,8},{10,11... | collective-permute-start | bytes 1572872 | tf_op jit(solution)/shard_map/ppermute | solution.py:28
  104.9 4.5 %collective-permute-start.22 = (bf16[128,2048]{1,0:T(8,128)(2,1)S(1)}, bf16[128,2048]{1,0:T(8,128)(2,1)S(1)}, u32[]{:S(2)}, u32[]{:S(2)}) collective-permute-start(bf16[128,2048]{1,0:T(8,128)(2,1)S(1)} %collective-permute-done.20.b_ref), channel_id=1, source_target_pairs={{0,1},{1,0},{2,3},{3,2},{4,5},{5,4},{6,7},{7,6},{8,9},{9,8},{10,11... | collective-permute-start | bytes 1572872 | tf_op jit(solution)/shard_map/ppermute | solution.py:28
  110.4 4.9 %collective-permute-start.21 = (bf16[128,2048]{1,0:T(8,128)(2,1)S(1)}, bf16[128,2048]{1,0:T(8,128)(2,1)S(1)}, u32[]{:S(2)}, u32[]{:S(2)}) collective-permute-start(bf16[128,2048]{1,0:T(8,128)(2,1)S(1)} %collective-permute-done.19.a_ref), channel_id=1, source_target_pairs={{0,1},{1,0},{2,3},{3,2},{4,5},{5,4},{6,7},{7,6},{8,9},{9,8},{10,11... | collective-permute-start | bytes 1572872 | tf_op jit(solution)/shard_map/ppermute | solution.py:28
  115.3 3.1 %collective-permute-start.17 = (bf16[128,2048]{1,0:T(8,128)(2,1)S(1)}, bf16[128,2048]{1,0:T(8,128)(2,1)S(1)}, u32[]{:S(2)}, u32[]{:S(2)}) collective-permute-start(bf16[128,2048]{1,0:T(8,128)(2,1)S(1)} %collective-permute-done.16.a_ref), channel_id=1, source_target_pairs={{0,1},{1,0},{2,3},{3,2},{4,5},{5,4},{6,7},{7,6},{8,9},{9,8},{10,11... | collective-permute-start | bytes 1572872 | tf_op jit(solution)/shard_map/ppermute | solution.py:28
  118.4 3.2 %shard_map.51.rows_ref.refs_4_ = bf16[1024,1024]{1,0:T(8,128)(2,1)S(1)} custom-call(s32[8,1024]{1,0:T(8,128)S(1)} %get-tuple-element.21.own_ref, bf16[1024,1408]{1,0:T(8,128)(2,1)S(1)} %bitcast.11), custom_call_target="tpu_custom_call" | custom-call | flops 2147483648 | bytes 4194304 | tf_op jit(solution)/shard_map/pallas_call | solution.py:276
  121.6 1.6 %shard_map.53.refs_1_ = bf16[1024,256]{1,0:T(8,128)(2,1)S(1)} custom-call(bf16[128,2048]{1,0:T(8,128)(2,1)S(1)} %collective-permute-done.19.a_ref, bf16[128,2048]{1,0:T(8,128)(2,1)S(1)} %collective-permute-done.20.b_ref, bf16[2,8,1,128,1024]{4,3,2,1,0:T(8,128)(2,1)S(1)} %copy-done, bf16[1024,1024]{1,0:T(8,128)(2,1)S(1)} %shard_map.51.rows_ref.refs_4_), custom_call_target="tpu_custom_call" | custom-call | flops 1073741824 | bytes 2097152 | tf_op jit(solution)/shard_map/pallas_call | solution.py:276
  123.2 1.6 %shard_map.52.refs_0_ = bf16[1024,256]{1,0:T(8,128)(2,1)S(1)} custom-call(bf16[128,2048]{1,0:T(8,128)(2,1)S(1)} %pad_maximum_fusion.a_ref, bf16[128,2048]{1,0:T(8,128)(2,1)S(1)} %collective-permute-done.18.b_ref, bf16[2,8,1,128,1024]{4,3,2,1,0:T(8,128)(2,1)S(1)} %copy-done, bf16[1024,1024]{1,0:T(8,128)(2,1)S(1)} %shard_map.51.rows_ref.refs_4_), custom_call_target="tpu_custom_call" | custom-call | flops 1073741824 | bytes 2097152 | tf_op jit(solution)/shard_map/pallas_call | solution.py:276
  124.8 1.6 %shard_map.54.refs_2_ = bf16[1024,256]{1,0:T(8,128)(2,1)S(1)} custom-call(bf16[128,2048]{1,0:T(8,128)(2,1)S(1)} %collective-permute-done.21.a_ref, bf16[128,2048]{1,0:T(8,128)(2,1)S(1)} %collective-permute-done.22.b_ref, bf16[2,8,1,128,1024]{4,3,2,1,0:T(8,128)(2,1)S(1)} %copy-done, bf16[1024,1024]{1,0:T(8,128)(2,1)S(1)} %shard_map.51.rows_ref.refs_4_), custom_call_target="tpu_custom_call" | custom-call | flops 1073741824 | bytes 2097152 | tf_op jit(solution)/shard_map/pallas_call | solution.py:276
  126.3 2.8 %shard_map.55 = bf16[1024,1024]{1,0:T(8,128)(2,1)} custom-call(bf16[128,2048]{1,0:T(8,128)(2,1)S(1)} %collective-permute-done.16.a_ref, bf16[128,2048]{1,0:T(8,128)(2,1)S(1)} %collective-permute-done.17.b_ref, bf16[1024,256]{1,0:T(8,128)(2,1)S(1)} %shard_map.52.refs_0_, bf16[1024,256]{1,0:T(8,128)(2,1)S(1)} %shard_map.53.refs_1_, ...), custom_call_target="tpu_custom_call" | custom-call | flops 1073741824 | bytes 2097152 | tf_op jit(solution)/shard_map/pallas_call | solution.py:276
  (34 shorter events, 8.6 us)
Async XLA Ops:
  6.4 60.8 %all-to-all-start = ((bf16[128,8,1408]{2,1,0:T(8,128)(2,1)}), bf16[128,8,1408]{2,1,0:T(8,128)(2,1)S(1)}, u32[]{:S(2)}, u32[]{:S(2)}) async-start(bf16[128,8,1408]{2,1,0:T(8,128)(2,1)} %bitcast.12), calls=%async_computation | async-start | bytes 5767168 | tf_op jit(solution)/shard_map/all_to_all | solution.py:348
  18.8 36.4 %collective-permute-start.5 = (bf16[128,1024]{1,0:T(8,128)(2,1)S(1)}, bf16[128,1024]{1,0:T(8,128)(2,1)S(1)}, u32[]{:S(2)}, u32[]{:S(2)}) collective-permute-start(bf16[128,1024]{1,0:T(8,128)(2,1)S(1)} %slice_bitcast_fusion), channel_id=1, source_target_pairs={{0,64},{1,17},{2,66},{3,19},{4,68},{5,21},{6,70},{7,23},{8,72},{9,... | collective-permute-start | bytes 786440 | tf_op jit(solution)/shard_map/ppermute | solution.py:28
  21.8 35.8 %collective-permute-start.4 = (bf16[128,1024]{1,0:T(8,128)(2,1)S(1)}, bf16[128,1024]{1,0:T(8,128)(2,1)}, u32[]{:S(2)}, u32[]{:S(2)}) collective-permute-start(bf16[128,1024]{1,0:T(8,128)(2,1)S(1)} %slice_bitcast_fusion), channel_id=1, source_target_pairs={{0,96},{1,25},{2,98},{3,27},{4,100},{5,29},{6,102},{7,31},{8,104},... | collective-permute-start | bytes 786440 | tf_op jit(solution)/shard_map/ppermute | solution.py:28
  22.7 35.0 %collective-permute-start.3 = (bf16[128,1024]{1,0:T(8,128)(2,1)S(1)}, bf16[128,1024]{1,0:T(8,128)(2,1)}, u32[]{:S(2)}, u32[]{:S(2)}) collective-permute-start(bf16[128,1024]{1,0:T(8,128)(2,1)S(1)} %slice_bitcast_fusion), channel_id=1, source_target_pairs={{0,32},{1,9},{2,34},{3,11},{4,36},{5,13},{6,38},{7,15},{8,40},{9,1... | collective-permute-start | bytes 786440 | tf_op jit(solution)/shard_map/ppermute | solution.py:28
  58.7 9.0 %collective-permute-start.8 = (bf16[128,1024]{1,0:T(8,128)(2,1)S(1)}, bf16[128,1024]{1,0:T(8,128)(2,1)S(1)}, u32[]{:S(2)}, u32[]{:S(2)}) collective-permute-start(bf16[128,1024]{1,0:T(8,128)(2,1)S(1)} %select_select_fusion), channel_id=1, source_target_pairs={{1,65},{3,67},{5,69},{7,71},{8,24},{9,73},{10,26},{11,75},{12,28},... | collective-permute-start | bytes 786440 | tf_op jit(solution)/shard_map/ppermute | solution.py:28
  63.1 4.6 %collective-permute-start.7 = (bf16[128,1024]{1,0:T(8,128)(2,1)S(1)}, bf16[128,1024]{1,0:T(8,128)(2,1)}, u32[]{:S(2)}, u32[]{:S(2)}) collective-permute-start(bf16[128,1024]{1,0:T(8,128)(2,1)S(1)} %select_select_fusion), channel_id=1, source_target_pairs={{1,97},{3,99},{5,101},{7,103},{8,16},{9,105},{10,18},{11,107},{12,... | collective-permute-start | bytes 786440 | tf_op jit(solution)/shard_map/ppermute | solution.py:28
  65.1 4.6 %collective-permute-start.6 = (bf16[128,1024]{1,0:T(8,128)(2,1)S(1)}, bf16[128,1024]{1,0:T(8,128)(2,1)}, u32[]{:S(2)}, u32[]{:S(2)}) collective-permute-start(bf16[128,1024]{1,0:T(8,128)(2,1)S(1)} %select_select_fusion), channel_id=1, source_target_pairs={{1,33},{3,35},{5,37},{7,39},{8,0},{9,41},{10,2},{11,43},{12,4},{13... | collective-permute-start | bytes 786440 | tf_op jit(solution)/shard_map/ppermute | solution.py:28
  67.1 10.2 %copy-start.1 = (bf16[2,1024,1024]{2,1,0:T(8,128)(2,1)S(1)}, bf16[2,1024,1024]{2,1,0:T(8,128)(2,1)}, u32[]{:S(2)}) copy-start(bf16[2,1024,1024]{2,1,0:T(8,128)(2,1)} %source_hbm) | copy-start | bytes 12582916
  70.8 9.9 %collective-permute-start.9 = (bf16[128,1024]{1,0:T(8,128)(2,1)S(1)}, bf16[128,1024]{1,0:T(8,128)(2,1)S(1)}, u32[]{:S(2)}, u32[]{:S(2)}) collective-permute-start(bf16[128,1024]{1,0:T(8,128)(2,1)S(1)} %add_add_fusion.own_ref), channel_id=1, source_target_pairs={{0,1},{1,0},{2,3},{3,2},{4,5},{5,4},{6,7},{7,6},{8,9},{9,8},{10,11... | collective-permute-start | bytes 786440 | tf_op jit(solution)/shard_map/ppermute | solution.py:28
  73.5 4.9 %collective-permute-start.2 = (bf16[64,256]{1,0:T(8,128)(2,1)S(1)}, bf16[64,256]{1,0:T(8,128)(2,1)S(1)}, u32[]{:S(2)}, u32[]{:S(2)}) collective-permute-start(bf16[64,256]{1,0:T(8,128)(2,1)S(1)} %get-tuple-element.17.p0), channel_id=1, source_target_pairs={{0,4},{1,5},{2,6},{3,7},{4,0},{5,1},{6,2},{7,3},{8,12},{9,13},{10,... | collective-permute-start | bytes 98312 | tf_op jit(solution)/shard_map/ppermute | solution.py:28
  76.7 4.0 %collective-permute-start.1 = (bf16[64,256]{1,0:T(8,128)(2,1)S(1)}, bf16[64,256]{1,0:T(8,128)(2,1)S(1)}, u32[]{:S(2)}, u32[]{:S(2)}) collective-permute-start(bf16[64,256]{1,0:T(8,128)(2,1)S(1)} %get-tuple-element.17.p0), channel_id=1, source_target_pairs={{0,6},{1,7},{2,4},{3,5},{4,2},{5,3},{6,0},{7,1},{8,14},{9,15},{10,... | collective-permute-start | bytes 98312 | tf_op jit(solution)/shard_map/ppermute | solution.py:28
  77.3 3.4 %collective-permute-start = (bf16[64,256]{1,0:T(8,128)(2,1)S(1)}, bf16[64,256]{1,0:T(8,128)(2,1)S(1)}, u32[]{:S(2)}, u32[]{:S(2)}) collective-permute-start(bf16[64,256]{1,0:T(8,128)(2,1)S(1)} %get-tuple-element.17.p0), channel_id=1, source_target_pairs={{0,2},{1,3},{2,0},{3,1},{4,6},{5,7},{6,4},{7,5},{8,10},{9,11},{10,... | collective-permute-start | bytes 98312 | tf_op jit(solution)/shard_map/ppermute | solution.py:28
  81.6 4.3 %collective-permute-start.12 = (bf16[64,256]{1,0:T(8,128)(2,1)S(1)}, bf16[64,256]{1,0:T(8,128)(2,1)S(1)}, u32[]{:S(2)}, u32[]{:S(2)}) collective-permute-start(bf16[64,256]{1,0:T(8,128)(2,1)S(1)} %get-tuple-element.26.p0), channel_id=1, source_target_pairs={{0,4},{1,5},{2,6},{3,7},{4,0},{5,1},{6,2},{7,3},{8,12},{9,13},{10,... | collective-permute-start | bytes 98312 | tf_op jit(solution)/shard_map/ppermute | solution.py:28
  83.1 4.0 %collective-permute-start.11 = (bf16[64,256]{1,0:T(8,128)(2,1)S(1)}, bf16[64,256]{1,0:T(8,128)(2,1)S(1)}, u32[]{:S(2)}, u32[]{:S(2)}) collective-permute-start(bf16[64,256]{1,0:T(8,128)(2,1)S(1)} %get-tuple-element.26.p0), channel_id=1, source_target_pairs={{0,6},{1,7},{2,4},{3,5},{4,2},{5,3},{6,0},{7,1},{8,14},{9,15},{10,... | collective-permute-start | bytes 98312 | tf_op jit(solution)/shard_map/ppermute | solution.py:28
  83.8 3.3 %collective-permute-start.10 = (bf16[64,256]{1,0:T(8,128)(2,1)S(1)}, bf16[64,256]{1,0:T(8,128)(2,1)S(1)}, u32[]{:S(2)}, u32[]{:S(2)}) collective-permute-start(bf16[64,256]{1,0:T(8,128)(2,1)S(1)} %get-tuple-element.26.p0), channel_id=1, source_target_pairs={{0,2},{1,3},{2,0},{3,1},{4,6},{5,7},{6,4},{7,5},{8,10},{9,11},{10,... | collective-permute-start | bytes 98312 | tf_op jit(solution)/shard_map/ppermute | solution.py:28
  87.9 5.5 %collective-permute-start.15 = (bf16[32,2048]{1,0:T(8,128)(2,1)S(1)}, bf16[32,2048]{1,0:T(8,128)(2,1)S(1)}, u32[]{:S(2)}, u32[]{:S(2)}) collective-permute-start(bf16[32,2048]{1,0:T(8,128)(2,1)S(1)} %shard_map.50), channel_id=1, source_target_pairs={{0,64},{1,17},{2,66},{3,19},{4,68},{5,21},{6,70},{7,23},{8,72},{9,... | collective-permute-start | bytes 393224 | tf_op jit(solution)/shard_map/ppermute | solution.py:28
  88.0 6.5 %collective-permute-start.14 = (bf16[32,2048]{1,0:T(8,128)(2,1)S(1)}, bf16[32,2048]{1,0:T(8,128)(2,1)S(1)}, u32[]{:S(2)}, u32[]{:S(2)}) collective-permute-start(bf16[32,2048]{1,0:T(8,128)(2,1)S(1)} %shard_map.50), channel_id=1, source_target_pairs={{0,96},{1,25},{2,98},{3,27},{4,100},{5,29},{6,102},{7,31},{8,104},... | collective-permute-start | bytes 393224 | tf_op jit(solution)/shard_map/ppermute | solution.py:28
  89.5 5.0 %collective-permute-start.13 = (bf16[32,2048]{1,0:T(8,128)(2,1)S(1)}, bf16[32,2048]{1,0:T(8,128)(2,1)S(1)}, u32[]{:S(2)}, u32[]{:S(2)}) collective-permute-start(bf16[32,2048]{1,0:T(8,128)(2,1)S(1)} %shard_map.50), channel_id=1, source_target_pairs={{0,32},{1,9},{2,34},{3,11},{4,36},{5,13},{6,38},{7,15},{8,40},{9,1... | collective-permute-start | bytes 393224 | tf_op jit(solution)/shard_map/ppermute | solution.py:28
  94.5 27.1 %copy-start = (bf16[2,8,1,128,1024]{4,3,2,1,0:T(8,128)(2,1)S(1)}, bf16[2,8,1,128,1024]{4,3,2,1,0:T(8,128)(2,1)}, u32[]{:S(2)}) copy-start(bf16[2,8,1,128,1024]{4,3,2,1,0:T(8,128)(2,1)} %refs_3_.1) | copy-start | bytes 12582916
  94.5 10.3 %collective-permute-start.20 = (bf16[128,2048]{1,0:T(8,128)(2,1)S(1)}, bf16[128,2048]{1,0:T(8,128)(2,1)S(1)}, u32[]{:S(2)}, u32[]{:S(2)}) collective-permute-start(bf16[128,2048]{1,0:T(8,128)(2,1)S(1)} %pad_maximum_fusion.a_ref), channel_id=1, source_target_pairs={{0,8},{1,33},{2,10},{3,35},{4,12},{5,37},{6,14},{7,39},{8,0},{9,41... | collective-permute-start | bytes 1572872 | tf_op jit(solution)/shard_map/ppermute | solution.py:28
  94.9 15.5 %collective-permute-start.19 = (bf16[128,2048]{1,0:T(8,128)(2,1)S(1)}, bf16[128,2048]{1,0:T(8,128)(2,1)S(1)}, u32[]{:S(2)}, u32[]{:S(2)}) collective-permute-start(bf16[128,2048]{1,0:T(8,128)(2,1)S(1)} %pad_maximum_fusion.a_ref), channel_id=1, source_target_pairs={{0,16},{1,65},{2,18},{3,67},{4,20},{5,69},{6,22},{7,71},{8,24},{9,... | collective-permute-start | bytes 1572872 | tf_op jit(solution)/shard_map/ppermute | solution.py:28
  96.4 18.8 %collective-permute-start.16 = (bf16[128,2048]{1,0:T(8,128)(2,1)S(1)}, bf16[128,2048]{1,0:T(8,128)(2,1)S(1)}, u32[]{:S(2)}, u32[]{:S(2)}) collective-permute-start(bf16[128,2048]{1,0:T(8,128)(2,1)S(1)} %pad_maximum_fusion.a_ref), channel_id=1, source_target_pairs={{0,24},{1,97},{2,26},{3,99},{4,28},{5,101},{6,30},{7,103},{8,16},{... | collective-permute-start | bytes 1572872 | tf_op jit(solution)/shard_map/ppermute | solution.py:28
  98.5 24.7 %collective-permute-start.18 = (bf16[128,2048]{1,0:T(8,128)(2,1)S(1)}, bf16[128,2048]{1,0:T(8,128)(2,1)S(1)}, u32[]{:S(2)}, u32[]{:S(2)}) collective-permute-start(bf16[128,2048]{1,0:T(8,128)(2,1)S(1)} %pad_maximum_fusion.a_ref), channel_id=1, source_target_pairs={{0,1},{1,0},{2,3},{3,2},{4,5},{5,4},{6,7},{7,6},{8,9},{9,8},{10,11... | collective-permute-start | bytes 1572872 | tf_op jit(solution)/shard_map/ppermute | solution.py:28
  104.9 19.9 %collective-permute-start.22 = (bf16[128,2048]{1,0:T(8,128)(2,1)S(1)}, bf16[128,2048]{1,0:T(8,128)(2,1)S(1)}, u32[]{:S(2)}, u32[]{:S(2)}) collective-permute-start(bf16[128,2048]{1,0:T(8,128)(2,1)S(1)} %collective-permute-done.20.b_ref), channel_id=1, source_target_pairs={{0,1},{1,0},{2,3},{3,2},{4,5},{5,4},{6,7},{7,6},{8,9},{9,8},{10,11... | collective-permute-start | bytes 1572872 | tf_op jit(solution)/shard_map/ppermute | solution.py:28
  110.4 14.4 %collective-permute-start.21 = (bf16[128,2048]{1,0:T(8,128)(2,1)S(1)}, bf16[128,2048]{1,0:T(8,128)(2,1)S(1)}, u32[]{:S(2)}, u32[]{:S(2)}) collective-permute-start(bf16[128,2048]{1,0:T(8,128)(2,1)S(1)} %collective-permute-done.19.a_ref), channel_id=1, source_target_pairs={{0,1},{1,0},{2,3},{3,2},{4,5},{5,4},{6,7},{7,6},{8,9},{9,8},{10,11... | collective-permute-start | bytes 1572872 | tf_op jit(solution)/shard_map/ppermute | solution.py:28
  115.3 11.1 %collective-permute-start.17 = (bf16[128,2048]{1,0:T(8,128)(2,1)S(1)}, bf16[128,2048]{1,0:T(8,128)(2,1)S(1)}, u32[]{:S(2)}, u32[]{:S(2)}) collective-permute-start(bf16[128,2048]{1,0:T(8,128)(2,1)S(1)} %collective-permute-done.16.a_ref), channel_id=1, source_target_pairs={{0,1},{1,0},{2,3},{3,2},{4,5},{5,4},{6,7},{7,6},{8,9},{9,8},{10,11... | collective-permute-start | bytes 1572872 | tf_op jit(solution)/shard_map/ppermute | solution.py:28

commit v6 on v5

--- a/solution.py
+++ b/solution.py
@@ -399,22 +399,20 @@
     )
     line = [both] + [send(both, along_first(i)) for i in range(3)]
     line = jnp.concatenate(line, axis=0)
-    side2, side0 = send(line, along_second(2)), send(line, along_second(0))
+    side0 = send(line, along_second(0))
+    side2 = send(line, along_second(2))
     side1 = send(line, along_second(1))
     line_other = send(line, other_core)
-    side2_other, side0_other = send(side2, other_core), send(side0, other_core)
+    side0_other, side2_other = send(side0, other_core), send(side2, other_core)
     side1_other = send(side1, other_core)
-    lines = ((0, 3), (1, 3))
-    owns = ((0, 2), (0, 0))
-    others = ((1, 2), (1, 0))
-    last = ((0, 1), (1, 1))
-    part0 = update(update_kernel, lines, (line, line_other), panels, rows)
-    part1 = update(update_kernel, owns, (side2, side0), panels, rows)
-    part2 = update(update_kernel, others, (side2_other, side0_other), panels, rows)
-    kernel = functools.partial(last_kernel, (lines, owns, others))
+    places = [((0, n), (1, n)) for n in (3, 0, 2, 1)]
+    part0 = update(update_kernel, places[0], (line, line_other), panels, rows)
+    part1 = update(update_kernel, places[1], (side0, side0_other), panels, rows)
+    part2 = update(update_kernel, places[2], (side2, side2_other), panels, rows)
+    kernel = functools.partial(last_kernel, places[:3])
     pieces = (side1, side1_other, part0, part1, part2)
     extra = (pltpu.VMEM((1024, 1024), BF16), pltpu.SemaphoreType.DMA((4,)))
-    updated = update(kernel, last, pieces, panels, rows, 1024, extra, HBM)
+    updated = update(kernel, places[3], pieces, panels, rows, 1024, extra, HBM)
     return updated.reshape(8, 1, 128, 1024)
 
 

time: 130 us -> 128 us (0.985)
  starting transfers between devices: 58.5 us -> 57.1 us
    ppermute x23, starting transfers between devices: 47 us -> 45.6 us  [send(): return lax.ppermute(value, AXES, pairs)]
where the time goes in v6:
time: 128 us
  starting transfers between devices  57.1 us (45%)
  waiting for transfers between devices  47.4 us (37%)
  Pallas kernels  19.6 us (15%)
  other arithmetic  2.21 us (2%)
    ppermute x23, waiting for transfers between devices, send(): return lax.ppermute(value, AXES, pairs)  47.3 us
    ppermute x23, starting transfers between devices, send(): return lax.ppermute(value, AXES, pairs)  45.6 us
    pallas_call x10, Pallas kernels, launch(): pl.pallas_call(kernel, out_shape=[jax.ShapeDtypeStruct(s, d) for s, d in...  19.6 us
    all_to_all x1, starting transfers between devices, steps(): lax.all_to_all(ordered.reshape(128, 8, 1408), AXES, split_axis=0, concat_...  11.5 us
  transfers between devices with their start and end apart: 24, of which 10 were waited for; matrix products, arithmetic and copies ran while one was open for 2% of the time, Pallas kernels for 7%

profile of v6, /device:TPU:1, one launch (start us, length us, event | category | flops | bytes accessed | tf_op | source)
XLA Modules:
  0.0 127.6 jit_solution(6204018890148266551)
XLA Ops:
  0.0 6.4 %shard_map.46 = bf16[1024,1408]{1,0:T(8,128)(2,1)} custom-call(s32[1,1024]{1,0:T(1,128)} %bitcast.13, bf16[1024,1024]{1,0:T(8,128)(2,1)} %rows_hbm.1), custom_call_target="tpu_custom_call" | custom-call | flops 3221225472 | bytes 5242880 | tf_op jit(solution)/shard_map/pallas_call | solution.py:276
  6.4 11.5 %all-to-all-start = ((bf16[128,8,1408]{2,1,0:T(8,128)(2,1)}), bf16[128,8,1408]{2,1,0:T(8,128)(2,1)S(1)}, u32[]{:S(2)}, u32[]{:S(2)}) async-start(bf16[128,8,1408]{2,1,0:T(8,128)(2,1)} %bitcast.12), calls=%async_computation | async-start | bytes 5767168 | tf_op jit(solution)/shard_map/all_to_all | solution.py:348
  18.8 2.9 %collective-permute-start.5 = (bf16[128,1024]{1,0:T(8,128)(2,1)S(1)}, bf16[128,1024]{1,0:T(8,128)(2,1)S(1)}, u32[]{:S(2)}, u32[]{:S(2)}) collective-permute-start(bf16[128,1024]{1,0:T(8,128)(2,1)S(1)} %slice_bitcast_fusion), channel_id=1, source_target_pairs={{0,64},{1,17},{2,66},{3,19},{4,68},{5,21},{6,70},{7,23},{8,72},{9,... | collective-permute-start | bytes 786440 | tf_op jit(solution)/shard_map/ppermute | solution.py:28
  22.7 32.6 %collective-permute-done.5 = bf16[128,1024]{1,0:T(8,128)(2,1)S(1)} collective-permute-done((bf16[128,1024]{1,0:T(8,128)(2,1)S(1)}, bf16[128,1024]{1,0:T(8,128)(2,1)S(1)}, u32[]{:S(2)}, u32[]{:S(2)}) %collective-permute-start.5) | collective-permute-done | bytes 262176 | tf_op jit(solution)/shard_map/ppermute | solution.py:28
  55.3 2.4 %collective-permute-done.4 = bf16[128,1024]{1,0:T(8,128)(2,1)} collective-permute-done((bf16[128,1024]{1,0:T(8,128)(2,1)S(1)}, bf16[128,1024]{1,0:T(8,128)(2,1)}, u32[]{:S(2)}, u32[]{:S(2)}) %collective-permute-start.4) | collective-permute-done | bytes 262176 | tf_op jit(solution)/shard_map/ppermute | solution.py:28
  57.6 1.1 select_select_fusion
  58.7 4.4 %collective-permute-start.8 = (bf16[128,1024]{1,0:T(8,128)(2,1)S(1)}, bf16[128,1024]{1,0:T(8,128)(2,1)S(1)}, u32[]{:S(2)}, u32[]{:S(2)}) collective-permute-start(bf16[128,1024]{1,0:T(8,128)(2,1)S(1)} %select_select_fusion), channel_id=1, source_target_pairs={{1,65},{3,67},{5,69},{7,71},{8,24},{9,73},{10,26},{11,75},{12,28},... | collective-permute-start | bytes 786440 | tf_op jit(solution)/shard_map/ppermute | solution.py:28
  63.1 2.0 %collective-permute-start.7 = (bf16[128,1024]{1,0:T(8,128)(2,1)S(1)}, bf16[128,1024]{1,0:T(8,128)(2,1)}, u32[]{:S(2)}, u32[]{:S(2)}) collective-permute-start(bf16[128,1024]{1,0:T(8,128)(2,1)S(1)} %select_select_fusion), channel_id=1, source_target_pairs={{1,97},{3,99},{5,101},{7,103},{8,16},{9,105},{10,18},{11,107},{12,... | collective-permute-start | bytes 786440 | tf_op jit(solution)/shard_map/ppermute | solution.py:28
  65.1 2.0 %collective-permute-start.6 = (bf16[128,1024]{1,0:T(8,128)(2,1)S(1)}, bf16[128,1024]{1,0:T(8,128)(2,1)}, u32[]{:S(2)}, u32[]{:S(2)}) collective-permute-start(bf16[128,1024]{1,0:T(8,128)(2,1)S(1)} %select_select_fusion), channel_id=1, source_target_pairs={{1,33},{3,35},{5,37},{7,39},{8,0},{9,41},{10,2},{11,43},{12,4},{13... | collective-permute-start | bytes 786440 | tf_op jit(solution)/shard_map/ppermute | solution.py:28
  67.8 1.9 %collective-permute-done.6 = bf16[128,1024]{1,0:T(8,128)(2,1)} collective-permute-done((bf16[128,1024]{1,0:T(8,128)(2,1)S(1)}, bf16[128,1024]{1,0:T(8,128)(2,1)}, u32[]{:S(2)}, u32[]{:S(2)}) %collective-permute-start.6) | collective-permute-done | bytes 262176 | tf_op jit(solution)/shard_map/ppermute | solution.py:28
  69.7 1.1 add_add_fusion.own_ref
  70.8 2.7 %collective-permute-start.9 = (bf16[128,1024]{1,0:T(8,128)(2,1)S(1)}, bf16[128,1024]{1,0:T(8,128)(2,1)S(1)}, u32[]{:S(2)}, u32[]{:S(2)}) collective-permute-start(bf16[128,1024]{1,0:T(8,128)(2,1)S(1)} %add_add_fusion.own_ref), channel_id=1, source_target_pairs={{0,1},{1,0},{2,3},{3,2},{4,5},{5,4},{6,7},{7,6},{8,9},{9,8},{10,11... | collective-permute-start | bytes 786440 | tf_op jit(solution)/shard_map/ppermute | solution.py:28
  73.5 3.2 %collective-permute-start.2 = (bf16[64,256]{1,0:T(8,128)(2,1)S(1)}, bf16[64,256]{1,0:T(8,128)(2,1)S(1)}, u32[]{:S(2)}, u32[]{:S(2)}) collective-permute-start(bf16[64,256]{1,0:T(8,128)(2,1)S(1)} %get-tuple-element.17.p0), channel_id=1, source_target_pairs={{0,4},{1,5},{2,6},{3,7},{4,0},{5,1},{6,2},{7,3},{8,12},{9,13},{10,... | collective-permute-start | bytes 98312 | tf_op jit(solution)/shard_map/ppermute | solution.py:28
  78.4 2.3 %collective-permute-done.1.p2 = bf16[64,256]{1,0:T(8,128)(2,1)S(1)} collective-permute-done((bf16[64,256]{1,0:T(8,128)(2,1)S(1)}, bf16[64,256]{1,0:T(8,128)(2,1)S(1)}, u32[]{:S(2)}, u32[]{:S(2)}) %collective-permute-start.1) | collective-permute-done | bytes 32800 | tf_op jit(solution)/shard_map/ppermute | solution.py:28
  81.6 1.5 %collective-permute-start.12 = (bf16[64,256]{1,0:T(8,128)(2,1)S(1)}, bf16[64,256]{1,0:T(8,128)(2,1)S(1)}, u32[]{:S(2)}, u32[]{:S(2)}) collective-permute-start(bf16[64,256]{1,0:T(8,128)(2,1)S(1)} %get-tuple-element.26.p0), channel_id=1, source_target_pairs={{0,4},{1,5},{2,6},{3,7},{4,0},{5,1},{6,2},{7,3},{8,12},{9,13},{10,... | collective-permute-start | bytes 98312 | tf_op jit(solution)/shard_map/ppermute | solution.py:28
  84.4 1.6 %collective-permute-done.12.p3 = bf16[64,256]{1,0:T(8,128)(2,1)S(1)} collective-permute-done((bf16[64,256]{1,0:T(8,128)(2,1)S(1)}, bf16[64,256]{1,0:T(8,128)(2,1)S(1)}, u32[]{:S(2)}, u32[]{:S(2)}) %collective-permute-start.12) | collective-permute-done | bytes 32800 | tf_op jit(solution)/shard_map/ppermute | solution.py:28
  86.0 1.1 collective-permute-done.11.p2
  88.0 1.5 %collective-permute-start.14 = (bf16[32,2048]{1,0:T(8,128)(2,1)S(1)}, bf16[32,2048]{1,0:T(8,128)(2,1)S(1)}, u32[]{:S(2)}, u32[]{:S(2)}) collective-permute-start(bf16[32,2048]{1,0:T(8,128)(2,1)S(1)} %shard_map.50), channel_id=1, source_target_pairs={{0,96},{1,25},{2,98},{3,27},{4,100},{5,29},{6,102},{7,31},{8,104},... | collective-permute-start | bytes 393224 | tf_op jit(solution)/shard_map/ppermute | solution.py:28
  89.5 1.1 collective-permute-start.13
  90.6 2.8 %collective-permute-done.15 = bf16[32,2048]{1,0:T(8,128)(2,1)S(1)} collective-permute-done((bf16[32,2048]{1,0:T(8,128)(2,1)S(1)}, bf16[32,2048]{1,0:T(8,128)(2,1)S(1)}, u32[]{:S(2)}, u32[]{:S(2)}) %collective-permute-start.15) | collective-permute-done | bytes 131104 | tf_op jit(solution)/shard_map/ppermute | solution.py:28
  93.4 1.1 collective-permute-done.14
  94.5 1.3 collective-permute-start.21
  95.8 2.0 %collective-permute-start.16 = (bf16[128,2048]{1,0:T(8,128)(2,1)S(1)}, bf16[128,2048]{1,0:T(8,128)(2,1)S(1)}, u32[]{:S(2)}, u32[]{:S(2)}) collective-permute-start(bf16[128,2048]{1,0:T(8,128)(2,1)S(1)} %pad_maximum_fusion.a_ref), channel_id=1, source_target_pairs={{0,24},{1,97},{2,26},{3,99},{4,28},{5,101},{6,30},{7,103},{8,16},{... | collective-permute-start | bytes 1572872 | tf_op jit(solution)/shard_map/ppermute | solution.py:28
  97.9 6.6 %collective-permute-start.18 = (bf16[128,2048]{1,0:T(8,128)(2,1)S(1)}, bf16[128,2048]{1,0:T(8,128)(2,1)S(1)}, u32[]{:S(2)}, u32[]{:S(2)}) collective-permute-start(bf16[128,2048]{1,0:T(8,128)(2,1)S(1)} %pad_maximum_fusion.a_ref), channel_id=1, source_target_pairs={{0,1},{1,0},{2,3},{3,2},{4,5},{5,4},{6,7},{7,6},{8,9},{9,8},{10,11... | collective-permute-start | bytes 1572872 | tf_op jit(solution)/shard_map/ppermute | solution.py:28
  105.3 5.9 %collective-permute-start.22 = (bf16[128,2048]{1,0:T(8,128)(2,1)S(1)}, bf16[128,2048]{1,0:T(8,128)(2,1)S(1)}, u32[]{:S(2)}, u32[]{:S(2)}) collective-permute-start(bf16[128,2048]{1,0:T(8,128)(2,1)S(1)} %collective-permute-done.21.a_ref), channel_id=1, source_target_pairs={{0,1},{1,0},{2,3},{3,2},{4,5},{5,4},{6,7},{7,6},{8,9},{9,8},{10,11... | collective-permute-start | bytes 1572872 | tf_op jit(solution)/shard_map/ppermute | solution.py:28
  111.2 3.7 %collective-permute-start.20 = (bf16[128,2048]{1,0:T(8,128)(2,1)S(1)}, bf16[128,2048]{1,0:T(8,128)(2,1)S(1)}, u32[]{:S(2)}, u32[]{:S(2)}) collective-permute-start(bf16[128,2048]{1,0:T(8,128)(2,1)S(1)} %collective-permute-done.19.a_ref), channel_id=1, source_target_pairs={{0,1},{1,0},{2,3},{3,2},{4,5},{5,4},{6,7},{7,6},{8,9},{9,8},{10,11... | collective-permute-start | bytes 1572872 | tf_op jit(solution)/shard_map/ppermute | solution.py:28
  114.9 1.8 %collective-permute-start.17 = (bf16[128,2048]{1,0:T(8,128)(2,1)S(1)}, bf16[128,2048]{1,0:T(8,128)(2,1)S(1)}, u32[]{:S(2)}, u32[]{:S(2)}) collective-permute-start(bf16[128,2048]{1,0:T(8,128)(2,1)S(1)} %collective-permute-done.16.a_ref), channel_id=1, source_target_pairs={{0,1},{1,0},{2,3},{3,2},{4,5},{5,4},{6,7},{7,6},{8,9},{9,8},{10,11... | collective-permute-start | bytes 1572872 | tf_op jit(solution)/shard_map/ppermute | solution.py:28
  116.7 3.2 %shard_map.51.rows_ref.refs_4_ = bf16[1024,1024]{1,0:T(8,128)(2,1)S(1)} custom-call(s32[8,1024]{1,0:T(8,128)S(1)} %get-tuple-element.21.own_ref, bf16[1024,1408]{1,0:T(8,128)(2,1)S(1)} %bitcast.11), custom_call_target="tpu_custom_call" | custom-call | flops 2147483648 | bytes 4194304 | tf_op jit(solution)/shard_map/pallas_call | solution.py:276
  119.9 1.6 %shard_map.52.refs_0_ = bf16[1024,256]{1,0:T(8,128)(2,1)S(1)} custom-call(bf16[128,2048]{1,0:T(8,128)(2,1)S(1)} %pad_maximum_fusion.a_ref, bf16[128,2048]{1,0:T(8,128)(2,1)S(1)} %collective-permute-done.18.b_ref, bf16[2,8,1,128,1024]{4,3,2,1,0:T(8,128)(2,1)S(1)} %copy-done, bf16[1024,1024]{1,0:T(8,128)(2,1)S(1)} %shard_map.51.rows_ref.refs_4_), custom_call_target="tpu_custom_call" | custom-call | flops 1073741824 | bytes 2097152 | tf_op jit(solution)/shard_map/pallas_call | solution.py:276
  121.5 1.6 %shard_map.54.refs_2_ = bf16[1024,256]{1,0:T(8,128)(2,1)S(1)} custom-call(bf16[128,2048]{1,0:T(8,128)(2,1)S(1)} %collective-permute-done.21.a_ref, bf16[128,2048]{1,0:T(8,128)(2,1)S(1)} %collective-permute-done.22.b_ref, bf16[2,8,1,128,1024]{4,3,2,1,0:T(8,128)(2,1)S(1)} %copy-done, bf16[1024,1024]{1,0:T(8,128)(2,1)S(1)} %shard_map.51.rows_ref.refs_4_), custom_call_target="tpu_custom_call" | custom-call | flops 1073741824 | bytes 2097152 | tf_op jit(solution)/shard_map/pallas_call | solution.py:276
  123.1 1.6 %shard_map.53.refs_1_ = bf16[1024,256]{1,0:T(8,128)(2,1)S(1)} custom-call(bf16[128,2048]{1,0:T(8,128)(2,1)S(1)} %collective-permute-done.19.a_ref, bf16[128,2048]{1,0:T(8,128)(2,1)S(1)} %collective-permute-done.20.b_ref, bf16[2,8,1,128,1024]{4,3,2,1,0:T(8,128)(2,1)S(1)} %copy-done, bf16[1024,1024]{1,0:T(8,128)(2,1)S(1)} %shard_map.51.rows_ref.refs_4_), custom_call_target="tpu_custom_call" | custom-call | flops 1073741824 | bytes 2097152 | tf_op jit(solution)/shard_map/pallas_call | solution.py:276
  124.6 2.8 %shard_map.55 = bf16[1024,1024]{1,0:T(8,128)(2,1)} custom-call(bf16[128,2048]{1,0:T(8,128)(2,1)S(1)} %collective-permute-done.16.a_ref, bf16[128,2048]{1,0:T(8,128)(2,1)S(1)} %collective-permute-done.17.b_ref, bf16[1024,256]{1,0:T(8,128)(2,1)S(1)} %shard_map.52.refs_0_, bf16[1024,256]{1,0:T(8,128)(2,1)S(1)} %shard_map.53.refs_1_, ...), custom_call_target="tpu_custom_call" | custom-call | flops 1073741824 | bytes 2097152 | tf_op jit(solution)/shard_map/pallas_call | solution.py:276
  (34 shorter events, 8.0 us)
Async XLA Ops:
  6.4 60.8 %all-to-all-start = ((bf16[128,8,1408]{2,1,0:T(8,128)(2,1)}), bf16[128,8,1408]{2,1,0:T(8,128)(2,1)S(1)}, u32[]{:S(2)}, u32[]{:S(2)}) async-start(bf16[128,8,1408]{2,1,0:T(8,128)(2,1)} %bitcast.12), calls=%async_computation | async-start | bytes 5767168 | tf_op jit(solution)/shard_map/all_to_all | solution.py:348
  18.8 36.4 %collective-permute-start.5 = (bf16[128,1024]{1,0:T(8,128)(2,1)S(1)}, bf16[128,1024]{1,0:T(8,128)(2,1)S(1)}, u32[]{:S(2)}, u32[]{:S(2)}) collective-permute-start(bf16[128,1024]{1,0:T(8,128)(2,1)S(1)} %slice_bitcast_fusion), channel_id=1, source_target_pairs={{0,64},{1,17},{2,66},{3,19},{4,68},{5,21},{6,70},{7,23},{8,72},{9,... | collective-permute-start | bytes 786440 | tf_op jit(solution)/shard_map/ppermute | solution.py:28
  21.8 35.8 %collective-permute-start.4 = (bf16[128,1024]{1,0:T(8,128)(2,1)S(1)}, bf16[128,1024]{1,0:T(8,128)(2,1)}, u32[]{:S(2)}, u32[]{:S(2)}) collective-permute-start(bf16[128,1024]{1,0:T(8,128)(2,1)S(1)} %slice_bitcast_fusion), channel_id=1, source_target_pairs={{0,96},{1,25},{2,98},{3,27},{4,100},{5,29},{6,102},{7,31},{8,104},... | collective-permute-start | bytes 786440 | tf_op jit(solution)/shard_map/ppermute | solution.py:28
  22.7 35.0 %collective-permute-start.3 = (bf16[128,1024]{1,0:T(8,128)(2,1)S(1)}, bf16[128,1024]{1,0:T(8,128)(2,1)}, u32[]{:S(2)}, u32[]{:S(2)}) collective-permute-start(bf16[128,1024]{1,0:T(8,128)(2,1)S(1)} %slice_bitcast_fusion), channel_id=1, source_target_pairs={{0,32},{1,9},{2,34},{3,11},{4,36},{5,13},{6,38},{7,15},{8,40},{9,1... | collective-permute-start | bytes 786440 | tf_op jit(solution)/shard_map/ppermute | solution.py:28
  58.7 9.0 %collective-permute-start.8 = (bf16[128,1024]{1,0:T(8,128)(2,1)S(1)}, bf16[128,1024]{1,0:T(8,128)(2,1)S(1)}, u32[]{:S(2)}, u32[]{:S(2)}) collective-permute-start(bf16[128,1024]{1,0:T(8,128)(2,1)S(1)} %select_select_fusion), channel_id=1, source_target_pairs={{1,65},{3,67},{5,69},{7,71},{8,24},{9,73},{10,26},{11,75},{12,28},... | collective-permute-start | bytes 786440 | tf_op jit(solution)/shard_map/ppermute | solution.py:28
  63.1 4.6 %collective-permute-start.7 = (bf16[128,1024]{1,0:T(8,128)(2,1)S(1)}, bf16[128,1024]{1,0:T(8,128)(2,1)}, u32[]{:S(2)}, u32[]{:S(2)}) collective-permute-start(bf16[128,1024]{1,0:T(8,128)(2,1)S(1)} %select_select_fusion), channel_id=1, source_target_pairs={{1,97},{3,99},{5,101},{7,103},{8,16},{9,105},{10,18},{11,107},{12,... | collective-permute-start | bytes 786440 | tf_op jit(solution)/shard_map/ppermute | solution.py:28
  65.1 4.6 %collective-permute-start.6 = (bf16[128,1024]{1,0:T(8,128)(2,1)S(1)}, bf16[128,1024]{1,0:T(8,128)(2,1)}, u32[]{:S(2)}, u32[]{:S(2)}) collective-permute-start(bf16[128,1024]{1,0:T(8,128)(2,1)S(1)} %select_select_fusion), channel_id=1, source_target_pairs={{1,33},{3,35},{5,37},{7,39},{8,0},{9,41},{10,2},{11,43},{12,4},{13... | collective-permute-start | bytes 786440 | tf_op jit(solution)/shard_map/ppermute | solution.py:28
  67.1 10.2 %copy-start.1 = (bf16[2,1024,1024]{2,1,0:T(8,128)(2,1)S(1)}, bf16[2,1024,1024]{2,1,0:T(8,128)(2,1)}, u32[]{:S(2)}) copy-start(bf16[2,1024,1024]{2,1,0:T(8,128)(2,1)} %source_hbm) | copy-start | bytes 12582916
  70.8 9.9 %collective-permute-start.9 = (bf16[128,1024]{1,0:T(8,128)(2,1)S(1)}, bf16[128,1024]{1,0:T(8,128)(2,1)S(1)}, u32[]{:S(2)}, u32[]{:S(2)}) collective-permute-start(bf16[128,1024]{1,0:T(8,128)(2,1)S(1)} %add_add_fusion.own_ref), channel_id=1, source_target_pairs={{0,1},{1,0},{2,3},{3,2},{4,5},{5,4},{6,7},{7,6},{8,9},{9,8},{10,11... | collective-permute-start | bytes 786440 | tf_op jit(solution)/shard_map/ppermute | solution.py:28
  73.5 4.9 %collective-permute-start.2 = (bf16[64,256]{1,0:T(8,128)(2,1)S(1)}, bf16[64,256]{1,0:T(8,128)(2,1)S(1)}, u32[]{:S(2)}, u32[]{:S(2)}) collective-permute-start(bf16[64,256]{1,0:T(8,128)(2,1)S(1)} %get-tuple-element.17.p0), channel_id=1, source_target_pairs={{0,4},{1,5},{2,6},{3,7},{4,0},{5,1},{6,2},{7,3},{8,12},{9,13},{10,... | collective-permute-start | bytes 98312 | tf_op jit(solution)/shard_map/ppermute | solution.py:28
  76.7 4.0 %collective-permute-start.1 = (bf16[64,256]{1,0:T(8,128)(2,1)S(1)}, bf16[64,256]{1,0:T(8,128)(2,1)S(1)}, u32[]{:S(2)}, u32[]{:S(2)}) collective-permute-start(bf16[64,256]{1,0:T(8,128)(2,1)S(1)} %get-tuple-element.17.p0), channel_id=1, source_target_pairs={{0,6},{1,7},{2,4},{3,5},{4,2},{5,3},{6,0},{7,1},{8,14},{9,15},{10,... | collective-permute-start | bytes 98312 | tf_op jit(solution)/shard_map/ppermute | solution.py:28
  77.3 3.4 %collective-permute-start = (bf16[64,256]{1,0:T(8,128)(2,1)S(1)}, bf16[64,256]{1,0:T(8,128)(2,1)S(1)}, u32[]{:S(2)}, u32[]{:S(2)}) collective-permute-start(bf16[64,256]{1,0:T(8,128)(2,1)S(1)} %get-tuple-element.17.p0), channel_id=1, source_target_pairs={{0,2},{1,3},{2,0},{3,1},{4,6},{5,7},{6,4},{7,5},{8,10},{9,11},{10,... | collective-permute-start | bytes 98312 | tf_op jit(solution)/shard_map/ppermute | solution.py:28
  81.6 4.3 %collective-permute-start.12 = (bf16[64,256]{1,0:T(8,128)(2,1)S(1)}, bf16[64,256]{1,0:T(8,128)(2,1)S(1)}, u32[]{:S(2)}, u32[]{:S(2)}) collective-permute-start(bf16[64,256]{1,0:T(8,128)(2,1)S(1)} %get-tuple-element.26.p0), channel_id=1, source_target_pairs={{0,4},{1,5},{2,6},{3,7},{4,0},{5,1},{6,2},{7,3},{8,12},{9,13},{10,... | collective-permute-start | bytes 98312 | tf_op jit(solution)/shard_map/ppermute | solution.py:28
  83.1 4.0 %collective-permute-start.11 = (bf16[64,256]{1,0:T(8,128)(2,1)S(1)}, bf16[64,256]{1,0:T(8,128)(2,1)S(1)}, u32[]{:S(2)}, u32[]{:S(2)}) collective-permute-start(bf16[64,256]{1,0:T(8,128)(2,1)S(1)} %get-tuple-element.26.p0), channel_id=1, source_target_pairs={{0,6},{1,7},{2,4},{3,5},{4,2},{5,3},{6,0},{7,1},{8,14},{9,15},{10,... | collective-permute-start | bytes 98312 | tf_op jit(solution)/shard_map/ppermute | solution.py:28
  83.8 3.3 %collective-permute-start.10 = (bf16[64,256]{1,0:T(8,128)(2,1)S(1)}, bf16[64,256]{1,0:T(8,128)(2,1)S(1)}, u32[]{:S(2)}, u32[]{:S(2)}) collective-permute-start(bf16[64,256]{1,0:T(8,128)(2,1)S(1)} %get-tuple-element.26.p0), channel_id=1, source_target_pairs={{0,2},{1,3},{2,0},{3,1},{4,6},{5,7},{6,4},{7,5},{8,10},{9,11},{10,... | collective-permute-start | bytes 98312 | tf_op jit(solution)/shard_map/ppermute | solution.py:28
  87.9 5.5 %collective-permute-start.15 = (bf16[32,2048]{1,0:T(8,128)(2,1)S(1)}, bf16[32,2048]{1,0:T(8,128)(2,1)S(1)}, u32[]{:S(2)}, u32[]{:S(2)}) collective-permute-start(bf16[32,2048]{1,0:T(8,128)(2,1)S(1)} %shard_map.50), channel_id=1, source_target_pairs={{0,64},{1,17},{2,66},{3,19},{4,68},{5,21},{6,70},{7,23},{8,72},{9,... | collective-permute-start | bytes 393224 | tf_op jit(solution)/shard_map/ppermute | solution.py:28
  88.0 6.5 %collective-permute-start.14 = (bf16[32,2048]{1,0:T(8,128)(2,1)S(1)}, bf16[32,2048]{1,0:T(8,128)(2,1)S(1)}, u32[]{:S(2)}, u32[]{:S(2)}) collective-permute-start(bf16[32,2048]{1,0:T(8,128)(2,1)S(1)} %shard_map.50), channel_id=1, source_target_pairs={{0,96},{1,25},{2,98},{3,27},{4,100},{5,29},{6,102},{7,31},{8,104},... | collective-permute-start | bytes 393224 | tf_op jit(solution)/shard_map/ppermute | solution.py:28
  89.5 5.0 %collective-permute-start.13 = (bf16[32,2048]{1,0:T(8,128)(2,1)S(1)}, bf16[32,2048]{1,0:T(8,128)(2,1)S(1)}, u32[]{:S(2)}, u32[]{:S(2)}) collective-permute-start(bf16[32,2048]{1,0:T(8,128)(2,1)S(1)} %shard_map.50), channel_id=1, source_target_pairs={{0,32},{1,9},{2,34},{3,11},{4,36},{5,13},{6,38},{7,15},{8,40},{9,1... | collective-permute-start | bytes 393224 | tf_op jit(solution)/shard_map/ppermute | solution.py:28
  94.5 25.4 %copy-start = (bf16[2,8,1,128,1024]{4,3,2,1,0:T(8,128)(2,1)S(1)}, bf16[2,8,1,128,1024]{4,3,2,1,0:T(8,128)(2,1)}, u32[]{:S(2)}) copy-start(bf16[2,8,1,128,1024]{4,3,2,1,0:T(8,128)(2,1)} %refs_3_.1) | copy-start | bytes 12582916
  94.5 10.7 %collective-permute-start.21 = (bf16[128,2048]{1,0:T(8,128)(2,1)S(1)}, bf16[128,2048]{1,0:T(8,128)(2,1)S(1)}, u32[]{:S(2)}, u32[]{:S(2)}) collective-permute-start(bf16[128,2048]{1,0:T(8,128)(2,1)S(1)} %pad_maximum_fusion.a_ref), channel_id=1, source_target_pairs={{0,16},{1,65},{2,18},{3,67},{4,20},{5,69},{6,22},{7,71},{8,24},{9,... | collective-permute-start | bytes 1572872 | tf_op jit(solution)/shard_map/ppermute | solution.py:28
  95.8 15.4 %collective-permute-start.19 = (bf16[128,2048]{1,0:T(8,128)(2,1)S(1)}, bf16[128,2048]{1,0:T(8,128)(2,1)S(1)}, u32[]{:S(2)}, u32[]{:S(2)}) collective-permute-start(bf16[128,2048]{1,0:T(8,128)(2,1)S(1)} %pad_maximum_fusion.a_ref), channel_id=1, source_target_pairs={{0,8},{1,33},{2,10},{3,35},{4,12},{5,37},{6,14},{7,39},{8,0},{9,41... | collective-permute-start | bytes 1572872 | tf_op jit(solution)/shard_map/ppermute | solution.py:28
  95.8 19.0 %collective-permute-start.16 = (bf16[128,2048]{1,0:T(8,128)(2,1)S(1)}, bf16[128,2048]{1,0:T(8,128)(2,1)S(1)}, u32[]{:S(2)}, u32[]{:S(2)}) collective-permute-start(bf16[128,2048]{1,0:T(8,128)(2,1)S(1)} %pad_maximum_fusion.a_ref), channel_id=1, source_target_pairs={{0,24},{1,97},{2,26},{3,99},{4,28},{5,101},{6,30},{7,103},{8,16},{... | collective-permute-start | bytes 1572872 | tf_op jit(solution)/shard_map/ppermute | solution.py:28
  97.9 22.0 %collective-permute-start.18 = (bf16[128,2048]{1,0:T(8,128)(2,1)S(1)}, bf16[128,2048]{1,0:T(8,128)(2,1)S(1)}, u32[]{:S(2)}, u32[]{:S(2)}) collective-permute-start(bf16[128,2048]{1,0:T(8,128)(2,1)S(1)} %pad_maximum_fusion.a_ref), channel_id=1, source_target_pairs={{0,1},{1,0},{2,3},{3,2},{4,5},{5,4},{6,7},{7,6},{8,9},{9,8},{10,11... | collective-permute-start | bytes 1572872 | tf_op jit(solution)/shard_map/ppermute | solution.py:28
  105.3 16.2 %collective-permute-start.22 = (bf16[128,2048]{1,0:T(8,128)(2,1)S(1)}, bf16[128,2048]{1,0:T(8,128)(2,1)S(1)}, u32[]{:S(2)}, u32[]{:S(2)}) collective-permute-start(bf16[128,2048]{1,0:T(8,128)(2,1)S(1)} %collective-permute-done.21.a_ref), channel_id=1, source_target_pairs={{0,1},{1,0},{2,3},{3,2},{4,5},{5,4},{6,7},{7,6},{8,9},{9,8},{10,11... | collective-permute-start | bytes 1572872 | tf_op jit(solution)/shard_map/ppermute | solution.py:28
  111.2 11.9 %collective-permute-start.20 = (bf16[128,2048]{1,0:T(8,128)(2,1)S(1)}, bf16[128,2048]{1,0:T(8,128)(2,1)S(1)}, u32[]{:S(2)}, u32[]{:S(2)}) collective-permute-start(bf16[128,2048]{1,0:T(8,128)(2,1)S(1)} %collective-permute-done.19.a_ref), channel_id=1, source_target_pairs={{0,1},{1,0},{2,3},{3,2},{4,5},{5,4},{6,7},{7,6},{8,9},{9,8},{10,11... | collective-permute-start | bytes 1572872 | tf_op jit(solution)/shard_map/ppermute | solution.py:28
  114.9 9.8 %collective-permute-start.17 = (bf16[128,2048]{1,0:T(8,128)(2,1)S(1)}, bf16[128,2048]{1,0:T(8,128)(2,1)S(1)}, u32[]{:S(2)}, u32[]{:S(2)}) collective-permute-start(bf16[128,2048]{1,0:T(8,128)(2,1)S(1)} %collective-permute-done.16.a_ref), channel_id=1, source_target_pairs={{0,1},{1,0},{2,3},{3,2},{4,5},{5,4},{6,7},{7,6},{8,9},{9,8},{10,11... | collective-permute-start | bytes 1572872 | tf_op jit(solution)/shard_map/ppermute | solution.py:28

commit v7 on v6

--- a/solution.py
+++ b/solution.py
@@ -72,7 +72,8 @@
     slot = target * 8 + rank
     perm_ref[...] = (iota((count, count), 0) == slot).astype(F32).astype(BF16)
     part = iota((128, count), 0)
-    digits = jnp.where(part < 10, jnp.where(part % 2 == 0, local >> 5, local & 31), 0).astype(F32).astype(BF16)
+    digit = jnp.where(part % 2 == 0, local >> 5, local & 31)
+    digits = jnp.where((part >= 64) & (part < 72), digit, 0).astype(F32).astype(BF16)
     ids = dot(perm_ref[...], digits, (1, 1))
     lane = iota((64, 128), 1)
 
@@ -80,30 +81,31 @@
         tiles = [value[first + 16 * z + 8 * odd : first + 16 * z + 8 * odd + 8] for z in range(4)]
         return jnp.concatenate([t for t in tiles for _ in range(2)], axis=0)
 
-    kinds = [(64 * t, odd) for t in range(2) for odd in range(2)]
-    shared = [both(ids, *kind) for kind in kinds]
+    shared = [both(ids, 0, 0), both(ids, 0, 1), ids[64:128]]
     stores = []
     load.wait()
     for x in range(4):
         chunk = slice(x * 256, x * 256 + 256)
         part_rows = dot(perm_ref[chunk, :], rows_ref[...], (1, 0))
-        out_ref[chunk, 384:1408] = part_rows.astype(BF16)
+        out_ref[chunk, 256:1280] = part_rows.astype(BF16)
         if x == 0:
             head_ref[...] = part_rows[0:128]
         for y in range(4):
             rows = slice(x * 256 + y * 64, x * 256 + y * 64 + 64)
             mixed = ids[rows]
-            for i in range(4):
-                mixed = jnp.where(lane < 2 + 2 * i, mixed, shared[i])
-            out_ref[rows, 256:384] = mixed.astype(BF16)
-            for t in range(2):
-                cut = None
-                for p in range(4):
-                    tile, at = (y, 32 * x) if p % 2 == 0 else (4 + x, 32 * y)
-                    tile = both(head_ref[:, 128 * tile : 128 * tile + 128], *kinds[2 * t + p // 2])
-                    moved = pltpu.roll(tile, (32 * p - at) % 128, 1) if (32 * p - at) % 128 else tile
-                    cut = moved if cut is None else jnp.where(lane < 32 * p, cut, moved)
-                out_ref[rows, t * 128 : t * 128 + 128] = cut.astype(BF16)
+            for i in range(3):
+                mixed = jnp.where(lane < 66 + 2 * i, mixed, shared[i])
+            cut = []
+            for p in range(6):
+                tile, at = (y, 32 * x) if p % 2 == 0 else (4 + x, 32 * y)
+                tile = head_ref[:, 128 * tile : 128 * tile + 128]
+                tile = both(tile, 0, p // 2) if p < 4 else tile[64:128]
+                shift = (32 * (p % 4) - at) % 128
+                cut.append(pltpu.roll(tile, shift, 1) if shift else tile)
+            lead = jnp.where(lane < 64, jnp.where(lane < 32, cut[0], cut[1]), jnp.where(lane < 96, cut[2], cut[3]))
+            out_ref[rows, 0:128] = lead.astype(BF16)
+            follow = jnp.where(lane < 64, jnp.where(lane < 32, cut[4], cut[5]), mixed)
+            out_ref[rows, 128:256] = follow.astype(BF16)
         span = pl.ds(x * 256, 256)
         stores.append(pltpu.make_async_copy(out_ref.at[span], out_hbm.at[span], out_sems.at[x]))
         stores[x].start()
@@ -114,19 +116,17 @@
 def compact_kernel(early_ref, own_ref, lead_ref, next_ref):
     count = early_ref.shape[0]
     pick = iota((8, 128), 0)
-    lane = iota((8, 128), 1)
+    lane = iota((8, 128), 1) - 64
     weight = jnp.where(lane == 2 * pick, 32.0, jnp.where(lane == 2 * pick + 1, 1.0, 0.0))
-    weight = jnp.where(pick < 5, weight, 0.0).astype(BF16)
-    locals_ = dot(weight, early_ref[:, 256:384], (1, 1)).astype(jnp.int32)
+    weight = jnp.where(pick < 4, weight, 0.0).astype(BF16)
+    locals_ = dot(weight, early_ref[:, 128:256], (1, 1)).astype(jnp.int32)
     own_ref[...] = locals_
     place = iota((128, count), 0)
-    for t, ref in enumerate((lead_ref, next_ref)):
-        data = early_ref[:, 128 * t : 128 * t + 128]
-        for odd in range(2):
-            i = 1 + 2 * t + odd
-            hit = (place == locals_[i : i + 1]).astype(F32).astype(BF16)
-            found = dot(data, hit, (0, 1))[64 * odd : 64 * odd + 64]
-            ref[:, 128 * odd : 128 * odd + 128] = found.astype(BF16)
+    hits = [(place == locals_[i : i + 1]).astype(F32).astype(BF16) for i in (1, 2, 3)]
+    for odd in range(2):
+        found = dot(early_ref[:, 0:128], hits[odd], (0, 1))[64 * odd : 64 * odd + 64]
+        lead_ref[:, 128 * odd : 128 * odd + 128] = found.astype(BF16)
+    next_ref[...] = dot(early_ref[:, 128:256], hits[2], (0, 1))[0:64].astype(BF16)
 
 
 def gather_cols(refs, scratch):
@@ -136,21 +136,21 @@
     return jnp.concatenate([scratch[i] for i in range(4)], axis=1)
 
 
-def first_kernel(p0, p1, p2, p3, inverse_ref, next_ref, own_ref, other_ref, solved_ref, second_ref, scratch):
+def first_kernel(p0, p1, p2, p3, inverse_ref, next_ref, l0, l1, l2, l3, solved_ref, second_ref, scratch):
     lead = gather_cols((p0, p1, p2, p3), scratch)
     solved = dot(lead, inverse_ref[...], (1, 1)).astype(BF16)
     solved_ref[...] = solved
-    own = dot(solved, own_ref[...], (1, 1))
-    other = dot(solved, other_ref[...], (1, 1))
-    even = lax.axis_index("col") % 2 == 0
-    low = jnp.where(even, own, other)
-    high = jnp.where(even, other, own)
-    second_ref[:, 0:128] = (next_ref[:, 0:128].astype(F32) - low).astype(BF16)
-    second_ref[:, 128:256] = (next_ref[:, 128:256].astype(F32) - high).astype(BF16)
+    link = (l0[...] + l1[...]) + (l2[...] + l3[...])
+    second_ref[...] = (next_ref[...].astype(F32) - dot(solved, link, (1, 1))).astype(BF16)
 
 
 def second_kernel(p0, p1, p2, p3, inverse_ref, solved_ref, both_ref, scratch):
-    second = gather_cols((p0, p1, p2, p3), scratch)
+    z = lax.axis_index("col") // 2
+    k = lax.axis_index("col") % 2
+    for ref, at in zip((p0, p1, p2, p3), (z, z ^ 1, 3 - z, z ^ 2)):
+        scratch[2 * at + k] = ref[0:64]
+        scratch[2 * at + 1 - k] = ref[64:128]
+    second = jnp.concatenate([scratch[i] for i in range(8)], axis=1)
     solved = dot(second, inverse_ref[...], (1, 1)).astype(BF16)
     even = lax.axis_index("col") % 2 == 0
     both_ref[:, 0:1024] = jnp.where(even, solved_ref[0:32], solved_ref[32:64])
@@ -159,7 +159,7 @@
 
 def scatter_kernel(own_ref, arrived_ref, out_ref, hit_ref, rows_ref, sem):
     count = arrived_ref.shape[0]
-    copy = pltpu.make_async_copy(arrived_ref.at[:, 384:1408], rows_ref, sem)
+    copy = pltpu.make_async_copy(arrived_ref.at[:, 256:1280], rows_ref, sem)
     copy.start()
     hit_ref[...] = (iota((count, count), 0) == own_ref[0:1]).astype(F32).astype(BF16)
     copy.wait()
@@ -294,12 +294,7 @@
 
 
 def spread_first(piece):
-    moved = [send(piece, along_first(kind)) for kind in range(3)]
-    first, second, core = place_of(0)
-    source = jnp.where(core == 0, 0, 1)
-    line = jnp.where(first ^ 1 == source, moved[0], jnp.where(3 - first == source, moved[1], moved[2]))
-    line = jnp.where(first == source, piece, line)
-    return jnp.where(second == 1 - source, line, jnp.zeros_like(line))
+    return spread_along(piece, True, lambda x, y, z, k: x == 0 and y == 1)
 
 
 def spread_second(piece):
@@ -327,10 +322,10 @@
     (ordered,) = launch(
         order_kernel,
         (source_point.reshape(1, 1024), b_ingest),
-        [((1024, 1408), BF16)],
+        [((1024, 1280), BF16)],
         [
             pltpu.VMEM((1024, 1024), BF16),
-            pltpu.VMEM((1024, 1408), BF16),
+            pltpu.VMEM((1024, 1280), BF16),
             pltpu.VMEM((1024, 1024), BF16),
             pltpu.VMEM((128, 1024), F32),
             pltpu.SemaphoreType.DMA((1,)),
@@ -344,8 +339,9 @@
     )
     piece = panels[0, 0, 0]
     line = spread_first(piece)
+    line = jnp.where(lax.axis_index("row") == 1, piece, jnp.zeros_like(piece)) + line[0] + line[1] + line[2]
     plane = spread_second(line)
-    arrived = lax.all_to_all(ordered.reshape(128, 8, 1408), AXES, split_axis=0, concat_axis=0, tiled=True)
+    arrived = lax.all_to_all(ordered.reshape(128, 8, 1280), AXES, split_axis=0, concat_axis=0, tiled=True)
     inverses, _ = lax.optimization_barrier((diag_inverse, ordered))
     inverses = launch(
         load_kernel,
@@ -356,33 +352,31 @@
         limit=6,
         moved=8 << 20,
     )
-    arrived = arrived.reshape(1024, 1408)
+    arrived = arrived.reshape(1024, 1280)
     own, lead, follow = launch(
         compact_kernel,
         (arrived,),
-        [((8, 1024), jnp.int32), ((64, 256), BF16), ((64, 256), BF16)],
-        specs=[pl.BlockSpec((1024, 384), lambda i: (0, 0))],
+        [((8, 1024), jnp.int32), ((64, 256), BF16), ((64, 128), BF16)],
+        specs=[pl.BlockSpec((1024, 256), lambda i: (0, 0))],
         limit=12,
         flops=1 << 27,
         moved=1 << 20,
     )
-    line, plane, _ = lax.optimization_barrier((line, plane, own))
-    link = line + plane[0] + plane[1] + plane[2]
-    link_other = send(link, other_core)
     solved, second = launch(
         first_kernel,
-        (*around_cols(lead), inverses[0], follow, link, link_other),
-        [((64, 1024), BF16), ((64, 256), BF16)],
+        (*around_cols(lead), inverses[0], follow, line, *plane),
+        [((64, 1024), BF16), ((64, 128), BF16)],
         [pltpu.VMEM((4, 64, 256), BF16)],
         limit=12,
         flops=1 << 28,
         moved=3 << 20,
     )
+    second = jnp.concatenate([second, send(second, other_core)], axis=0)
     (both,) = launch(
         second_kernel,
         (*around_cols(second), inverses[1], solved),
         [((32, 2048), BF16)],
-        [pltpu.VMEM((4, 64, 256), BF16)],
+        [pltpu.VMEM((8, 64, 128), BF16)],
         limit=12,
         flops=1 << 28,
         moved=3 << 20,

time: 128 us -> 116 us (0.906); the launches traced: 128 us -> 114 us
  starting transfers between devices: 57.1 us -> 46.5 us
  waiting for transfers between devices: 47.4 us -> 42.7 us
  local copies, waits for them, and re-layouts: 0.98 us -> 3.17 us
    ppermute x23, starting transfers between devices: 45.6 us -> 35 us  [send(): return lax.ppermute(value, AXES, pairs)]
    ppermute x23, waiting for transfers between devices: 47.3 us -> 42.7 us  [send(): return lax.ppermute(value, AXES, pairs)]
    unnamed x4 -> x5, local copies, waits for them, and re-layouts: 0.01 us -> 2.19 us
  transfers between devices with their start and end apart: 24 -> 24, of which waited for: 10 -> 9; matrix products, arithmetic and copies ran while one was open for 2% -> 2% of each run, Pallas kernels for 7% -> 8%
where the time goes in v7:
time: 116 us; the launch traced here: 114 us
  starting transfers between devices  46.5 us (40%)
  waiting for transfers between devices  42.7 us (37%)
  Pallas kernels  20.5 us (18%)
  local copies, waits for them, and re-layouts  3.17 us (3%)
    ppermute x23, waiting for transfers between devices, send(): return lax.ppermute(value, AXES, pairs)  42.7 us
    ppermute x23, starting transfers between devices, send(): return lax.ppermute(value, AXES, pairs)  35 us
    pallas_call x10, Pallas kernels, launch(): pl.pallas_call(kernel, out_shape=[jax.ShapeDtypeStruct(s, d) for s, d in...  20.5 us
    all_to_all x1, starting transfers between devices, steps(): lax.all_to_all(ordered.reshape(128, 8, 1280), AXES, split_axis=0, concat_...  11.5 us
  transfers between devices with their start and end apart: 24, of which 9 were waited for; matrix products, arithmetic and copies ran while one was open for 2% of the time, Pallas kernels for 8%

profile of v7, /device:TPU:1, one launch (start us, length us, event | category | flops | bytes accessed | tf_op | source)
XLA Modules:
  0.0 114.3 jit_solution(18002227265556608052)
XLA Ops:
  0.0 6.3 %shard_map.46 = bf16[1024,1280]{1,0:T(8,128)(2,1)} custom-call(s32[1,1024]{1,0:T(1,128)} %bitcast.13, bf16[1024,1024]{1,0:T(8,128)(2,1)} %rows_hbm.1), custom_call_target="tpu_custom_call" | custom-call | flops 3221225472 | bytes 5242880 | tf_op jit(solution)/shard_map/pallas_call | solution.py:276
  6.3 11.5 %all-to-all-start = ((bf16[128,8,1280]{2,1,0:T(8,128)(2,1)}), bf16[128,8,1280]{2,1,0:T(8,128)(2,1)S(1)}, u32[]{:S(2)}, u32[]{:S(2)}) async-start(bf16[128,8,1280]{2,1,0:T(8,128)(2,1)} %bitcast.12), calls=%async_computation | async-start | bytes 5242880 | tf_op jit(solution)/shard_map/all_to_all | solution.py:344
  17.8 1.0 slice_bitcast_fusion
  19.4 1.3 %collective-permute-start.3 = (bf16[128,1024]{1,0:T(8,128)(2,1)S(1)}, bf16[128,1024]{1,0:T(8,128)(2,1)S(1)}, u32[]{:S(2)}, u32[]{:S(2)}) collective-permute-start(bf16[128,1024]{1,0:T(8,128)(2,1)S(1)} %slice_bitcast_fusion), channel_id=1, source_target_pairs={{8,40},{9,1},{10,42},{11,3},{12,44},{13,5},{14,46},{15,7}} | collective-permute-start | bytes 786440 | tf_op jit(solution)/shard_map/ppermute | solution.py:28
  20.7 1.4 %collective-permute-start.5 = (bf16[128,1024]{1,0:T(8,128)(2,1)S(1)}, bf16[128,1024]{1,0:T(8,128)(2,1)}, u32[]{:S(2)}, u32[]{:S(2)}) collective-permute-start(bf16[128,1024]{1,0:T(8,128)(2,1)S(1)} %slice_bitcast_fusion), channel_id=1, source_target_pairs={{8,72},{9,25},{10,74},{11,27},{12,76},{13,29},{14,78},{15,31}} | collective-permute-start | bytes 786440 | tf_op jit(solution)/shard_map/ppermute | solution.py:28
  22.1 28.5 %collective-permute-done.3 = bf16[128,1024]{1,0:T(8,128)(2,1)S(1)} collective-permute-done((bf16[128,1024]{1,0:T(8,128)(2,1)S(1)}, bf16[128,1024]{1,0:T(8,128)(2,1)S(1)}, u32[]{:S(2)}, u32[]{:S(2)}) %collective-permute-start.3) | collective-permute-done | bytes 262176 | tf_op jit(solution)/shard_map/ppermute | solution.py:28
  50.6 1.1 add_add_fusion.l0
  51.7 1.3 %collective-permute-start.8 = (bf16[128,1024]{1,0:T(8,128)(2,1)S(1)}, bf16[128,1024]{1,0:T(8,128)(2,1)S(1)}, u32[]{:S(2)}, u32[]{:S(2)}) collective-permute-start(bf16[128,1024]{1,0:T(8,128)(2,1)S(1)} %add_add_fusion.l0), channel_id=1, source_target_pairs={{1,65},{3,67},{5,69},{7,71},{8,24},{9,73},{10,26},{11,75},{12,28},... | collective-permute-start | bytes 786440 | tf_op jit(solution)/shard_map/ppermute | solution.py:28
  53.0 1.3 %collective-permute-start.7 = (bf16[128,1024]{1,0:T(8,128)(2,1)S(1)}, bf16[128,1024]{1,0:T(8,128)(2,1)S(1)}, u32[]{:S(2)}, u32[]{:S(2)}) collective-permute-start(bf16[128,1024]{1,0:T(8,128)(2,1)S(1)} %add_add_fusion.l0), channel_id=1, source_target_pairs={{1,97},{3,99},{5,101},{7,103},{8,16},{9,105},{10,18},{11,107},{12,... | collective-permute-start | bytes 786440 | tf_op jit(solution)/shard_map/ppermute | solution.py:28
  54.3 2.0 %collective-permute-start.6 = (bf16[128,1024]{1,0:T(8,128)(2,1)S(1)}, bf16[128,1024]{1,0:T(8,128)(2,1)}, u32[]{:S(2)}, u32[]{:S(2)}) collective-permute-start(bf16[128,1024]{1,0:T(8,128)(2,1)S(1)} %add_add_fusion.l0), channel_id=1, source_target_pairs={{1,33},{3,35},{5,37},{7,39},{8,0},{9,41},{10,2},{11,43},{12,4},{13... | collective-permute-start | bytes 786440 | tf_op jit(solution)/shard_map/ppermute | solution.py:28
  56.9 3.3 %collective-permute-start.2 = (bf16[64,256]{1,0:T(8,128)(2,1)S(1)}, bf16[64,256]{1,0:T(8,128)(2,1)S(1)}, u32[]{:S(2)}, u32[]{:S(2)}) collective-permute-start(bf16[64,256]{1,0:T(8,128)(2,1)S(1)} %get-tuple-element.13.p0), channel_id=1, source_target_pairs={{0,4},{1,5},{2,6},{3,7},{4,0},{5,1},{6,2},{7,3},{8,12},{9,13},{10,... | collective-permute-start | bytes 98312 | tf_op jit(solution)/shard_map/ppermute | solution.py:28
  60.8 2.2 %copy-done.1 = bf16[2,1024,1024]{2,1,0:T(8,128)(2,1)S(1)} copy-done((bf16[2,1024,1024]{2,1,0:T(8,128)(2,1)S(1)}, bf16[2,1024,1024]{2,1,0:T(8,128)(2,1)}, u32[]{:S(2)}) %copy-start.1) | copy-done | bytes 4194328
  64.3 1.9 %shard_map.49 = (bf16[64,1024]{1,0:T(8,128)(2,1)S(1)}, bf16[64,128]{1,0:T(8,128)(2,1)S(1)}) custom-call(bf16[64,256]{1,0:T(8,128)(2,1)S(1)} %get-tuple-element.13.p0, bf16[64,256]{1,0:T(8,128)(2,1)S(1)} %collective-permute-done.p1, bf16[64,256]{1,0:T(8,128)(2,1)S(1)} %collective-permute-done.1.p2, bf16[64,256]{1,0:T(8,128)(2,1)S(1)} %collective-permute-done.2.p3, ...), custom_call_target="tpu_custom_call" | custom-call | flops 268435456 | bytes 3145728 | tf_op jit(solution)/shard_map/pallas_call | solution.py:276
  66.3 1.2 %collective-permute-done.9 = bf16[64,128]{1,0:T(8,128)(2,1)S(1)} collective-permute-done((bf16[64,128]{1,0:T(8,128)(2,1)S(1)}, bf16[64,128]{1,0:T(8,128)(2,1)S(1)}, u32[]{:S(2)}, u32[]{:S(2)}) %collective-permute-start.9) | collective-permute-done | bytes 16416 | tf_op jit(solution)/shard_map/ppermute | solution.py:28
  67.4 2.4 %collective-permute-start.12 = (bf16[128,128]{1,0:T(8,128)(2,1)S(1)}, bf16[128,128]{1,0:T(8,128)(2,1)S(1)}, u32[]{:S(2)}, u32[]{:S(2)}) collective-permute-start(bf16[128,128]{1,0:T(8,128)(2,1)S(1)} %constant_dynamic-update-slice_fusion.p0), channel_id=1, source_target_pairs={{0,4},{1,5},{2,6},{3,7},{4,0},{5,1},{6,2},{7,3},{8,12},{9,13},{10,... | collective-permute-start | bytes 98312 | tf_op jit(solution)/shard_map/ppermute | solution.py:28
  70.4 1.3 %collective-permute-done.12.p3 = bf16[128,128]{1,0:T(8,128)(2,1)S(1)} collective-permute-done((bf16[128,128]{1,0:T(8,128)(2,1)S(1)}, bf16[128,128]{1,0:T(8,128)(2,1)S(1)}, u32[]{:S(2)}, u32[]{:S(2)}) %collective-permute-start.12) | collective-permute-done | bytes 32800 | tf_op jit(solution)/shard_map/ppermute | solution.py:28
  71.7 2.1 %collective-permute-done.11.p2 = bf16[128,128]{1,0:T(8,128)(2,1)S(1)} collective-permute-done((bf16[128,128]{1,0:T(8,128)(2,1)S(1)}, bf16[128,128]{1,0:T(8,128)(2,1)S(1)}, u32[]{:S(2)}, u32[]{:S(2)}) %collective-permute-start.11) | collective-permute-done | bytes 32800 | tf_op jit(solution)/shard_map/ppermute | solution.py:28
  74.6 1.7 %collective-permute-start.15 = (bf16[32,2048]{1,0:T(8,128)(2,1)S(1)}, bf16[32,2048]{1,0:T(8,128)(2,1)S(1)}, u32[]{:S(2)}, u32[]{:S(2)}) collective-permute-start(bf16[32,2048]{1,0:T(8,128)(2,1)S(1)} %shard_map.50), channel_id=1, source_target_pairs={{0,64},{1,17},{2,66},{3,19},{4,68},{5,21},{6,70},{7,23},{8,72},{9,... | collective-permute-start | bytes 393224 | tf_op jit(solution)/shard_map/ppermute | solution.py:28
  76.3 3.6 %collective-permute-start.14 = (bf16[32,2048]{1,0:T(8,128)(2,1)S(1)}, bf16[32,2048]{1,0:T(8,128)(2,1)S(1)}, u32[]{:S(2)}, u32[]{:S(2)}) collective-permute-start(bf16[32,2048]{1,0:T(8,128)(2,1)S(1)} %shard_map.50), channel_id=1, source_target_pairs={{0,96},{1,25},{2,98},{3,27},{4,100},{5,29},{6,102},{7,31},{8,104},... | collective-permute-start | bytes 393224 | tf_op jit(solution)/shard_map/ppermute | solution.py:28
  80.3 3.0 %collective-permute-done.14 = bf16[32,2048]{1,0:T(8,128)(2,1)S(1)} collective-permute-done((bf16[32,2048]{1,0:T(8,128)(2,1)S(1)}, bf16[32,2048]{1,0:T(8,128)(2,1)S(1)}, u32[]{:S(2)}, u32[]{:S(2)}) %collective-permute-start.14) | collective-permute-done | bytes 131104 | tf_op jit(solution)/shard_map/ppermute | solution.py:28
  83.3 1.1 collective-permute-done.13
  84.4 3.3 %collective-permute-start.21 = (bf16[128,2048]{1,0:T(8,128)(2,1)S(1)}, bf16[128,2048]{1,0:T(8,128)(2,1)S(1)}, u32[]{:S(2)}, u32[]{:S(2)}) collective-permute-start(bf16[128,2048]{1,0:T(8,128)(2,1)S(1)} %pad_maximum_fusion.a_ref), channel_id=1, source_target_pairs={{0,16},{1,65},{2,18},{3,67},{4,20},{5,69},{6,22},{7,71},{8,24},{9,... | collective-permute-start | bytes 1572872 | tf_op jit(solution)/shard_map/ppermute | solution.py:28
  88.1 4.8 %collective-permute-start.18 = (bf16[128,2048]{1,0:T(8,128)(2,1)S(1)}, bf16[128,2048]{1,0:T(8,128)(2,1)S(1)}, u32[]{:S(2)}, u32[]{:S(2)}) collective-permute-start(bf16[128,2048]{1,0:T(8,128)(2,1)S(1)} %pad_maximum_fusion.a_ref), channel_id=1, source_target_pairs={{0,1},{1,0},{2,3},{3,2},{4,5},{5,4},{6,7},{7,6},{8,9},{9,8},{10,11... | collective-permute-start | bytes 1572872 | tf_op jit(solution)/shard_map/ppermute | solution.py:28
  92.8 1.8 %collective-permute-done.21.a_ref = bf16[128,2048]{1,0:T(8,128)(2,1)S(1)} collective-permute-done((bf16[128,2048]{1,0:T(8,128)(2,1)S(1)}, bf16[128,2048]{1,0:T(8,128)(2,1)S(1)}, u32[]{:S(2)}, u32[]{:S(2)}) %collective-permute-start.21) | collective-permute-done | bytes 524320 | tf_op jit(solution)/shard_map/ppermute | solution.py:28
  94.6 2.2 %collective-permute-start.22 = (bf16[128,2048]{1,0:T(8,128)(2,1)S(1)}, bf16[128,2048]{1,0:T(8,128)(2,1)S(1)}, u32[]{:S(2)}, u32[]{:S(2)}) collective-permute-start(bf16[128,2048]{1,0:T(8,128)(2,1)S(1)} %collective-permute-done.21.a_ref), channel_id=1, source_target_pairs={{0,1},{1,0},{2,3},{3,2},{4,5},{5,4},{6,7},{7,6},{8,9},{9,8},{10,11... | collective-permute-start | bytes 1572872 | tf_op jit(solution)/shard_map/ppermute | solution.py:28
  96.8 2.7 %collective-permute-done.19.a_ref = bf16[128,2048]{1,0:T(8,128)(2,1)S(1)} collective-permute-done((bf16[128,2048]{1,0:T(8,128)(2,1)S(1)}, bf16[128,2048]{1,0:T(8,128)(2,1)S(1)}, u32[]{:S(2)}, u32[]{:S(2)}) %collective-permute-start.19) | collective-permute-done | bytes 524320 | tf_op jit(solution)/shard_map/ppermute | solution.py:28
  99.5 3.9 %collective-permute-start.20 = (bf16[128,2048]{1,0:T(8,128)(2,1)S(1)}, bf16[128,2048]{1,0:T(8,128)(2,1)S(1)}, u32[]{:S(2)}, u32[]{:S(2)}) collective-permute-start(bf16[128,2048]{1,0:T(8,128)(2,1)S(1)} %collective-permute-done.19.a_ref), channel_id=1, source_target_pairs={{0,1},{1,0},{2,3},{3,2},{4,5},{5,4},{6,7},{7,6},{8,9},{9,8},{10,11... | collective-permute-start | bytes 1572872 | tf_op jit(solution)/shard_map/ppermute | solution.py:28
  103.4 3.2 %shard_map.51.rows_ref.refs_4_ = bf16[1024,1024]{1,0:T(8,128)(2,1)S(1)} custom-call(s32[8,1024]{1,0:T(8,128)S(1)} %get-tuple-element.20.own_ref, bf16[1024,1280]{1,0:T(8,128)(2,1)S(1)} %bitcast.11), custom_call_target="tpu_custom_call" | custom-call | flops 2147483648 | bytes 4194304 | tf_op jit(solution)/shard_map/pallas_call | solution.py:276
  106.6 1.6 %shard_map.52.refs_0_ = bf16[1024,256]{1,0:T(8,128)(2,1)S(1)} custom-call(bf16[128,2048]{1,0:T(8,128)(2,1)S(1)} %pad_maximum_fusion.a_ref, bf16[128,2048]{1,0:T(8,128)(2,1)S(1)} %collective-permute-done.18.b_ref, bf16[2,8,1,128,1024]{4,3,2,1,0:T(8,128)(2,1)S(1)} %copy-done, bf16[1024,1024]{1,0:T(8,128)(2,1)S(1)} %shard_map.51.rows_ref.refs_4_), custom_call_target="tpu_custom_call" | custom-call | flops 1073741824 | bytes 2097152 | tf_op jit(solution)/shard_map/pallas_call | solution.py:276
  108.2 1.6 %shard_map.54.refs_2_ = bf16[1024,256]{1,0:T(8,128)(2,1)S(1)} custom-call(bf16[128,2048]{1,0:T(8,128)(2,1)S(1)} %collective-permute-done.21.a_ref, bf16[128,2048]{1,0:T(8,128)(2,1)S(1)} %collective-permute-done.22.b_ref, bf16[2,8,1,128,1024]{4,3,2,1,0:T(8,128)(2,1)S(1)} %copy-done, bf16[1024,1024]{1,0:T(8,128)(2,1)S(1)} %shard_map.51.rows_ref.refs_4_), custom_call_target="tpu_custom_call" | custom-call | flops 1073741824 | bytes 2097152 | tf_op jit(solution)/shard_map/pallas_call | solution.py:276
  109.7 1.6 %shard_map.53.refs_1_ = bf16[1024,256]{1,0:T(8,128)(2,1)S(1)} custom-call(bf16[128,2048]{1,0:T(8,128)(2,1)S(1)} %collective-permute-done.19.a_ref, bf16[128,2048]{1,0:T(8,128)(2,1)S(1)} %collective-permute-done.20.b_ref, bf16[2,8,1,128,1024]{4,3,2,1,0:T(8,128)(2,1)S(1)} %copy-done, bf16[1024,1024]{1,0:T(8,128)(2,1)S(1)} %shard_map.51.rows_ref.refs_4_), custom_call_target="tpu_custom_call" | custom-call | flops 1073741824 | bytes 2097152 | tf_op jit(solution)/shard_map/pallas_call | solution.py:276
  111.3 2.8 %shard_map.55 = bf16[1024,1024]{1,0:T(8,128)(2,1)} custom-call(bf16[128,2048]{1,0:T(8,128)(2,1)S(1)} %collective-permute-done.16.a_ref, bf16[128,2048]{1,0:T(8,128)(2,1)S(1)} %collective-permute-done.17.b_ref, bf16[1024,256]{1,0:T(8,128)(2,1)S(1)} %shard_map.52.refs_0_, bf16[1024,256]{1,0:T(8,128)(2,1)S(1)} %shard_map.53.refs_1_, ...), custom_call_target="tpu_custom_call" | custom-call | flops 1073741824 | bytes 2097152 | tf_op jit(solution)/shard_map/pallas_call | solution.py:276
  (35 shorter events, 5.2 us)
Async XLA Ops:
  6.3 50.1 %all-to-all-start = ((bf16[128,8,1280]{2,1,0:T(8,128)(2,1)}), bf16[128,8,1280]{2,1,0:T(8,128)(2,1)S(1)}, u32[]{:S(2)}, u32[]{:S(2)}) async-start(bf16[128,8,1280]{2,1,0:T(8,128)(2,1)} %bitcast.12), calls=%async_computation | async-start | bytes 5242880 | tf_op jit(solution)/shard_map/all_to_all | solution.py:344
  18.7 3.4 %collective-permute-start.4 = (bf16[128,1024]{1,0:T(8,128)(2,1)S(1)}, bf16[128,1024]{1,0:T(8,128)(2,1)S(1)}, u32[]{:S(2)}, u32[]{:S(2)}) collective-permute-start(bf16[128,1024]{1,0:T(8,128)(2,1)S(1)} %slice_bitcast_fusion), channel_id=1, source_target_pairs={{8,104},{9,17},{10,106},{11,19},{12,108},{13,21},{14,110},{15,23}} | collective-permute-start | bytes 786440 | tf_op jit(solution)/shard_map/ppermute | solution.py:28
  19.4 31.2 %collective-permute-start.3 = (bf16[128,1024]{1,0:T(8,128)(2,1)S(1)}, bf16[128,1024]{1,0:T(8,128)(2,1)S(1)}, u32[]{:S(2)}, u32[]{:S(2)}) collective-permute-start(bf16[128,1024]{1,0:T(8,128)(2,1)S(1)} %slice_bitcast_fusion), channel_id=1, source_target_pairs={{8,40},{9,1},{10,42},{11,3},{12,44},{13,5},{14,46},{15,7}} | collective-permute-start | bytes 786440 | tf_op jit(solution)/shard_map/ppermute | solution.py:28
  20.7 29.9 %collective-permute-start.5 = (bf16[128,1024]{1,0:T(8,128)(2,1)S(1)}, bf16[128,1024]{1,0:T(8,128)(2,1)}, u32[]{:S(2)}, u32[]{:S(2)}) collective-permute-start(bf16[128,1024]{1,0:T(8,128)(2,1)S(1)} %slice_bitcast_fusion), channel_id=1, source_target_pairs={{8,72},{9,25},{10,74},{11,27},{12,76},{13,29},{14,78},{15,31}} | collective-permute-start | bytes 786440 | tf_op jit(solution)/shard_map/ppermute | solution.py:28
  51.7 9.1 %collective-permute-start.8 = (bf16[128,1024]{1,0:T(8,128)(2,1)S(1)}, bf16[128,1024]{1,0:T(8,128)(2,1)S(1)}, u32[]{:S(2)}, u32[]{:S(2)}) collective-permute-start(bf16[128,1024]{1,0:T(8,128)(2,1)S(1)} %add_add_fusion.l0), channel_id=1, source_target_pairs={{1,65},{3,67},{5,69},{7,71},{8,24},{9,73},{10,26},{11,75},{12,28},... | collective-permute-start | bytes 786440 | tf_op jit(solution)/shard_map/ppermute | solution.py:28
  53.0 10.3 %collective-permute-start.7 = (bf16[128,1024]{1,0:T(8,128)(2,1)S(1)}, bf16[128,1024]{1,0:T(8,128)(2,1)S(1)}, u32[]{:S(2)}, u32[]{:S(2)}) collective-permute-start(bf16[128,1024]{1,0:T(8,128)(2,1)S(1)} %add_add_fusion.l0), channel_id=1, source_target_pairs={{1,97},{3,99},{5,101},{7,103},{8,16},{9,105},{10,18},{11,107},{12,... | collective-permute-start | bytes 786440 | tf_op jit(solution)/shard_map/ppermute | solution.py:28
  54.3 9.0 %collective-permute-start.6 = (bf16[128,1024]{1,0:T(8,128)(2,1)S(1)}, bf16[128,1024]{1,0:T(8,128)(2,1)}, u32[]{:S(2)}, u32[]{:S(2)}) collective-permute-start(bf16[128,1024]{1,0:T(8,128)(2,1)S(1)} %add_add_fusion.l0), channel_id=1, source_target_pairs={{1,33},{3,35},{5,37},{7,39},{8,0},{9,41},{10,2},{11,43},{12,4},{13... | collective-permute-start | bytes 786440 | tf_op jit(solution)/shard_map/ppermute | solution.py:28
  56.9 6.4 %collective-permute-start.2 = (bf16[64,256]{1,0:T(8,128)(2,1)S(1)}, bf16[64,256]{1,0:T(8,128)(2,1)S(1)}, u32[]{:S(2)}, u32[]{:S(2)}) collective-permute-start(bf16[64,256]{1,0:T(8,128)(2,1)S(1)} %get-tuple-element.13.p0), channel_id=1, source_target_pairs={{0,4},{1,5},{2,6},{3,7},{4,0},{5,1},{6,2},{7,3},{8,12},{9,13},{10,... | collective-permute-start | bytes 98312 | tf_op jit(solution)/shard_map/ppermute | solution.py:28
  60.3 4.0 %collective-permute-start.1 = (bf16[64,256]{1,0:T(8,128)(2,1)S(1)}, bf16[64,256]{1,0:T(8,128)(2,1)S(1)}, u32[]{:S(2)}, u32[]{:S(2)}) collective-permute-start(bf16[64,256]{1,0:T(8,128)(2,1)S(1)} %get-tuple-element.13.p0), channel_id=1, source_target_pairs={{0,6},{1,7},{2,4},{3,5},{4,2},{5,3},{6,0},{7,1},{8,14},{9,15},{10,... | collective-permute-start | bytes 98312 | tf_op jit(solution)/shard_map/ppermute | solution.py:28
  60.8 3.5 %collective-permute-start = (bf16[64,256]{1,0:T(8,128)(2,1)S(1)}, bf16[64,256]{1,0:T(8,128)(2,1)S(1)}, u32[]{:S(2)}, u32[]{:S(2)}) collective-permute-start(bf16[64,256]{1,0:T(8,128)(2,1)S(1)} %get-tuple-element.13.p0), channel_id=1, source_target_pairs={{0,2},{1,3},{2,0},{3,1},{4,6},{5,7},{6,4},{7,5},{8,10},{9,11},{10,... | collective-permute-start | bytes 98312 | tf_op jit(solution)/shard_map/ppermute | solution.py:28
  60.8 2.2 %copy-start.1 = (bf16[2,1024,1024]{2,1,0:T(8,128)(2,1)S(1)}, bf16[2,1024,1024]{2,1,0:T(8,128)(2,1)}, u32[]{:S(2)}) copy-start(bf16[2,1024,1024]{2,1,0:T(8,128)(2,1)} %source_hbm) | copy-start | bytes 12582916
  66.2 1.3 %collective-permute-start.9 = (bf16[64,128]{1,0:T(8,128)(2,1)S(1)}, bf16[64,128]{1,0:T(8,128)(2,1)S(1)}, u32[]{:S(2)}, u32[]{:S(2)}) collective-permute-start(bf16[64,128]{1,0:T(8,128)(2,1)S(1)} %get-tuple-element.17), channel_id=1, source_target_pairs={{0,1},{1,0},{2,3},{3,2},{4,5},{5,4},{6,7},{7,6},{8,9},{9,8},{10,11... | collective-permute-start | bytes 49160 | tf_op jit(solution)/shard_map/ppermute | solution.py:28
  67.4 4.3 %collective-permute-start.12 = (bf16[128,128]{1,0:T(8,128)(2,1)S(1)}, bf16[128,128]{1,0:T(8,128)(2,1)S(1)}, u32[]{:S(2)}, u32[]{:S(2)}) collective-permute-start(bf16[128,128]{1,0:T(8,128)(2,1)S(1)} %constant_dynamic-update-slice_fusion.p0), channel_id=1, source_target_pairs={{0,4},{1,5},{2,6},{3,7},{4,0},{5,1},{6,2},{7,3},{8,12},{9,13},{10,... | collective-permute-start | bytes 98312 | tf_op jit(solution)/shard_map/ppermute | solution.py:28
  69.9 4.0 %collective-permute-start.11 = (bf16[128,128]{1,0:T(8,128)(2,1)S(1)}, bf16[128,128]{1,0:T(8,128)(2,1)S(1)}, u32[]{:S(2)}, u32[]{:S(2)}) collective-permute-start(bf16[128,128]{1,0:T(8,128)(2,1)S(1)} %constant_dynamic-update-slice_fusion.p0), channel_id=1, source_target_pairs={{0,6},{1,7},{2,4},{3,5},{4,2},{5,3},{6,0},{7,1},{8,14},{9,15},{10,... | collective-permute-start | bytes 98312 | tf_op jit(solution)/shard_map/ppermute | solution.py:28
  70.4 3.5 %collective-permute-start.10 = (bf16[128,128]{1,0:T(8,128)(2,1)S(1)}, bf16[128,128]{1,0:T(8,128)(2,1)S(1)}, u32[]{:S(2)}, u32[]{:S(2)}) collective-permute-start(bf16[128,128]{1,0:T(8,128)(2,1)S(1)} %constant_dynamic-update-slice_fusion.p0), channel_id=1, source_target_pairs={{0,2},{1,3},{2,0},{3,1},{4,6},{5,7},{6,4},{7,5},{8,10},{9,11},{10,... | collective-permute-start | bytes 98312 | tf_op jit(solution)/shard_map/ppermute | solution.py:28
  74.6 5.7 %collective-permute-start.15 = (bf16[32,2048]{1,0:T(8,128)(2,1)S(1)}, bf16[32,2048]{1,0:T(8,128)(2,1)S(1)}, u32[]{:S(2)}, u32[]{:S(2)}) collective-permute-start(bf16[32,2048]{1,0:T(8,128)(2,1)S(1)} %shard_map.50), channel_id=1, source_target_pairs={{0,64},{1,17},{2,66},{3,19},{4,68},{5,21},{6,70},{7,23},{8,72},{9,... | collective-permute-start | bytes 393224 | tf_op jit(solution)/shard_map/ppermute | solution.py:28
  76.3 6.9 %collective-permute-start.14 = (bf16[32,2048]{1,0:T(8,128)(2,1)S(1)}, bf16[32,2048]{1,0:T(8,128)(2,1)S(1)}, u32[]{:S(2)}, u32[]{:S(2)}) collective-permute-start(bf16[32,2048]{1,0:T(8,128)(2,1)S(1)} %shard_map.50), channel_id=1, source_target_pairs={{0,96},{1,25},{2,98},{3,27},{4,100},{5,29},{6,102},{7,31},{8,104},... | collective-permute-start | bytes 393224 | tf_op jit(solution)/shard_map/ppermute | solution.py:28
  79.9 4.4 %collective-permute-start.13 = (bf16[32,2048]{1,0:T(8,128)(2,1)S(1)}, bf16[32,2048]{1,0:T(8,128)(2,1)S(1)}, u32[]{:S(2)}, u32[]{:S(2)}) collective-permute-start(bf16[32,2048]{1,0:T(8,128)(2,1)S(1)} %shard_map.50), channel_id=1, source_target_pairs={{0,32},{1,9},{2,34},{3,11},{4,36},{5,13},{6,38},{7,15},{8,40},{9,1... | collective-permute-start | bytes 393224 | tf_op jit(solution)/shard_map/ppermute | solution.py:28
  84.4 10.2 %collective-permute-start.21 = (bf16[128,2048]{1,0:T(8,128)(2,1)S(1)}, bf16[128,2048]{1,0:T(8,128)(2,1)S(1)}, u32[]{:S(2)}, u32[]{:S(2)}) collective-permute-start(bf16[128,2048]{1,0:T(8,128)(2,1)S(1)} %pad_maximum_fusion.a_ref), channel_id=1, source_target_pairs={{0,16},{1,65},{2,18},{3,67},{4,20},{5,69},{6,22},{7,71},{8,24},{9,... | collective-permute-start | bytes 1572872 | tf_op jit(solution)/shard_map/ppermute | solution.py:28
  87.7 11.8 %collective-permute-start.19 = (bf16[128,2048]{1,0:T(8,128)(2,1)S(1)}, bf16[128,2048]{1,0:T(8,128)(2,1)S(1)}, u32[]{:S(2)}, u32[]{:S(2)}) collective-permute-start(bf16[128,2048]{1,0:T(8,128)(2,1)S(1)} %pad_maximum_fusion.a_ref), channel_id=1, source_target_pairs={{0,8},{1,33},{2,10},{3,35},{4,12},{5,37},{6,14},{7,39},{8,0},{9,41... | collective-permute-start | bytes 1572872 | tf_op jit(solution)/shard_map/ppermute | solution.py:28
  87.7 15.7 %collective-permute-start.16 = (bf16[128,2048]{1,0:T(8,128)(2,1)S(1)}, bf16[128,2048]{1,0:T(8,128)(2,1)S(1)}, u32[]{:S(2)}, u32[]{:S(2)}) collective-permute-start(bf16[128,2048]{1,0:T(8,128)(2,1)S(1)} %pad_maximum_fusion.a_ref), channel_id=1, source_target_pairs={{0,24},{1,97},{2,26},{3,99},{4,28},{5,101},{6,30},{7,103},{8,16},{... | collective-permute-start | bytes 1572872 | tf_op jit(solution)/shard_map/ppermute | solution.py:28
  88.1 18.5 %collective-permute-start.18 = (bf16[128,2048]{1,0:T(8,128)(2,1)S(1)}, bf16[128,2048]{1,0:T(8,128)(2,1)S(1)}, u32[]{:S(2)}, u32[]{:S(2)}) collective-permute-start(bf16[128,2048]{1,0:T(8,128)(2,1)S(1)} %pad_maximum_fusion.a_ref), channel_id=1, source_target_pairs={{0,1},{1,0},{2,3},{3,2},{4,5},{5,4},{6,7},{7,6},{8,9},{9,8},{10,11... | collective-permute-start | bytes 1572872 | tf_op jit(solution)/shard_map/ppermute | solution.py:28
  94.6 13.6 %collective-permute-start.22 = (bf16[128,2048]{1,0:T(8,128)(2,1)S(1)}, bf16[128,2048]{1,0:T(8,128)(2,1)S(1)}, u32[]{:S(2)}, u32[]{:S(2)}) collective-permute-start(bf16[128,2048]{1,0:T(8,128)(2,1)S(1)} %collective-permute-done.21.a_ref), channel_id=1, source_target_pairs={{0,1},{1,0},{2,3},{3,2},{4,5},{5,4},{6,7},{7,6},{8,9},{9,8},{10,11... | collective-permute-start | bytes 1572872 | tf_op jit(solution)/shard_map/ppermute | solution.py:28
  99.5 10.3 %collective-permute-start.20 = (bf16[128,2048]{1,0:T(8,128)(2,1)S(1)}, bf16[128,2048]{1,0:T(8,128)(2,1)S(1)}, u32[]{:S(2)}, u32[]{:S(2)}) collective-permute-start(bf16[128,2048]{1,0:T(8,128)(2,1)S(1)} %collective-permute-done.19.a_ref), channel_id=1, source_target_pairs={{0,1},{1,0},{2,3},{3,2},{4,5},{5,4},{6,7},{7,6},{8,9},{9,8},{10,11... | collective-permute-start | bytes 1572872 | tf_op jit(solution)/shard_map/ppermute | solution.py:28
  103.4 7.9 %collective-permute-start.17 = (bf16[128,2048]{1,0:T(8,128)(2,1)S(1)}, bf16[128,2048]{1,0:T(8,128)(2,1)S(1)}, u32[]{:S(2)}, u32[]{:S(2)}) collective-permute-start(bf16[128,2048]{1,0:T(8,128)(2,1)S(1)} %collective-permute-done.16.a_ref), channel_id=1, source_target_pairs={{0,1},{1,0},{2,3},{3,2},{4,5},{5,4},{6,7},{7,6},{8,9},{9,8},{10,11... | collective-permute-start | bytes 1572872 | tf_op jit(solution)/shard_map/ppermute | solution.py:28
  103.4 3.2 %copy-start = (bf16[2,8,1,128,1024]{4,3,2,1,0:T(8,128)(2,1)S(1)}, bf16[2,8,1,128,1024]{4,3,2,1,0:T(8,128)(2,1)}, u32[]{:S(2)}) copy-start(bf16[2,8,1,128,1024]{4,3,2,1,0:T(8,128)(2,1)} %refs_3_.1) | copy-start | bytes 12582916

commit v8 on v7

--- a/solution.py
+++ b/solution.py
@@ -136,11 +136,16 @@
     return jnp.concatenate([scratch[i] for i in range(4)], axis=1)
 
 
-def first_kernel(p0, p1, p2, p3, inverse_ref, next_ref, l0, l1, l2, l3, solved_ref, second_ref, scratch):
+def first_kernel(p0, p1, p2, p3, inverse_ref, next_ref, l0, l1, l2, l3, solved_ref, second_ref, scratch, link_ref, sems):
+    loads = [pltpu.make_async_copy(ref, link_ref.at[i], sems.at[i]) for i, ref in enumerate((l0, l1, l2, l3))]
+    for load in loads:
+        load.start()
     lead = gather_cols((p0, p1, p2, p3), scratch)
     solved = dot(lead, inverse_ref[...], (1, 1)).astype(BF16)
     solved_ref[...] = solved
-    link = (l0[...] + l1[...]) + (l2[...] + l3[...])
+    for load in loads:
+        load.wait()
+    link = (link_ref[0] + link_ref[1]) + (link_ref[2] + link_ref[3])
     second_ref[...] = (next_ref[...].astype(F32) - dot(solved, link, (1, 1))).astype(BF16)
 
 
@@ -294,7 +299,12 @@
 
 
 def spread_first(piece):
-    return spread_along(piece, True, lambda x, y, z, k: x == 0 and y == 1)
+    moved = [send(piece, along_first(kind)) for kind in range(3)]
+    first, second, core = place_of(0)
+    source = jnp.where(core == 0, 0, 1)
+    line = jnp.where(first ^ 1 == source, moved[0], jnp.where(3 - first == source, moved[1], moved[2]))
+    line = jnp.where(first == source, piece, line)
+    return jnp.where(second == 1 - source, line, jnp.zeros_like(line))
 
 
 def spread_second(piece):
@@ -339,7 +349,6 @@
     )
     piece = panels[0, 0, 0]
     line = spread_first(piece)
-    line = jnp.where(lax.axis_index("row") == 1, piece, jnp.zeros_like(piece)) + line[0] + line[1] + line[2]
     plane = spread_second(line)
     arrived = lax.all_to_all(ordered.reshape(128, 8, 1280), AXES, split_axis=0, concat_axis=0, tiled=True)
     inverses, _ = lax.optimization_barrier((diag_inverse, ordered))
@@ -366,7 +375,8 @@
         first_kernel,
         (*around_cols(lead), inverses[0], follow, line, *plane),
         [((64, 1024), BF16), ((64, 128), BF16)],
-        [pltpu.VMEM((4, 64, 256), BF16)],
+        [pltpu.VMEM((4, 64, 256), BF16), pltpu.VMEM((4, 128, 1024), BF16), pltpu.SemaphoreType.DMA((4,))],
+        specs=[VMEM] * 6 + [HBM] * 4,
         limit=12,
         flops=1 << 28,
         moved=3 << 20,

time: 116 us -> 118 us (1.017); the launches traced: 114 us -> 118 us
  waiting for transfers between devices: 42.7 us -> 46.7 us
    ppermute x23, waiting for transfers between devices: 42.7 us -> 46.7 us  [send(): return lax.ppermute(value, AXES, pairs)]
  transfers between devices with their start and end apart: 24 -> 24, of which waited for: 9 -> 11; matrix products, arithmetic and copies ran while one was open for 2% -> 2% of each run, Pallas kernels for 8% -> 7%
where the time goes in v8:
time: 118 us
  starting transfers between devices  46.9 us (40%)
  waiting for transfers between devices  46.7 us (40%)
  Pallas kernels  19.8 us (17%)
  local copies, waits for them, and re-layouts  3.17 us (3%)
    ppermute x23, waiting for transfers between devices, send(): return lax.ppermute(value, AXES, pairs)  46.7 us
    ppermute x23, starting transfers between devices, send(): return lax.ppermute(value, AXES, pairs)  35.4 us
    pallas_call x10, Pallas kernels, launch(): pl.pallas_call(kernel, out_shape=[jax.ShapeDtypeStruct(s, d) for s, d in...  19.8 us
    all_to_all x1, starting transfers between devices, steps(): lax.all_to_all(ordered.reshape(128, 8, 1280), AXES, split_axis=0, concat_...  11.5 us
  transfers between devices with their start and end apart: 24, of which 11 were waited for; matrix products, arithmetic and copies ran while one was open for 2% of the time, Pallas kernels for 7%

profile of v8, /device:TPU:1, one launch (start us, length us, event | category | flops | bytes accessed | tf_op | source)
XLA Modules:
  0.0 118.1 jit_solution(17114586875119949597)
XLA Ops:
  0.0 6.3 %shard_map.46 = bf16[1024,1280]{1,0:T(8,128)(2,1)} custom-call(s32[1,1024]{1,0:T(1,128)} %bitcast.13, bf16[1024,1024]{1,0:T(8,128)(2,1)} %rows_hbm.1), custom_call_target="tpu_custom_call" | custom-call | flops 3221225472 | bytes 5242880 | tf_op jit(solution)/shard_map/pallas_call | solution.py:281
  6.3 11.5 %all-to-all-start = ((bf16[128,8,1280]{2,1,0:T(8,128)(2,1)}), bf16[128,8,1280]{2,1,0:T(8,128)(2,1)S(1)}, u32[]{:S(2)}, u32[]{:S(2)}) async-start(bf16[128,8,1280]{2,1,0:T(8,128)(2,1)} %bitcast.12), calls=%async_computation | async-start | bytes 5242880 | tf_op jit(solution)/shard_map/all_to_all | solution.py:353
  18.7 2.9 %collective-permute-start.5 = (bf16[128,1024]{1,0:T(8,128)(2,1)S(1)}, bf16[128,1024]{1,0:T(8,128)(2,1)S(1)}, u32[]{:S(2)}, u32[]{:S(2)}) collective-permute-start(bf16[128,1024]{1,0:T(8,128)(2,1)S(1)} %slice_bitcast_fusion), channel_id=1, source_target_pairs={{0,64},{1,17},{2,66},{3,19},{4,68},{5,21},{6,70},{7,23},{8,72},{9,... | collective-permute-start | bytes 786440 | tf_op jit(solution)/shard_map/ppermute | solution.py:28
  22.6 29.8 %collective-permute-done.5 = bf16[128,1024]{1,0:T(8,128)(2,1)S(1)} collective-permute-done((bf16[128,1024]{1,0:T(8,128)(2,1)S(1)}, bf16[128,1024]{1,0:T(8,128)(2,1)S(1)}, u32[]{:S(2)}, u32[]{:S(2)}) %collective-permute-start.5) | collective-permute-done | bytes 262176 | tf_op jit(solution)/shard_map/ppermute | solution.py:28
  52.4 2.3 %collective-permute-done.4 = bf16[128,1024]{1,0:T(8,128)(2,1)S(1)} collective-permute-done((bf16[128,1024]{1,0:T(8,128)(2,1)S(1)}, bf16[128,1024]{1,0:T(8,128)(2,1)S(1)}, u32[]{:S(2)}, u32[]{:S(2)}) %collective-permute-start.4) | collective-permute-done | bytes 262176 | tf_op jit(solution)/shard_map/ppermute | solution.py:28
  54.6 1.1 select_select_fusion.l0
  55.7 4.4 %collective-permute-start.8 = (bf16[128,1024]{1,0:T(8,128)(2,1)S(1)}, bf16[128,1024]{1,0:T(8,128)(2,1)S(1)}, u32[]{:S(2)}, u32[]{:S(2)}) collective-permute-start(bf16[128,1024]{1,0:T(8,128)(2,1)S(1)} %select_select_fusion.l0), channel_id=1, source_target_pairs={{1,65},{3,67},{5,69},{7,71},{8,24},{9,73},{10,26},{11,75},{12,28},... | collective-permute-start | bytes 786440 | tf_op jit(solution)/shard_map/ppermute | solution.py:28
  60.1 1.3 %collective-permute-start.7 = (bf16[128,1024]{1,0:T(8,128)(2,1)S(1)}, bf16[128,1024]{1,0:T(8,128)(2,1)S(1)}, u32[]{:S(2)}, u32[]{:S(2)}) collective-permute-start(bf16[128,1024]{1,0:T(8,128)(2,1)S(1)} %select_select_fusion.l0), channel_id=1, source_target_pairs={{1,97},{3,99},{5,101},{7,103},{8,16},{9,105},{10,18},{11,107},{12,... | collective-permute-start | bytes 786440 | tf_op jit(solution)/shard_map/ppermute | solution.py:28
  61.4 2.0 %collective-permute-start.6 = (bf16[128,1024]{1,0:T(8,128)(2,1)S(1)}, bf16[128,1024]{1,0:T(8,128)(2,1)}, u32[]{:S(2)}, u32[]{:S(2)}) collective-permute-start(bf16[128,1024]{1,0:T(8,128)(2,1)S(1)} %select_select_fusion.l0), channel_id=1, source_target_pairs={{1,33},{3,35},{5,37},{7,39},{8,0},{9,41},{10,2},{11,43},{12,4},{13... | collective-permute-start | bytes 786440 | tf_op jit(solution)/shard_map/ppermute | solution.py:28
  64.1 3.4 %collective-permute-start.2 = (bf16[64,256]{1,0:T(8,128)(2,1)S(1)}, bf16[64,256]{1,0:T(8,128)(2,1)S(1)}, u32[]{:S(2)}, u32[]{:S(2)}) collective-permute-start(bf16[64,256]{1,0:T(8,128)(2,1)S(1)} %get-tuple-element.13.p0), channel_id=1, source_target_pairs={{0,4},{1,5},{2,6},{3,7},{4,0},{5,1},{6,2},{7,3},{8,12},{9,13},{10,... | collective-permute-start | bytes 98312 | tf_op jit(solution)/shard_map/ppermute | solution.py:28
  68.1 2.2 %copy-done.1 = bf16[2,1024,1024]{2,1,0:T(8,128)(2,1)S(1)} copy-done((bf16[2,1024,1024]{2,1,0:T(8,128)(2,1)S(1)}, bf16[2,1024,1024]{2,1,0:T(8,128)(2,1)}, u32[]{:S(2)}) %copy-start.1) | copy-done | bytes 4194328
  71.5 1.3 %shard_map.49 = (bf16[64,1024]{1,0:T(8,128)(2,1)S(1)}, bf16[64,128]{1,0:T(8,128)(2,1)S(1)}) custom-call(bf16[64,256]{1,0:T(8,128)(2,1)S(1)} %get-tuple-element.13.p0, bf16[64,256]{1,0:T(8,128)(2,1)S(1)} %collective-permute-done.p1, bf16[64,256]{1,0:T(8,128)(2,1)S(1)} %collective-permute-done.1.p2, bf16[64,256]{1,0:T(8,128)(2,1)S(1)} %collective-permute-done.2.p3, ...), custom_call_target="tpu_custom_call" | custom-call | flops 268435456 | bytes 3145728 | tf_op jit(solution)/shard_map/pallas_call | solution.py:281
  72.9 1.2 collective-permute-done.9
  74.0 2.4 %collective-permute-start.12 = (bf16[128,128]{1,0:T(8,128)(2,1)S(1)}, bf16[128,128]{1,0:T(8,128)(2,1)S(1)}, u32[]{:S(2)}, u32[]{:S(2)}) collective-permute-start(bf16[128,128]{1,0:T(8,128)(2,1)S(1)} %constant_dynamic-update-slice_fusion.p0), channel_id=1, source_target_pairs={{0,4},{1,5},{2,6},{3,7},{4,0},{5,1},{6,2},{7,3},{8,12},{9,13},{10,... | collective-permute-start | bytes 98312 | tf_op jit(solution)/shard_map/ppermute | solution.py:28
  77.0 1.3 %collective-permute-done.12.p3 = bf16[128,128]{1,0:T(8,128)(2,1)S(1)} collective-permute-done((bf16[128,128]{1,0:T(8,128)(2,1)S(1)}, bf16[128,128]{1,0:T(8,128)(2,1)S(1)}, u32[]{:S(2)}, u32[]{:S(2)}) %collective-permute-start.12) | collective-permute-done | bytes 32800 | tf_op jit(solution)/shard_map/ppermute | solution.py:28
  78.3 2.1 %collective-permute-done.11.p2 = bf16[128,128]{1,0:T(8,128)(2,1)S(1)} collective-permute-done((bf16[128,128]{1,0:T(8,128)(2,1)S(1)}, bf16[128,128]{1,0:T(8,128)(2,1)S(1)}, u32[]{:S(2)}, u32[]{:S(2)}) %collective-permute-start.11) | collective-permute-done | bytes 32800 | tf_op jit(solution)/shard_map/ppermute | solution.py:28
  81.2 1.4 %collective-permute-start.15 = (bf16[32,2048]{1,0:T(8,128)(2,1)S(1)}, bf16[32,2048]{1,0:T(8,128)(2,1)S(1)}, u32[]{:S(2)}, u32[]{:S(2)}) collective-permute-start(bf16[32,2048]{1,0:T(8,128)(2,1)S(1)} %shard_map.50), channel_id=1, source_target_pairs={{0,64},{1,17},{2,66},{3,19},{4,68},{5,21},{6,70},{7,23},{8,72},{9,... | collective-permute-start | bytes 393224 | tf_op jit(solution)/shard_map/ppermute | solution.py:28
  82.6 2.6 %collective-permute-start.14 = (bf16[32,2048]{1,0:T(8,128)(2,1)S(1)}, bf16[32,2048]{1,0:T(8,128)(2,1)S(1)}, u32[]{:S(2)}, u32[]{:S(2)}) collective-permute-start(bf16[32,2048]{1,0:T(8,128)(2,1)S(1)} %shard_map.50), channel_id=1, source_target_pairs={{0,96},{1,25},{2,98},{3,27},{4,100},{5,29},{6,102},{7,31},{8,104},... | collective-permute-start | bytes 393224 | tf_op jit(solution)/shard_map/ppermute | solution.py:28
  85.2 1.4 %collective-permute-done.15 = bf16[32,2048]{1,0:T(8,128)(2,1)S(1)} collective-permute-done((bf16[32,2048]{1,0:T(8,128)(2,1)S(1)}, bf16[32,2048]{1,0:T(8,128)(2,1)S(1)}, u32[]{:S(2)}, u32[]{:S(2)}) %collective-permute-start.15) | collective-permute-done | bytes 131104 | tf_op jit(solution)/shard_map/ppermute | solution.py:28
  86.6 1.7 %collective-permute-done.14 = bf16[32,2048]{1,0:T(8,128)(2,1)S(1)} collective-permute-done((bf16[32,2048]{1,0:T(8,128)(2,1)S(1)}, bf16[32,2048]{1,0:T(8,128)(2,1)S(1)}, u32[]{:S(2)}, u32[]{:S(2)}) %collective-permute-start.14) | collective-permute-done | bytes 131104 | tf_op jit(solution)/shard_map/ppermute | solution.py:28
  89.4 1.4 %collective-permute-start.21 = (bf16[128,2048]{1,0:T(8,128)(2,1)S(1)}, bf16[128,2048]{1,0:T(8,128)(2,1)S(1)}, u32[]{:S(2)}, u32[]{:S(2)}) collective-permute-start(bf16[128,2048]{1,0:T(8,128)(2,1)S(1)} %pad_maximum_fusion.a_ref), channel_id=1, source_target_pairs={{0,16},{1,65},{2,18},{3,67},{4,20},{5,69},{6,22},{7,71},{8,24},{9,... | collective-permute-start | bytes 1572872 | tf_op jit(solution)/shard_map/ppermute | solution.py:28
  90.8 2.0 %collective-permute-start.16 = (bf16[128,2048]{1,0:T(8,128)(2,1)S(1)}, bf16[128,2048]{1,0:T(8,128)(2,1)S(1)}, u32[]{:S(2)}, u32[]{:S(2)}) collective-permute-start(bf16[128,2048]{1,0:T(8,128)(2,1)S(1)} %pad_maximum_fusion.a_ref), channel_id=1, source_target_pairs={{0,24},{1,97},{2,26},{3,99},{4,28},{5,101},{6,30},{7,103},{8,16},{... | collective-permute-start | bytes 1572872 | tf_op jit(solution)/shard_map/ppermute | solution.py:28
  92.7 3.2 %collective-permute-start.18 = (bf16[128,2048]{1,0:T(8,128)(2,1)S(1)}, bf16[128,2048]{1,0:T(8,128)(2,1)S(1)}, u32[]{:S(2)}, u32[]{:S(2)}) collective-permute-start(bf16[128,2048]{1,0:T(8,128)(2,1)S(1)} %pad_maximum_fusion.a_ref), channel_id=1, source_target_pairs={{0,1},{1,0},{2,3},{3,2},{4,5},{5,4},{6,7},{7,6},{8,9},{9,8},{10,11... | collective-permute-start | bytes 1572872 | tf_op jit(solution)/shard_map/ppermute | solution.py:28
  95.9 3.5 %collective-permute-done.21.a_ref = bf16[128,2048]{1,0:T(8,128)(2,1)S(1)} collective-permute-done((bf16[128,2048]{1,0:T(8,128)(2,1)S(1)}, bf16[128,2048]{1,0:T(8,128)(2,1)S(1)}, u32[]{:S(2)}, u32[]{:S(2)}) %collective-permute-start.21) | collective-permute-done | bytes 524320 | tf_op jit(solution)/shard_map/ppermute | solution.py:28
  99.4 2.3 %collective-permute-start.22 = (bf16[128,2048]{1,0:T(8,128)(2,1)S(1)}, bf16[128,2048]{1,0:T(8,128)(2,1)S(1)}, u32[]{:S(2)}, u32[]{:S(2)}) collective-permute-start(bf16[128,2048]{1,0:T(8,128)(2,1)S(1)} %collective-permute-done.21.a_ref), channel_id=1, source_target_pairs={{0,1},{1,0},{2,3},{3,2},{4,5},{5,4},{6,7},{7,6},{8,9},{9,8},{10,11... | collective-permute-start | bytes 1572872 | tf_op jit(solution)/shard_map/ppermute | solution.py:28
  101.7 1.6 %collective-permute-done.19.a_ref = bf16[128,2048]{1,0:T(8,128)(2,1)S(1)} collective-permute-done((bf16[128,2048]{1,0:T(8,128)(2,1)S(1)}, bf16[128,2048]{1,0:T(8,128)(2,1)S(1)}, u32[]{:S(2)}, u32[]{:S(2)}) %collective-permute-start.19) | collective-permute-done | bytes 524320 | tf_op jit(solution)/shard_map/ppermute | solution.py:28
  103.2 3.1 %collective-permute-start.20 = (bf16[128,2048]{1,0:T(8,128)(2,1)S(1)}, bf16[128,2048]{1,0:T(8,128)(2,1)S(1)}, u32[]{:S(2)}, u32[]{:S(2)}) collective-permute-start(bf16[128,2048]{1,0:T(8,128)(2,1)S(1)} %collective-permute-done.19.a_ref), channel_id=1, source_target_pairs={{0,1},{1,0},{2,3},{3,2},{4,5},{5,4},{6,7},{7,6},{8,9},{9,8},{10,11... | collective-permute-start | bytes 1572872 | tf_op jit(solution)/shard_map/ppermute | solution.py:28
  107.2 3.2 %shard_map.51.rows_ref.refs_4_ = bf16[1024,1024]{1,0:T(8,128)(2,1)S(1)} custom-call(s32[8,1024]{1,0:T(8,128)S(1)} %get-tuple-element.20.own_ref, bf16[1024,1280]{1,0:T(8,128)(2,1)S(1)} %bitcast.11), custom_call_target="tpu_custom_call" | custom-call | flops 2147483648 | bytes 4194304 | tf_op jit(solution)/shard_map/pallas_call | solution.py:281
  110.4 1.6 %shard_map.52.refs_0_ = bf16[1024,256]{1,0:T(8,128)(2,1)S(1)} custom-call(bf16[128,2048]{1,0:T(8,128)(2,1)S(1)} %pad_maximum_fusion.a_ref, bf16[128,2048]{1,0:T(8,128)(2,1)S(1)} %collective-permute-done.18.b_ref, bf16[2,8,1,128,1024]{4,3,2,1,0:T(8,128)(2,1)S(1)} %copy-done, bf16[1024,1024]{1,0:T(8,128)(2,1)S(1)} %shard_map.51.rows_ref.refs_4_), custom_call_target="tpu_custom_call" | custom-call | flops 1073741824 | bytes 2097152 | tf_op jit(solution)/shard_map/pallas_call | solution.py:281
  112.0 1.6 %shard_map.54.refs_2_ = bf16[1024,256]{1,0:T(8,128)(2,1)S(1)} custom-call(bf16[128,2048]{1,0:T(8,128)(2,1)S(1)} %collective-permute-done.21.a_ref, bf16[128,2048]{1,0:T(8,128)(2,1)S(1)} %collective-permute-done.22.b_ref, bf16[2,8,1,128,1024]{4,3,2,1,0:T(8,128)(2,1)S(1)} %copy-done, bf16[1024,1024]{1,0:T(8,128)(2,1)S(1)} %shard_map.51.rows_ref.refs_4_), custom_call_target="tpu_custom_call" | custom-call | flops 1073741824 | bytes 2097152 | tf_op jit(solution)/shard_map/pallas_call | solution.py:281
  113.5 1.6 %shard_map.53.refs_1_ = bf16[1024,256]{1,0:T(8,128)(2,1)S(1)} custom-call(bf16[128,2048]{1,0:T(8,128)(2,1)S(1)} %collective-permute-done.19.a_ref, bf16[128,2048]{1,0:T(8,128)(2,1)S(1)} %collective-permute-done.20.b_ref, bf16[2,8,1,128,1024]{4,3,2,1,0:T(8,128)(2,1)S(1)} %copy-done, bf16[1024,1024]{1,0:T(8,128)(2,1)S(1)} %shard_map.51.rows_ref.refs_4_), custom_call_target="tpu_custom_call" | custom-call | flops 1073741824 | bytes 2097152 | tf_op jit(solution)/shard_map/pallas_call | solution.py:281
  115.1 2.8 %shard_map.55 = bf16[1024,1024]{1,0:T(8,128)(2,1)} custom-call(bf16[128,2048]{1,0:T(8,128)(2,1)S(1)} %collective-permute-done.16.a_ref, bf16[128,2048]{1,0:T(8,128)(2,1)S(1)} %collective-permute-done.17.b_ref, bf16[1024,256]{1,0:T(8,128)(2,1)S(1)} %shard_map.52.refs_0_, bf16[1024,256]{1,0:T(8,128)(2,1)S(1)} %shard_map.53.refs_1_, ...), custom_call_target="tpu_custom_call" | custom-call | flops 1073741824 | bytes 2097152 | tf_op jit(solution)/shard_map/pallas_call | solution.py:281
  (35 shorter events, 7.5 us)
Async XLA Ops:
  6.3 57.2 %all-to-all-start = ((bf16[128,8,1280]{2,1,0:T(8,128)(2,1)}), bf16[128,8,1280]{2,1,0:T(8,128)(2,1)S(1)}, u32[]{:S(2)}, u32[]{:S(2)}) async-start(bf16[128,8,1280]{2,1,0:T(8,128)(2,1)} %bitcast.12), calls=%async_computation | async-start | bytes 5242880 | tf_op jit(solution)/shard_map/all_to_all | solution.py:353
  18.7 33.6 %collective-permute-start.5 = (bf16[128,1024]{1,0:T(8,128)(2,1)S(1)}, bf16[128,1024]{1,0:T(8,128)(2,1)S(1)}, u32[]{:S(2)}, u32[]{:S(2)}) collective-permute-start(bf16[128,1024]{1,0:T(8,128)(2,1)S(1)} %slice_bitcast_fusion), channel_id=1, source_target_pairs={{0,64},{1,17},{2,66},{3,19},{4,68},{5,21},{6,70},{7,23},{8,72},{9,... | collective-permute-start | bytes 786440 | tf_op jit(solution)/shard_map/ppermute | solution.py:28
  21.7 33.0 %collective-permute-start.4 = (bf16[128,1024]{1,0:T(8,128)(2,1)S(1)}, bf16[128,1024]{1,0:T(8,128)(2,1)S(1)}, u32[]{:S(2)}, u32[]{:S(2)}) collective-permute-start(bf16[128,1024]{1,0:T(8,128)(2,1)S(1)} %slice_bitcast_fusion), channel_id=1, source_target_pairs={{0,96},{1,25},{2,98},{3,27},{4,100},{5,29},{6,102},{7,31},{8,104},... | collective-permute-start | bytes 786440 | tf_op jit(solution)/shard_map/ppermute | solution.py:28
  22.6 32.1 %collective-permute-start.3 = (bf16[128,1024]{1,0:T(8,128)(2,1)S(1)}, bf16[128,1024]{1,0:T(8,128)(2,1)}, u32[]{:S(2)}, u32[]{:S(2)}) collective-permute-start(bf16[128,1024]{1,0:T(8,128)(2,1)S(1)} %slice_bitcast_fusion), channel_id=1, source_target_pairs={{0,32},{1,9},{2,34},{3,11},{4,36},{5,13},{6,38},{7,15},{8,40},{9,1... | collective-permute-start | bytes 786440 | tf_op jit(solution)/shard_map/ppermute | solution.py:28
  55.7 12.3 %collective-permute-start.8 = (bf16[128,1024]{1,0:T(8,128)(2,1)S(1)}, bf16[128,1024]{1,0:T(8,128)(2,1)S(1)}, u32[]{:S(2)}, u32[]{:S(2)}) collective-permute-start(bf16[128,1024]{1,0:T(8,128)(2,1)S(1)} %select_select_fusion.l0), channel_id=1, source_target_pairs={{1,65},{3,67},{5,69},{7,71},{8,24},{9,73},{10,26},{11,75},{12,28},... | collective-permute-start | bytes 786440 | tf_op jit(solution)/shard_map/ppermute | solution.py:28
  60.1 10.5 %collective-permute-start.7 = (bf16[128,1024]{1,0:T(8,128)(2,1)S(1)}, bf16[128,1024]{1,0:T(8,128)(2,1)S(1)}, u32[]{:S(2)}, u32[]{:S(2)}) collective-permute-start(bf16[128,1024]{1,0:T(8,128)(2,1)S(1)} %select_select_fusion.l0), channel_id=1, source_target_pairs={{1,97},{3,99},{5,101},{7,103},{8,16},{9,105},{10,18},{11,107},{12,... | collective-permute-start | bytes 786440 | tf_op jit(solution)/shard_map/ppermute | solution.py:28
  61.4 9.2 %collective-permute-start.6 = (bf16[128,1024]{1,0:T(8,128)(2,1)S(1)}, bf16[128,1024]{1,0:T(8,128)(2,1)}, u32[]{:S(2)}, u32[]{:S(2)}) collective-permute-start(bf16[128,1024]{1,0:T(8,128)(2,1)S(1)} %select_select_fusion.l0), channel_id=1, source_target_pairs={{1,33},{3,35},{5,37},{7,39},{8,0},{9,41},{10,2},{11,43},{12,4},{13... | collective-permute-start | bytes 786440 | tf_op jit(solution)/shard_map/ppermute | solution.py:28
  64.1 6.6 %collective-permute-start.2 = (bf16[64,256]{1,0:T(8,128)(2,1)S(1)}, bf16[64,256]{1,0:T(8,128)(2,1)S(1)}, u32[]{:S(2)}, u32[]{:S(2)}) collective-permute-start(bf16[64,256]{1,0:T(8,128)(2,1)S(1)} %get-tuple-element.13.p0), channel_id=1, source_target_pairs={{0,4},{1,5},{2,6},{3,7},{4,0},{5,1},{6,2},{7,3},{8,12},{9,13},{10,... | collective-permute-start | bytes 98312 | tf_op jit(solution)/shard_map/ppermute | solution.py:28
  67.5 4.0 %collective-permute-start.1 = (bf16[64,256]{1,0:T(8,128)(2,1)S(1)}, bf16[64,256]{1,0:T(8,128)(2,1)S(1)}, u32[]{:S(2)}, u32[]{:S(2)}) collective-permute-start(bf16[64,256]{1,0:T(8,128)(2,1)S(1)} %get-tuple-element.13.p0), channel_id=1, source_target_pairs={{0,6},{1,7},{2,4},{3,5},{4,2},{5,3},{6,0},{7,1},{8,14},{9,15},{10,... | collective-permute-start | bytes 98312 | tf_op jit(solution)/shard_map/ppermute | solution.py:28
  68.0 3.5 %collective-permute-start = (bf16[64,256]{1,0:T(8,128)(2,1)S(1)}, bf16[64,256]{1,0:T(8,128)(2,1)S(1)}, u32[]{:S(2)}, u32[]{:S(2)}) collective-permute-start(bf16[64,256]{1,0:T(8,128)(2,1)S(1)} %get-tuple-element.13.p0), channel_id=1, source_target_pairs={{0,2},{1,3},{2,0},{3,1},{4,6},{5,7},{6,4},{7,5},{8,10},{9,11},{10,... | collective-permute-start | bytes 98312 | tf_op jit(solution)/shard_map/ppermute | solution.py:28
  68.1 2.2 %copy-start.1 = (bf16[2,1024,1024]{2,1,0:T(8,128)(2,1)S(1)}, bf16[2,1024,1024]{2,1,0:T(8,128)(2,1)}, u32[]{:S(2)}) copy-start(bf16[2,1024,1024]{2,1,0:T(8,128)(2,1)} %source_hbm) | copy-start | bytes 12582916
  72.8 1.3 %collective-permute-start.9 = (bf16[64,128]{1,0:T(8,128)(2,1)S(1)}, bf16[64,128]{1,0:T(8,128)(2,1)S(1)}, u32[]{:S(2)}, u32[]{:S(2)}) collective-permute-start(bf16[64,128]{1,0:T(8,128)(2,1)S(1)} %get-tuple-element.17), channel_id=1, source_target_pairs={{0,1},{1,0},{2,3},{3,2},{4,5},{5,4},{6,7},{7,6},{8,9},{9,8},{10,11... | collective-permute-start | bytes 49160 | tf_op jit(solution)/shard_map/ppermute | solution.py:28
  74.0 4.3 %collective-permute-start.12 = (bf16[128,128]{1,0:T(8,128)(2,1)S(1)}, bf16[128,128]{1,0:T(8,128)(2,1)S(1)}, u32[]{:S(2)}, u32[]{:S(2)}) collective-permute-start(bf16[128,128]{1,0:T(8,128)(2,1)S(1)} %constant_dynamic-update-slice_fusion.p0), channel_id=1, source_target_pairs={{0,4},{1,5},{2,6},{3,7},{4,0},{5,1},{6,2},{7,3},{8,12},{9,13},{10,... | collective-permute-start | bytes 98312 | tf_op jit(solution)/shard_map/ppermute | solution.py:28
  76.5 4.0 %collective-permute-start.11 = (bf16[128,128]{1,0:T(8,128)(2,1)S(1)}, bf16[128,128]{1,0:T(8,128)(2,1)S(1)}, u32[]{:S(2)}, u32[]{:S(2)}) collective-permute-start(bf16[128,128]{1,0:T(8,128)(2,1)S(1)} %constant_dynamic-update-slice_fusion.p0), channel_id=1, source_target_pairs={{0,6},{1,7},{2,4},{3,5},{4,2},{5,3},{6,0},{7,1},{8,14},{9,15},{10,... | collective-permute-start | bytes 98312 | tf_op jit(solution)/shard_map/ppermute | solution.py:28
  77.0 3.5 %collective-permute-start.10 = (bf16[128,128]{1,0:T(8,128)(2,1)S(1)}, bf16[128,128]{1,0:T(8,128)(2,1)S(1)}, u32[]{:S(2)}, u32[]{:S(2)}) collective-permute-start(bf16[128,128]{1,0:T(8,128)(2,1)S(1)} %constant_dynamic-update-slice_fusion.p0), channel_id=1, source_target_pairs={{0,2},{1,3},{2,0},{3,1},{4,6},{5,7},{6,4},{7,5},{8,10},{9,11},{10,... | collective-permute-start | bytes 98312 | tf_op jit(solution)/shard_map/ppermute | solution.py:28
  81.2 5.4 %collective-permute-start.15 = (bf16[32,2048]{1,0:T(8,128)(2,1)S(1)}, bf16[32,2048]{1,0:T(8,128)(2,1)S(1)}, u32[]{:S(2)}, u32[]{:S(2)}) collective-permute-start(bf16[32,2048]{1,0:T(8,128)(2,1)S(1)} %shard_map.50), channel_id=1, source_target_pairs={{0,64},{1,17},{2,66},{3,19},{4,68},{5,21},{6,70},{7,23},{8,72},{9,... | collective-permute-start | bytes 393224 | tf_op jit(solution)/shard_map/ppermute | solution.py:28
  82.6 5.7 %collective-permute-start.14 = (bf16[32,2048]{1,0:T(8,128)(2,1)S(1)}, bf16[32,2048]{1,0:T(8,128)(2,1)S(1)}, u32[]{:S(2)}, u32[]{:S(2)}) collective-permute-start(bf16[32,2048]{1,0:T(8,128)(2,1)S(1)} %shard_map.50), channel_id=1, source_target_pairs={{0,96},{1,25},{2,98},{3,27},{4,100},{5,29},{6,102},{7,31},{8,104},... | collective-permute-start | bytes 393224 | tf_op jit(solution)/shard_map/ppermute | solution.py:28
  85.2 4.1 %collective-permute-start.13 = (bf16[32,2048]{1,0:T(8,128)(2,1)S(1)}, bf16[32,2048]{1,0:T(8,128)(2,1)S(1)}, u32[]{:S(2)}, u32[]{:S(2)}) collective-permute-start(bf16[32,2048]{1,0:T(8,128)(2,1)S(1)} %shard_map.50), channel_id=1, source_target_pairs={{0,32},{1,9},{2,34},{3,11},{4,36},{5,13},{6,38},{7,15},{8,40},{9,1... | collective-permute-start | bytes 393224 | tf_op jit(solution)/shard_map/ppermute | solution.py:28
  89.4 10.0 %collective-permute-start.21 = (bf16[128,2048]{1,0:T(8,128)(2,1)S(1)}, bf16[128,2048]{1,0:T(8,128)(2,1)S(1)}, u32[]{:S(2)}, u32[]{:S(2)}) collective-permute-start(bf16[128,2048]{1,0:T(8,128)(2,1)S(1)} %pad_maximum_fusion.a_ref), channel_id=1, source_target_pairs={{0,16},{1,65},{2,18},{3,67},{4,20},{5,69},{6,22},{7,71},{8,24},{9,... | collective-permute-start | bytes 1572872 | tf_op jit(solution)/shard_map/ppermute | solution.py:28
  90.8 12.5 %collective-permute-start.19 = (bf16[128,2048]{1,0:T(8,128)(2,1)S(1)}, bf16[128,2048]{1,0:T(8,128)(2,1)S(1)}, u32[]{:S(2)}, u32[]{:S(2)}) collective-permute-start(bf16[128,2048]{1,0:T(8,128)(2,1)S(1)} %pad_maximum_fusion.a_ref), channel_id=1, source_target_pairs={{0,8},{1,33},{2,10},{3,35},{4,12},{5,37},{6,14},{7,39},{8,0},{9,41... | collective-permute-start | bytes 1572872 | tf_op jit(solution)/shard_map/ppermute | solution.py:28
  90.8 15.6 %collective-permute-start.16 = (bf16[128,2048]{1,0:T(8,128)(2,1)S(1)}, bf16[128,2048]{1,0:T(8,128)(2,1)S(1)}, u32[]{:S(2)}, u32[]{:S(2)}) collective-permute-start(bf16[128,2048]{1,0:T(8,128)(2,1)S(1)} %pad_maximum_fusion.a_ref), channel_id=1, source_target_pairs={{0,24},{1,97},{2,26},{3,99},{4,28},{5,101},{6,30},{7,103},{8,16},{... | collective-permute-start | bytes 1572872 | tf_op jit(solution)/shard_map/ppermute | solution.py:28
  92.7 17.6 %collective-permute-start.18 = (bf16[128,2048]{1,0:T(8,128)(2,1)S(1)}, bf16[128,2048]{1,0:T(8,128)(2,1)S(1)}, u32[]{:S(2)}, u32[]{:S(2)}) collective-permute-start(bf16[128,2048]{1,0:T(8,128)(2,1)S(1)} %pad_maximum_fusion.a_ref), channel_id=1, source_target_pairs={{0,1},{1,0},{2,3},{3,2},{4,5},{5,4},{6,7},{7,6},{8,9},{9,8},{10,11... | collective-permute-start | bytes 1572872 | tf_op jit(solution)/shard_map/ppermute | solution.py:28
  99.4 12.6 %collective-permute-start.22 = (bf16[128,2048]{1,0:T(8,128)(2,1)S(1)}, bf16[128,2048]{1,0:T(8,128)(2,1)S(1)}, u32[]{:S(2)}, u32[]{:S(2)}) collective-permute-start(bf16[128,2048]{1,0:T(8,128)(2,1)S(1)} %collective-permute-done.21.a_ref), channel_id=1, source_target_pairs={{0,1},{1,0},{2,3},{3,2},{4,5},{5,4},{6,7},{7,6},{8,9},{9,8},{10,11... | collective-permute-start | bytes 1572872 | tf_op jit(solution)/shard_map/ppermute | solution.py:28
  103.2 10.3 %collective-permute-start.20 = (bf16[128,2048]{1,0:T(8,128)(2,1)S(1)}, bf16[128,2048]{1,0:T(8,128)(2,1)S(1)}, u32[]{:S(2)}, u32[]{:S(2)}) collective-permute-start(bf16[128,2048]{1,0:T(8,128)(2,1)S(1)} %collective-permute-done.19.a_ref), channel_id=1, source_target_pairs={{0,1},{1,0},{2,3},{3,2},{4,5},{5,4},{6,7},{7,6},{8,9},{9,8},{10,11... | collective-permute-start | bytes 1572872 | tf_op jit(solution)/shard_map/ppermute | solution.py:28
  106.4 8.7 %collective-permute-start.17 = (bf16[128,2048]{1,0:T(8,128)(2,1)S(1)}, bf16[128,2048]{1,0:T(8,128)(2,1)S(1)}, u32[]{:S(2)}, u32[]{:S(2)}) collective-permute-start(bf16[128,2048]{1,0:T(8,128)(2,1)S(1)} %collective-permute-done.16.a_ref), channel_id=1, source_target_pairs={{0,1},{1,0},{2,3},{3,2},{4,5},{5,4},{6,7},{7,6},{8,9},{9,8},{10,11... | collective-permute-start | bytes 1572872 | tf_op jit(solution)/shard_map/ppermute | solution.py:28
  107.2 3.2 %copy-start = (bf16[2,8,1,128,1024]{4,3,2,1,0:T(8,128)(2,1)S(1)}, bf16[2,8,1,128,1024]{4,3,2,1,0:T(8,128)(2,1)}, u32[]{:S(2)}) copy-start(bf16[2,8,1,128,1024]{4,3,2,1,0:T(8,128)(2,1)} %refs_3_.1) | copy-start | bytes 12582916

commit v9 on v8

--- a/solution.py
+++ b/solution.py
@@ -56,10 +56,12 @@
     return lax.dot_general(a, b, ((contract[:1], contract[1:]), ((), ())), preferred_element_type=F32)
 
 
-def order_kernel(points_ref, rows_hbm, out_hbm, rows_ref, out_ref, perm_ref, head_ref, in_sems, out_sems):
+def order_kernel(points_ref, rows_hbm, panels_hbm, out_hbm, piece_hbm, rows_ref, out_ref, perm_ref, head_ref, piece_ref, in_sems, out_sems):
     count = rows_ref.shape[0]
     load = pltpu.make_async_copy(rows_hbm, rows_ref, in_sems.at[0])
     load.start()
+    piece = pltpu.make_async_copy(panels_hbm.at[0, 0, 0], piece_ref, in_sems.at[1])
+    piece.start()
     points = points_ref[...]
     block = points >> 10
     offset = points & 1023
@@ -84,6 +86,9 @@
     shared = [both(ids, 0, 0), both(ids, 0, 1), ids[64:128]]
     stores = []
     load.wait()
+    piece.wait()
+    keep_piece = pltpu.make_async_copy(piece_ref, piece_hbm, out_sems.at[4])
+    keep_piece.start()
     for x in range(4):
         chunk = slice(x * 256, x * 256 + 256)
         part_rows = dot(perm_ref[chunk, :], rows_ref[...], (1, 0))
@@ -109,6 +114,7 @@
         span = pl.ds(x * 256, 256)
         stores.append(pltpu.make_async_copy(out_ref.at[span], out_hbm.at[span], out_sems.at[x]))
         stores[x].start()
+    keep_piece.wait()
     for store in stores:
         store.wait()
 
@@ -329,25 +335,25 @@
 
 
 def steps(b_ingest, source_point, panels, diag_inverse):
-    (ordered,) = launch(
+    ordered, piece = launch(
         order_kernel,
-        (source_point.reshape(1, 1024), b_ingest),
-        [((1024, 1280), BF16)],
+        (source_point.reshape(1, 1024), b_ingest, panels),
+        [((1024, 1280), BF16), ((128, 1024), BF16)],
         [
             pltpu.VMEM((1024, 1024), BF16),
             pltpu.VMEM((1024, 1280), BF16),
             pltpu.VMEM((1024, 1024), BF16),
             pltpu.VMEM((128, 1024), F32),
-            pltpu.SemaphoreType.DMA((1,)),
-            pltpu.SemaphoreType.DMA((4,)),
+            pltpu.VMEM((128, 1024), BF16),
+            pltpu.SemaphoreType.DMA((2,)),
+            pltpu.SemaphoreType.DMA((5,)),
         ],
-        specs=[VMEM, HBM],
-        out_specs=[HBM],
+        specs=[VMEM, HBM, HBM],
+        out_specs=[HBM, HBM],
         limit=61.4,
         flops=3 << 30,
         moved=5 << 20,
     )
-    piece = panels[0, 0, 0]
     line = spread_first(piece)
     plane = spread_second(line)
     arrived = lax.all_to_all(ordered.reshape(128, 8, 1280), AXES, split_axis=0, concat_axis=0, tiled=True)

time: 118 us -> 119 us (level)
  starting transfers between devices: 46.9 us -> 48.4 us
    ppermute x23, starting transfers between devices: 35.4 us -> 36.9 us  [send(): return lax.ppermute(value, AXES, pairs)]
    unnamed x5 -> x9, local copies, waits for them, and re-layouts: 2.19 us -> 2.9 us
  transfers between devices with their start and end apart: 24 -> 24, of which waited for: 11 -> 11; matrix products, arithmetic and copies ran while one was open for 2% -> 1% of each run, Pallas kernels for 7% -> 7%
where the time goes in v9:
time: 119 us
  starting transfers between devices  48.4 us (41%)
  waiting for transfers between devices  46.1 us (39%)
  Pallas kernels  19.9 us (17%)
  local copies, waits for them, and re-layouts  2.91 us (2%)
    ppermute x23, waiting for transfers between devices, send(): return lax.ppermute(value, AXES, pairs)  46.1 us
    ppermute x23, starting transfers between devices, send(): return lax.ppermute(value, AXES, pairs)  36.9 us
    pallas_call x10, Pallas kernels, launch(): pl.pallas_call(kernel, out_shape=[jax.ShapeDtypeStruct(s, d) for s, d in...  19.9 us
    all_to_all x1, starting transfers between devices, steps(): lax.all_to_all(ordered.reshape(128, 8, 1280), AXES, split_axis=0, concat_...  11.5 us
    unnamed x9, local copies, waits for them, and re-layouts  2.9 us
  transfers between devices with their start and end apart: 24, of which 11 were waited for; matrix products, arithmetic and copies ran while one was open for 1% of the time, Pallas kernels for 7%

profile of v9, /device:TPU:1, one launch (start us, length us, event | category | flops | bytes accessed | tf_op | source)
XLA Modules:
  0.0 118.7 jit_solution(3180879996477831604)
XLA Ops:
  0.0 6.3 %shard_map.46 = (bf16[1024,1280]{1,0:T(8,128)(2,1)}, bf16[128,1024]{1,0:T(8,128)(2,1)}) custom-call(s32[1,1024]{1,0:T(1,128)} %bitcast.9, bf16[1024,1024]{1,0:T(8,128)(2,1)} %rows_hbm.1, bf16[2,8,1,128,1024]{4,3,2,1,0:T(8,128)(2,1)} %refs_3_.1), custom_call_target="tpu_custom_call" | custom-call | flops 3221225472 | bytes 5242880 | tf_op jit(solution)/shard_map/pallas_call | solution.py:287
  6.3 11.5 %all-to-all-start = ((bf16[128,8,1280]{2,1,0:T(8,128)(2,1)}), bf16[128,8,1280]{2,1,0:T(8,128)(2,1)S(1)}, u32[]{:S(2)}, u32[]{:S(2)}) async-start(bf16[128,8,1280]{2,1,0:T(8,128)(2,1)} %bitcast.8), calls=%async_computation | async-start | bytes 5242880 | tf_op jit(solution)/shard_map/all_to_all | solution.py:359
  17.8 2.9 %collective-permute-start.5 = (bf16[128,1024]{1,0:T(8,128)(2,1)S(1)}, bf16[128,1024]{1,0:T(8,128)(2,1)S(1)}, u32[]{:S(2)}, u32[]{:S(2)}) collective-permute-start(bf16[128,1024]{1,0:T(8,128)(2,1)S(1)} %copy-done.2), channel_id=1, source_target_pairs={{0,64},{1,17},{2,66},{3,19},{4,68},{5,21},{6,70},{7,23},{8,72},{9,... | collective-permute-start | bytes 786440 | tf_op jit(solution)/shard_map/ppermute | solution.py:28
  20.8 0.9 collective-permute-start.4
  21.7 30.8 %collective-permute-done.5 = bf16[128,1024]{1,0:T(8,128)(2,1)S(1)} collective-permute-done((bf16[128,1024]{1,0:T(8,128)(2,1)S(1)}, bf16[128,1024]{1,0:T(8,128)(2,1)S(1)}, u32[]{:S(2)}, u32[]{:S(2)}) %collective-permute-start.5) | collective-permute-done | bytes 262176 | tf_op jit(solution)/shard_map/ppermute | solution.py:28
  52.4 2.3 %collective-permute-done.4 = bf16[128,1024]{1,0:T(8,128)(2,1)S(1)} collective-permute-done((bf16[128,1024]{1,0:T(8,128)(2,1)S(1)}, bf16[128,1024]{1,0:T(8,128)(2,1)S(1)}, u32[]{:S(2)}, u32[]{:S(2)}) %collective-permute-start.4) | collective-permute-done | bytes 262176 | tf_op jit(solution)/shard_map/ppermute | solution.py:28
  55.4 1.0 select_select_fusion.l0
  56.4 4.4 %collective-permute-start.8 = (bf16[128,1024]{1,0:T(8,128)(2,1)S(1)}, bf16[128,1024]{1,0:T(8,128)(2,1)S(1)}, u32[]{:S(2)}, u32[]{:S(2)}) collective-permute-start(bf16[128,1024]{1,0:T(8,128)(2,1)S(1)} %select_select_fusion.l0), channel_id=1, source_target_pairs={{1,65},{3,67},{5,69},{7,71},{8,24},{9,73},{10,26},{11,75},{12,28},... | collective-permute-start | bytes 786440 | tf_op jit(solution)/shard_map/ppermute | solution.py:28
  60.8 1.3 %collective-permute-start.7 = (bf16[128,1024]{1,0:T(8,128)(2,1)S(1)}, bf16[128,1024]{1,0:T(8,128)(2,1)S(1)}, u32[]{:S(2)}, u32[]{:S(2)}) collective-permute-start(bf16[128,1024]{1,0:T(8,128)(2,1)S(1)} %select_select_fusion.l0), channel_id=1, source_target_pairs={{1,97},{3,99},{5,101},{7,103},{8,16},{9,105},{10,18},{11,107},{12,... | collective-permute-start | bytes 786440 | tf_op jit(solution)/shard_map/ppermute | solution.py:28
  62.1 2.0 %collective-permute-start.6 = (bf16[128,1024]{1,0:T(8,128)(2,1)S(1)}, bf16[128,1024]{1,0:T(8,128)(2,1)}, u32[]{:S(2)}, u32[]{:S(2)}) collective-permute-start(bf16[128,1024]{1,0:T(8,128)(2,1)S(1)} %select_select_fusion.l0), channel_id=1, source_target_pairs={{1,33},{3,35},{5,37},{7,39},{8,0},{9,41},{10,2},{11,43},{12,4},{13... | collective-permute-start | bytes 786440 | tf_op jit(solution)/shard_map/ppermute | solution.py:28
  64.7 3.4 %collective-permute-start.2 = (bf16[64,256]{1,0:T(8,128)(2,1)S(1)}, bf16[64,256]{1,0:T(8,128)(2,1)S(1)}, u32[]{:S(2)}, u32[]{:S(2)}) collective-permute-start(bf16[64,256]{1,0:T(8,128)(2,1)S(1)} %get-tuple-element.16.p0), channel_id=1, source_target_pairs={{0,4},{1,5},{2,6},{3,7},{4,0},{5,1},{6,2},{7,3},{8,12},{9,13},{10,... | collective-permute-start | bytes 98312 | tf_op jit(solution)/shard_map/ppermute | solution.py:28
  68.8 2.2 %copy-done.1 = bf16[2,1024,1024]{2,1,0:T(8,128)(2,1)S(1)} copy-done((bf16[2,1024,1024]{2,1,0:T(8,128)(2,1)S(1)}, bf16[2,1024,1024]{2,1,0:T(8,128)(2,1)}, u32[]{:S(2)}) %copy-start.1) | copy-done | bytes 4194328
  72.1 1.3 %shard_map.49 = (bf16[64,1024]{1,0:T(8,128)(2,1)S(1)}, bf16[64,128]{1,0:T(8,128)(2,1)S(1)}) custom-call(bf16[64,256]{1,0:T(8,128)(2,1)S(1)} %get-tuple-element.16.p0, bf16[64,256]{1,0:T(8,128)(2,1)S(1)} %collective-permute-done.p1, bf16[64,256]{1,0:T(8,128)(2,1)S(1)} %collective-permute-done.1.p2, bf16[64,256]{1,0:T(8,128)(2,1)S(1)} %collective-permute-done.2.p3, ...), custom_call_target="tpu_custom_call" | custom-call | flops 268435456 | bytes 3145728 | tf_op jit(solution)/shard_map/pallas_call | solution.py:287
  73.5 1.2 collective-permute-done.9
  74.7 2.4 %collective-permute-start.12 = (bf16[128,128]{1,0:T(8,128)(2,1)S(1)}, bf16[128,128]{1,0:T(8,128)(2,1)S(1)}, u32[]{:S(2)}, u32[]{:S(2)}) collective-permute-start(bf16[128,128]{1,0:T(8,128)(2,1)S(1)} %constant_dynamic-update-slice_fusion.p0), channel_id=1, source_target_pairs={{0,4},{1,5},{2,6},{3,7},{4,0},{5,1},{6,2},{7,3},{8,12},{9,13},{10,... | collective-permute-start | bytes 98312 | tf_op jit(solution)/shard_map/ppermute | solution.py:28
  77.6 1.3 %collective-permute-done.12.p3 = bf16[128,128]{1,0:T(8,128)(2,1)S(1)} collective-permute-done((bf16[128,128]{1,0:T(8,128)(2,1)S(1)}, bf16[128,128]{1,0:T(8,128)(2,1)S(1)}, u32[]{:S(2)}, u32[]{:S(2)}) %collective-permute-start.12) | collective-permute-done | bytes 32800 | tf_op jit(solution)/shard_map/ppermute | solution.py:28
  79.0 2.1 %collective-permute-done.11.p2 = bf16[128,128]{1,0:T(8,128)(2,1)S(1)} collective-permute-done((bf16[128,128]{1,0:T(8,128)(2,1)S(1)}, bf16[128,128]{1,0:T(8,128)(2,1)S(1)}, u32[]{:S(2)}, u32[]{:S(2)}) %collective-permute-start.11) | collective-permute-done | bytes 32800 | tf_op jit(solution)/shard_map/ppermute | solution.py:28
  82.7 2.4 %collective-permute-start.14 = (bf16[32,2048]{1,0:T(8,128)(2,1)S(1)}, bf16[32,2048]{1,0:T(8,128)(2,1)S(1)}, u32[]{:S(2)}, u32[]{:S(2)}) collective-permute-start(bf16[32,2048]{1,0:T(8,128)(2,1)S(1)} %shard_map.50), channel_id=1, source_target_pairs={{0,96},{1,25},{2,98},{3,27},{4,100},{5,29},{6,102},{7,31},{8,104},... | collective-permute-start | bytes 393224 | tf_op jit(solution)/shard_map/ppermute | solution.py:28
  85.0 2.3 %collective-permute-done.15 = bf16[32,2048]{1,0:T(8,128)(2,1)S(1)} collective-permute-done((bf16[32,2048]{1,0:T(8,128)(2,1)S(1)}, bf16[32,2048]{1,0:T(8,128)(2,1)S(1)}, u32[]{:S(2)}, u32[]{:S(2)}) %collective-permute-start.15) | collective-permute-done | bytes 131104 | tf_op jit(solution)/shard_map/ppermute | solution.py:28
  87.4 1.6 %collective-permute-done.14 = bf16[32,2048]{1,0:T(8,128)(2,1)S(1)} collective-permute-done((bf16[32,2048]{1,0:T(8,128)(2,1)S(1)}, bf16[32,2048]{1,0:T(8,128)(2,1)S(1)}, u32[]{:S(2)}, u32[]{:S(2)}) %collective-permute-start.14) | collective-permute-done | bytes 131104 | tf_op jit(solution)/shard_map/ppermute | solution.py:28
  89.8 1.2 %collective-permute-start.19 = (bf16[128,2048]{1,0:T(8,128)(2,1)S(1)}, bf16[128,2048]{1,0:T(8,128)(2,1)S(1)}, u32[]{:S(2)}, u32[]{:S(2)}) collective-permute-start(bf16[128,2048]{1,0:T(8,128)(2,1)S(1)} %pad_maximum_fusion.a_ref), channel_id=1, source_target_pairs={{0,8},{1,33},{2,10},{3,35},{4,12},{5,37},{6,14},{7,39},{8,0},{9,41... | collective-permute-start | bytes 1572872 | tf_op jit(solution)/shard_map/ppermute | solution.py:28
  91.0 1.5 %collective-permute-start.16 = (bf16[128,2048]{1,0:T(8,128)(2,1)S(1)}, bf16[128,2048]{1,0:T(8,128)(2,1)S(1)}, u32[]{:S(2)}, u32[]{:S(2)}) collective-permute-start(bf16[128,2048]{1,0:T(8,128)(2,1)S(1)} %pad_maximum_fusion.a_ref), channel_id=1, source_target_pairs={{0,24},{1,97},{2,26},{3,99},{4,28},{5,101},{6,30},{7,103},{8,16},{... | collective-permute-start | bytes 1572872 | tf_op jit(solution)/shard_map/ppermute | solution.py:28
  92.6 4.3 %collective-permute-start.18 = (bf16[128,2048]{1,0:T(8,128)(2,1)S(1)}, bf16[128,2048]{1,0:T(8,128)(2,1)S(1)}, u32[]{:S(2)}, u32[]{:S(2)}) collective-permute-start(bf16[128,2048]{1,0:T(8,128)(2,1)S(1)} %pad_maximum_fusion.a_ref), channel_id=1, source_target_pairs={{0,1},{1,0},{2,3},{3,2},{4,5},{5,4},{6,7},{7,6},{8,9},{9,8},{10,11... | collective-permute-start | bytes 1572872 | tf_op jit(solution)/shard_map/ppermute | solution.py:28
  96.9 2.3 %collective-permute-done.21.a_ref = bf16[128,2048]{1,0:T(8,128)(2,1)S(1)} collective-permute-done((bf16[128,2048]{1,0:T(8,128)(2,1)S(1)}, bf16[128,2048]{1,0:T(8,128)(2,1)S(1)}, u32[]{:S(2)}, u32[]{:S(2)}) %collective-permute-start.21) | collective-permute-done | bytes 524320 | tf_op jit(solution)/shard_map/ppermute | solution.py:28
  99.2 3.2 %collective-permute-start.22 = (bf16[128,2048]{1,0:T(8,128)(2,1)S(1)}, bf16[128,2048]{1,0:T(8,128)(2,1)S(1)}, u32[]{:S(2)}, u32[]{:S(2)}) collective-permute-start(bf16[128,2048]{1,0:T(8,128)(2,1)S(1)} %collective-permute-done.21.a_ref), channel_id=1, source_target_pairs={{0,1},{1,0},{2,3},{3,2},{4,5},{5,4},{6,7},{7,6},{8,9},{9,8},{10,11... | collective-permute-start | bytes 1572872 | tf_op jit(solution)/shard_map/ppermute | solution.py:28
  102.3 1.2 %collective-permute-done.19.a_ref = bf16[128,2048]{1,0:T(8,128)(2,1)S(1)} collective-permute-done((bf16[128,2048]{1,0:T(8,128)(2,1)S(1)}, bf16[128,2048]{1,0:T(8,128)(2,1)S(1)}, u32[]{:S(2)}, u32[]{:S(2)}) %collective-permute-start.19) | collective-permute-done | bytes 524320 | tf_op jit(solution)/shard_map/ppermute | solution.py:28
  103.6 3.5 %collective-permute-start.20 = (bf16[128,2048]{1,0:T(8,128)(2,1)S(1)}, bf16[128,2048]{1,0:T(8,128)(2,1)S(1)}, u32[]{:S(2)}, u32[]{:S(2)}) collective-permute-start(bf16[128,2048]{1,0:T(8,128)(2,1)S(1)} %collective-permute-done.19.a_ref), channel_id=1, source_target_pairs={{0,1},{1,0},{2,3},{3,2},{4,5},{5,4},{6,7},{7,6},{8,9},{9,8},{10,11... | collective-permute-start | bytes 1572872 | tf_op jit(solution)/shard_map/ppermute | solution.py:28
  107.9 3.2 %shard_map.51.rows_ref.refs_4_ = bf16[1024,1024]{1,0:T(8,128)(2,1)S(1)} custom-call(s32[8,1024]{1,0:T(8,128)S(1)} %get-tuple-element.24.own_ref, bf16[1024,1280]{1,0:T(8,128)(2,1)S(1)} %bitcast.7), custom_call_target="tpu_custom_call" | custom-call | flops 2147483648 | bytes 4194304 | tf_op jit(solution)/shard_map/pallas_call | solution.py:287
  111.0 1.6 %shard_map.52.refs_0_ = bf16[1024,256]{1,0:T(8,128)(2,1)S(1)} custom-call(bf16[128,2048]{1,0:T(8,128)(2,1)S(1)} %pad_maximum_fusion.a_ref, bf16[128,2048]{1,0:T(8,128)(2,1)S(1)} %collective-permute-done.18.b_ref, bf16[2,8,1,128,1024]{4,3,2,1,0:T(8,128)(2,1)S(1)} %copy-done, bf16[1024,1024]{1,0:T(8,128)(2,1)S(1)} %shard_map.51.rows_ref.refs_4_), custom_call_target="tpu_custom_call" | custom-call | flops 1073741824 | bytes 2097152 | tf_op jit(solution)/shard_map/pallas_call | solution.py:287
  112.6 1.6 %shard_map.54.refs_2_ = bf16[1024,256]{1,0:T(8,128)(2,1)S(1)} custom-call(bf16[128,2048]{1,0:T(8,128)(2,1)S(1)} %collective-permute-done.21.a_ref, bf16[128,2048]{1,0:T(8,128)(2,1)S(1)} %collective-permute-done.22.b_ref, bf16[2,8,1,128,1024]{4,3,2,1,0:T(8,128)(2,1)S(1)} %copy-done, bf16[1024,1024]{1,0:T(8,128)(2,1)S(1)} %shard_map.51.rows_ref.refs_4_), custom_call_target="tpu_custom_call" | custom-call | flops 1073741824 | bytes 2097152 | tf_op jit(solution)/shard_map/pallas_call | solution.py:287
  114.2 1.6 %shard_map.53.refs_1_ = bf16[1024,256]{1,0:T(8,128)(2,1)S(1)} custom-call(bf16[128,2048]{1,0:T(8,128)(2,1)S(1)} %collective-permute-done.19.a_ref, bf16[128,2048]{1,0:T(8,128)(2,1)S(1)} %collective-permute-done.20.b_ref, bf16[2,8,1,128,1024]{4,3,2,1,0:T(8,128)(2,1)S(1)} %copy-done, bf16[1024,1024]{1,0:T(8,128)(2,1)S(1)} %shard_map.51.rows_ref.refs_4_), custom_call_target="tpu_custom_call" | custom-call | flops 1073741824 | bytes 2097152 | tf_op jit(solution)/shard_map/pallas_call | solution.py:287
  115.8 2.8 %shard_map.55 = bf16[1024,1024]{1,0:T(8,128)(2,1)} custom-call(bf16[128,2048]{1,0:T(8,128)(2,1)S(1)} %collective-permute-done.16.a_ref, bf16[128,2048]{1,0:T(8,128)(2,1)S(1)} %collective-permute-done.17.b_ref, bf16[1024,256]{1,0:T(8,128)(2,1)S(1)} %shard_map.52.refs_0_, bf16[1024,256]{1,0:T(8,128)(2,1)S(1)} %shard_map.53.refs_1_, ...), custom_call_target="tpu_custom_call" | custom-call | flops 1073741824 | bytes 2097152 | tf_op jit(solution)/shard_map/pallas_call | solution.py:287
  (38 shorter events, 6.9 us)
Async XLA Ops:
  6.3 11.5 %copy-start.2 = (bf16[128,1024]{1,0:T(8,128)(2,1)S(1)}, bf16[128,1024]{1,0:T(8,128)(2,1)}, u32[]{:S(2)}) copy-start(bf16[128,1024]{1,0:T(8,128)(2,1)} %get-tuple-element.20) | copy-start | bytes 786436
  6.3 57.8 %all-to-all-start = ((bf16[128,8,1280]{2,1,0:T(8,128)(2,1)}), bf16[128,8,1280]{2,1,0:T(8,128)(2,1)S(1)}, u32[]{:S(2)}, u32[]{:S(2)}) async-start(bf16[128,8,1280]{2,1,0:T(8,128)(2,1)} %bitcast.8), calls=%async_computation | async-start | bytes 5242880 | tf_op jit(solution)/shard_map/all_to_all | solution.py:359
  17.8 34.6 %collective-permute-start.5 = (bf16[128,1024]{1,0:T(8,128)(2,1)S(1)}, bf16[128,1024]{1,0:T(8,128)(2,1)S(1)}, u32[]{:S(2)}, u32[]{:S(2)}) collective-permute-start(bf16[128,1024]{1,0:T(8,128)(2,1)S(1)} %copy-done.2), channel_id=1, source_target_pairs={{0,64},{1,17},{2,66},{3,19},{4,68},{5,21},{6,70},{7,23},{8,72},{9,... | collective-permute-start | bytes 786440 | tf_op jit(solution)/shard_map/ppermute | solution.py:28
  20.8 33.9 %collective-permute-start.4 = (bf16[128,1024]{1,0:T(8,128)(2,1)S(1)}, bf16[128,1024]{1,0:T(8,128)(2,1)S(1)}, u32[]{:S(2)}, u32[]{:S(2)}) collective-permute-start(bf16[128,1024]{1,0:T(8,128)(2,1)S(1)} %copy-done.2), channel_id=1, source_target_pairs={{0,96},{1,25},{2,98},{3,27},{4,100},{5,29},{6,102},{7,31},{8,104},... | collective-permute-start | bytes 786440 | tf_op jit(solution)/shard_map/ppermute | solution.py:28
  21.6 33.7 %collective-permute-start.3 = (bf16[128,1024]{1,0:T(8,128)(2,1)S(1)}, bf16[128,1024]{1,0:T(8,128)(2,1)}, u32[]{:S(2)}, u32[]{:S(2)}) collective-permute-start(bf16[128,1024]{1,0:T(8,128)(2,1)S(1)} %copy-done.2), channel_id=1, source_target_pairs={{0,32},{1,9},{2,34},{3,11},{4,36},{5,13},{6,38},{7,15},{8,40},{9,1... | collective-permute-start | bytes 786440 | tf_op jit(solution)/shard_map/ppermute | solution.py:28
  54.7 0.7 copy-start.3
  56.4 12.3 %collective-permute-start.8 = (bf16[128,1024]{1,0:T(8,128)(2,1)S(1)}, bf16[128,1024]{1,0:T(8,128)(2,1)S(1)}, u32[]{:S(2)}, u32[]{:S(2)}) collective-permute-start(bf16[128,1024]{1,0:T(8,128)(2,1)S(1)} %select_select_fusion.l0), channel_id=1, source_target_pairs={{1,65},{3,67},{5,69},{7,71},{8,24},{9,73},{10,26},{11,75},{12,28},... | collective-permute-start | bytes 786440 | tf_op jit(solution)/shard_map/ppermute | solution.py:28
  60.8 10.5 %collective-permute-start.7 = (bf16[128,1024]{1,0:T(8,128)(2,1)S(1)}, bf16[128,1024]{1,0:T(8,128)(2,1)S(1)}, u32[]{:S(2)}, u32[]{:S(2)}) collective-permute-start(bf16[128,1024]{1,0:T(8,128)(2,1)S(1)} %select_select_fusion.l0), channel_id=1, source_target_pairs={{1,97},{3,99},{5,101},{7,103},{8,16},{9,105},{10,18},{11,107},{12,... | collective-permute-start | bytes 786440 | tf_op jit(solution)/shard_map/ppermute | solution.py:28
  62.1 9.2 %collective-permute-start.6 = (bf16[128,1024]{1,0:T(8,128)(2,1)S(1)}, bf16[128,1024]{1,0:T(8,128)(2,1)}, u32[]{:S(2)}, u32[]{:S(2)}) collective-permute-start(bf16[128,1024]{1,0:T(8,128)(2,1)S(1)} %select_select_fusion.l0), channel_id=1, source_target_pairs={{1,33},{3,35},{5,37},{7,39},{8,0},{9,41},{10,2},{11,43},{12,4},{13... | collective-permute-start | bytes 786440 | tf_op jit(solution)/shard_map/ppermute | solution.py:28
  64.7 6.6 %collective-permute-start.2 = (bf16[64,256]{1,0:T(8,128)(2,1)S(1)}, bf16[64,256]{1,0:T(8,128)(2,1)S(1)}, u32[]{:S(2)}, u32[]{:S(2)}) collective-permute-start(bf16[64,256]{1,0:T(8,128)(2,1)S(1)} %get-tuple-element.16.p0), channel_id=1, source_target_pairs={{0,4},{1,5},{2,6},{3,7},{4,0},{5,1},{6,2},{7,3},{8,12},{9,13},{10,... | collective-permute-start | bytes 98312 | tf_op jit(solution)/shard_map/ppermute | solution.py:28
  68.1 4.0 %collective-permute-start.1 = (bf16[64,256]{1,0:T(8,128)(2,1)S(1)}, bf16[64,256]{1,0:T(8,128)(2,1)S(1)}, u32[]{:S(2)}, u32[]{:S(2)}) collective-permute-start(bf16[64,256]{1,0:T(8,128)(2,1)S(1)} %get-tuple-element.16.p0), channel_id=1, source_target_pairs={{0,6},{1,7},{2,4},{3,5},{4,2},{5,3},{6,0},{7,1},{8,14},{9,15},{10,... | collective-permute-start | bytes 98312 | tf_op jit(solution)/shard_map/ppermute | solution.py:28
  68.6 3.5 %collective-permute-start = (bf16[64,256]{1,0:T(8,128)(2,1)S(1)}, bf16[64,256]{1,0:T(8,128)(2,1)S(1)}, u32[]{:S(2)}, u32[]{:S(2)}) collective-permute-start(bf16[64,256]{1,0:T(8,128)(2,1)S(1)} %get-tuple-element.16.p0), channel_id=1, source_target_pairs={{0,2},{1,3},{2,0},{3,1},{4,6},{5,7},{6,4},{7,5},{8,10},{9,11},{10,... | collective-permute-start | bytes 98312 | tf_op jit(solution)/shard_map/ppermute | solution.py:28
  68.8 2.2 %copy-start.1 = (bf16[2,1024,1024]{2,1,0:T(8,128)(2,1)S(1)}, bf16[2,1024,1024]{2,1,0:T(8,128)(2,1)}, u32[]{:S(2)}) copy-start(bf16[2,1024,1024]{2,1,0:T(8,128)(2,1)} %source_hbm) | copy-start | bytes 12582916
  73.4 1.3 %collective-permute-start.9 = (bf16[64,128]{1,0:T(8,128)(2,1)S(1)}, bf16[64,128]{1,0:T(8,128)(2,1)S(1)}, u32[]{:S(2)}, u32[]{:S(2)}) collective-permute-start(bf16[64,128]{1,0:T(8,128)(2,1)S(1)} %get-tuple-element.21), channel_id=1, source_target_pairs={{0,1},{1,0},{2,3},{3,2},{4,5},{5,4},{6,7},{7,6},{8,9},{9,8},{10,11... | collective-permute-start | bytes 49160 | tf_op jit(solution)/shard_map/ppermute | solution.py:28
  74.7 4.3 %collective-permute-start.12 = (bf16[128,128]{1,0:T(8,128)(2,1)S(1)}, bf16[128,128]{1,0:T(8,128)(2,1)S(1)}, u32[]{:S(2)}, u32[]{:S(2)}) collective-permute-start(bf16[128,128]{1,0:T(8,128)(2,1)S(1)} %constant_dynamic-update-slice_fusion.p0), channel_id=1, source_target_pairs={{0,4},{1,5},{2,6},{3,7},{4,0},{5,1},{6,2},{7,3},{8,12},{9,13},{10,... | collective-permute-start | bytes 98312 | tf_op jit(solution)/shard_map/ppermute | solution.py:28
  77.1 4.0 %collective-permute-start.11 = (bf16[128,128]{1,0:T(8,128)(2,1)S(1)}, bf16[128,128]{1,0:T(8,128)(2,1)S(1)}, u32[]{:S(2)}, u32[]{:S(2)}) collective-permute-start(bf16[128,128]{1,0:T(8,128)(2,1)S(1)} %constant_dynamic-update-slice_fusion.p0), channel_id=1, source_target_pairs={{0,6},{1,7},{2,4},{3,5},{4,2},{5,3},{6,0},{7,1},{8,14},{9,15},{10,... | collective-permute-start | bytes 98312 | tf_op jit(solution)/shard_map/ppermute | solution.py:28
  77.6 3.5 %collective-permute-start.10 = (bf16[128,128]{1,0:T(8,128)(2,1)S(1)}, bf16[128,128]{1,0:T(8,128)(2,1)S(1)}, u32[]{:S(2)}, u32[]{:S(2)}) collective-permute-start(bf16[128,128]{1,0:T(8,128)(2,1)S(1)} %constant_dynamic-update-slice_fusion.p0), channel_id=1, source_target_pairs={{0,2},{1,3},{2,0},{3,1},{4,6},{5,7},{6,4},{7,5},{8,10},{9,11},{10,... | collective-permute-start | bytes 98312 | tf_op jit(solution)/shard_map/ppermute | solution.py:28
  81.9 5.5 %collective-permute-start.15 = (bf16[32,2048]{1,0:T(8,128)(2,1)S(1)}, bf16[32,2048]{1,0:T(8,128)(2,1)S(1)}, u32[]{:S(2)}, u32[]{:S(2)}) collective-permute-start(bf16[32,2048]{1,0:T(8,128)(2,1)S(1)} %shard_map.50), channel_id=1, source_target_pairs={{0,64},{1,17},{2,66},{3,19},{4,68},{5,21},{6,70},{7,23},{8,72},{9,... | collective-permute-start | bytes 393224 | tf_op jit(solution)/shard_map/ppermute | solution.py:28
  82.7 6.3 %collective-permute-start.14 = (bf16[32,2048]{1,0:T(8,128)(2,1)S(1)}, bf16[32,2048]{1,0:T(8,128)(2,1)S(1)}, u32[]{:S(2)}, u32[]{:S(2)}) collective-permute-start(bf16[32,2048]{1,0:T(8,128)(2,1)S(1)} %shard_map.50), channel_id=1, source_target_pairs={{0,96},{1,25},{2,98},{3,27},{4,100},{5,29},{6,102},{7,31},{8,104},... | collective-permute-start | bytes 393224 | tf_op jit(solution)/shard_map/ppermute | solution.py:28
  85.0 4.1 %collective-permute-start.13 = (bf16[32,2048]{1,0:T(8,128)(2,1)S(1)}, bf16[32,2048]{1,0:T(8,128)(2,1)S(1)}, u32[]{:S(2)}, u32[]{:S(2)}) collective-permute-start(bf16[32,2048]{1,0:T(8,128)(2,1)S(1)} %shard_map.50), channel_id=1, source_target_pairs={{0,32},{1,9},{2,34},{3,11},{4,36},{5,13},{6,38},{7,15},{8,40},{9,1... | collective-permute-start | bytes 393224 | tf_op jit(solution)/shard_map/ppermute | solution.py:28
  89.2 10.0 %collective-permute-start.21 = (bf16[128,2048]{1,0:T(8,128)(2,1)S(1)}, bf16[128,2048]{1,0:T(8,128)(2,1)S(1)}, u32[]{:S(2)}, u32[]{:S(2)}) collective-permute-start(bf16[128,2048]{1,0:T(8,128)(2,1)S(1)} %pad_maximum_fusion.a_ref), channel_id=1, source_target_pairs={{0,16},{1,65},{2,18},{3,67},{4,20},{5,69},{6,22},{7,71},{8,24},{9,... | collective-permute-start | bytes 1572872 | tf_op jit(solution)/shard_map/ppermute | solution.py:28
  89.8 13.8 %collective-permute-start.19 = (bf16[128,2048]{1,0:T(8,128)(2,1)S(1)}, bf16[128,2048]{1,0:T(8,128)(2,1)S(1)}, u32[]{:S(2)}, u32[]{:S(2)}) collective-permute-start(bf16[128,2048]{1,0:T(8,128)(2,1)S(1)} %pad_maximum_fusion.a_ref), channel_id=1, source_target_pairs={{0,8},{1,33},{2,10},{3,35},{4,12},{5,37},{6,14},{7,39},{8,0},{9,41... | collective-permute-start | bytes 1572872 | tf_op jit(solution)/shard_map/ppermute | solution.py:28
  91.0 16.0 %collective-permute-start.16 = (bf16[128,2048]{1,0:T(8,128)(2,1)S(1)}, bf16[128,2048]{1,0:T(8,128)(2,1)S(1)}, u32[]{:S(2)}, u32[]{:S(2)}) collective-permute-start(bf16[128,2048]{1,0:T(8,128)(2,1)S(1)} %pad_maximum_fusion.a_ref), channel_id=1, source_target_pairs={{0,24},{1,97},{2,26},{3,99},{4,28},{5,101},{6,30},{7,103},{8,16},{... | collective-permute-start | bytes 1572872 | tf_op jit(solution)/shard_map/ppermute | solution.py:28
  92.6 18.4 %collective-permute-start.18 = (bf16[128,2048]{1,0:T(8,128)(2,1)S(1)}, bf16[128,2048]{1,0:T(8,128)(2,1)S(1)}, u32[]{:S(2)}, u32[]{:S(2)}) collective-permute-start(bf16[128,2048]{1,0:T(8,128)(2,1)S(1)} %pad_maximum_fusion.a_ref), channel_id=1, source_target_pairs={{0,1},{1,0},{2,3},{3,2},{4,5},{5,4},{6,7},{7,6},{8,9},{9,8},{10,11... | collective-permute-start | bytes 1572872 | tf_op jit(solution)/shard_map/ppermute | solution.py:28
  99.2 13.5 %collective-permute-start.22 = (bf16[128,2048]{1,0:T(8,128)(2,1)S(1)}, bf16[128,2048]{1,0:T(8,128)(2,1)S(1)}, u32[]{:S(2)}, u32[]{:S(2)}) collective-permute-start(bf16[128,2048]{1,0:T(8,128)(2,1)S(1)} %collective-permute-done.21.a_ref), channel_id=1, source_target_pairs={{0,1},{1,0},{2,3},{3,2},{4,5},{5,4},{6,7},{7,6},{8,9},{9,8},{10,11... | collective-permute-start | bytes 1572872 | tf_op jit(solution)/shard_map/ppermute | solution.py:28
  103.6 10.6 %collective-permute-start.20 = (bf16[128,2048]{1,0:T(8,128)(2,1)S(1)}, bf16[128,2048]{1,0:T(8,128)(2,1)S(1)}, u32[]{:S(2)}, u32[]{:S(2)}) collective-permute-start(bf16[128,2048]{1,0:T(8,128)(2,1)S(1)} %collective-permute-done.19.a_ref), channel_id=1, source_target_pairs={{0,1},{1,0},{2,3},{3,2},{4,5},{5,4},{6,7},{7,6},{8,9},{9,8},{10,11... | collective-permute-start | bytes 1572872 | tf_op jit(solution)/shard_map/ppermute | solution.py:28
  107.0 8.7 %collective-permute-start.17 = (bf16[128,2048]{1,0:T(8,128)(2,1)S(1)}, bf16[128,2048]{1,0:T(8,128)(2,1)S(1)}, u32[]{:S(2)}, u32[]{:S(2)}) collective-permute-start(bf16[128,2048]{1,0:T(8,128)(2,1)S(1)} %collective-permute-done.16.a_ref), channel_id=1, source_target_pairs={{0,1},{1,0},{2,3},{3,2},{4,5},{5,4},{6,7},{7,6},{8,9},{9,8},{10,11... | collective-permute-start | bytes 1572872 | tf_op jit(solution)/shard_map/ppermute | solution.py:28
  107.9 3.2 %copy-start = (bf16[2,8,1,128,1024]{4,3,2,1,0:T(8,128)(2,1)S(1)}, bf16[2,8,1,128,1024]{4,3,2,1,0:T(8,128)(2,1)}, u32[]{:S(2)}) copy-start(bf16[2,8,1,128,1024]{4,3,2,1,0:T(8,128)(2,1)} %refs_3_.1) | copy-start | bytes 12582916

commit v10 on v9

--- a/solution.py
+++ b/solution.py
@@ -58,9 +58,12 @@
 
 def order_kernel(points_ref, rows_hbm, panels_hbm, out_hbm, piece_hbm, rows_ref, out_ref, perm_ref, head_ref, piece_ref, in_sems, out_sems):
     count = rows_ref.shape[0]
-    load = pltpu.make_async_copy(rows_hbm, rows_ref, in_sems.at[0])
-    load.start()
-    piece = pltpu.make_async_copy(panels_hbm.at[0, 0, 0], piece_ref, in_sems.at[1])
+    loads = []
+    for i in range(8):
+        span = pl.ds(i * 128, 128)
+        loads.append(pltpu.make_async_copy(rows_hbm.at[span], rows_ref.at[span], in_sems.at[1 + i]))
+        loads[i].start()
+    piece = pltpu.make_async_copy(panels_hbm.at[0, 0, 0], piece_ref, in_sems.at[0])
     piece.start()
     points = points_ref[...]
     block = points >> 10
@@ -85,7 +88,8 @@
 
     shared = [both(ids, 0, 0), both(ids, 0, 1), ids[64:128]]
     stores = []
-    load.wait()
+    for load in loads:
+        load.wait()
     piece.wait()
     keep_piece = pltpu.make_async_copy(piece_ref, piece_hbm, out_sems.at[4])
     keep_piece.start()
@@ -168,12 +172,16 @@
     both_ref[:, 1024:2048] = jnp.where(even, solved[0:32], solved[32:64])
 
 
-def scatter_kernel(own_ref, arrived_ref, out_ref, hit_ref, rows_ref, sem):
+def scatter_kernel(own_ref, arrived_ref, out_ref, hit_ref, rows_ref, sems):
     count = arrived_ref.shape[0]
-    copy = pltpu.make_async_copy(arrived_ref.at[:, 256:1280], rows_ref, sem)
-    copy.start()
+    loads = []
+    for i in range(4):
+        span = pl.ds(i * 256, 256)
+        loads.append(pltpu.make_async_copy(arrived_ref.at[span, 256:1280], rows_ref.at[span], sems.at[i]))
+        loads[i].start()
     hit_ref[...] = (iota((count, count), 0) == own_ref[0:1]).astype(F32).astype(BF16)
-    copy.wait()
+    for load in loads:
+        load.wait()
     for q in range(4):
         cols = slice(q * 256, q * 256 + 256)
         out_ref[:, cols] = dot(hit_ref[...], rows_ref[:, cols], (1, 0)).astype(BF16)
@@ -345,7 +353,7 @@
             pltpu.VMEM((1024, 1024), BF16),
             pltpu.VMEM((128, 1024), F32),
             pltpu.VMEM((128, 1024), BF16),
-            pltpu.SemaphoreType.DMA((2,)),
+            pltpu.SemaphoreType.DMA((9,)),
             pltpu.SemaphoreType.DMA((5,)),
         ],
         specs=[VMEM, HBM, HBM],
@@ -401,7 +409,7 @@
         scatter_kernel,
         (own, arrived),
         [((1024, 1024), BF16)],
-        [pltpu.VMEM((1024, 1024), BF16), pltpu.VMEM((1024, 1024), BF16), pltpu.SemaphoreType.DMA],
+        [pltpu.VMEM((1024, 1024), BF16), pltpu.VMEM((1024, 1024), BF16), pltpu.SemaphoreType.DMA((4,))],
         specs=[VMEM, ANY],
         limit=20,
         flops=1 << 31,
@@ -410,17 +418,17 @@
     line = [both] + [send(both, along_first(i)) for i in range(3)]
     line = jnp.concatenate(line, axis=0)
     side0 = send(line, along_second(0))
+    side1 = send(line, along_second(1))
     side2 = send(line, along_second(2))
-    side1 = send(line, along_second(1))
     line_other = send(line, other_core)
-    side0_other, side2_other = send(side0, other_core), send(side2, other_core)
-    side1_other = send(side1, other_core)
-    places = [((0, n), (1, n)) for n in (3, 0, 2, 1)]
+    side0_other, side1_other = send(side0, other_core), send(side1, other_core)
+    side2_other = send(side2, other_core)
+    places = [((0, n), (1, n)) for n in (3, 0, 1, 2)]
     part0 = update(update_kernel, places[0], (line, line_other), panels, rows)
     part1 = update(update_kernel, places[1], (side0, side0_other), panels, rows)
-    part2 = update(update_kernel, places[2], (side2, side2_other), panels, rows)
+    part2 = update(update_kernel, places[2], (side1, side1_other), panels, rows)
     kernel = functools.partial(last_kernel, places[:3])
-    pieces = (side1, side1_other, part0, part1, part2)
+    pieces = (side2, side2_other, part0, part1, part2)
     extra = (pltpu.VMEM((1024, 1024), BF16), pltpu.SemaphoreType.DMA((4,)))
     updated = update(kernel, places[3], pieces, panels, rows, 1024, extra, HBM)
     return updated.reshape(8, 1, 128, 1024)

time: 119 us -> 120 us (level)
  waiting for transfers between devices: 46.1 us -> 48.3 us
    ppermute x23, waiting for transfers between devices: 46.1 us -> 48.3 us  [send(): return lax.ppermute(value, AXES, pairs)]
where the time goes in v10:
time: 120 us
  waiting for transfers between devices  48.3 us (40%)
  starting transfers between devices  47.4 us (40%)
  Pallas kernels  19.8 us (16%)
  local copies, waits for them, and re-layouts  2.91 us (2%)
    ppermute x23, waiting for transfers between devices, send(): return lax.ppermute(value, AXES, pairs)  48.3 us
    ppermute x23, starting transfers between devices, send(): return lax.ppermute(value, AXES, pairs)  35.9 us
    pallas_call x10, Pallas kernels, launch(): pl.pallas_call(kernel, out_shape=[jax.ShapeDtypeStruct(s, d) for s, d in...  19.8 us
    all_to_all x1, starting transfers between devices, steps(): lax.all_to_all(ordered.reshape(128, 8, 1280), AXES, split_axis=0, concat_...  11.5 us
    unnamed x9, local copies, waits for them, and re-layouts  2.9 us
  transfers between devices with their start and end apart: 24, of which 11 were waited for; matrix products, arithmetic and copies ran while one was open for 1% of the time, Pallas kernels for 7%

profile of v10, /device:TPU:1, one launch (start us, length us, event | category | flops | bytes accessed | tf_op | source)
XLA Modules:
  0.0 119.9 jit_solution(1736777324689785054)
XLA Ops:
  0.0 6.4 %shard_map.46 = (bf16[1024,1280]{1,0:T(8,128)(2,1)}, bf16[128,1024]{1,0:T(8,128)(2,1)}) custom-call(s32[1,1024]{1,0:T(1,128)} %bitcast.9, bf16[1024,1024]{1,0:T(8,128)(2,1)} %rows_hbm.1, bf16[2,8,1,128,1024]{4,3,2,1,0:T(8,128)(2,1)} %refs_3_.1), custom_call_target="tpu_custom_call" | custom-call | flops 3221225472 | bytes 5242880 | tf_op jit(solution)/shard_map/pallas_call | solution.py:295
  6.4 11.5 %all-to-all-start = ((bf16[128,8,1280]{2,1,0:T(8,128)(2,1)}), bf16[128,8,1280]{2,1,0:T(8,128)(2,1)S(1)}, u32[]{:S(2)}, u32[]{:S(2)}) async-start(bf16[128,8,1280]{2,1,0:T(8,128)(2,1)} %bitcast.8), calls=%async_computation | async-start | bytes 5242880 | tf_op jit(solution)/shard_map/all_to_all | solution.py:367
  17.9 2.9 %collective-permute-start.5 = (bf16[128,1024]{1,0:T(8,128)(2,1)S(1)}, bf16[128,1024]{1,0:T(8,128)(2,1)S(1)}, u32[]{:S(2)}, u32[]{:S(2)}) collective-permute-start(bf16[128,1024]{1,0:T(8,128)(2,1)S(1)} %copy-done.2), channel_id=1, source_target_pairs={{0,64},{1,17},{2,66},{3,19},{4,68},{5,21},{6,70},{7,23},{8,72},{9,... | collective-permute-start | bytes 786440 | tf_op jit(solution)/shard_map/ppermute | solution.py:28
  20.8 0.9 collective-permute-start.4
  21.7 30.8 %collective-permute-done.5 = bf16[128,1024]{1,0:T(8,128)(2,1)S(1)} collective-permute-done((bf16[128,1024]{1,0:T(8,128)(2,1)S(1)}, bf16[128,1024]{1,0:T(8,128)(2,1)S(1)}, u32[]{:S(2)}, u32[]{:S(2)}) %collective-permute-start.5) | collective-permute-done | bytes 262176 | tf_op jit(solution)/shard_map/ppermute | solution.py:28
  52.5 2.3 %collective-permute-done.4 = bf16[128,1024]{1,0:T(8,128)(2,1)S(1)} collective-permute-done((bf16[128,1024]{1,0:T(8,128)(2,1)S(1)}, bf16[128,1024]{1,0:T(8,128)(2,1)S(1)}, u32[]{:S(2)}, u32[]{:S(2)}) %collective-permute-start.4) | collective-permute-done | bytes 262176 | tf_op jit(solution)/shard_map/ppermute | solution.py:28
  55.5 1.0 select_select_fusion.l0
  56.5 4.4 %collective-permute-start.8 = (bf16[128,1024]{1,0:T(8,128)(2,1)S(1)}, bf16[128,1024]{1,0:T(8,128)(2,1)S(1)}, u32[]{:S(2)}, u32[]{:S(2)}) collective-permute-start(bf16[128,1024]{1,0:T(8,128)(2,1)S(1)} %select_select_fusion.l0), channel_id=1, source_target_pairs={{1,65},{3,67},{5,69},{7,71},{8,24},{9,73},{10,26},{11,75},{12,28},... | collective-permute-start | bytes 786440 | tf_op jit(solution)/shard_map/ppermute | solution.py:28
  60.9 1.3 %collective-permute-start.7 = (bf16[128,1024]{1,0:T(8,128)(2,1)S(1)}, bf16[128,1024]{1,0:T(8,128)(2,1)S(1)}, u32[]{:S(2)}, u32[]{:S(2)}) collective-permute-start(bf16[128,1024]{1,0:T(8,128)(2,1)S(1)} %select_select_fusion.l0), channel_id=1, source_target_pairs={{1,97},{3,99},{5,101},{7,103},{8,16},{9,105},{10,18},{11,107},{12,... | collective-permute-start | bytes 786440 | tf_op jit(solution)/shard_map/ppermute | solution.py:28
  62.2 2.0 %collective-permute-start.6 = (bf16[128,1024]{1,0:T(8,128)(2,1)S(1)}, bf16[128,1024]{1,0:T(8,128)(2,1)}, u32[]{:S(2)}, u32[]{:S(2)}) collective-permute-start(bf16[128,1024]{1,0:T(8,128)(2,1)S(1)} %select_select_fusion.l0), channel_id=1, source_target_pairs={{1,33},{3,35},{5,37},{7,39},{8,0},{9,41},{10,2},{11,43},{12,4},{13... | collective-permute-start | bytes 786440 | tf_op jit(solution)/shard_map/ppermute | solution.py:28
  64.8 3.4 %collective-permute-start.2 = (bf16[64,256]{1,0:T(8,128)(2,1)S(1)}, bf16[64,256]{1,0:T(8,128)(2,1)S(1)}, u32[]{:S(2)}, u32[]{:S(2)}) collective-permute-start(bf16[64,256]{1,0:T(8,128)(2,1)S(1)} %get-tuple-element.16.p0), channel_id=1, source_target_pairs={{0,4},{1,5},{2,6},{3,7},{4,0},{5,1},{6,2},{7,3},{8,12},{9,13},{10,... | collective-permute-start | bytes 98312 | tf_op jit(solution)/shard_map/ppermute | solution.py:28
  68.9 2.2 %copy-done.1 = bf16[2,1024,1024]{2,1,0:T(8,128)(2,1)S(1)} copy-done((bf16[2,1024,1024]{2,1,0:T(8,128)(2,1)S(1)}, bf16[2,1024,1024]{2,1,0:T(8,128)(2,1)}, u32[]{:S(2)}) %copy-start.1) | copy-done | bytes 4194328
  72.2 1.3 %shard_map.49 = (bf16[64,1024]{1,0:T(8,128)(2,1)S(1)}, bf16[64,128]{1,0:T(8,128)(2,1)S(1)}) custom-call(bf16[64,256]{1,0:T(8,128)(2,1)S(1)} %get-tuple-element.16.p0, bf16[64,256]{1,0:T(8,128)(2,1)S(1)} %collective-permute-done.p1, bf16[64,256]{1,0:T(8,128)(2,1)S(1)} %collective-permute-done.1.p2, bf16[64,256]{1,0:T(8,128)(2,1)S(1)} %collective-permute-done.2.p3, ...), custom_call_target="tpu_custom_call" | custom-call | flops 268435456 | bytes 3145728 | tf_op jit(solution)/shard_map/pallas_call | solution.py:295
  73.6 1.2 collective-permute-done.9
  74.8 2.4 %collective-permute-start.12 = (bf16[128,128]{1,0:T(8,128)(2,1)S(1)}, bf16[128,128]{1,0:T(8,128)(2,1)S(1)}, u32[]{:S(2)}, u32[]{:S(2)}) collective-permute-start(bf16[128,128]{1,0:T(8,128)(2,1)S(1)} %constant_dynamic-update-slice_fusion.p0), channel_id=1, source_target_pairs={{0,4},{1,5},{2,6},{3,7},{4,0},{5,1},{6,2},{7,3},{8,12},{9,13},{10,... | collective-permute-start | bytes 98312 | tf_op jit(solution)/shard_map/ppermute | solution.py:28
  77.7 1.3 %collective-permute-done.12.p3 = bf16[128,128]{1,0:T(8,128)(2,1)S(1)} collective-permute-done((bf16[128,128]{1,0:T(8,128)(2,1)S(1)}, bf16[128,128]{1,0:T(8,128)(2,1)S(1)}, u32[]{:S(2)}, u32[]{:S(2)}) %collective-permute-start.12) | collective-permute-done | bytes 32800 | tf_op jit(solution)/shard_map/ppermute | solution.py:28
  79.0 2.1 %collective-permute-done.11.p2 = bf16[128,128]{1,0:T(8,128)(2,1)S(1)} collective-permute-done((bf16[128,128]{1,0:T(8,128)(2,1)S(1)}, bf16[128,128]{1,0:T(8,128)(2,1)S(1)}, u32[]{:S(2)}, u32[]{:S(2)}) %collective-permute-start.11) | collective-permute-done | bytes 32800 | tf_op jit(solution)/shard_map/ppermute | solution.py:28
  82.7 2.4 %collective-permute-start.14 = (bf16[32,2048]{1,0:T(8,128)(2,1)S(1)}, bf16[32,2048]{1,0:T(8,128)(2,1)S(1)}, u32[]{:S(2)}, u32[]{:S(2)}) collective-permute-start(bf16[32,2048]{1,0:T(8,128)(2,1)S(1)} %shard_map.50), channel_id=1, source_target_pairs={{0,96},{1,25},{2,98},{3,27},{4,100},{5,29},{6,102},{7,31},{8,104},... | collective-permute-start | bytes 393224 | tf_op jit(solution)/shard_map/ppermute | solution.py:28
  85.1 2.3 %collective-permute-done.15 = bf16[32,2048]{1,0:T(8,128)(2,1)S(1)} collective-permute-done((bf16[32,2048]{1,0:T(8,128)(2,1)S(1)}, bf16[32,2048]{1,0:T(8,128)(2,1)S(1)}, u32[]{:S(2)}, u32[]{:S(2)}) %collective-permute-start.15) | collective-permute-done | bytes 131104 | tf_op jit(solution)/shard_map/ppermute | solution.py:28
  87.4 1.6 %collective-permute-done.14 = bf16[32,2048]{1,0:T(8,128)(2,1)S(1)} collective-permute-done((bf16[32,2048]{1,0:T(8,128)(2,1)S(1)}, bf16[32,2048]{1,0:T(8,128)(2,1)S(1)}, u32[]{:S(2)}, u32[]{:S(2)}) %collective-permute-start.14) | collective-permute-done | bytes 131104 | tf_op jit(solution)/shard_map/ppermute | solution.py:28
  89.3 1.3 %collective-permute-start.21 = (bf16[128,2048]{1,0:T(8,128)(2,1)S(1)}, bf16[128,2048]{1,0:T(8,128)(2,1)S(1)}, u32[]{:S(2)}, u32[]{:S(2)}) collective-permute-start(bf16[128,2048]{1,0:T(8,128)(2,1)S(1)} %pad_maximum_fusion.a_ref), channel_id=1, source_target_pairs={{0,24},{1,97},{2,26},{3,99},{4,28},{5,101},{6,30},{7,103},{8,16},{... | collective-permute-start | bytes 1572872 | tf_op jit(solution)/shard_map/ppermute | solution.py:28
  90.5 2.7 %collective-permute-start.16 = (bf16[128,2048]{1,0:T(8,128)(2,1)S(1)}, bf16[128,2048]{1,0:T(8,128)(2,1)S(1)}, u32[]{:S(2)}, u32[]{:S(2)}) collective-permute-start(bf16[128,2048]{1,0:T(8,128)(2,1)S(1)} %pad_maximum_fusion.a_ref), channel_id=1, source_target_pairs={{0,16},{1,65},{2,18},{3,67},{4,20},{5,69},{6,22},{7,71},{8,24},{9,... | collective-permute-start | bytes 1572872 | tf_op jit(solution)/shard_map/ppermute | solution.py:28
  93.2 3.1 %collective-permute-start.18 = (bf16[128,2048]{1,0:T(8,128)(2,1)S(1)}, bf16[128,2048]{1,0:T(8,128)(2,1)S(1)}, u32[]{:S(2)}, u32[]{:S(2)}) collective-permute-start(bf16[128,2048]{1,0:T(8,128)(2,1)S(1)} %pad_maximum_fusion.a_ref), channel_id=1, source_target_pairs={{0,1},{1,0},{2,3},{3,2},{4,5},{5,4},{6,7},{7,6},{8,9},{9,8},{10,11... | collective-permute-start | bytes 1572872 | tf_op jit(solution)/shard_map/ppermute | solution.py:28
  96.3 2.6 %collective-permute-done.21.a_ref = bf16[128,2048]{1,0:T(8,128)(2,1)S(1)} collective-permute-done((bf16[128,2048]{1,0:T(8,128)(2,1)S(1)}, bf16[128,2048]{1,0:T(8,128)(2,1)S(1)}, u32[]{:S(2)}, u32[]{:S(2)}) %collective-permute-start.21) | collective-permute-done | bytes 524320 | tf_op jit(solution)/shard_map/ppermute | solution.py:28
  98.9 3.1 %collective-permute-start.22 = (bf16[128,2048]{1,0:T(8,128)(2,1)S(1)}, bf16[128,2048]{1,0:T(8,128)(2,1)S(1)}, u32[]{:S(2)}, u32[]{:S(2)}) collective-permute-start(bf16[128,2048]{1,0:T(8,128)(2,1)S(1)} %collective-permute-done.21.a_ref), channel_id=1, source_target_pairs={{0,1},{1,0},{2,3},{3,2},{4,5},{5,4},{6,7},{7,6},{8,9},{9,8},{10,11... | collective-permute-start | bytes 1572872 | tf_op jit(solution)/shard_map/ppermute | solution.py:28
  102.6 3.1 %collective-permute-done.16.a_ref = bf16[128,2048]{1,0:T(8,128)(2,1)S(1)} collective-permute-done((bf16[128,2048]{1,0:T(8,128)(2,1)S(1)}, bf16[128,2048]{1,0:T(8,128)(2,1)S(1)}, u32[]{:S(2)}, u32[]{:S(2)}) %collective-permute-start.16) | collective-permute-done | bytes 524320 | tf_op jit(solution)/shard_map/ppermute | solution.py:28
  105.7 3.4 %collective-permute-start.17 = (bf16[128,2048]{1,0:T(8,128)(2,1)S(1)}, bf16[128,2048]{1,0:T(8,128)(2,1)S(1)}, u32[]{:S(2)}, u32[]{:S(2)}) collective-permute-start(bf16[128,2048]{1,0:T(8,128)(2,1)S(1)} %collective-permute-done.16.a_ref), channel_id=1, source_target_pairs={{0,1},{1,0},{2,3},{3,2},{4,5},{5,4},{6,7},{7,6},{8,9},{9,8},{10,11... | collective-permute-start | bytes 1572872 | tf_op jit(solution)/shard_map/ppermute | solution.py:28
  109.1 3.0 %shard_map.51.rows_ref.refs_4_ = bf16[1024,1024]{1,0:T(8,128)(2,1)S(1)} custom-call(s32[8,1024]{1,0:T(8,128)S(1)} %get-tuple-element.24.own_ref, bf16[1024,1280]{1,0:T(8,128)(2,1)S(1)} %bitcast.7), custom_call_target="tpu_custom_call" | custom-call | flops 2147483648 | bytes 4194304 | tf_op jit(solution)/shard_map/pallas_call | solution.py:295
  112.2 1.6 %shard_map.52.refs_0_ = bf16[1024,256]{1,0:T(8,128)(2,1)S(1)} custom-call(bf16[128,2048]{1,0:T(8,128)(2,1)S(1)} %pad_maximum_fusion.a_ref, bf16[128,2048]{1,0:T(8,128)(2,1)S(1)} %collective-permute-done.18.b_ref, bf16[2,8,1,128,1024]{4,3,2,1,0:T(8,128)(2,1)S(1)} %copy-done, bf16[1024,1024]{1,0:T(8,128)(2,1)S(1)} %shard_map.51.rows_ref.refs_4_), custom_call_target="tpu_custom_call" | custom-call | flops 1073741824 | bytes 2097152 | tf_op jit(solution)/shard_map/pallas_call | solution.py:295
  113.7 1.6 %shard_map.54.refs_2_ = bf16[1024,256]{1,0:T(8,128)(2,1)S(1)} custom-call(bf16[128,2048]{1,0:T(8,128)(2,1)S(1)} %collective-permute-done.21.a_ref, bf16[128,2048]{1,0:T(8,128)(2,1)S(1)} %collective-permute-done.22.b_ref, bf16[2,8,1,128,1024]{4,3,2,1,0:T(8,128)(2,1)S(1)} %copy-done, bf16[1024,1024]{1,0:T(8,128)(2,1)S(1)} %shard_map.51.rows_ref.refs_4_), custom_call_target="tpu_custom_call" | custom-call | flops 1073741824 | bytes 2097152 | tf_op jit(solution)/shard_map/pallas_call | solution.py:295
  115.3 1.6 %shard_map.53.refs_1_ = bf16[1024,256]{1,0:T(8,128)(2,1)S(1)} custom-call(bf16[128,2048]{1,0:T(8,128)(2,1)S(1)} %collective-permute-done.19.a_ref, bf16[128,2048]{1,0:T(8,128)(2,1)S(1)} %collective-permute-done.20.b_ref, bf16[2,8,1,128,1024]{4,3,2,1,0:T(8,128)(2,1)S(1)} %copy-done, bf16[1024,1024]{1,0:T(8,128)(2,1)S(1)} %shard_map.51.rows_ref.refs_4_), custom_call_target="tpu_custom_call" | custom-call | flops 1073741824 | bytes 2097152 | tf_op jit(solution)/shard_map/pallas_call | solution.py:295
  116.9 2.8 %shard_map.55 = bf16[1024,1024]{1,0:T(8,128)(2,1)} custom-call(bf16[128,2048]{1,0:T(8,128)(2,1)S(1)} %collective-permute-done.16.a_ref, bf16[128,2048]{1,0:T(8,128)(2,1)S(1)} %collective-permute-done.17.b_ref, bf16[1024,256]{1,0:T(8,128)(2,1)S(1)} %shard_map.52.refs_0_, bf16[1024,256]{1,0:T(8,128)(2,1)S(1)} %shard_map.53.refs_1_, ...), custom_call_target="tpu_custom_call" | custom-call | flops 1073741824 | bytes 2097152 | tf_op jit(solution)/shard_map/pallas_call | solution.py:295
  (38 shorter events, 6.1 us)
Async XLA Ops:
  6.4 11.5 %copy-start.2 = (bf16[128,1024]{1,0:T(8,128)(2,1)S(1)}, bf16[128,1024]{1,0:T(8,128)(2,1)}, u32[]{:S(2)}) copy-start(bf16[128,1024]{1,0:T(8,128)(2,1)} %get-tuple-element.20) | copy-start | bytes 786436
  6.4 57.8 %all-to-all-start = ((bf16[128,8,1280]{2,1,0:T(8,128)(2,1)}), bf16[128,8,1280]{2,1,0:T(8,128)(2,1)S(1)}, u32[]{:S(2)}, u32[]{:S(2)}) async-start(bf16[128,8,1280]{2,1,0:T(8,128)(2,1)} %bitcast.8), calls=%async_computation | async-start | bytes 5242880 | tf_op jit(solution)/shard_map/all_to_all | solution.py:367
  17.9 34.6 %collective-permute-start.5 = (bf16[128,1024]{1,0:T(8,128)(2,1)S(1)}, bf16[128,1024]{1,0:T(8,128)(2,1)S(1)}, u32[]{:S(2)}, u32[]{:S(2)}) collective-permute-start(bf16[128,1024]{1,0:T(8,128)(2,1)S(1)} %copy-done.2), channel_id=1, source_target_pairs={{0,64},{1,17},{2,66},{3,19},{4,68},{5,21},{6,70},{7,23},{8,72},{9,... | collective-permute-start | bytes 786440 | tf_op jit(solution)/shard_map/ppermute | solution.py:28
  20.8 33.9 %collective-permute-start.4 = (bf16[128,1024]{1,0:T(8,128)(2,1)S(1)}, bf16[128,1024]{1,0:T(8,128)(2,1)S(1)}, u32[]{:S(2)}, u32[]{:S(2)}) collective-permute-start(bf16[128,1024]{1,0:T(8,128)(2,1)S(1)} %copy-done.2), channel_id=1, source_target_pairs={{0,96},{1,25},{2,98},{3,27},{4,100},{5,29},{6,102},{7,31},{8,104},... | collective-permute-start | bytes 786440 | tf_op jit(solution)/shard_map/ppermute | solution.py:28
  21.7 33.7 %collective-permute-start.3 = (bf16[128,1024]{1,0:T(8,128)(2,1)S(1)}, bf16[128,1024]{1,0:T(8,128)(2,1)}, u32[]{:S(2)}, u32[]{:S(2)}) collective-permute-start(bf16[128,1024]{1,0:T(8,128)(2,1)S(1)} %copy-done.2), channel_id=1, source_target_pairs={{0,32},{1,9},{2,34},{3,11},{4,36},{5,13},{6,38},{7,15},{8,40},{9,1... | collective-permute-start | bytes 786440 | tf_op jit(solution)/shard_map/ppermute | solution.py:28
  54.8 0.7 copy-start.3
  56.5 12.3 %collective-permute-start.8 = (bf16[128,1024]{1,0:T(8,128)(2,1)S(1)}, bf16[128,1024]{1,0:T(8,128)(2,1)S(1)}, u32[]{:S(2)}, u32[]{:S(2)}) collective-permute-start(bf16[128,1024]{1,0:T(8,128)(2,1)S(1)} %select_select_fusion.l0), channel_id=1, source_target_pairs={{1,65},{3,67},{5,69},{7,71},{8,24},{9,73},{10,26},{11,75},{12,28},... | collective-permute-start | bytes 786440 | tf_op jit(solution)/shard_map/ppermute | solution.py:28
  60.9 10.5 %collective-permute-start.7 = (bf16[128,1024]{1,0:T(8,128)(2,1)S(1)}, bf16[128,1024]{1,0:T(8,128)(2,1)S(1)}, u32[]{:S(2)}, u32[]{:S(2)}) collective-permute-start(bf16[128,1024]{1,0:T(8,128)(2,1)S(1)} %select_select_fusion.l0), channel_id=1, source_target_pairs={{1,97},{3,99},{5,101},{7,103},{8,16},{9,105},{10,18},{11,107},{12,... | collective-permute-start | bytes 786440 | tf_op jit(solution)/shard_map/ppermute | solution.py:28
  62.2 9.2 %collective-permute-start.6 = (bf16[128,1024]{1,0:T(8,128)(2,1)S(1)}, bf16[128,1024]{1,0:T(8,128)(2,1)}, u32[]{:S(2)}, u32[]{:S(2)}) collective-permute-start(bf16[128,1024]{1,0:T(8,128)(2,1)S(1)} %select_select_fusion.l0), channel_id=1, source_target_pairs={{1,33},{3,35},{5,37},{7,39},{8,0},{9,41},{10,2},{11,43},{12,4},{13... | collective-permute-start | bytes 786440 | tf_op jit(solution)/shard_map/ppermute | solution.py:28
  64.8 6.6 %collective-permute-start.2 = (bf16[64,256]{1,0:T(8,128)(2,1)S(1)}, bf16[64,256]{1,0:T(8,128)(2,1)S(1)}, u32[]{:S(2)}, u32[]{:S(2)}) collective-permute-start(bf16[64,256]{1,0:T(8,128)(2,1)S(1)} %get-tuple-element.16.p0), channel_id=1, source_target_pairs={{0,4},{1,5},{2,6},{3,7},{4,0},{5,1},{6,2},{7,3},{8,12},{9,13},{10,... | collective-permute-start | bytes 98312 | tf_op jit(solution)/shard_map/ppermute | solution.py:28
  68.2 4.0 %collective-permute-start.1 = (bf16[64,256]{1,0:T(8,128)(2,1)S(1)}, bf16[64,256]{1,0:T(8,128)(2,1)S(1)}, u32[]{:S(2)}, u32[]{:S(2)}) collective-permute-start(bf16[64,256]{1,0:T(8,128)(2,1)S(1)} %get-tuple-element.16.p0), channel_id=1, source_target_pairs={{0,6},{1,7},{2,4},{3,5},{4,2},{5,3},{6,0},{7,1},{8,14},{9,15},{10,... | collective-permute-start | bytes 98312 | tf_op jit(solution)/shard_map/ppermute | solution.py:28
  68.7 3.5 %collective-permute-start = (bf16[64,256]{1,0:T(8,128)(2,1)S(1)}, bf16[64,256]{1,0:T(8,128)(2,1)S(1)}, u32[]{:S(2)}, u32[]{:S(2)}) collective-permute-start(bf16[64,256]{1,0:T(8,128)(2,1)S(1)} %get-tuple-element.16.p0), channel_id=1, source_target_pairs={{0,2},{1,3},{2,0},{3,1},{4,6},{5,7},{6,4},{7,5},{8,10},{9,11},{10,... | collective-permute-start | bytes 98312 | tf_op jit(solution)/shard_map/ppermute | solution.py:28
  68.9 2.2 %copy-start.1 = (bf16[2,1024,1024]{2,1,0:T(8,128)(2,1)S(1)}, bf16[2,1024,1024]{2,1,0:T(8,128)(2,1)}, u32[]{:S(2)}) copy-start(bf16[2,1024,1024]{2,1,0:T(8,128)(2,1)} %source_hbm) | copy-start | bytes 12582916
  73.5 1.3 %collective-permute-start.9 = (bf16[64,128]{1,0:T(8,128)(2,1)S(1)}, bf16[64,128]{1,0:T(8,128)(2,1)S(1)}, u32[]{:S(2)}, u32[]{:S(2)}) collective-permute-start(bf16[64,128]{1,0:T(8,128)(2,1)S(1)} %get-tuple-element.21), channel_id=1, source_target_pairs={{0,1},{1,0},{2,3},{3,2},{4,5},{5,4},{6,7},{7,6},{8,9},{9,8},{10,11... | collective-permute-start | bytes 49160 | tf_op jit(solution)/shard_map/ppermute | solution.py:28
  74.8 4.3 %collective-permute-start.12 = (bf16[128,128]{1,0:T(8,128)(2,1)S(1)}, bf16[128,128]{1,0:T(8,128)(2,1)S(1)}, u32[]{:S(2)}, u32[]{:S(2)}) collective-permute-start(bf16[128,128]{1,0:T(8,128)(2,1)S(1)} %constant_dynamic-update-slice_fusion.p0), channel_id=1, source_target_pairs={{0,4},{1,5},{2,6},{3,7},{4,0},{5,1},{6,2},{7,3},{8,12},{9,13},{10,... | collective-permute-start | bytes 98312 | tf_op jit(solution)/shard_map/ppermute | solution.py:28
  77.2 4.0 %collective-permute-start.11 = (bf16[128,128]{1,0:T(8,128)(2,1)S(1)}, bf16[128,128]{1,0:T(8,128)(2,1)S(1)}, u32[]{:S(2)}, u32[]{:S(2)}) collective-permute-start(bf16[128,128]{1,0:T(8,128)(2,1)S(1)} %constant_dynamic-update-slice_fusion.p0), channel_id=1, source_target_pairs={{0,6},{1,7},{2,4},{3,5},{4,2},{5,3},{6,0},{7,1},{8,14},{9,15},{10,... | collective-permute-start | bytes 98312 | tf_op jit(solution)/shard_map/ppermute | solution.py:28
  77.7 3.5 %collective-permute-start.10 = (bf16[128,128]{1,0:T(8,128)(2,1)S(1)}, bf16[128,128]{1,0:T(8,128)(2,1)S(1)}, u32[]{:S(2)}, u32[]{:S(2)}) collective-permute-start(bf16[128,128]{1,0:T(8,128)(2,1)S(1)} %constant_dynamic-update-slice_fusion.p0), channel_id=1, source_target_pairs={{0,2},{1,3},{2,0},{3,1},{4,6},{5,7},{6,4},{7,5},{8,10},{9,11},{10,... | collective-permute-start | bytes 98312 | tf_op jit(solution)/shard_map/ppermute | solution.py:28
  81.9 5.5 %collective-permute-start.15 = (bf16[32,2048]{1,0:T(8,128)(2,1)S(1)}, bf16[32,2048]{1,0:T(8,128)(2,1)S(1)}, u32[]{:S(2)}, u32[]{:S(2)}) collective-permute-start(bf16[32,2048]{1,0:T(8,128)(2,1)S(1)} %shard_map.50), channel_id=1, source_target_pairs={{0,64},{1,17},{2,66},{3,19},{4,68},{5,21},{6,70},{7,23},{8,72},{9,... | collective-permute-start | bytes 393224 | tf_op jit(solution)/shard_map/ppermute | solution.py:28
  82.7 6.3 %collective-permute-start.14 = (bf16[32,2048]{1,0:T(8,128)(2,1)S(1)}, bf16[32,2048]{1,0:T(8,128)(2,1)S(1)}, u32[]{:S(2)}, u32[]{:S(2)}) collective-permute-start(bf16[32,2048]{1,0:T(8,128)(2,1)S(1)} %shard_map.50), channel_id=1, source_target_pairs={{0,96},{1,25},{2,98},{3,27},{4,100},{5,29},{6,102},{7,31},{8,104},... | collective-permute-start | bytes 393224 | tf_op jit(solution)/shard_map/ppermute | solution.py:28
  85.1 4.1 %collective-permute-start.13 = (bf16[32,2048]{1,0:T(8,128)(2,1)S(1)}, bf16[32,2048]{1,0:T(8,128)(2,1)S(1)}, u32[]{:S(2)}, u32[]{:S(2)}) collective-permute-start(bf16[32,2048]{1,0:T(8,128)(2,1)S(1)} %shard_map.50), channel_id=1, source_target_pairs={{0,32},{1,9},{2,34},{3,11},{4,36},{5,13},{6,38},{7,15},{8,40},{9,1... | collective-permute-start | bytes 393224 | tf_op jit(solution)/shard_map/ppermute | solution.py:28
  89.3 9.6 %collective-permute-start.21 = (bf16[128,2048]{1,0:T(8,128)(2,1)S(1)}, bf16[128,2048]{1,0:T(8,128)(2,1)S(1)}, u32[]{:S(2)}, u32[]{:S(2)}) collective-permute-start(bf16[128,2048]{1,0:T(8,128)(2,1)S(1)} %pad_maximum_fusion.a_ref), channel_id=1, source_target_pairs={{0,24},{1,97},{2,26},{3,99},{4,28},{5,101},{6,30},{7,103},{8,16},{... | collective-permute-start | bytes 1572872 | tf_op jit(solution)/shard_map/ppermute | solution.py:28
  90.5 11.5 %collective-permute-start.19 = (bf16[128,2048]{1,0:T(8,128)(2,1)S(1)}, bf16[128,2048]{1,0:T(8,128)(2,1)S(1)}, u32[]{:S(2)}, u32[]{:S(2)}) collective-permute-start(bf16[128,2048]{1,0:T(8,128)(2,1)S(1)} %pad_maximum_fusion.a_ref), channel_id=1, source_target_pairs={{0,8},{1,33},{2,10},{3,35},{4,12},{5,37},{6,14},{7,39},{8,0},{9,41... | collective-permute-start | bytes 1572872 | tf_op jit(solution)/shard_map/ppermute | solution.py:28
  90.5 15.2 %collective-permute-start.16 = (bf16[128,2048]{1,0:T(8,128)(2,1)S(1)}, bf16[128,2048]{1,0:T(8,128)(2,1)S(1)}, u32[]{:S(2)}, u32[]{:S(2)}) collective-permute-start(bf16[128,2048]{1,0:T(8,128)(2,1)S(1)} %pad_maximum_fusion.a_ref), channel_id=1, source_target_pairs={{0,16},{1,65},{2,18},{3,67},{4,20},{5,69},{6,22},{7,71},{8,24},{9,... | collective-permute-start | bytes 1572872 | tf_op jit(solution)/shard_map/ppermute | solution.py:28
  93.2 18.9 %collective-permute-start.18 = (bf16[128,2048]{1,0:T(8,128)(2,1)S(1)}, bf16[128,2048]{1,0:T(8,128)(2,1)S(1)}, u32[]{:S(2)}, u32[]{:S(2)}) collective-permute-start(bf16[128,2048]{1,0:T(8,128)(2,1)S(1)} %pad_maximum_fusion.a_ref), channel_id=1, source_target_pairs={{0,1},{1,0},{2,3},{3,2},{4,5},{5,4},{6,7},{7,6},{8,9},{9,8},{10,11... | collective-permute-start | bytes 1572872 | tf_op jit(solution)/shard_map/ppermute | solution.py:28
  98.9 14.8 %collective-permute-start.22 = (bf16[128,2048]{1,0:T(8,128)(2,1)S(1)}, bf16[128,2048]{1,0:T(8,128)(2,1)S(1)}, u32[]{:S(2)}, u32[]{:S(2)}) collective-permute-start(bf16[128,2048]{1,0:T(8,128)(2,1)S(1)} %collective-permute-done.21.a_ref), channel_id=1, source_target_pairs={{0,1},{1,0},{2,3},{3,2},{4,5},{5,4},{6,7},{7,6},{8,9},{9,8},{10,11... | collective-permute-start | bytes 1572872 | tf_op jit(solution)/shard_map/ppermute | solution.py:28
  102.0 13.3 %collective-permute-start.20 = (bf16[128,2048]{1,0:T(8,128)(2,1)S(1)}, bf16[128,2048]{1,0:T(8,128)(2,1)S(1)}, u32[]{:S(2)}, u32[]{:S(2)}) collective-permute-start(bf16[128,2048]{1,0:T(8,128)(2,1)S(1)} %collective-permute-done.19.a_ref), channel_id=1, source_target_pairs={{0,1},{1,0},{2,3},{3,2},{4,5},{5,4},{6,7},{7,6},{8,9},{9,8},{10,11... | collective-permute-start | bytes 1572872 | tf_op jit(solution)/shard_map/ppermute | solution.py:28
  105.7 11.2 %collective-permute-start.17 = (bf16[128,2048]{1,0:T(8,128)(2,1)S(1)}, bf16[128,2048]{1,0:T(8,128)(2,1)S(1)}, u32[]{:S(2)}, u32[]{:S(2)}) collective-permute-start(bf16[128,2048]{1,0:T(8,128)(2,1)S(1)} %collective-permute-done.16.a_ref), channel_id=1, source_target_pairs={{0,1},{1,0},{2,3},{3,2},{4,5},{5,4},{6,7},{7,6},{8,9},{9,8},{10,11... | collective-permute-start | bytes 1572872 | tf_op jit(solution)/shard_map/ppermute | solution.py:28
  109.1 3.1 %copy-start = (bf16[2,8,1,128,1024]{4,3,2,1,0:T(8,128)(2,1)S(1)}, bf16[2,8,1,128,1024]{4,3,2,1,0:T(8,128)(2,1)}, u32[]{:S(2)}) copy-start(bf16[2,8,1,128,1024]{4,3,2,1,0:T(8,128)(2,1)} %refs_3_.1) | copy-start | bytes 12582916

commit v11 on v10

--- a/solution.py
+++ b/solution.py
@@ -313,7 +313,9 @@
 
 
 def spread_first(piece):
-    moved = [send(piece, along_first(kind)) for kind in range(3)]
+    moved = []
+    for kind in range(3):
+        moved.append(send(piece, along_first(kind)))
     first, second, core = place_of(0)
     source = jnp.where(core == 0, 0, 1)
     line = jnp.where(first ^ 1 == source, moved[0], jnp.where(3 - first == source, moved[1], moved[2]))
@@ -418,17 +420,17 @@
     line = [both] + [send(both, along_first(i)) for i in range(3)]
     line = jnp.concatenate(line, axis=0)
     side0 = send(line, along_second(0))
+    side2 = send(line, along_second(2))
     side1 = send(line, along_second(1))
-    side2 = send(line, along_second(2))
     line_other = send(line, other_core)
-    side0_other, side1_other = send(side0, other_core), send(side1, other_core)
-    side2_other = send(side2, other_core)
-    places = [((0, n), (1, n)) for n in (3, 0, 1, 2)]
+    side0_other, side2_other = send(side0, other_core), send(side2, other_core)
+    side1_other = send(side1, other_core)
+    places = [((0, n), (1, n)) for n in (3, 0, 2, 1)]
     part0 = update(update_kernel, places[0], (line, line_other), panels, rows)
     part1 = update(update_kernel, places[1], (side0, side0_other), panels, rows)
-    part2 = update(update_kernel, places[2], (side1, side1_other), panels, rows)
+    part2 = update(update_kernel, places[2], (side2, side2_other), panels, rows)
     kernel = functools.partial(last_kernel, places[:3])
-    pieces = (side2, side2_other, part0, part1, part2)
+    pieces = (side1, side1_other, part0, part1, part2)
     extra = (pltpu.VMEM((1024, 1024), BF16), pltpu.SemaphoreType.DMA((4,)))
     updated = update(kernel, places[3], pieces, panels, rows, 1024, extra, HBM)
     return updated.reshape(8, 1, 128, 1024)

time: 120 us -> 119 us (level)
  waiting for transfers between devices: 48.3 us -> 46.1 us
    ppermute x23, waiting for transfers between devices: 48.3 us -> 46.1 us  [send(): return lax.ppermute(value, AXES, pairs)]
where the time goes in v11:
time: 119 us
  starting transfers between devices  48.4 us (41%)
  waiting for transfers between devices  46.1 us (39%)
  Pallas kernels  19.8 us (17%)
  local copies, waits for them, and re-layouts  2.91 us (2%)
    ppermute x23, waiting for transfers between devices, send(): return lax.ppermute(value, AXES, pairs)  46.1 us
    ppermute x23, starting transfers between devices, send(): return lax.ppermute(value, AXES, pairs)  36.9 us
    pallas_call x10, Pallas kernels, launch(): pl.pallas_call(kernel, out_shape=[jax.ShapeDtypeStruct(s, d) for s, d in...  19.8 us
    all_to_all x1, starting transfers between devices, steps(): lax.all_to_all(ordered.reshape(128, 8, 1280), AXES, split_axis=0, concat_...  11.5 us
    unnamed x9, local copies, waits for them, and re-layouts  2.9 us
  transfers between devices with their start and end apart: 24, of which 11 were waited for; matrix products, arithmetic and copies ran while one was open for 1% of the time, Pallas kernels for 7%

profile of v11, /device:TPU:1, one launch (start us, length us, event | category | flops | bytes accessed | tf_op | source)
XLA Modules:
  0.0 118.7 jit_solution(8353415396001090602)
XLA Ops:
  0.0 6.4 %shard_map.46 = (bf16[1024,1280]{1,0:T(8,128)(2,1)}, bf16[128,1024]{1,0:T(8,128)(2,1)}) custom-call(s32[1,1024]{1,0:T(1,128)} %bitcast.9, bf16[1024,1024]{1,0:T(8,128)(2,1)} %rows_hbm.1, bf16[2,8,1,128,1024]{4,3,2,1,0:T(8,128)(2,1)} %refs_3_.1), custom_call_target="tpu_custom_call" | custom-call | flops 3221225472 | bytes 5242880 | tf_op jit(solution)/shard_map/pallas_call | solution.py:295
  6.4 11.5 %all-to-all-start = ((bf16[128,8,1280]{2,1,0:T(8,128)(2,1)}), bf16[128,8,1280]{2,1,0:T(8,128)(2,1)S(1)}, u32[]{:S(2)}, u32[]{:S(2)}) async-start(bf16[128,8,1280]{2,1,0:T(8,128)(2,1)} %bitcast.8), calls=%async_computation | async-start | bytes 5242880 | tf_op jit(solution)/shard_map/all_to_all | solution.py:369
  17.9 2.9 %collective-permute-start.5 = (bf16[128,1024]{1,0:T(8,128)(2,1)S(1)}, bf16[128,1024]{1,0:T(8,128)(2,1)S(1)}, u32[]{:S(2)}, u32[]{:S(2)}) collective-permute-start(bf16[128,1024]{1,0:T(8,128)(2,1)S(1)} %copy-done.2), channel_id=1, source_target_pairs={{0,64},{1,17},{2,66},{3,19},{4,68},{5,21},{6,70},{7,23},{8,72},{9,... | collective-permute-start | bytes 786440 | tf_op jit(solution)/shard_map/ppermute | solution.py:28
  20.8 0.9 collective-permute-start.4
  21.7 30.8 %collective-permute-done.5 = bf16[128,1024]{1,0:T(8,128)(2,1)S(1)} collective-permute-done((bf16[128,1024]{1,0:T(8,128)(2,1)S(1)}, bf16[128,1024]{1,0:T(8,128)(2,1)S(1)}, u32[]{:S(2)}, u32[]{:S(2)}) %collective-permute-start.5) | collective-permute-done | bytes 262176 | tf_op jit(solution)/shard_map/ppermute | solution.py:28
  52.5 2.3 %collective-permute-done.4 = bf16[128,1024]{1,0:T(8,128)(2,1)S(1)} collective-permute-done((bf16[128,1024]{1,0:T(8,128)(2,1)S(1)}, bf16[128,1024]{1,0:T(8,128)(2,1)S(1)}, u32[]{:S(2)}, u32[]{:S(2)}) %collective-permute-start.4) | collective-permute-done | bytes 262176 | tf_op jit(solution)/shard_map/ppermute | solution.py:28
  55.5 1.0 select_select_fusion.l0
  56.5 4.4 %collective-permute-start.8 = (bf16[128,1024]{1,0:T(8,128)(2,1)S(1)}, bf16[128,1024]{1,0:T(8,128)(2,1)S(1)}, u32[]{:S(2)}, u32[]{:S(2)}) collective-permute-start(bf16[128,1024]{1,0:T(8,128)(2,1)S(1)} %select_select_fusion.l0), channel_id=1, source_target_pairs={{1,65},{3,67},{5,69},{7,71},{8,24},{9,73},{10,26},{11,75},{12,28},... | collective-permute-start | bytes 786440 | tf_op jit(solution)/shard_map/ppermute | solution.py:28
  60.9 1.3 %collective-permute-start.7 = (bf16[128,1024]{1,0:T(8,128)(2,1)S(1)}, bf16[128,1024]{1,0:T(8,128)(2,1)S(1)}, u32[]{:S(2)}, u32[]{:S(2)}) collective-permute-start(bf16[128,1024]{1,0:T(8,128)(2,1)S(1)} %select_select_fusion.l0), channel_id=1, source_target_pairs={{1,97},{3,99},{5,101},{7,103},{8,16},{9,105},{10,18},{11,107},{12,... | collective-permute-start | bytes 786440 | tf_op jit(solution)/shard_map/ppermute | solution.py:28
  62.2 2.0 %collective-permute-start.6 = (bf16[128,1024]{1,0:T(8,128)(2,1)S(1)}, bf16[128,1024]{1,0:T(8,128)(2,1)}, u32[]{:S(2)}, u32[]{:S(2)}) collective-permute-start(bf16[128,1024]{1,0:T(8,128)(2,1)S(1)} %select_select_fusion.l0), channel_id=1, source_target_pairs={{1,33},{3,35},{5,37},{7,39},{8,0},{9,41},{10,2},{11,43},{12,4},{13... | collective-permute-start | bytes 786440 | tf_op jit(solution)/shard_map/ppermute | solution.py:28
  64.8 3.4 %collective-permute-start.2 = (bf16[64,256]{1,0:T(8,128)(2,1)S(1)}, bf16[64,256]{1,0:T(8,128)(2,1)S(1)}, u32[]{:S(2)}, u32[]{:S(2)}) collective-permute-start(bf16[64,256]{1,0:T(8,128)(2,1)S(1)} %get-tuple-element.16.p0), channel_id=1, source_target_pairs={{0,4},{1,5},{2,6},{3,7},{4,0},{5,1},{6,2},{7,3},{8,12},{9,13},{10,... | collective-permute-start | bytes 98312 | tf_op jit(solution)/shard_map/ppermute | solution.py:28
  68.9 2.2 %copy-done.1 = bf16[2,1024,1024]{2,1,0:T(8,128)(2,1)S(1)} copy-done((bf16[2,1024,1024]{2,1,0:T(8,128)(2,1)S(1)}, bf16[2,1024,1024]{2,1,0:T(8,128)(2,1)}, u32[]{:S(2)}) %copy-start.1) | copy-done | bytes 4194328
  72.2 1.3 %shard_map.49 = (bf16[64,1024]{1,0:T(8,128)(2,1)S(1)}, bf16[64,128]{1,0:T(8,128)(2,1)S(1)}) custom-call(bf16[64,256]{1,0:T(8,128)(2,1)S(1)} %get-tuple-element.16.p0, bf16[64,256]{1,0:T(8,128)(2,1)S(1)} %collective-permute-done.p1, bf16[64,256]{1,0:T(8,128)(2,1)S(1)} %collective-permute-done.1.p2, bf16[64,256]{1,0:T(8,128)(2,1)S(1)} %collective-permute-done.2.p3, ...), custom_call_target="tpu_custom_call" | custom-call | flops 268435456 | bytes 3145728 | tf_op jit(solution)/shard_map/pallas_call | solution.py:295
  73.6 1.2 collective-permute-done.9
  74.8 2.4 %collective-permute-start.12 = (bf16[128,128]{1,0:T(8,128)(2,1)S(1)}, bf16[128,128]{1,0:T(8,128)(2,1)S(1)}, u32[]{:S(2)}, u32[]{:S(2)}) collective-permute-start(bf16[128,128]{1,0:T(8,128)(2,1)S(1)} %constant_dynamic-update-slice_fusion.p0), channel_id=1, source_target_pairs={{0,4},{1,5},{2,6},{3,7},{4,0},{5,1},{6,2},{7,3},{8,12},{9,13},{10,... | collective-permute-start | bytes 98312 | tf_op jit(solution)/shard_map/ppermute | solution.py:28
  77.7 1.3 %collective-permute-done.12.p3 = bf16[128,128]{1,0:T(8,128)(2,1)S(1)} collective-permute-done((bf16[128,128]{1,0:T(8,128)(2,1)S(1)}, bf16[128,128]{1,0:T(8,128)(2,1)S(1)}, u32[]{:S(2)}, u32[]{:S(2)}) %collective-permute-start.12) | collective-permute-done | bytes 32800 | tf_op jit(solution)/shard_map/ppermute | solution.py:28
  79.0 2.1 %collective-permute-done.11.p2 = bf16[128,128]{1,0:T(8,128)(2,1)S(1)} collective-permute-done((bf16[128,128]{1,0:T(8,128)(2,1)S(1)}, bf16[128,128]{1,0:T(8,128)(2,1)S(1)}, u32[]{:S(2)}, u32[]{:S(2)}) %collective-permute-start.11) | collective-permute-done | bytes 32800 | tf_op jit(solution)/shard_map/ppermute | solution.py:28
  82.7 2.4 %collective-permute-start.14 = (bf16[32,2048]{1,0:T(8,128)(2,1)S(1)}, bf16[32,2048]{1,0:T(8,128)(2,1)S(1)}, u32[]{:S(2)}, u32[]{:S(2)}) collective-permute-start(bf16[32,2048]{1,0:T(8,128)(2,1)S(1)} %shard_map.50), channel_id=1, source_target_pairs={{0,96},{1,25},{2,98},{3,27},{4,100},{5,29},{6,102},{7,31},{8,104},... | collective-permute-start | bytes 393224 | tf_op jit(solution)/shard_map/ppermute | solution.py:28
  85.1 2.3 %collective-permute-done.15 = bf16[32,2048]{1,0:T(8,128)(2,1)S(1)} collective-permute-done((bf16[32,2048]{1,0:T(8,128)(2,1)S(1)}, bf16[32,2048]{1,0:T(8,128)(2,1)S(1)}, u32[]{:S(2)}, u32[]{:S(2)}) %collective-permute-start.15) | collective-permute-done | bytes 131104 | tf_op jit(solution)/shard_map/ppermute | solution.py:28
  87.4 1.6 %collective-permute-done.14 = bf16[32,2048]{1,0:T(8,128)(2,1)S(1)} collective-permute-done((bf16[32,2048]{1,0:T(8,128)(2,1)S(1)}, bf16[32,2048]{1,0:T(8,128)(2,1)S(1)}, u32[]{:S(2)}, u32[]{:S(2)}) %collective-permute-start.14) | collective-permute-done | bytes 131104 | tf_op jit(solution)/shard_map/ppermute | solution.py:28
  89.9 1.2 %collective-permute-start.19 = (bf16[128,2048]{1,0:T(8,128)(2,1)S(1)}, bf16[128,2048]{1,0:T(8,128)(2,1)S(1)}, u32[]{:S(2)}, u32[]{:S(2)}) collective-permute-start(bf16[128,2048]{1,0:T(8,128)(2,1)S(1)} %pad_maximum_fusion.a_ref), channel_id=1, source_target_pairs={{0,8},{1,33},{2,10},{3,35},{4,12},{5,37},{6,14},{7,39},{8,0},{9,41... | collective-permute-start | bytes 1572872 | tf_op jit(solution)/shard_map/ppermute | solution.py:28
  91.1 1.5 %collective-permute-start.16 = (bf16[128,2048]{1,0:T(8,128)(2,1)S(1)}, bf16[128,2048]{1,0:T(8,128)(2,1)S(1)}, u32[]{:S(2)}, u32[]{:S(2)}) collective-permute-start(bf16[128,2048]{1,0:T(8,128)(2,1)S(1)} %pad_maximum_fusion.a_ref), channel_id=1, source_target_pairs={{0,24},{1,97},{2,26},{3,99},{4,28},{5,101},{6,30},{7,103},{8,16},{... | collective-permute-start | bytes 1572872 | tf_op jit(solution)/shard_map/ppermute | solution.py:28
  92.7 4.3 %collective-permute-start.18 = (bf16[128,2048]{1,0:T(8,128)(2,1)S(1)}, bf16[128,2048]{1,0:T(8,128)(2,1)S(1)}, u32[]{:S(2)}, u32[]{:S(2)}) collective-permute-start(bf16[128,2048]{1,0:T(8,128)(2,1)S(1)} %pad_maximum_fusion.a_ref), channel_id=1, source_target_pairs={{0,1},{1,0},{2,3},{3,2},{4,5},{5,4},{6,7},{7,6},{8,9},{9,8},{10,11... | collective-permute-start | bytes 1572872 | tf_op jit(solution)/shard_map/ppermute | solution.py:28
  97.0 2.3 %collective-permute-done.21.a_ref = bf16[128,2048]{1,0:T(8,128)(2,1)S(1)} collective-permute-done((bf16[128,2048]{1,0:T(8,128)(2,1)S(1)}, bf16[128,2048]{1,0:T(8,128)(2,1)S(1)}, u32[]{:S(2)}, u32[]{:S(2)}) %collective-permute-start.21) | collective-permute-done | bytes 524320 | tf_op jit(solution)/shard_map/ppermute | solution.py:28
  99.2 3.2 %collective-permute-start.22 = (bf16[128,2048]{1,0:T(8,128)(2,1)S(1)}, bf16[128,2048]{1,0:T(8,128)(2,1)S(1)}, u32[]{:S(2)}, u32[]{:S(2)}) collective-permute-start(bf16[128,2048]{1,0:T(8,128)(2,1)S(1)} %collective-permute-done.21.a_ref), channel_id=1, source_target_pairs={{0,1},{1,0},{2,3},{3,2},{4,5},{5,4},{6,7},{7,6},{8,9},{9,8},{10,11... | collective-permute-start | bytes 1572872 | tf_op jit(solution)/shard_map/ppermute | solution.py:28
  102.4 1.2 %collective-permute-done.19.a_ref = bf16[128,2048]{1,0:T(8,128)(2,1)S(1)} collective-permute-done((bf16[128,2048]{1,0:T(8,128)(2,1)S(1)}, bf16[128,2048]{1,0:T(8,128)(2,1)S(1)}, u32[]{:S(2)}, u32[]{:S(2)}) %collective-permute-start.19) | collective-permute-done | bytes 524320 | tf_op jit(solution)/shard_map/ppermute | solution.py:28
  103.6 3.5 %collective-permute-start.20 = (bf16[128,2048]{1,0:T(8,128)(2,1)S(1)}, bf16[128,2048]{1,0:T(8,128)(2,1)S(1)}, u32[]{:S(2)}, u32[]{:S(2)}) collective-permute-start(bf16[128,2048]{1,0:T(8,128)(2,1)S(1)} %collective-permute-done.19.a_ref), channel_id=1, source_target_pairs={{0,1},{1,0},{2,3},{3,2},{4,5},{5,4},{6,7},{7,6},{8,9},{9,8},{10,11... | collective-permute-start | bytes 1572872 | tf_op jit(solution)/shard_map/ppermute | solution.py:28
  107.9 3.0 %shard_map.51.rows_ref.refs_4_ = bf16[1024,1024]{1,0:T(8,128)(2,1)S(1)} custom-call(s32[8,1024]{1,0:T(8,128)S(1)} %get-tuple-element.24.own_ref, bf16[1024,1280]{1,0:T(8,128)(2,1)S(1)} %bitcast.7), custom_call_target="tpu_custom_call" | custom-call | flops 2147483648 | bytes 4194304 | tf_op jit(solution)/shard_map/pallas_call | solution.py:295
  111.0 1.6 %shard_map.52.refs_0_ = bf16[1024,256]{1,0:T(8,128)(2,1)S(1)} custom-call(bf16[128,2048]{1,0:T(8,128)(2,1)S(1)} %pad_maximum_fusion.a_ref, bf16[128,2048]{1,0:T(8,128)(2,1)S(1)} %collective-permute-done.18.b_ref, bf16[2,8,1,128,1024]{4,3,2,1,0:T(8,128)(2,1)S(1)} %copy-done, bf16[1024,1024]{1,0:T(8,128)(2,1)S(1)} %shard_map.51.rows_ref.refs_4_), custom_call_target="tpu_custom_call" | custom-call | flops 1073741824 | bytes 2097152 | tf_op jit(solution)/shard_map/pallas_call | solution.py:295
  112.6 1.6 %shard_map.54.refs_2_ = bf16[1024,256]{1,0:T(8,128)(2,1)S(1)} custom-call(bf16[128,2048]{1,0:T(8,128)(2,1)S(1)} %collective-permute-done.21.a_ref, bf16[128,2048]{1,0:T(8,128)(2,1)S(1)} %collective-permute-done.22.b_ref, bf16[2,8,1,128,1024]{4,3,2,1,0:T(8,128)(2,1)S(1)} %copy-done, bf16[1024,1024]{1,0:T(8,128)(2,1)S(1)} %shard_map.51.rows_ref.refs_4_), custom_call_target="tpu_custom_call" | custom-call | flops 1073741824 | bytes 2097152 | tf_op jit(solution)/shard_map/pallas_call | solution.py:295
  114.2 1.6 %shard_map.53.refs_1_ = bf16[1024,256]{1,0:T(8,128)(2,1)S(1)} custom-call(bf16[128,2048]{1,0:T(8,128)(2,1)S(1)} %collective-permute-done.19.a_ref, bf16[128,2048]{1,0:T(8,128)(2,1)S(1)} %collective-permute-done.20.b_ref, bf16[2,8,1,128,1024]{4,3,2,1,0:T(8,128)(2,1)S(1)} %copy-done, bf16[1024,1024]{1,0:T(8,128)(2,1)S(1)} %shard_map.51.rows_ref.refs_4_), custom_call_target="tpu_custom_call" | custom-call | flops 1073741824 | bytes 2097152 | tf_op jit(solution)/shard_map/pallas_call | solution.py:295
  115.7 2.8 %shard_map.55 = bf16[1024,1024]{1,0:T(8,128)(2,1)} custom-call(bf16[128,2048]{1,0:T(8,128)(2,1)S(1)} %collective-permute-done.16.a_ref, bf16[128,2048]{1,0:T(8,128)(2,1)S(1)} %collective-permute-done.17.b_ref, bf16[1024,256]{1,0:T(8,128)(2,1)S(1)} %shard_map.52.refs_0_, bf16[1024,256]{1,0:T(8,128)(2,1)S(1)} %shard_map.53.refs_1_, ...), custom_call_target="tpu_custom_call" | custom-call | flops 1073741824 | bytes 2097152 | tf_op jit(solution)/shard_map/pallas_call | solution.py:295
  (38 shorter events, 6.9 us)
Async XLA Ops:
  6.4 11.5 %copy-start.2 = (bf16[128,1024]{1,0:T(8,128)(2,1)S(1)}, bf16[128,1024]{1,0:T(8,128)(2,1)}, u32[]{:S(2)}) copy-start(bf16[128,1024]{1,0:T(8,128)(2,1)} %get-tuple-element.20) | copy-start | bytes 786436
  6.4 57.8 %all-to-all-start = ((bf16[128,8,1280]{2,1,0:T(8,128)(2,1)}), bf16[128,8,1280]{2,1,0:T(8,128)(2,1)S(1)}, u32[]{:S(2)}, u32[]{:S(2)}) async-start(bf16[128,8,1280]{2,1,0:T(8,128)(2,1)} %bitcast.8), calls=%async_computation | async-start | bytes 5242880 | tf_op jit(solution)/shard_map/all_to_all | solution.py:369
  17.9 34.6 %collective-permute-start.5 = (bf16[128,1024]{1,0:T(8,128)(2,1)S(1)}, bf16[128,1024]{1,0:T(8,128)(2,1)S(1)}, u32[]{:S(2)}, u32[]{:S(2)}) collective-permute-start(bf16[128,1024]{1,0:T(8,128)(2,1)S(1)} %copy-done.2), channel_id=1, source_target_pairs={{0,64},{1,17},{2,66},{3,19},{4,68},{5,21},{6,70},{7,23},{8,72},{9,... | collective-permute-start | bytes 786440 | tf_op jit(solution)/shard_map/ppermute | solution.py:28
  20.8 33.9 %collective-permute-start.4 = (bf16[128,1024]{1,0:T(8,128)(2,1)S(1)}, bf16[128,1024]{1,0:T(8,128)(2,1)S(1)}, u32[]{:S(2)}, u32[]{:S(2)}) collective-permute-start(bf16[128,1024]{1,0:T(8,128)(2,1)S(1)} %copy-done.2), channel_id=1, source_target_pairs={{0,96},{1,25},{2,98},{3,27},{4,100},{5,29},{6,102},{7,31},{8,104},... | collective-permute-start | bytes 786440 | tf_op jit(solution)/shard_map/ppermute | solution.py:28
  21.7 33.7 %collective-permute-start.3 = (bf16[128,1024]{1,0:T(8,128)(2,1)S(1)}, bf16[128,1024]{1,0:T(8,128)(2,1)}, u32[]{:S(2)}, u32[]{:S(2)}) collective-permute-start(bf16[128,1024]{1,0:T(8,128)(2,1)S(1)} %copy-done.2), channel_id=1, source_target_pairs={{0,32},{1,9},{2,34},{3,11},{4,36},{5,13},{6,38},{7,15},{8,40},{9,1... | collective-permute-start | bytes 786440 | tf_op jit(solution)/shard_map/ppermute | solution.py:28
  54.8 0.7 copy-start.3
  56.5 12.3 %collective-permute-start.8 = (bf16[128,1024]{1,0:T(8,128)(2,1)S(1)}, bf16[128,1024]{1,0:T(8,128)(2,1)S(1)}, u32[]{:S(2)}, u32[]{:S(2)}) collective-permute-start(bf16[128,1024]{1,0:T(8,128)(2,1)S(1)} %select_select_fusion.l0), channel_id=1, source_target_pairs={{1,65},{3,67},{5,69},{7,71},{8,24},{9,73},{10,26},{11,75},{12,28},... | collective-permute-start | bytes 786440 | tf_op jit(solution)/shard_map/ppermute | solution.py:28
  60.9 10.5 %collective-permute-start.7 = (bf16[128,1024]{1,0:T(8,128)(2,1)S(1)}, bf16[128,1024]{1,0:T(8,128)(2,1)S(1)}, u32[]{:S(2)}, u32[]{:S(2)}) collective-permute-start(bf16[128,1024]{1,0:T(8,128)(2,1)S(1)} %select_select_fusion.l0), channel_id=1, source_target_pairs={{1,97},{3,99},{5,101},{7,103},{8,16},{9,105},{10,18},{11,107},{12,... | collective-permute-start | bytes 786440 | tf_op jit(solution)/shard_map/ppermute | solution.py:28
  62.2 9.2 %collective-permute-start.6 = (bf16[128,1024]{1,0:T(8,128)(2,1)S(1)}, bf16[128,1024]{1,0:T(8,128)(2,1)}, u32[]{:S(2)}, u32[]{:S(2)}) collective-permute-start(bf16[128,1024]{1,0:T(8,128)(2,1)S(1)} %select_select_fusion.l0), channel_id=1, source_target_pairs={{1,33},{3,35},{5,37},{7,39},{8,0},{9,41},{10,2},{11,43},{12,4},{13... | collective-permute-start | bytes 786440 | tf_op jit(solution)/shard_map/ppermute | solution.py:28
  64.8 6.6 %collective-permute-start.2 = (bf16[64,256]{1,0:T(8,128)(2,1)S(1)}, bf16[64,256]{1,0:T(8,128)(2,1)S(1)}, u32[]{:S(2)}, u32[]{:S(2)}) collective-permute-start(bf16[64,256]{1,0:T(8,128)(2,1)S(1)} %get-tuple-element.16.p0), channel_id=1, source_target_pairs={{0,4},{1,5},{2,6},{3,7},{4,0},{5,1},{6,2},{7,3},{8,12},{9,13},{10,... | collective-permute-start | bytes 98312 | tf_op jit(solution)/shard_map/ppermute | solution.py:28
  68.2 4.0 %collective-permute-start.1 = (bf16[64,256]{1,0:T(8,128)(2,1)S(1)}, bf16[64,256]{1,0:T(8,128)(2,1)S(1)}, u32[]{:S(2)}, u32[]{:S(2)}) collective-permute-start(bf16[64,256]{1,0:T(8,128)(2,1)S(1)} %get-tuple-element.16.p0), channel_id=1, source_target_pairs={{0,6},{1,7},{2,4},{3,5},{4,2},{5,3},{6,0},{7,1},{8,14},{9,15},{10,... | collective-permute-start | bytes 98312 | tf_op jit(solution)/shard_map/ppermute | solution.py:28
  68.7 3.5 %collective-permute-start = (bf16[64,256]{1,0:T(8,128)(2,1)S(1)}, bf16[64,256]{1,0:T(8,128)(2,1)S(1)}, u32[]{:S(2)}, u32[]{:S(2)}) collective-permute-start(bf16[64,256]{1,0:T(8,128)(2,1)S(1)} %get-tuple-element.16.p0), channel_id=1, source_target_pairs={{0,2},{1,3},{2,0},{3,1},{4,6},{5,7},{6,4},{7,5},{8,10},{9,11},{10,... | collective-permute-start | bytes 98312 | tf_op jit(solution)/shard_map/ppermute | solution.py:28
  68.9 2.2 %copy-start.1 = (bf16[2,1024,1024]{2,1,0:T(8,128)(2,1)S(1)}, bf16[2,1024,1024]{2,1,0:T(8,128)(2,1)}, u32[]{:S(2)}) copy-start(bf16[2,1024,1024]{2,1,0:T(8,128)(2,1)} %source_hbm) | copy-start | bytes 12582916
  73.5 1.3 %collective-permute-start.9 = (bf16[64,128]{1,0:T(8,128)(2,1)S(1)}, bf16[64,128]{1,0:T(8,128)(2,1)S(1)}, u32[]{:S(2)}, u32[]{:S(2)}) collective-permute-start(bf16[64,128]{1,0:T(8,128)(2,1)S(1)} %get-tuple-element.21), channel_id=1, source_target_pairs={{0,1},{1,0},{2,3},{3,2},{4,5},{5,4},{6,7},{7,6},{8,9},{9,8},{10,11... | collective-permute-start | bytes 49160 | tf_op jit(solution)/shard_map/ppermute | solution.py:28
  74.8 4.3 %collective-permute-start.12 = (bf16[128,128]{1,0:T(8,128)(2,1)S(1)}, bf16[128,128]{1,0:T(8,128)(2,1)S(1)}, u32[]{:S(2)}, u32[]{:S(2)}) collective-permute-start(bf16[128,128]{1,0:T(8,128)(2,1)S(1)} %constant_dynamic-update-slice_fusion.p0), channel_id=1, source_target_pairs={{0,4},{1,5},{2,6},{3,7},{4,0},{5,1},{6,2},{7,3},{8,12},{9,13},{10,... | collective-permute-start | bytes 98312 | tf_op jit(solution)/shard_map/ppermute | solution.py:28
  77.2 4.0 %collective-permute-start.11 = (bf16[128,128]{1,0:T(8,128)(2,1)S(1)}, bf16[128,128]{1,0:T(8,128)(2,1)S(1)}, u32[]{:S(2)}, u32[]{:S(2)}) collective-permute-start(bf16[128,128]{1,0:T(8,128)(2,1)S(1)} %constant_dynamic-update-slice_fusion.p0), channel_id=1, source_target_pairs={{0,6},{1,7},{2,4},{3,5},{4,2},{5,3},{6,0},{7,1},{8,14},{9,15},{10,... | collective-permute-start | bytes 98312 | tf_op jit(solution)/shard_map/ppermute | solution.py:28
  77.7 3.5 %collective-permute-start.10 = (bf16[128,128]{1,0:T(8,128)(2,1)S(1)}, bf16[128,128]{1,0:T(8,128)(2,1)S(1)}, u32[]{:S(2)}, u32[]{:S(2)}) collective-permute-start(bf16[128,128]{1,0:T(8,128)(2,1)S(1)} %constant_dynamic-update-slice_fusion.p0), channel_id=1, source_target_pairs={{0,2},{1,3},{2,0},{3,1},{4,6},{5,7},{6,4},{7,5},{8,10},{9,11},{10,... | collective-permute-start | bytes 98312 | tf_op jit(solution)/shard_map/ppermute | solution.py:28
  81.9 5.5 %collective-permute-start.15 = (bf16[32,2048]{1,0:T(8,128)(2,1)S(1)}, bf16[32,2048]{1,0:T(8,128)(2,1)S(1)}, u32[]{:S(2)}, u32[]{:S(2)}) collective-permute-start(bf16[32,2048]{1,0:T(8,128)(2,1)S(1)} %shard_map.50), channel_id=1, source_target_pairs={{0,64},{1,17},{2,66},{3,19},{4,68},{5,21},{6,70},{7,23},{8,72},{9,... | collective-permute-start | bytes 393224 | tf_op jit(solution)/shard_map/ppermute | solution.py:28
  82.7 6.3 %collective-permute-start.14 = (bf16[32,2048]{1,0:T(8,128)(2,1)S(1)}, bf16[32,2048]{1,0:T(8,128)(2,1)S(1)}, u32[]{:S(2)}, u32[]{:S(2)}) collective-permute-start(bf16[32,2048]{1,0:T(8,128)(2,1)S(1)} %shard_map.50), channel_id=1, source_target_pairs={{0,96},{1,25},{2,98},{3,27},{4,100},{5,29},{6,102},{7,31},{8,104},... | collective-permute-start | bytes 393224 | tf_op jit(solution)/shard_map/ppermute | solution.py:28
  85.1 4.1 %collective-permute-start.13 = (bf16[32,2048]{1,0:T(8,128)(2,1)S(1)}, bf16[32,2048]{1,0:T(8,128)(2,1)S(1)}, u32[]{:S(2)}, u32[]{:S(2)}) collective-permute-start(bf16[32,2048]{1,0:T(8,128)(2,1)S(1)} %shard_map.50), channel_id=1, source_target_pairs={{0,32},{1,9},{2,34},{3,11},{4,36},{5,13},{6,38},{7,15},{8,40},{9,1... | collective-permute-start | bytes 393224 | tf_op jit(solution)/shard_map/ppermute | solution.py:28
  89.3 10.0 %collective-permute-start.21 = (bf16[128,2048]{1,0:T(8,128)(2,1)S(1)}, bf16[128,2048]{1,0:T(8,128)(2,1)S(1)}, u32[]{:S(2)}, u32[]{:S(2)}) collective-permute-start(bf16[128,2048]{1,0:T(8,128)(2,1)S(1)} %pad_maximum_fusion.a_ref), channel_id=1, source_target_pairs={{0,16},{1,65},{2,18},{3,67},{4,20},{5,69},{6,22},{7,71},{8,24},{9,... | collective-permute-start | bytes 1572872 | tf_op jit(solution)/shard_map/ppermute | solution.py:28
  89.9 13.8 %collective-permute-start.19 = (bf16[128,2048]{1,0:T(8,128)(2,1)S(1)}, bf16[128,2048]{1,0:T(8,128)(2,1)S(1)}, u32[]{:S(2)}, u32[]{:S(2)}) collective-permute-start(bf16[128,2048]{1,0:T(8,128)(2,1)S(1)} %pad_maximum_fusion.a_ref), channel_id=1, source_target_pairs={{0,8},{1,33},{2,10},{3,35},{4,12},{5,37},{6,14},{7,39},{8,0},{9,41... | collective-permute-start | bytes 1572872 | tf_op jit(solution)/shard_map/ppermute | solution.py:28
  91.1 16.0 %collective-permute-start.16 = (bf16[128,2048]{1,0:T(8,128)(2,1)S(1)}, bf16[128,2048]{1,0:T(8,128)(2,1)S(1)}, u32[]{:S(2)}, u32[]{:S(2)}) collective-permute-start(bf16[128,2048]{1,0:T(8,128)(2,1)S(1)} %pad_maximum_fusion.a_ref), channel_id=1, source_target_pairs={{0,24},{1,97},{2,26},{3,99},{4,28},{5,101},{6,30},{7,103},{8,16},{... | collective-permute-start | bytes 1572872 | tf_op jit(solution)/shard_map/ppermute | solution.py:28
  92.7 18.3 %collective-permute-start.18 = (bf16[128,2048]{1,0:T(8,128)(2,1)S(1)}, bf16[128,2048]{1,0:T(8,128)(2,1)S(1)}, u32[]{:S(2)}, u32[]{:S(2)}) collective-permute-start(bf16[128,2048]{1,0:T(8,128)(2,1)S(1)} %pad_maximum_fusion.a_ref), channel_id=1, source_target_pairs={{0,1},{1,0},{2,3},{3,2},{4,5},{5,4},{6,7},{7,6},{8,9},{9,8},{10,11... | collective-permute-start | bytes 1572872 | tf_op jit(solution)/shard_map/ppermute | solution.py:28
  99.2 13.3 %collective-permute-start.22 = (bf16[128,2048]{1,0:T(8,128)(2,1)S(1)}, bf16[128,2048]{1,0:T(8,128)(2,1)S(1)}, u32[]{:S(2)}, u32[]{:S(2)}) collective-permute-start(bf16[128,2048]{1,0:T(8,128)(2,1)S(1)} %collective-permute-done.21.a_ref), channel_id=1, source_target_pairs={{0,1},{1,0},{2,3},{3,2},{4,5},{5,4},{6,7},{7,6},{8,9},{9,8},{10,11... | collective-permute-start | bytes 1572872 | tf_op jit(solution)/shard_map/ppermute | solution.py:28
  103.6 10.5 %collective-permute-start.20 = (bf16[128,2048]{1,0:T(8,128)(2,1)S(1)}, bf16[128,2048]{1,0:T(8,128)(2,1)S(1)}, u32[]{:S(2)}, u32[]{:S(2)}) collective-permute-start(bf16[128,2048]{1,0:T(8,128)(2,1)S(1)} %collective-permute-done.19.a_ref), channel_id=1, source_target_pairs={{0,1},{1,0},{2,3},{3,2},{4,5},{5,4},{6,7},{7,6},{8,9},{9,8},{10,11... | collective-permute-start | bytes 1572872 | tf_op jit(solution)/shard_map/ppermute | solution.py:28
  107.1 8.6 %collective-permute-start.17 = (bf16[128,2048]{1,0:T(8,128)(2,1)S(1)}, bf16[128,2048]{1,0:T(8,128)(2,1)S(1)}, u32[]{:S(2)}, u32[]{:S(2)}) collective-permute-start(bf16[128,2048]{1,0:T(8,128)(2,1)S(1)} %collective-permute-done.16.a_ref), channel_id=1, source_target_pairs={{0,1},{1,0},{2,3},{3,2},{4,5},{5,4},{6,7},{7,6},{8,9},{9,8},{10,11... | collective-permute-start | bytes 1572872 | tf_op jit(solution)/shard_map/ppermute | solution.py:28
  107.9 3.1 %copy-start = (bf16[2,8,1,128,1024]{4,3,2,1,0:T(8,128)(2,1)S(1)}, bf16[2,8,1,128,1024]{4,3,2,1,0:T(8,128)(2,1)}, u32[]{:S(2)}) copy-start(bf16[2,8,1,128,1024]{4,3,2,1,0:T(8,128)(2,1)} %refs_3_.1) | copy-start | bytes 12582916
